TPU v7x, 32 devices: a whole 2x2x4 slice. The times are simulated.
32 devices in a mesh: hyd: 4 (over y, x), src: 8 (over z, core).
Axes of the slice: x: 2, y: 2, z: 4, core: 2. Of those that a mesh axis runs over, the one named last changes fastest.
Arguments:
- record: float32 [2, 4096, 128], P(None, 'hyd'), may hold values from -6 to 6
- tile_data: bfloat16 [4, 8, 24, 2, 128, 128], P('hyd', 'src'), may hold values from -0.125 to 0.125
- tile_rows: int32 [4, 8, 24], P('hyd', 'src'), may hold values from 0 to 7, as said below
- tile_cols: int32 [4, 8, 24], P('hyd', 'src'), may hold values from 0 to 7, as said below
- tile_counts: int32 [4, 8], P('hyd', 'src'), may hold values from 3 to 24, as said below
Outputs:
- solution: float32 [2, 8192, 128], P(None, 'src')
- residual: float32 [2, 4096, 128], P(None, 'hyd')
Inputs may be any that keep to these rules, and one draw needn't show every extreme that they name: `tile_rows`: together with tile_cols, the 24 slots of one device name different tile pairs. `tile_cols`: column tiles below 4 belong to the upper layer. `tile_counts`: slots at and beyond a device's count hold no tiles of A.
All inputs are finite; a program needn't handle non-finite values.
Results may differ from a plain program's by a relative error of at most 0.014.
Values may be sent and summed in bfloat16 or wider, within the bound.
No kernel may reach another device: no remote copies, remote signals or barrier semaphores. Data moves between devices by JAX's collectives and lax.ppermute only.
A program may use at most 64 MiB of HBM per device.

v0:
```python
import jax
import jax.numpy as jnp
from jax import lax
from jax.sharding import PartitionSpec as P

SRC_DEV = 512
ITERS = 3


EPSILON = 1e-06


def place_tiles(total, products, target, usable):
    for slot in range(products.shape[1]):
        current = lax.dynamic_slice_in_dim(total, target[slot], 1, 1)
        added = current + products[:, slot][:, None] * usable[slot]
        total = lax.dynamic_update_slice_in_dim(total, added, target[slot], 1)
    return total


def tile_forward(tile_group_all, rows_list, cols_list, first_slot, end_slot, vector_b, row_tiles):
    group_slots = 8
    tile_size = tile_group_all.shape[-1]
    shot_count = vector_b.shape[2]
    col_tiles = vector_b.shape[1] // tile_size
    blocks = vector_b.reshape(2, col_tiles, tile_size, shot_count)

    def one_turn(group, total):
        start = group * group_slots
        tile_group = lax.dynamic_slice_in_dim(tile_group_all, start, group_slots, 0)
        col_pick = lax.dynamic_slice_in_dim(cols_list, start, group_slots, 0)
        row_pick = lax.dynamic_slice_in_dim(rows_list, start, group_slots, 0)
        slot_ids = start + jnp.arange(group_slots)
        usable = ((slot_ids >= first_slot) & (slot_ids < end_slot)).astype(jnp.float32)
        chosen = jnp.take(blocks, col_pick, axis=1)
        real_part = jnp.einsum(
            "gij,gjn->gin", tile_group[:, 0], chosen[0], preferred_element_type=jnp.float32
        ) - jnp.einsum(
            "gij,gjn->gin", tile_group[:, 1], chosen[1], preferred_element_type=jnp.float32
        )
        imag_part = jnp.einsum(
            "gij,gjn->gin", tile_group[:, 0], chosen[1], preferred_element_type=jnp.float32
        ) + jnp.einsum(
            "gij,gjn->gin", tile_group[:, 1], chosen[0], preferred_element_type=jnp.float32
        )
        return place_tiles(total, jnp.stack([real_part, imag_part]), row_pick, usable)

    empty = jnp.zeros((2, row_tiles, tile_size, shot_count), jnp.float32)
    result = lax.fori_loop(
        first_slot // group_slots, (end_slot + group_slots - 1) // group_slots, one_turn, empty
    )
    return result.reshape(2, row_tiles * tile_size, shot_count)


def tile_adjoint(tile_group_all, rows_list, cols_list, first_slot, end_slot, residual_b, col_tiles):
    group_slots = 8
    tile_size = tile_group_all.shape[-1]
    shot_count = residual_b.shape[2]
    row_tiles = residual_b.shape[1] // tile_size
    blocks = residual_b.reshape(2, row_tiles, tile_size, shot_count)

    def one_turn(group, total):
        start = group * group_slots
        tile_group = lax.dynamic_slice_in_dim(tile_group_all, start, group_slots, 0)
        col_pick = lax.dynamic_slice_in_dim(cols_list, start, group_slots, 0)
        row_pick = lax.dynamic_slice_in_dim(rows_list, start, group_slots, 0)
        slot_ids = start + jnp.arange(group_slots)
        usable = ((slot_ids >= first_slot) & (slot_ids < end_slot)).astype(jnp.float32)
        chosen = jnp.take(blocks, row_pick, axis=1)
        real_part = jnp.einsum(
            "gji,gjn->gin", tile_group[:, 0], chosen[0], preferred_element_type=jnp.float32
        ) + jnp.einsum(
            "gji,gjn->gin", tile_group[:, 1], chosen[1], preferred_element_type=jnp.float32
        )
        imag_part = jnp.einsum(
            "gji,gjn->gin", tile_group[:, 0], chosen[1], preferred_element_type=jnp.float32
        ) - jnp.einsum(
            "gji,gjn->gin", tile_group[:, 1], chosen[0], preferred_element_type=jnp.float32
        )
        return place_tiles(total, jnp.stack([real_part, imag_part]), col_pick, usable)

    empty = jnp.zeros((2, col_tiles, tile_size, shot_count), jnp.float32)
    result = lax.fori_loop(
        first_slot // group_slots, (end_slot + group_slots - 1) // group_slots, one_turn, empty
    )
    return result.reshape(2, col_tiles * tile_size, shot_count)


def body(record, tile_data, tile_rows, tile_cols, tile_counts):
    own_tiles = tile_data[0, 0]
    own_rows = tile_rows[0, 0]
    own_cols = tile_cols[0, 0]
    own_count = tile_counts[0, 0]
    tile_size = own_tiles.shape[-1]
    row_tiles = record.shape[1] // tile_size
    col_tiles = 2 * SRC_DEV // tile_size

    def gradient_of(residual_b):
        partial_value = tile_adjoint(
            own_tiles, own_rows, own_cols, 0, own_count, residual_b, col_tiles
        )
        gradient = lax.psum(partial_value, "hyd")
        squares = lax.psum(jnp.sum(gradient * gradient, axis=(0, 1)), "src")
        return (gradient, squares)

    residual = record
    gradient, gamma_now = gradient_of(record.astype(jnp.bfloat16))
    direction = gradient
    solution = jnp.zeros_like(gradient)
    for step_index in range(ITERS):
        direction_b = direction.astype(jnp.bfloat16)
        forward_partial_value = tile_forward(
            own_tiles, own_rows, own_cols, 0, own_count, direction_b, row_tiles
        )
        image = lax.psum(forward_partial_value, "src")
        image_sq = lax.psum(jnp.sum(image * image, axis=(0, 1)), "hyd")
        image, image_sq = (image, image_sq)
        alpha_step = gamma_now / (image_sq + EPSILON)
        solution = solution + alpha_step * direction
        residual = residual - alpha_step * image
        if step_index + 1 < ITERS:
            residual_b = residual.astype(jnp.bfloat16)
            gradient, gamma_next = gradient_of(residual_b)
            direction = gradient + gamma_next / (gamma_now + EPSILON) * direction
            gamma_now = gamma_next
    return (solution, residual)


def solution(mesh):
    in_specs = (
        P(None, "hyd", None),
        P("hyd", "src", None, None, None, None),
        P("hyd", "src", None),
        P("hyd", "src", None),
        P("hyd", "src"),
    )
    out_specs = (P(None, "src", None), P(None, "hyd", None))
    return jax.shard_map(body, mesh=mesh, in_specs=in_specs, out_specs=out_specs, check_vma=False)
```

profile of v0, /device:TPU:0, one launch (start us, length us, event | category | flops | bytes accessed | tf_op | source)
XLA Modules:
  0.0 1105.5 jit_solution(888676539581461893)
XLA Ops:
  7.9 2.7 copy.18
  11.3 56.1 %while.60 = (s32[]{:T(128)}, f32[2,8,128,128]{3,2,1,0:T(8,128)S(1)}, s32[]{:T(128)}, s32[24]{0:T(128)S(1)}, bf16[24,2,128,128]{2,3,0,1:T(8,128)(2,1)}, /*index=5...) while((s32[]{:T(128)}, ...), condition=%wide.region_1.3_spmd, body=%wide.region_0.2_spmd.sunk | while | flops 135529568 | bytes 17830816 | solution.py:83
  70.0 80.8 %all-reduce.7.cloned.1.call-done = f32[2,1024,128]{2,1,0:T(8,128)} async-done(((f32[2,1024,128]{2,1,0:T(8,128)}), f32[2,1024,128]{2,1,0:T(8,128)}) %all-reduce.7.cloned.1.call-update) | async-done | bytes 1048592 | tf_op jit(solution)/shard_map/psum | solution.py:102
  150.9 2.5 multiply_reduce_fusion.5
  154.5 76.0 %while.61 = (s32[]{:T(128)}, f32[2,8,128,128]{3,2,1,0:T(8,128)}, s32[]{:T(128)}, s32[24]{0:T(128)S(1)}, bf16[24,2,128,128]{3,2,0,1:T(8,128)(2,1)S(1)}, /*index=5...) while((s32[]{:T(128)}, f32[2,8,128,128]{3,2,1,0:T(8,128)}, ...), condition=%wide.region_6.8_spmd, body=%wide.region_5.7_spmd.sunk | while | flops 135529568 | bytes 17834880 | solution.py:49
  186.3 2.3 fusion.374
  224.3 2.3 fusion.374
  230.5 54.3 %psum.85 = f32[128]{0:T(128)S(1)} all-reduce(f32[128]{0:T(128)S(1)} %get-tuple-element.527), channel_id=1, replica_groups=mesh['hyd'=4,'src'=8] {'src'}, use_global_device_ids=true, to_apply=%region_4.6 | all-reduce | flops 128 | bytes 1024 | tf_op jit(solution)/shard_map/psum | solution.py:103
  284.8 42.9 %all-reduce.9.cloned.1.call-done = f32[2,1024,128]{2,1,0:T(8,128)} async-done(((f32[2,1024,128]{2,1,0:T(8,128)}), f32[2,1024,128]{2,1,0:T(8,128)}) %all-reduce.9.cloned.1.call-update) | async-done | bytes 1048592 | tf_op jit(solution)/shard_map/psum | solution.py:115
  329.3 9.8 psum.87
  342.3 83.6 %while.62 = (s32[]{:T(128)}, f32[2,8,128,128]{3,2,1,0:T(8,128)}, s32[]{:T(128)}, s32[24]{0:T(128)S(1)}, bf16[24,2,128,128]{2,3,0,1:T(8,128)(2,1)}, /*index=5*/s3...) while((s32[]{:T(128)}, f32[2,8,128,128]{3,2,1,0:T(8,128)}, ...), condition=%wide.region_11.13_spmd, body=%wide.region_10.12_spmd.sunk | while | flops 135529568 | bytes 17834880 | solution.py:83
  378.0 2.3 fusion.389
  419.8 2.3 fusion.389
  426.0 91.7 %all-reduce.11.cloned.1.call-done = f32[2,1024,128]{2,1,0:T(8,128)} async-done(((f32[2,1024,128]{2,1,0:T(8,128)}), f32[2,1024,128]{2,1,0:T(8,128)}) %all-reduce.11.cloned.1.call-update) | async-done | bytes 1048592 | tf_op jit(solution)/shard_map/psum | solution.py:102
  519.2 16.2 %psum.89 = f32[128]{0:T(128)S(1)} all-reduce(f32[128]{0:T(128)S(1)} %multiply_reduce_fusion.3), channel_id=1, replica_groups=mesh['hyd'=4,'src'=8] {'src'}, use_global_device_ids=true, to_apply=%region_14.16 | all-reduce | flops 128 | bytes 1024 | tf_op jit(solution)/shard_map/psum | solution.py:103
  538.6 75.9 %while.63 = (s32[]{:T(128)}, f32[2,8,128,128]{3,2,1,0:T(8,128)}, s32[]{:T(128)}, s32[24]{0:T(128)S(1)}, bf16[24,2,128,128]{3,2,0,1:T(8,128)(2,1)S(1)}, /*index=5...) while((s32[]{:T(128)}, f32[2,8,128,128]{3,2,1,0:T(8,128)}, ...), condition=%wide.region_16.18_spmd, body=%wide.region_15.17_spmd.sunk | while | flops 135529568 | bytes 17834880 | solution.py:49
  558.1 2.3 fusion.401
  574.3 2.3 fusion.405
  612.3 2.3 fusion.405
  614.6 92.6 %all-reduce.13.cloned.1.call-done = f32[2,1024,128]{2,1,0:T(8,128)} async-done(((f32[2,1024,128]{2,1,0:T(8,128)}), f32[2,1024,128]{2,1,0:T(8,128)}) %all-reduce.13.cloned.1.call-update) | async-done | bytes 1048592 | tf_op jit(solution)/shard_map/psum | solution.py:115
  708.7 9.8 psum.91
  718.5 2.9 fusion.243
  722.5 82.2 %while.64 = (s32[]{:T(128)}, f32[2,8,128,128]{3,2,1,0:T(8,128)}, s32[]{:T(128)}, s32[24]{0:T(128)S(1)}, bf16[24,2,128,128]{2,3,0,1:T(8,128)(2,1)}, /*index=5*/s3...) while((s32[]{:T(128)}, f32[2,8,128,128]{3,2,1,0:T(8,128)}, ...), condition=%wide.region_21.23_spmd, body=%wide.region_20.22_spmd.sunk | while | flops 135529568 | bytes 17834880 | solution.py:83
  804.8 91.0 %all-reduce.15.cloned.1.call-done = f32[2,1024,128]{2,1,0:T(8,128)} async-done(((f32[2,1024,128]{2,1,0:T(8,128)}), f32[2,1024,128]{2,1,0:T(8,128)}) %all-reduce.15.cloned.1.call-update) | async-done | bytes 1048592 | tf_op jit(solution)/shard_map/psum | solution.py:102
  897.3 16.2 %psum.93 = f32[128]{0:T(128)S(1)} all-reduce(f32[128]{0:T(128)S(1)} %multiply_reduce_fusion.1), channel_id=1, replica_groups=mesh['hyd'=4,'src'=8] {'src'}, use_global_device_ids=true, to_apply=%region_24.26 | all-reduce | flops 128 | bytes 1024 | tf_op jit(solution)/shard_map/psum | solution.py:103
  913.5 2.5 fusion.240
  917.1 74.6 %while.65 = (s32[]{:T(128)}, f32[2,8,128,128]{3,2,1,0:T(8,128)}, s32[]{:T(128)}, s32[24]{0:T(128)S(1)}, bf16[24,2,128,128]{3,2,0,1:T(8,128)(2,1)S(1)}, /*index=5...) while((s32[]{:T(128)}, f32[2,8,128,128]{3,2,1,0:T(8,128)}, ...), condition=%wide.region_26.28_spmd, body=%wide.region_25.27_spmd.sunk | while | flops 135529568 | bytes 17834880 | solution.py:49
  948.1 2.3 fusion.434
  985.3 2.3 fusion.434
  991.8 92.0 %all-reduce.17.cloned.1.call-done = f32[2,1024,128]{2,1,0:T(8,128)} async-done(((f32[2,1024,128]{2,1,0:T(8,128)}), f32[2,1024,128]{2,1,0:T(8,128)}) %all-reduce.17.cloned.1.call-update) | async-done | bytes 1048592 | tf_op jit(solution)/shard_map/psum | solution.py:115
  1085.3 9.8 psum.95
  1095.1 3.6 multiply_subtract_fusion
  (271 shorter events, 265.6 us)
Async XLA Ops:
  7.2 143.7 %all-reduce.7.cloned.1.call-start = ((), (), s32[]{:S(2)}) async-start(), calls=%async_computation | async-start | bytes 2097152 | tf_op jit(solution)/shard_map/psum | solution.py:102
  7.9 2.7 copy-start.5
  10.6 0.7 copy-start.8
  10.6 0.7 copy-start.9
  67.4 1.0 copy-start
  68.4 259.4 %all-reduce.9.cloned.1.call-start = ((), (), s32[]{:S(2)}) async-start(), calls=%async_computation.1 | async-start | bytes 2097152 | tf_op jit(solution)/shard_map/psum | solution.py:115
  230.4 108.6 %copy-start.6 = (f32[2,1024,128]{2,1,0:T(8,128)S(1)}, f32[2,1024,128]{2,1,0:T(8,128)}, u32[]{:S(2)}) copy-start(f32[2,1024,128]{2,1,0:T(8,128)} %param.19) | copy-start | bytes 3145732
  230.5 287.2 %all-reduce.11.cloned.1.call-start = ((), (), s32[]{:S(2)}) async-start(), calls=%async_computation.2 | async-start | bytes 2097152 | tf_op jit(solution)/shard_map/psum | solution.py:102
  425.9 109.5 %copy-start.1 = (f32[2,1024,128]{2,1,0:T(8,128)S(1)}, f32[2,1024,128]{2,1,0:T(8,128)}, u32[]{:S(2)}) copy-start(f32[2,1024,128]{2,1,0:T(8,128)} %all-reduce.7.cloned.1.call-done) | copy-start | bytes 3145732
  425.9 281.3 %all-reduce.13.cloned.1.call-start = ((), (), s32[]{:S(2)}) async-start(), calls=%async_computation.3 | async-start | bytes 2097152 | tf_op jit(solution)/shard_map/psum | solution.py:115
  614.6 104.0 %copy-start.7 = (f32[2,1024,128]{2,1,0:T(8,128)S(1)}, f32[2,1024,128]{2,1,0:T(8,128)}, u32[]{:S(2)}) copy-start(f32[2,1024,128]{2,1,0:T(8,128)} %param.19) | copy-start | bytes 3145732
  614.6 281.3 %all-reduce.15.cloned.1.call-start = ((), (), s32[]{:S(2)}) async-start(), calls=%async_computation.4 | async-start | bytes 2097152 | tf_op jit(solution)/shard_map/psum | solution.py:102
  804.7 108.8 %copy-start.2 = (f32[2,1024,128]{2,1,0:T(8,128)S(1)}, f32[2,1024,128]{2,1,0:T(8,128)}, u32[]{:S(2)}) copy-start(f32[2,1024,128]{2,1,0:T(8,128)} %all-reduce.7.cloned.1.call-done) | copy-start | bytes 3145732
  804.7 279.1 %all-reduce.17.cloned.1.call-start = ((), (), s32[]{:S(2)}) async-start(), calls=%async_computation.5 | async-start | bytes 2097152 | tf_op jit(solution)/shard_map/psum | solution.py:115
  991.7 103.4 %copy-start.3 = (f32[2,1024,128]{2,1,0:T(8,128)S(1)}, f32[2,1024,128]{2,1,0:T(8,128)}, u32[]{:S(2)}) copy-start(f32[2,1024,128]{2,1,0:T(8,128)} %all-reduce.7.cloned.1.call-done) | copy-start | bytes 3145732
  991.7 103.4 %copy-start.4 = (f32[2,1024,128]{2,1,0:T(8,128)S(1)}, f32[2,1024,128]{2,1,0:T(8,128)}, u32[]{:S(2)}) copy-start(f32[2,1024,128]{2,1,0:T(8,128)} %all-reduce.11.cloned.1.call-done) | copy-start | bytes 3145732
Sparse Core Ops, SparseCore 0:
  68.5 82.3 all-reduce.6
  230.6 97.1 all-reduce.8
  426.0 91.6 all-reduce.10
  614.7 92.4 all-reduce.12
  804.9 90.9 all-reduce.14
  991.9 91.8 all-reduce.16
where the time goes:
time: 1120 us; the launch traced here: 1110 us
  waiting for transfers between devices  491 us (44%)
  other arithmetic  220 us (20%)
  loops' own time  183 us (16%)
  blocking collectives  116 us (10%)
  local copies, waits for them, and re-layouts  46.7 us (4%)
  matrix products  33.3 us (3%)
  between operations  14.9 us (1%)
    psum x3, waiting for transfers between devices, gradient_of(): gradient = lax.psum(partial_value, 'hyd')  264 us
    psum x3, waiting for transfers between devices, body(): image = lax.psum(forward_partial_value, 'src')  228 us
    dynamic_update_slice x96, other arithmetic, place_tiles(): total = lax.dynamic_update_slice_in_dim(total, added, target[slot], 1)  186 us
    another operation x3, loops' own time, tile_forward(): lax.fori_loop(first_slot // group_slots, (end_slot + group_slots - 1) //...  91.8 us
    another operation x3, loops' own time, tile_adjoint(): lax.fori_loop(first_slot // group_slots, (end_slot + group_slots - 1) //...  91.4 us
    psum x3, blocking collectives, gradient_of(): squares = lax.psum(jnp.sum(gradient * gradient, axis=(0, 1)), 'src')  86.7 us
    psum x3, blocking collectives, body(): image_sq = lax.psum(jnp.sum(image * image, axis=(0, 1)), 'hyd')  29.3 us
  transfers between devices with their start and end apart: 6, of which 6 were waited for; matrix products, arithmetic and copies ran while one was open for 0% of the time, Pallas kernels for 0%

commit v1 on v0

v1 whole, which is shorter than its diff:
```python
import functools

import jax
import jax.numpy as jnp
from jax import lax
from jax.experimental import pallas as pl
from jax.experimental.pallas import tpu as pltpu
from jax.sharding import PartitionSpec as P

SRC_DEV = 512
ITERS = 3
EPSILON = 1e-06
GROUP = 8
TAIL = 16

F32 = jnp.float32
BF16 = jnp.bfloat16


def call(kernel, name, outs, scratch, *ins):
    def space(dtype):
        return pltpu.SMEM if dtype == jnp.int32 else pltpu.VMEM

    return pl.pallas_call(
        kernel,
        name=name,
        out_shape=[jax.ShapeDtypeStruct(s, d) for s, d in outs],
        in_specs=[pl.BlockSpec(memory_space=space(a.dtype)) for a in ins],
        out_specs=[pl.BlockSpec(memory_space=pltpu.VMEM) for _ in outs],
        scratch_shapes=[pltpu.VMEM(s, d) for s, d in scratch],
    )(*ins)


def low_half(shape):
    return lax.broadcasted_iota(jnp.int32, shape, len(shape) - 1) < shape[-1] // 2


def turn(value):
    return pltpu.roll(value, value.shape[-1] // 2, value.ndim - 1)


def times_i(value, sign):
    rolled = turn(value)
    return jnp.where(low_half(value.shape), -sign * rolled, sign * rolled)


def both_parts(row):
    return row + turn(row)


def fold_squares(value):
    return jnp.sum((value * value).reshape(-1, 8, value.shape[-1]), axis=0)


def rows_of_norm(folded):
    row = both_parts(jnp.sum(folded, axis=0, keepdims=True))
    return jnp.broadcast_to(row, (8, folded.shape[-1]))


def norm_tail(norm):
    row = jnp.broadcast_to(norm[:1], (TAIL, norm.shape[-1]))
    high = row.astype(BF16).astype(F32)
    at = lax.broadcasted_iota(jnp.int32, row.shape, 0)
    return jnp.where(at == 0, high, jnp.where(at == 1, row - high, 0.0)).astype(BF16)


def norm_from(tail):
    tail = tail.astype(F32)
    return jnp.broadcast_to(tail[:1] + tail[1:2], (8, tail.shape[-1]))


def spans(size, count):
    return pl.ds(pl.multiple_of(count * size, size), size)


def slots(index_ref, step):
    used = index_ref[2, 0]

    def turn_of(group, carry):
        for lane in range(GROUP):
            slot = group * GROUP + lane
            step(slot, slot < used, index_ref[0, slot], index_ref[1, slot])
        return carry

    lax.fori_loop(0, (used + GROUP - 1) // GROUP, turn_of, 0)


def add_tile(acc_ref, weights, plain_ref, turned_ref, source, target):
    size = weights.shape[0]
    right = jnp.concatenate([plain_ref[spans(size, source), :], turned_ref[spans(size, source), :]], axis=0)
    at = spans(size, target)
    acc_ref[at, :] = acc_ref[at, :] + jnp.dot(weights, right, preferred_element_type=F32)


def put_chunk(chunk, plain_ref, turned_ref, at, sign):
    wide = chunk.astype(F32)
    plain_ref[at, :] = chunk
    turned_ref[at, :] = times_i(wide, sign).astype(BF16)
    return fold_squares(wide)


def pack_kernel(core_axis, tiles, record_ref, tile_ref, index_ref, turned_tile_ref, total_ref, plain_ref, turned_ref):
    core = lax.rem(lax.axis_index(core_axis), 2)
    rows = plain_ref.shape[0]
    for at in range(0, rows, 128):
        real = record_ref[0, pl.ds(at, 128), :]
        imag = record_ref[1, pl.ds(at, 128), :]
        first = jnp.where(core == 0, real, turn(real))
        second = jnp.where(core == 0, turn(imag), imag)
        packed = jnp.where(low_half(real.shape), first, second).astype(BF16)
        put_chunk(packed, plain_ref, turned_ref, pl.ds(at, 128), -1.0)
    total_ref[...] = jnp.zeros_like(total_ref)
    turn_tiles(tiles, tile_ref, index_ref, turned_tile_ref, total_ref, plain_ref, turned_ref)


def turn_tiles(tiles, tile_ref, index_ref, turned_tile_ref, total_ref, plain_ref, turned_ref):
    def step(slot, valid, row, col):
        weights = jnp.concatenate([tile_ref[slot, 0].T, tile_ref[slot, 1].T], axis=1)
        turned_tile_ref[slot] = weights
        add_tile(total_ref, weights, plain_ref, turned_ref, row, jnp.where(valid, col, tiles))

    slots(index_ref, step)


def first_adjoint_kernel(hyd_axis, hyds, tiles, tile_ref, index_ref, own_total_ref, plain_ref, turned_ref, *refs):
    turned_tile_ref, own_ref, sends, total_ref = refs[0], refs[1], refs[2:-1], refs[-1]
    total_ref[...] = jnp.zeros_like(total_ref)
    turn_tiles(tiles, tile_ref, index_ref, turned_tile_ref, total_ref, plain_ref, turned_ref)
    give_columns(hyd_axis, hyds, own_total_ref, total_ref, own_ref, sends, None)


def give_columns(hyd_axis, hyds, first_ref, second_ref, own_ref, sends, tail):
    here = lax.axis_index(hyd_axis)
    part = own_ref.shape[0] // 2
    own_ref[:part, :] = first_ref[spans(part, here), :]
    own_ref[part:, :] = second_ref[spans(part, here), :]
    for offset in range(1, hyds):
        there = here ^ offset
        send = sends[offset - 1]
        send[:part, :] = first_ref[spans(part, there), :].astype(BF16)
        send[part : 2 * part, :] = second_ref[spans(part, there), :].astype(BF16)
        if tail is not None:
            send[2 * part :, :] = tail


def adjoint_kernel(hyd_axis, core_axis, hyds, zs, tiles, *refs):
    tile_a, tile_b, index_a, index_b = refs[:4]
    chunks = refs[4 : 4 + zs]
    plain_ref, own_ref, norm_ref = refs[4 + zs : 7 + zs]
    sends = refs[7 + zs : 6 + zs + hyds]
    turned_ref, first_ref, second_ref = refs[6 + zs + hyds :]
    here = lax.axis_index(core_axis) // 2
    rows = chunks[0].shape[0]
    folded = jnp.zeros((8, plain_ref.shape[-1]), F32)
    for offset in range(zs):
        folded += put_chunk(chunks[offset][...], plain_ref, turned_ref, spans(rows, here ^ offset), -1.0)
    norm = rows_of_norm(folded)
    norm_ref[...] = norm
    for index_ref, tile_ref, total_ref in ((index_a, tile_a, first_ref), (index_b, tile_b, second_ref)):
        total_ref[...] = jnp.zeros_like(total_ref)

        def step(slot, valid, row, col):
            add_tile(total_ref, tile_ref[slot], plain_ref, turned_ref, row, jnp.where(valid, col, tiles))

        slots(index_ref, step)
    give_columns(hyd_axis, hyds, first_ref, second_ref, own_ref, sends, norm_tail(norm))


def forward_kernel(hyd_axis, core_axis, hyds, zs, tiles, *refs):
    tile_a, tile_b, index_a, index_b = refs[:4]
    chunks = refs[4 : 4 + hyds]
    plain_a, plain_b, own_ref, norm_ref = refs[4 + hyds : 8 + hyds]
    sends = refs[8 + hyds : 7 + hyds + zs]
    turned_a, turned_b, total_ref = refs[7 + hyds + zs :]
    here = lax.axis_index(hyd_axis)
    part = chunks[0].shape[0] // 2
    folded = jnp.zeros((8, plain_a.shape[-1]), F32)
    for offset in range(hyds):
        at = spans(part, here ^ offset)
        folded += put_chunk(chunks[offset][:part, :], plain_a, turned_a, at, 1.0)
        folded += put_chunk(chunks[offset][part:, :], plain_b, turned_b, at, 1.0)
    norm = rows_of_norm(folded)
    norm_ref[...] = norm
    total_ref[...] = jnp.zeros_like(total_ref)
    for index_ref, tile_ref, plain_ref, turned_ref in (
        (index_a, tile_a, plain_a, turned_a),
        (index_b, tile_b, plain_b, turned_b),
    ):

        def step(slot, valid, row, col):
            weights = jnp.concatenate([tile_ref[slot, 0], tile_ref[slot, 1]], axis=1)
            add_tile(total_ref, weights, plain_ref, turned_ref, col, jnp.where(valid, row, tiles))

        slots(index_ref, step)
    here = lax.axis_index(core_axis) // 2
    rows = own_ref.shape[0]
    own_ref[...] = total_ref[spans(rows, here), :]
    tail = norm_tail(norm)
    for offset in range(1, zs):
        sends[offset - 1][:rows, :] = total_ref[spans(rows, here ^ offset), :].astype(BF16)
        sends[offset - 1][rows:, :] = tail


def summed(own_ref, others):
    value = own_ref[...]
    for other in others:
        value = value + other[: own_ref.shape[0], :].astype(F32)
    return value


def norm_sum(own_norm, others, size):
    norm = own_norm
    for other in others:
        norm = norm + norm_from(other[size:, :])
    return norm


def start_kernel(others, own_ref, *refs):
    gradient = summed(own_ref, refs[:others])
    refs[-2][...] = gradient
    refs[-1][...] = gradient.astype(BF16)


def image_kernel(others, later, own_ref, norm_ref, *refs):
    ins, refs = refs[:others], refs[others:]
    image = summed(own_ref, ins)
    gamma = norm_sum(norm_ref[...], ins, own_ref.shape[0])
    if later:
        before_ref, gamma_ref = refs[:2]
        beta = gamma / (gamma_ref[...] + EPSILON)
        image = image + beta[:1] * before_ref[...]
        refs = refs[2:]
        refs[3][...] = beta
    refs[0][...] = image
    refs[1][...] = image.astype(BF16)
    refs[2][...] = gamma


def gradient_kernel(others, own_ref, norm_ref, *refs):
    ins, (before_ref, gamma_ref, wide_ref, narrow_ref, alpha_ref) = refs[:others], refs[others:]
    change = summed(own_ref, ins)
    alpha = gamma_ref[...] / (norm_sum(norm_ref[...], ins, own_ref.shape[0]) + EPSILON)
    gradient = before_ref[...] - alpha[:1] * change
    wide_ref[...] = gradient
    narrow_ref[...] = gradient.astype(BF16)
    alpha_ref[...] = alpha


def gather_kernel(core_axis, zs, *refs):
    chunks, (plain_ref, norm_ref) = refs[:zs], refs[zs:]
    here = lax.axis_index(core_axis) // 2
    rows = chunks[0].shape[0]
    folded = jnp.zeros((8, plain_ref.shape[-1]), F32)
    for offset in range(zs):
        chunk = chunks[offset][...]
        plain_ref[spans(rows, here ^ offset), :] = chunk
        folded += fold_squares(chunk.astype(F32))
    norm_ref[...] = rows_of_norm(folded)


def answer_kernel(core_axis, norms, record_ref, gamma_ref, *refs):
    norm = refs[0][...]
    for other in refs[1:norms]:
        norm = norm + other[...]
    refs = refs[norms:]
    alphas = [ref[...] for ref in refs[: ITERS - 1]] + [gamma_ref[...] / (norm + EPSILON)]
    refs = refs[ITERS - 1 :]
    betas = [ref[...] for ref in refs[: ITERS - 1]]
    refs = refs[ITERS - 1 :]
    own_g, pair_g, images = refs[:ITERS], refs[ITERS : 2 * ITERS], refs[2 * ITERS : 3 * ITERS]
    own_x, pair_x, wide_r, narrow_r = refs[3 * ITERS :]
    weights = [None] * ITERS
    weights[-1] = alphas[-1]
    for k in range(ITERS - 2, -1, -1):
        weights[k] = alphas[k] + betas[k] * weights[k + 1]
    core = lax.rem(lax.axis_index(core_axis), 2)
    for at in range(0, own_x.shape[0], 128):
        span = pl.ds(at, 128)
        own_x[span, :] = sum(w[:1] * g[span, :].astype(F32) for w, g in zip(weights, own_g))
        pair_x[span, :] = sum(w[:1] * g[span, :].astype(F32) for w, g in zip(weights, pair_g)).astype(BF16)
    for at in range(0, wide_r.shape[0], 128):
        span = pl.ds(at, 128)
        real, imag = record_ref[0, span, :], record_ref[1, span, :]
        first = jnp.where(core == 0, real, turn(real))
        second = jnp.where(core == 0, turn(imag), imag)
        residual = jnp.where(low_half(real.shape), first, second)
        for alpha, image in zip(alphas, images):
            residual = residual - alpha[:1] * image[span, :].astype(F32)
        wide_r[span, :] = residual
        narrow_r[span, :] = residual.astype(BF16)


def unpack_kernel(core_axis, own_x, own_r, pair_x, pair_r, x_ref, r_ref):
    core = lax.rem(lax.axis_index(core_axis), 2)
    for own, pair, out in ((own_x, pair_x, x_ref), (own_r, pair_r, r_ref)):
        for at in range(0, own.shape[0], 128):
            span = pl.ds(at, 128)
            mine, theirs = own[span, :], pair[span, :].astype(F32)
            first = jnp.where(core == 0, mine, theirs)
            second = jnp.where(core == 0, theirs, mine)
            low = low_half(mine.shape)
            out[0, span, :] = jnp.where(low, first, turn(second))
            out[1, span, :] = jnp.where(low, turn(first), second)


def solution(mesh):
    hyds, srcs = mesh.shape["hyd"], mesh.shape["src"]
    zs = srcs // 2

    def swap(value, axis, size, offset):
        return lax.ppermute(value, axis, [(i, i ^ offset) for i in range(size)])

    def over_hyd(values):
        return [swap(v, "hyd", hyds, o + 1) for o, v in enumerate(values)]

    def over_z(values):
        return [swap(v, "src", srcs, 2 * (o + 1)) for o, v in enumerate(values)]

    def body(record, tile_data, tile_rows, tile_cols, tile_counts):
        own_tiles = tile_data[0, 0]
        slot_count, _, size, _ = own_tiles.shape
        rows, shots = record.shape[1:]
        cols = 2 * SRC_DEV
        row_tiles, col_tiles = rows // size, cols // size
        row_part, col_part = rows // zs, cols // hyds
        norm = ((8, shots), F32)
        row_sends = [((row_part + TAIL, shots), BF16)] * (zs - 1)
        col_sends = [((2 * col_part + TAIL, shots), BF16)] * (hyds - 1)
        row_total, col_total = ((rows + size, shots), F32), ((cols + size, shots), F32)
        vector = lambda n, dtype: ((n, shots), dtype)

        index = jnp.stack([tile_rows[0, 0], tile_cols[0, 0], jnp.broadcast_to(tile_counts[0, 0], (slot_count,))])
        pair_index = swap(index, "src", srcs, 1)
        pair_tiles = swap(own_tiles, "src", srcs, 1)

        turned_shape = ((slot_count, size, 2 * size), BF16)
        turned_own, total, plain, turned = call(
            functools.partial(pack_kernel, "src", col_tiles), "pack",
            [turned_shape, col_total, vector(rows, BF16), vector(rows, BF16)], [],
            record, own_tiles, index,
        )
        turned_pair, own, *sends = call(
            functools.partial(first_adjoint_kernel, "hyd", hyds, col_tiles), "first_adjoint",
            [turned_shape, vector(2 * col_part, F32)] + [vector(2 * col_part, BF16)] * (hyds - 1), [col_total],
            pair_tiles, pair_index, total, plain, turned,
        )
        gradient, narrow = call(
            functools.partial(start_kernel, hyds - 1), "start",
            [vector(2 * col_part, F32), vector(2 * col_part, BF16)], [],
            own, *over_hyd(sends),
        )

        alphas, betas, own_g, pair_g, images = [], [], [], [], []
        image = gamma = None
        for step in range(ITERS):
            plain_a, plain_b, own, own_norm, *sends = call(
                functools.partial(forward_kernel, "hyd", "src", hyds, zs, row_tiles), "forward",
                [vector(cols, BF16), vector(cols, BF16), vector(row_part, F32), norm] + row_sends,
                [vector(cols, BF16), vector(cols, BF16), row_total],
                own_tiles, pair_tiles, index, pair_index, narrow, *over_hyd([narrow] * (hyds - 1)),
            )
            own_g.append(plain_a)
            pair_g.append(plain_b)
            outs = [vector(row_part, F32), vector(row_part, BF16), norm]
            before = [image, gamma] if step else []
            image, narrow, gamma, *beta = call(
                functools.partial(image_kernel, zs - 1, step > 0), "image",
                outs + [norm] * (step > 0), [],
                own, own_norm, *over_z(sends), *before,
            )
            betas += beta
            chunks = [narrow] + over_z([narrow] * (zs - 1))
            if step + 1 == ITERS:
                break
            plain, own, own_norm, *sends = call(
                functools.partial(adjoint_kernel, "hyd", "src", hyds, zs, col_tiles), "adjoint",
                [vector(rows, BF16), vector(2 * col_part, F32), norm] + col_sends,
                [vector(rows, BF16), col_total, col_total],
                turned_own, turned_pair, index, pair_index, *chunks,
            )
            images.append(plain)
            gradient, narrow, alpha = call(
                functools.partial(gradient_kernel, hyds - 1), "gradient",
                [vector(2 * col_part, F32), vector(2 * col_part, BF16), norm], [],
                own, own_norm, *over_hyd(sends), gradient, gamma,
            )
            alphas.append(alpha)

        plain, own_norm = call(functools.partial(gather_kernel, "src", zs), "gather", [vector(rows, BF16), norm], [], *chunks)
        images.append(plain)
        norms = [own_norm] + over_hyd([own_norm] * (hyds - 1))
        own_x, pair_x, wide_r, narrow_r = call(
            functools.partial(answer_kernel, "src", hyds), "answer",
            [vector(cols, F32), vector(cols, BF16), vector(rows, F32), vector(rows, BF16)], [],
            record, gamma, *norms, *alphas, *betas, *own_g, *pair_g, *images,
        )
        return call(
            functools.partial(unpack_kernel, "src"), "unpack",
            [((2, cols, shots), F32), ((2, rows, shots), F32)], [],
            own_x, wide_r, swap(pair_x, "src", srcs, 1), swap(narrow_r, "src", srcs, 1),
        )

    in_specs = (
        P(None, "hyd", None),
        P("hyd", "src", None, None, None, None),
        P("hyd", "src", None),
        P("hyd", "src", None),
        P("hyd", "src"),
    )
    out_specs = (P(None, "src", None), P(None, "hyd", None))
    return jax.shard_map(body, mesh=mesh, in_specs=in_specs, out_specs=out_specs, check_vma=False)
```

time: 1120 us -> 180 us (0.16); the launches traced: 1110 us -> 179 us
  waiting for transfers between devices: 491 us -> 63.4 us
  other arithmetic: 220 us -> 0.74 us
  loops' own time: 183 us -> 0 us
  blocking collectives: 116 us -> 0 us
  starting transfers between devices: 0.24 us -> 53.6 us
  Pallas kernels: 0 us -> 48 us
  local copies, waits for them, and re-layouts: 46.7 us -> 12.1 us
  matrix products: 33.3 us -> 0 us
  between operations: 14.9 us -> 1.42 us
    psum x6 -> x0, waiting for transfers between devices: 491 us -> none  [the longest x3 264 us: gradient_of(): gradient = lax.psum(partial_value, 'hyd')]
    dynamic_update_slice x96 -> x0, other arithmetic: 186 us -> none  [place_tiles(): total = lax.dynamic_update_slice_in_dim(total, added, target[slot], 1)]
    another operation x6 -> x0, loops' own time: 183 us -> none  [the longest x3 91.8 us: tile_forward(): lax.fori_loop(first_slot // group_slots, (end_slot + group_slots - 1) //...]
    psum x6 -> x0, blocking collectives: 116 us -> none  [the longest x3 86.7 us: gradient_of(): squares = lax.psum(jnp.sum(gradient * gradient, axis=(0, 1)), 'src')]
    ppermute x0 -> x43, waiting for transfers between devices: none -> 63.4 us  [swap(): return lax.ppermute(value, axis, [(i, i ^ offset) for i in range(size)])]
    ppermute x0 -> x43, starting transfers between devices: none -> 53.6 us  [swap(): return lax.ppermute(value, axis, [(i, i ^ offset) for i in range(size)])]
    pallas_call x0 -> x16, Pallas kernels: none -> 48 us  [call(): pl.pallas_call(kernel, name=name, out_shape=[jax.ShapeDtypeStruct(s, d) f...]
    dot_general x48 -> x0, matrix products: 33.3 us -> none  [the longest x6 7.04 us: one_turn(): jnp.einsum('gji,gjn->gin', tile_group[:, 1], chosen[1], preferred_element...]
  transfers between devices with their start and end apart: 6 -> 43, of which waited for: 6 -> 34; matrix products, arithmetic and copies ran while one was open for 0% -> 0% of each run, Pallas kernels for 0% -> 2%
where the time goes in v1:
time: 180 us; the launch traced here: 179 us
  waiting for transfers between devices  63.4 us (35%)
  starting transfers between devices  53.6 us (30%)
  Pallas kernels  48 us (27%)
  local copies, waits for them, and re-layouts  12.1 us (7%)
    ppermute x43, waiting for transfers between devices, swap(): return lax.ppermute(value, axis, [(i, i ^ offset) for i in range(size)])  63.4 us
    ppermute x43, starting transfers between devices, swap(): return lax.ppermute(value, axis, [(i, i ^ offset) for i in range(size)])  53.6 us
    pallas_call x16, Pallas kernels, call(): pl.pallas_call(kernel, name=name, out_shape=[jax.ShapeDtypeStruct(s, d) f...  48 us
    unnamed x88, local copies, waits for them, and re-layouts  12.1 us
  transfers between devices with their start and end apart: 43, of which 34 were waited for; matrix products, arithmetic and copies ran while one was open for 0% of the time, Pallas kernels for 2%

profile of v1, /device:TPU:0, one launch (start us, length us, event | category | flops | bytes accessed | tf_op | source)
XLA Modules:
  0.0 179.3 jit_solution(17920232702876995530)
XLA Ops:
  3.2 4.1 %pack.1 = (bf16[24,128,256]{2,1,0:T(8,128)(2,1)}, f32[1152,128]{1,0:T(8,128)}, bf16[1024,128]{1,0:T(8,128)(2,1)}, bf16[1024,128]{1,0:T(8,128)(2,1)}) custom-call(f32[2,1024,128]{2,1,0:T(8,128)} %record_ref.3, bf16[24,2,128,128]{3,2,1,0:T(8,128)(2,1)} %bitcast.8, s32[3,24]{1,0:T(4,128)} %copy-done.21), custom_call_target="tpu_custom_call" | custom-call | tf_op jit(solution)/shard_map/pack/pallas_call | solution.py:24
  8.5 3.8 %first_adjoint.1 = (bf16[24,128,256]{2,1,0:T(8,128)(2,1)}, f32[512,128]{1,0:T(8,128)}, bf16[512,128]{1,0:T(8,128)(2,1)}, bf16[512,128]{1,0:T(8,128)(2,1)}, bf16[512,128]{1,0:T(8,128)(2,1)}) custom-call(bf16[24,2,128,128]{3,2,1,0:T(8,128)(2,1)} %copy-done, s32[3,24]{1,0:T(4,128)} %copy-done.22, f32[1152,128]{1,0:T(8,128)} %get-tuple-element.68.own_total_ref, ...), custom_call_target="tpu_custom_call" | custom-call | tf_op jit(solution)/shard_map/first_adjoint/pallas_call | solution.py:24
  12.3 2.5 %collective-permute-start.2 = (bf16[512,128]{1,0:T(8,128)(2,1)}, bf16[512,128]{1,0:T(8,128)(2,1)S(1)}, u32[]{:S(2)}, u32[]{:S(2)}) collective-permute-start(bf16[512,128]{1,0:T(8,128)(2,1)} %get-tuple-element.73), channel_id=1, source_target_pairs={{0,8},{8,0},{16,24},{24,16},{1,9},{9,1},{17,25},{25,17},{2,10},{10... | collective-permute-start | bytes 393224 | tf_op jit(solution)/shard_map/ppermute | solution.py:311
  16.7 2.6 %collective-permute-done.2.refs_0_ = bf16[512,128]{1,0:T(8,128)(2,1)S(1)} collective-permute-done((bf16[512,128]{1,0:T(8,128)(2,1)}, bf16[512,128]{1,0:T(8,128)(2,1)S(1)}, u32[]{:S(2)}, u32[]{:S(2)}) %collective-permute-start.2) | collective-permute-done | bytes 131104 | tf_op jit(solution)/shard_map/ppermute | solution.py:311
  19.2 4.3 %collective-permute-done.3.refs_1_ = bf16[512,128]{1,0:T(8,128)(2,1)S(1)} collective-permute-done((bf16[512,128]{1,0:T(8,128)(2,1)}, bf16[512,128]{1,0:T(8,128)(2,1)S(1)}, u32[]{:S(2)}, u32[]{:S(2)}) %collective-permute-start.3) | collective-permute-done | bytes 131104 | tf_op jit(solution)/shard_map/ppermute | solution.py:311
  24.3 1.9 %start.1 = (f32[512,128]{1,0:T(8,128)}, bf16[512,128]{1,0:T(8,128)(2,1)}) custom-call(f32[512,128]{1,0:T(8,128)} %get-tuple-element.72.own_ref, bf16[512,128]{1,0:T(8,128)(2,1)} %copy-done.13, bf16[512,128]{1,0:T(8,128)(2,1)} %copy-done.17, bf16[512,128]{1,0:T(8,128)(2,1)} %copy-done.20), custom_call_target="tpu_custom_call" | custom-call | tf_op jit(solution)/shard_map/start/pallas_call | solution.py:24
  29.7 4.0 %collective-permute-done.7.refs_7_ = bf16[512,128]{1,0:T(8,128)(2,1)S(1)} collective-permute-done((bf16[512,128]{1,0:T(8,128)(2,1)}, bf16[512,128]{1,0:T(8,128)(2,1)S(1)}, u32[]{:S(2)}, u32[]{:S(2)}) %collective-permute-start.7) | collective-permute-done | bytes 131104 | tf_op jit(solution)/shard_map/ppermute | solution.py:311
  35.8 4.1 %forward.3 = (bf16[1024,128]{1,0:T(8,128)(2,1)}, bf16[1024,128]{1,0:T(8,128)(2,1)}, f32[256,128]{1,0:T(8,128)}, f32[8,128]{1,0:T(8,128)}, bf16[272,128]{1,0:T(8,...) custom-call(bf16[24,2,128,128]{3,2,1,0:T(8,128)(2,1)} %bitcast.9, bf16[24,2,128,128]{3,2,1,0:T(8,128)(2,1)} %copy-done, ...), custom_call_target="tpu_custom_call" | custom-call | tf_op jit(solution)/shard_map/forward/pallas_call | solution.py:24
  39.9 2.8 %collective-permute-start.8 = (bf16[272,128]{1,0:T(8,128)(2,1)}, bf16[272,128]{1,0:T(8,128)(2,1)S(1)}, u32[]{:S(2)}, u32[]{:S(2)}) collective-permute-start(bf16[272,128]{1,0:T(8,128)(2,1)} %get-tuple-element.79), channel_id=1, source_target_pairs={{0,2},{1,3},{2,0},{3,1},{4,6},{5,7},{6,4},{7,5},{8,10},{9,11},{10,... | collective-permute-start | bytes 208904 | tf_op jit(solution)/shard_map/ppermute | solution.py:311
  45.4 5.5 %collective-permute-done.9.refs_1_ = bf16[272,128]{1,0:T(8,128)(2,1)S(1)} collective-permute-done((bf16[272,128]{1,0:T(8,128)(2,1)}, bf16[272,128]{1,0:T(8,128)(2,1)S(1)}, u32[]{:S(2)}, u32[]{:S(2)}) %collective-permute-start.9) | collective-permute-done | bytes 69664 | tf_op jit(solution)/shard_map/ppermute | solution.py:311
  57.7 2.0 %collective-permute-done.13.refs_7_ = bf16[256,128]{1,0:T(8,128)(2,1)S(1)} collective-permute-done((bf16[256,128]{1,0:T(8,128)(2,1)}, bf16[256,128]{1,0:T(8,128)(2,1)S(1)}, u32[]{:S(2)}, u32[]{:S(2)}) %collective-permute-start.13) | collective-permute-done | bytes 65568 | tf_op jit(solution)/shard_map/ppermute | solution.py:311
  61.9 4.1 %adjoint.2 = (bf16[1024,128]{1,0:T(8,128)(2,1)}, f32[512,128]{1,0:T(8,128)}, f32[8,128]{1,0:T(8,128)}, bf16[528,128]{1,0:T(8,128)(2,1)}, bf16[528,128]{1,0:T(8,128)(2,1)}, /*index=5*/bf16[528,128]{1,0:T(8,128)(2,1)}) custom-call(bf16[24,128,256]{2,1,0:T(8,128)(2,1)} %get-tuple-element.67.refs_0_, bf16[24,128,256]{2,1,0:T(8,128)(2,1)} %get-tuple-element.71.refs_1_, ...), custom_call_target="tpu_custom_call" | custom-call | tf_op jit(solution)/shard_map/adjoint/pallas_call | solution.py:24
  75.1 2.0 %gradient.2 = (f32[512,128]{1,0:T(8,128)}, bf16[512,128]{1,0:T(8,128)(2,1)}, f32[8,128]{1,0:T(8,128)}) custom-call(f32[512,128]{1,0:T(8,128)} %get-tuple-element.83.own_ref, f32[8,128]{1,0:T(8,128)} %get-tuple-element.84.norm_ref, bf16[528,128]{1,0:T(8,128)(2,1)} %copy-done.3, bf16[528,128]{1,0:T(8,128)(2,1)} %copy-done.5, bf16[528,128]{1,0:T(8,128)(2,1)} %copy-done.7, ...), custom_call_target="tpu_custom_call" | custom-call | tf_op jit(solution)/shard_map/gradient/pallas_call | solution.py:24
  80.6 2.6 %collective-permute-done.19.refs_7_ = bf16[512,128]{1,0:T(8,128)(2,1)S(1)} collective-permute-done((bf16[512,128]{1,0:T(8,128)(2,1)}, bf16[512,128]{1,0:T(8,128)(2,1)S(1)}, u32[]{:S(2)}, u32[]{:S(2)}) %collective-permute-start.19) | collective-permute-done | bytes 131104 | tf_op jit(solution)/shard_map/ppermute | solution.py:311
  86.1 4.1 %forward.4 = (bf16[1024,128]{1,0:T(8,128)(2,1)}, bf16[1024,128]{1,0:T(8,128)(2,1)}, f32[256,128]{1,0:T(8,128)}, f32[8,128]{1,0:T(8,128)}, bf16[272,128]{1,0:T(8,...) custom-call(bf16[24,2,128,128]{3,2,1,0:T(8,128)(2,1)} %bitcast.10, bf16[24,2,128,128]{3,2,1,0:T(8,128)(2,1)} %copy-done, ...), custom_call_target="tpu_custom_call" | custom-call | tf_op jit(solution)/shard_map/forward/pallas_call | solution.py:24
  92.6 2.0 %collective-permute-start.22 = (bf16[272,128]{1,0:T(8,128)(2,1)}, bf16[272,128]{1,0:T(8,128)(2,1)S(1)}, u32[]{:S(2)}, u32[]{:S(2)}) collective-permute-start(bf16[272,128]{1,0:T(8,128)(2,1)} %get-tuple-element.95), channel_id=1, source_target_pairs={{0,6},{1,7},{2,4},{3,5},{4,2},{5,3},{6,0},{7,1},{8,14},{9,15},{10,... | collective-permute-start | bytes 208904 | tf_op jit(solution)/shard_map/ppermute | solution.py:311
  94.8 3.1 %collective-permute-done.21.refs_1_ = bf16[272,128]{1,0:T(8,128)(2,1)S(1)} collective-permute-done((bf16[272,128]{1,0:T(8,128)(2,1)}, bf16[272,128]{1,0:T(8,128)(2,1)S(1)}, u32[]{:S(2)}, u32[]{:S(2)}) %collective-permute-start.21) | collective-permute-done | bytes 69664 | tf_op jit(solution)/shard_map/ppermute | solution.py:311
  101.5 2.0 %collective-permute-start.25 = (bf16[256,128]{1,0:T(8,128)(2,1)}, bf16[256,128]{1,0:T(8,128)(2,1)S(1)}, u32[]{:S(2)}, u32[]{:S(2)}) collective-permute-start(bf16[256,128]{1,0:T(8,128)(2,1)} %get-tuple-element.97.refs_4_), channel_id=1, source_target_pairs={{0,6},{1,7},{2,4},{3,5},{4,2},{5,3},{6,0},{7,1},{8,14},{9,15},{10,... | collective-permute-start | bytes 196616 | tf_op jit(solution)/shard_map/ppermute | solution.py:311
  103.5 2.4 %collective-permute-start.24 = (bf16[256,128]{1,0:T(8,128)(2,1)}, bf16[256,128]{1,0:T(8,128)(2,1)S(1)}, u32[]{:S(2)}, u32[]{:S(2)}) collective-permute-start(bf16[256,128]{1,0:T(8,128)(2,1)} %get-tuple-element.97.refs_4_), channel_id=1, source_target_pairs={{0,4},{1,5},{2,6},{3,7},{4,0},{5,1},{6,2},{7,3},{8,12},{9,13},{10,... | collective-permute-start | bytes 196616 | tf_op jit(solution)/shard_map/ppermute | solution.py:311
  107.8 2.1 %collective-permute-done.24.refs_6_ = bf16[256,128]{1,0:T(8,128)(2,1)S(1)} collective-permute-done((bf16[256,128]{1,0:T(8,128)(2,1)}, bf16[256,128]{1,0:T(8,128)(2,1)S(1)}, u32[]{:S(2)}, u32[]{:S(2)}) %collective-permute-start.24) | collective-permute-done | bytes 65568 | tf_op jit(solution)/shard_map/ppermute | solution.py:311
  111.2 4.1 %adjoint.3 = (bf16[1024,128]{1,0:T(8,128)(2,1)}, f32[512,128]{1,0:T(8,128)}, f32[8,128]{1,0:T(8,128)}, bf16[528,128]{1,0:T(8,128)(2,1)}, bf16[528,128]{1,0:T(8,128)(2,1)}, /*index=5*/bf16[528,128]{1,0:T(8,128)(2,1)}) custom-call(bf16[24,128,256]{2,1,0:T(8,128)(2,1)} %get-tuple-element.67.refs_0_, bf16[24,128,256]{2,1,0:T(8,128)(2,1)} %get-tuple-element.71.refs_1_, ...), custom_call_target="tpu_custom_call" | custom-call | tf_op jit(solution)/shard_map/adjoint/pallas_call | solution.py:24
  118.8 2.4 %collective-permute-done.26.refs_0_ = bf16[528,128]{1,0:T(8,128)(2,1)S(1)} collective-permute-done((bf16[528,128]{1,0:T(8,128)(2,1)}, bf16[528,128]{1,0:T(8,128)(2,1)S(1)}, u32[]{:S(2)}, u32[]{:S(2)}) %collective-permute-start.26) | collective-permute-done | bytes 135200 | tf_op jit(solution)/shard_map/ppermute | solution.py:311
  121.1 5.0 %collective-permute-done.27.refs_1_ = bf16[528,128]{1,0:T(8,128)(2,1)S(1)} collective-permute-done((bf16[528,128]{1,0:T(8,128)(2,1)}, bf16[528,128]{1,0:T(8,128)(2,1)S(1)}, u32[]{:S(2)}, u32[]{:S(2)}) %collective-permute-start.27) | collective-permute-done | bytes 135200 | tf_op jit(solution)/shard_map/ppermute | solution.py:311
  126.8 2.0 %gradient.3 = (f32[512,128]{1,0:T(8,128)}, bf16[512,128]{1,0:T(8,128)(2,1)}, f32[8,128]{1,0:T(8,128)}) custom-call(f32[512,128]{1,0:T(8,128)} %get-tuple-element.98.own_ref, f32[8,128]{1,0:T(8,128)} %get-tuple-element.99.norm_ref, bf16[528,128]{1,0:T(8,128)(2,1)} %copy-done.4, bf16[528,128]{1,0:T(8,128)(2,1)} %copy-done.6, bf16[528,128]{1,0:T(8,128)(2,1)} %copy-done.8, ...), custom_call_target="tpu_custom_call" | custom-call | tf_op jit(solution)/shard_map/gradient/pallas_call | solution.py:24
  132.3 2.7 %collective-permute-done.31.refs_7_ = bf16[512,128]{1,0:T(8,128)(2,1)S(1)} collective-permute-done((bf16[512,128]{1,0:T(8,128)(2,1)}, bf16[512,128]{1,0:T(8,128)(2,1)S(1)}, u32[]{:S(2)}, u32[]{:S(2)}) %collective-permute-start.31) | collective-permute-done | bytes 131104 | tf_op jit(solution)/shard_map/ppermute | solution.py:311
  137.6 4.1 %forward.5 = (bf16[1024,128]{1,0:T(8,128)(2,1)}, bf16[1024,128]{1,0:T(8,128)(2,1)}, f32[256,128]{1,0:T(8,128)}, f32[8,128]{1,0:T(8,128)}, bf16[272,128]{1,0:T(8,...) custom-call(bf16[24,2,128,128]{3,2,1,0:T(8,128)(2,1)} %bitcast.11, bf16[24,2,128,128]{3,2,1,0:T(8,128)(2,1)} %copy-done, ...), custom_call_target="tpu_custom_call" | custom-call | tf_op jit(solution)/shard_map/forward/pallas_call | solution.py:24
  144.1 2.0 %collective-permute-start.34 = (bf16[272,128]{1,0:T(8,128)(2,1)}, bf16[272,128]{1,0:T(8,128)(2,1)S(1)}, u32[]{:S(2)}, u32[]{:S(2)}) collective-permute-start(bf16[272,128]{1,0:T(8,128)(2,1)} %get-tuple-element.110), channel_id=1, source_target_pairs={{0,6},{1,7},{2,4},{3,5},{4,2},{5,3},{6,0},{7,1},{8,14},{9,15},{10,... | collective-permute-start | bytes 208904 | tf_op jit(solution)/shard_map/ppermute | solution.py:311
  146.2 2.0 %collective-permute-done.32.refs_0_ = bf16[272,128]{1,0:T(8,128)(2,1)S(1)} collective-permute-done((bf16[272,128]{1,0:T(8,128)(2,1)}, bf16[272,128]{1,0:T(8,128)(2,1)S(1)}, u32[]{:S(2)}, u32[]{:S(2)}) %collective-permute-start.32) | collective-permute-done | bytes 69664 | tf_op jit(solution)/shard_map/ppermute | solution.py:311
  153.0 2.0 %collective-permute-start.37 = (bf16[256,128]{1,0:T(8,128)(2,1)}, bf16[256,128]{1,0:T(8,128)(2,1)S(1)}, u32[]{:S(2)}, u32[]{:S(2)}) collective-permute-start(bf16[256,128]{1,0:T(8,128)(2,1)} %get-tuple-element.113.refs_0_), channel_id=1, source_target_pairs={{0,6},{1,7},{2,4},{3,5},{4,2},{5,3},{6,0},{7,1},{8,14},{9,15},{10,... | collective-permute-start | bytes 196616 | tf_op jit(solution)/shard_map/ppermute | solution.py:311
  157.4 1.9 %collective-permute-done.37.refs_3_ = bf16[256,128]{1,0:T(8,128)(2,1)S(1)} collective-permute-done((bf16[256,128]{1,0:T(8,128)(2,1)}, bf16[256,128]{1,0:T(8,128)(2,1)S(1)}, u32[]{:S(2)}, u32[]{:S(2)}) %collective-permute-start.37) | collective-permute-done | bytes 65568 | tf_op jit(solution)/shard_map/ppermute | solution.py:311
  169.9 3.5 %answer.1 = (f32[1024,128]{1,0:T(8,128)}, bf16[1024,128]{1,0:T(8,128)(2,1)}, f32[1024,128]{1,0:T(8,128)}, bf16[1024,128]{1,0:T(8,128)(2,1)}) custom-call(f32[2,1024,128]{2,1,0:T(8,128)} %record_ref.3, f32[8,128]{1,0:T(8,128)} %get-tuple-element.112.gamma_ref, f32[8,128]{1,0:T(8,128)} %get-tuple-element.114.refs_0_, f32[8,128]{1,0:T(8,128)} %copy-done.43, ...), custom_call_target="tpu_custom_call" | custom-call | tf_op jit(solution)/shard_map/answer/pallas_call | solution.py:24
  176.3 3.0 %unpack.1 = (f32[2,1024,128]{2,1,0:T(8,128)}, f32[2,1024,128]{2,1,0:T(8,128)}) custom-call(f32[1024,128]{1,0:T(8,128)} %get-tuple-element.128.own_x, f32[1024,128]{1,0:T(8,128)} %get-tuple-element.129.own_r, bf16[1024,128]{1,0:T(8,128)(2,1)} %copy-done.1, bf16[1024,128]{1,0:T(8,128)(2,1)} %copy-done.2), custom_call_target="tpu_custom_call" | custom-call | tf_op jit(solution)/shard_map/unpack/pallas_call | solution.py:24
  (160 shorter events, 81.1 us)
Async XLA Ops:
  0.6 6.8 %collective-permute-start = (bf16[24,2,128,128]{3,2,1,0:T(8,128)(2,1)}, bf16[24,2,128,128]{3,2,1,0:T(8,128)(2,1)S(1)}, u32[]{:S(2)}, u32[]{:S(2)}) collective-permute-start(bf16[24,2,128,128]{3,2,1,0:T(8,128)(2,1)} %bitcast.7), channel_id=1, source_target_pairs={{0,1},{1,0},{2,3},{3,2},{4,5},{5,4},{6,7},{7,6},{8,9},{9,8},{10,11... | collective-permute-start | bytes 4718600 | tf_op jit(solution)/shard_map/ppermute | solution.py:311
  12.3 6.9 %collective-permute-start.2 = (bf16[512,128]{1,0:T(8,128)(2,1)}, bf16[512,128]{1,0:T(8,128)(2,1)S(1)}, u32[]{:S(2)}, u32[]{:S(2)}) collective-permute-start(bf16[512,128]{1,0:T(8,128)(2,1)} %get-tuple-element.73), channel_id=1, source_target_pairs={{0,8},{8,0},{16,24},{24,16},{1,9},{9,1},{17,25},{25,17},{2,10},{10... | collective-permute-start | bytes 393224 | tf_op jit(solution)/shard_map/ppermute | solution.py:311
  14.8 8.8 %collective-permute-start.3 = (bf16[512,128]{1,0:T(8,128)(2,1)}, bf16[512,128]{1,0:T(8,128)(2,1)S(1)}, u32[]{:S(2)}, u32[]{:S(2)}) collective-permute-start(bf16[512,128]{1,0:T(8,128)(2,1)} %get-tuple-element.74), channel_id=1, source_target_pairs={{0,16},{8,24},{16,0},{24,8},{1,17},{9,25},{17,1},{25,9},{2,18},{10... | collective-permute-start | bytes 393224 | tf_op jit(solution)/shard_map/ppermute | solution.py:311
  16.7 6.9 %collective-permute-start.4 = (bf16[512,128]{1,0:T(8,128)(2,1)}, bf16[512,128]{1,0:T(8,128)(2,1)S(1)}, u32[]{:S(2)}, u32[]{:S(2)}) collective-permute-start(bf16[512,128]{1,0:T(8,128)(2,1)} %get-tuple-element.75), channel_id=1, source_target_pairs={{0,24},{8,16},{16,8},{24,0},{1,25},{9,17},{17,9},{25,1},{2,26},{10... | collective-permute-start | bytes 393224 | tf_op jit(solution)/shard_map/ppermute | solution.py:311
  26.2 7.5 %collective-permute-start.7 = (bf16[512,128]{1,0:T(8,128)(2,1)}, bf16[512,128]{1,0:T(8,128)(2,1)S(1)}, u32[]{:S(2)}, u32[]{:S(2)}) collective-permute-start(bf16[512,128]{1,0:T(8,128)(2,1)} %get-tuple-element.76.refs_4_), channel_id=1, source_target_pairs={{0,24},{8,16},{16,8},{24,0},{1,25},{9,17},{17,9},{25,1},{2,26},{10... | collective-permute-start | bytes 393224 | tf_op jit(solution)/shard_map/ppermute | solution.py:311
  27.6 6.8 %collective-permute-start.6 = (bf16[512,128]{1,0:T(8,128)(2,1)}, bf16[512,128]{1,0:T(8,128)(2,1)S(1)}, u32[]{:S(2)}, u32[]{:S(2)}) collective-permute-start(bf16[512,128]{1,0:T(8,128)(2,1)} %get-tuple-element.76.refs_4_), channel_id=1, source_target_pairs={{0,16},{8,24},{16,0},{24,8},{1,17},{9,25},{17,1},{25,9},{2,18},{10... | collective-permute-start | bytes 393224 | tf_op jit(solution)/shard_map/ppermute | solution.py:311
  29.1 6.1 %collective-permute-start.5 = (bf16[512,128]{1,0:T(8,128)(2,1)}, bf16[512,128]{1,0:T(8,128)(2,1)S(1)}, u32[]{:S(2)}, u32[]{:S(2)}) collective-permute-start(bf16[512,128]{1,0:T(8,128)(2,1)} %get-tuple-element.76.refs_4_), channel_id=1, source_target_pairs={{0,8},{8,0},{16,24},{24,16},{1,9},{9,1},{17,25},{25,17},{2,10},{10... | collective-permute-start | bytes 393224 | tf_op jit(solution)/shard_map/ppermute | solution.py:311
  39.9 5.4 %collective-permute-start.8 = (bf16[272,128]{1,0:T(8,128)(2,1)}, bf16[272,128]{1,0:T(8,128)(2,1)S(1)}, u32[]{:S(2)}, u32[]{:S(2)}) collective-permute-start(bf16[272,128]{1,0:T(8,128)(2,1)} %get-tuple-element.79), channel_id=1, source_target_pairs={{0,2},{1,3},{2,0},{3,1},{4,6},{5,7},{6,4},{7,5},{8,10},{9,11},{10,... | collective-permute-start | bytes 208904 | tf_op jit(solution)/shard_map/ppermute | solution.py:311
  42.7 8.2 %collective-permute-start.9 = (bf16[272,128]{1,0:T(8,128)(2,1)}, bf16[272,128]{1,0:T(8,128)(2,1)S(1)}, u32[]{:S(2)}, u32[]{:S(2)}) collective-permute-start(bf16[272,128]{1,0:T(8,128)(2,1)} %get-tuple-element.80), channel_id=1, source_target_pairs={{0,4},{1,5},{2,6},{3,7},{4,0},{5,1},{6,2},{7,3},{8,12},{9,13},{10,... | collective-permute-start | bytes 208904 | tf_op jit(solution)/shard_map/ppermute | solution.py:311
  44.1 6.8 %collective-permute-start.10 = (bf16[272,128]{1,0:T(8,128)(2,1)}, bf16[272,128]{1,0:T(8,128)(2,1)S(1)}, u32[]{:S(2)}, u32[]{:S(2)}) collective-permute-start(bf16[272,128]{1,0:T(8,128)(2,1)} %get-tuple-element.81), channel_id=1, source_target_pairs={{0,6},{1,7},{2,4},{3,5},{4,2},{5,3},{6,0},{7,1},{8,14},{9,15},{10,... | collective-permute-start | bytes 208904 | tf_op jit(solution)/shard_map/ppermute | solution.py:311
  53.3 6.4 %collective-permute-start.13 = (bf16[256,128]{1,0:T(8,128)(2,1)}, bf16[256,128]{1,0:T(8,128)(2,1)S(1)}, u32[]{:S(2)}, u32[]{:S(2)}) collective-permute-start(bf16[256,128]{1,0:T(8,128)(2,1)} %get-tuple-element.82.refs_4_), channel_id=1, source_target_pairs={{0,6},{1,7},{2,4},{3,5},{4,2},{5,3},{6,0},{7,1},{8,14},{9,15},{10,... | collective-permute-start | bytes 196616 | tf_op jit(solution)/shard_map/ppermute | solution.py:311
  54.9 6.3 %collective-permute-start.12 = (bf16[256,128]{1,0:T(8,128)(2,1)}, bf16[256,128]{1,0:T(8,128)(2,1)S(1)}, u32[]{:S(2)}, u32[]{:S(2)}) collective-permute-start(bf16[256,128]{1,0:T(8,128)(2,1)} %get-tuple-element.82.refs_4_), channel_id=1, source_target_pairs={{0,4},{1,5},{2,6},{3,7},{4,0},{5,1},{6,2},{7,3},{8,12},{9,13},{10,... | collective-permute-start | bytes 196616 | tf_op jit(solution)/shard_map/ppermute | solution.py:311
  66.0 5.2 %collective-permute-start.14 = (bf16[528,128]{1,0:T(8,128)(2,1)}, bf16[528,128]{1,0:T(8,128)(2,1)S(1)}, u32[]{:S(2)}, u32[]{:S(2)}) collective-permute-start(bf16[528,128]{1,0:T(8,128)(2,1)} %get-tuple-element.85), channel_id=1, source_target_pairs={{0,8},{8,0},{16,24},{24,16},{1,9},{9,1},{17,25},{25,17},{2,10},{10... | collective-permute-start | bytes 405512 | tf_op jit(solution)/shard_map/ppermute | solution.py:311
  67.4 5.2 %collective-permute-start.15 = (bf16[528,128]{1,0:T(8,128)(2,1)}, bf16[528,128]{1,0:T(8,128)(2,1)S(1)}, u32[]{:S(2)}, u32[]{:S(2)}) collective-permute-start(bf16[528,128]{1,0:T(8,128)(2,1)} %get-tuple-element.86), channel_id=1, source_target_pairs={{0,16},{8,24},{16,0},{24,8},{1,17},{9,25},{17,1},{25,9},{2,18},{10... | collective-permute-start | bytes 405512 | tf_op jit(solution)/shard_map/ppermute | solution.py:311
  68.3 6.1 %collective-permute-start.16 = (bf16[528,128]{1,0:T(8,128)(2,1)}, bf16[528,128]{1,0:T(8,128)(2,1)S(1)}, u32[]{:S(2)}, u32[]{:S(2)}) collective-permute-start(bf16[528,128]{1,0:T(8,128)(2,1)} %get-tuple-element.87), channel_id=1, source_target_pairs={{0,24},{8,16},{16,8},{24,0},{1,25},{9,17},{17,9},{25,1},{2,26},{10... | collective-permute-start | bytes 405512 | tf_op jit(solution)/shard_map/ppermute | solution.py:311
  77.1 6.1 %collective-permute-start.19 = (bf16[512,128]{1,0:T(8,128)(2,1)}, bf16[512,128]{1,0:T(8,128)(2,1)S(1)}, u32[]{:S(2)}, u32[]{:S(2)}) collective-permute-start(bf16[512,128]{1,0:T(8,128)(2,1)} %get-tuple-element.90.refs_4_), channel_id=1, source_target_pairs={{0,24},{8,16},{16,8},{24,0},{1,25},{9,17},{17,9},{25,1},{2,26},{10... | collective-permute-start | bytes 393224 | tf_op jit(solution)/shard_map/ppermute | solution.py:311
  78.9 5.7 %collective-permute-start.18 = (bf16[512,128]{1,0:T(8,128)(2,1)}, bf16[512,128]{1,0:T(8,128)(2,1)S(1)}, u32[]{:S(2)}, u32[]{:S(2)}) collective-permute-start(bf16[512,128]{1,0:T(8,128)(2,1)} %get-tuple-element.90.refs_4_), channel_id=1, source_target_pairs={{0,16},{8,24},{16,0},{24,8},{1,17},{9,25},{17,1},{25,9},{2,18},{10... | collective-permute-start | bytes 393224 | tf_op jit(solution)/shard_map/ppermute | solution.py:311
  91.7 6.2 %collective-permute-start.21 = (bf16[272,128]{1,0:T(8,128)(2,1)}, bf16[272,128]{1,0:T(8,128)(2,1)S(1)}, u32[]{:S(2)}, u32[]{:S(2)}) collective-permute-start(bf16[272,128]{1,0:T(8,128)(2,1)} %get-tuple-element.94), channel_id=1, source_target_pairs={{0,4},{1,5},{2,6},{3,7},{4,0},{5,1},{6,2},{7,3},{8,12},{9,13},{10,... | collective-permute-start | bytes 208904 | tf_op jit(solution)/shard_map/ppermute | solution.py:311
  92.6 6.4 %collective-permute-start.22 = (bf16[272,128]{1,0:T(8,128)(2,1)}, bf16[272,128]{1,0:T(8,128)(2,1)S(1)}, u32[]{:S(2)}, u32[]{:S(2)}) collective-permute-start(bf16[272,128]{1,0:T(8,128)(2,1)} %get-tuple-element.95), channel_id=1, source_target_pairs={{0,6},{1,7},{2,4},{3,5},{4,2},{5,3},{6,0},{7,1},{8,14},{9,15},{10,... | collective-permute-start | bytes 208904 | tf_op jit(solution)/shard_map/ppermute | solution.py:311
  101.5 6.3 %collective-permute-start.25 = (bf16[256,128]{1,0:T(8,128)(2,1)}, bf16[256,128]{1,0:T(8,128)(2,1)S(1)}, u32[]{:S(2)}, u32[]{:S(2)}) collective-permute-start(bf16[256,128]{1,0:T(8,128)(2,1)} %get-tuple-element.97.refs_4_), channel_id=1, source_target_pairs={{0,6},{1,7},{2,4},{3,5},{4,2},{5,3},{6,0},{7,1},{8,14},{9,15},{10,... | collective-permute-start | bytes 196616 | tf_op jit(solution)/shard_map/ppermute | solution.py:311
  103.5 6.4 %collective-permute-start.24 = (bf16[256,128]{1,0:T(8,128)(2,1)}, bf16[256,128]{1,0:T(8,128)(2,1)S(1)}, u32[]{:S(2)}, u32[]{:S(2)}) collective-permute-start(bf16[256,128]{1,0:T(8,128)(2,1)} %get-tuple-element.97.refs_4_), channel_id=1, source_target_pairs={{0,4},{1,5},{2,6},{3,7},{4,0},{5,1},{6,2},{7,3},{8,12},{9,13},{10,... | collective-permute-start | bytes 196616 | tf_op jit(solution)/shard_map/ppermute | solution.py:311
  115.3 5.8 %collective-permute-start.26 = (bf16[528,128]{1,0:T(8,128)(2,1)}, bf16[528,128]{1,0:T(8,128)(2,1)S(1)}, u32[]{:S(2)}, u32[]{:S(2)}) collective-permute-start(bf16[528,128]{1,0:T(8,128)(2,1)} %get-tuple-element.100), channel_id=1, source_target_pairs={{0,8},{8,0},{16,24},{24,16},{1,9},{9,1},{17,25},{25,17},{2,10},{10... | collective-permute-start | bytes 405512 | tf_op jit(solution)/shard_map/ppermute | solution.py:311
  116.8 9.4 %collective-permute-start.27 = (bf16[528,128]{1,0:T(8,128)(2,1)}, bf16[528,128]{1,0:T(8,128)(2,1)S(1)}, u32[]{:S(2)}, u32[]{:S(2)}) collective-permute-start(bf16[528,128]{1,0:T(8,128)(2,1)} %get-tuple-element.101), channel_id=1, source_target_pairs={{0,16},{8,24},{16,0},{24,8},{1,17},{9,25},{17,1},{25,9},{2,18},{10... | collective-permute-start | bytes 405512 | tf_op jit(solution)/shard_map/ppermute | solution.py:311
  117.8 8.3 %collective-permute-start.28 = (bf16[528,128]{1,0:T(8,128)(2,1)}, bf16[528,128]{1,0:T(8,128)(2,1)S(1)}, u32[]{:S(2)}, u32[]{:S(2)}) collective-permute-start(bf16[528,128]{1,0:T(8,128)(2,1)} %get-tuple-element.102), channel_id=1, source_target_pairs={{0,24},{8,16},{16,8},{24,0},{1,25},{9,17},{17,9},{25,1},{2,26},{10... | collective-permute-start | bytes 405512 | tf_op jit(solution)/shard_map/ppermute | solution.py:311
  128.8 6.2 %collective-permute-start.31 = (bf16[512,128]{1,0:T(8,128)(2,1)}, bf16[512,128]{1,0:T(8,128)(2,1)S(1)}, u32[]{:S(2)}, u32[]{:S(2)}) collective-permute-start(bf16[512,128]{1,0:T(8,128)(2,1)} %get-tuple-element.105.refs_4_), channel_id=1, source_target_pairs={{0,24},{8,16},{16,8},{24,0},{1,25},{9,17},{17,9},{25,1},{2,26},{10... | collective-permute-start | bytes 393224 | tf_op jit(solution)/shard_map/ppermute | solution.py:311
  129.7 6.6 %collective-permute-start.30 = (bf16[512,128]{1,0:T(8,128)(2,1)}, bf16[512,128]{1,0:T(8,128)(2,1)S(1)}, u32[]{:S(2)}, u32[]{:S(2)}) collective-permute-start(bf16[512,128]{1,0:T(8,128)(2,1)} %get-tuple-element.105.refs_4_), channel_id=1, source_target_pairs={{0,16},{8,24},{16,0},{24,8},{1,17},{9,25},{17,1},{25,9},{2,18},{10... | collective-permute-start | bytes 393224 | tf_op jit(solution)/shard_map/ppermute | solution.py:311
  130.8 5.5 %collective-permute-start.29 = (bf16[512,128]{1,0:T(8,128)(2,1)}, bf16[512,128]{1,0:T(8,128)(2,1)S(1)}, u32[]{:S(2)}, u32[]{:S(2)}) collective-permute-start(bf16[512,128]{1,0:T(8,128)(2,1)} %get-tuple-element.105.refs_4_), channel_id=1, source_target_pairs={{0,8},{8,0},{16,24},{24,16},{1,9},{9,1},{17,25},{25,17},{2,10},{10... | collective-permute-start | bytes 393224 | tf_op jit(solution)/shard_map/ppermute | solution.py:311
  141.8 6.4 %collective-permute-start.32 = (bf16[272,128]{1,0:T(8,128)(2,1)}, bf16[272,128]{1,0:T(8,128)(2,1)S(1)}, u32[]{:S(2)}, u32[]{:S(2)}) collective-permute-start(bf16[272,128]{1,0:T(8,128)(2,1)} %get-tuple-element.108), channel_id=1, source_target_pairs={{0,2},{1,3},{2,0},{3,1},{4,6},{5,7},{6,4},{7,5},{8,10},{9,11},{10,... | collective-permute-start | bytes 208904 | tf_op jit(solution)/shard_map/ppermute | solution.py:311
  142.4 7.2 %collective-permute-start.33 = (bf16[272,128]{1,0:T(8,128)(2,1)}, bf16[272,128]{1,0:T(8,128)(2,1)S(1)}, u32[]{:S(2)}, u32[]{:S(2)}) collective-permute-start(bf16[272,128]{1,0:T(8,128)(2,1)} %get-tuple-element.109), channel_id=1, source_target_pairs={{0,4},{1,5},{2,6},{3,7},{4,0},{5,1},{6,2},{7,3},{8,12},{9,13},{10,... | collective-permute-start | bytes 208904 | tf_op jit(solution)/shard_map/ppermute | solution.py:311
  144.1 6.4 %collective-permute-start.34 = (bf16[272,128]{1,0:T(8,128)(2,1)}, bf16[272,128]{1,0:T(8,128)(2,1)S(1)}, u32[]{:S(2)}, u32[]{:S(2)}) collective-permute-start(bf16[272,128]{1,0:T(8,128)(2,1)} %get-tuple-element.110), channel_id=1, source_target_pairs={{0,6},{1,7},{2,4},{3,5},{4,2},{5,3},{6,0},{7,1},{8,14},{9,15},{10,... | collective-permute-start | bytes 208904 | tf_op jit(solution)/shard_map/ppermute | solution.py:311
  153.0 6.3 %collective-permute-start.37 = (bf16[256,128]{1,0:T(8,128)(2,1)}, bf16[256,128]{1,0:T(8,128)(2,1)S(1)}, u32[]{:S(2)}, u32[]{:S(2)}) collective-permute-start(bf16[256,128]{1,0:T(8,128)(2,1)} %get-tuple-element.113.refs_0_), channel_id=1, source_target_pairs={{0,6},{1,7},{2,4},{3,5},{4,2},{5,3},{6,0},{7,1},{8,14},{9,15},{10,... | collective-permute-start | bytes 196616 | tf_op jit(solution)/shard_map/ppermute | solution.py:311
  155.0 5.7 %collective-permute-start.36 = (bf16[256,128]{1,0:T(8,128)(2,1)}, bf16[256,128]{1,0:T(8,128)(2,1)S(1)}, u32[]{:S(2)}, u32[]{:S(2)}) collective-permute-start(bf16[256,128]{1,0:T(8,128)(2,1)} %get-tuple-element.113.refs_0_), channel_id=1, source_target_pairs={{0,4},{1,5},{2,6},{3,7},{4,0},{5,1},{6,2},{7,3},{8,12},{9,13},{10,... | collective-permute-start | bytes 196616 | tf_op jit(solution)/shard_map/ppermute | solution.py:311
  (55 other events, 105.5 us)

commit v2 on v1

--- a/solution.py
+++ b/solution.py
@@ -12,6 +12,7 @@
 EPSILON = 1e-06
 GROUP = 8
 TAIL = 16
+VMEM_BYTES = 16 << 20
 
 F32 = jnp.float32
 BF16 = jnp.bfloat16
@@ -28,6 +29,7 @@
         in_specs=[pl.BlockSpec(memory_space=space(a.dtype)) for a in ins],
         out_specs=[pl.BlockSpec(memory_space=pltpu.VMEM) for _ in outs],
         scratch_shapes=[pltpu.VMEM(s, d) for s, d in scratch],
+        compiler_params=pltpu.CompilerParams(vmem_limit_bytes=VMEM_BYTES),
     )(*ins)
 
 

time: 180 us -> 137 us (0.76); the launches traced: 179 us -> 139 us
  Pallas kernels: 48 us -> 16.5 us
  local copies, waits for them, and re-layouts: 12.1 us -> 2.72 us
    pallas_call x16, Pallas kernels: 48 us -> 16.5 us  [call(): pl.pallas_call(kernel, name=name, out_shape=[jax.ShapeDtypeStruct(s, d) f...]
    unnamed x88 -> x8, local copies, waits for them, and re-layouts: 12.1 us -> 2.64 us
  transfers between devices with their start and end apart: 43 -> 43, of which waited for: 34 -> 34; matrix products, arithmetic and copies ran while one was open for 0% -> 1% of each run, Pallas kernels for 2% -> 1%
where the time goes in v2:
time: 137 us; the launch traced here: 139 us
  waiting for transfers between devices  61.9 us (45%)
  starting transfers between devices  55.4 us (40%)
  Pallas kernels  16.5 us (12%)
  local copies, waits for them, and re-layouts  2.72 us (2%)
  between operations  1.43 us (1%)
    ppermute x43, waiting for transfers between devices, swap(): return lax.ppermute(value, axis, [(i, i ^ offset) for i in range(size)])  61.9 us
    ppermute x43, starting transfers between devices, swap(): return lax.ppermute(value, axis, [(i, i ^ offset) for i in range(size)])  55.4 us
    pallas_call x16, Pallas kernels, call(): pl.pallas_call(kernel, name=name, out_shape=[jax.ShapeDtypeStruct(s, d) f...  16.5 us
  transfers between devices with their start and end apart: 43, of which 34 were waited for; matrix products, arithmetic and copies ran while one was open for 1% of the time, Pallas kernels for 1%

profile of v2, /device:TPU:0, one launch (start us, length us, event | category | flops | bytes accessed | tf_op | source)
XLA Modules:
  0.0 138.7 jit_solution(13888325099388877351)
XLA Ops:
  5.3 1.8 %pack.1 = (bf16[24,128,256]{2,1,0:T(8,128)(2,1)S(1)}, f32[1152,128]{1,0:T(8,128)S(1)}, bf16[1024,128]{1,0:T(8,128)(2,1)S(1)}, bf16[1024,128]{1,0:T(8,128)(2,1)S(1)}) custom-call(f32[2,1024,128]{2,1,0:T(8,128)S(1)} %copy-done.2, bf16[24,2,128,128]{3,2,1,0:T(8,128)(2,1)S(1)} %bitcast.8, s32[3,24]{1,0:T(4,128)S(1)} %add_add_fusion.index_ref.refs_2_), custom_call_target="tpu_custom_call" | custom-call | tf_op jit(solution)/shard_map/pack/pallas_call | solution.py:25
  8.2 3.7 %collective-permute-start.2 = (bf16[512,128]{1,0:T(8,128)(2,1)S(1)}, bf16[512,128]{1,0:T(8,128)(2,1)S(1)}, u32[]{:S(2)}, u32[]{:S(2)}) collective-permute-start(bf16[512,128]{1,0:T(8,128)(2,1)S(1)} %get-tuple-element.73), channel_id=1, source_target_pairs={{0,8},{8,0},{16,24},{24,16},{1,9},{9,1},{17,25},{25,17},{2,10},{10... | collective-permute-start | bytes 393224 | tf_op jit(solution)/shard_map/ppermute | solution.py:313
  13.5 2.3 %collective-permute-done.2.refs_0_ = bf16[512,128]{1,0:T(8,128)(2,1)S(1)} collective-permute-done((bf16[512,128]{1,0:T(8,128)(2,1)S(1)}, bf16[512,128]{1,0:T(8,128)(2,1)S(1)}, u32[]{:S(2)}, u32[]{:S(2)}) %collective-permute-start.2) | collective-permute-done | bytes 131104 | tf_op jit(solution)/shard_map/ppermute | solution.py:313
  15.8 4.1 %collective-permute-done.3.refs_1_ = bf16[512,128]{1,0:T(8,128)(2,1)S(1)} collective-permute-done((bf16[512,128]{1,0:T(8,128)(2,1)S(1)}, bf16[512,128]{1,0:T(8,128)(2,1)S(1)}, u32[]{:S(2)}, u32[]{:S(2)}) %collective-permute-start.3) | collective-permute-done | bytes 131104 | tf_op jit(solution)/shard_map/ppermute | solution.py:313
  23.5 3.3 %collective-permute-done.7.refs_7_ = bf16[512,128]{1,0:T(8,128)(2,1)S(1)} collective-permute-done((bf16[512,128]{1,0:T(8,128)(2,1)S(1)}, bf16[512,128]{1,0:T(8,128)(2,1)S(1)}, u32[]{:S(2)}, u32[]{:S(2)}) %collective-permute-start.7) | collective-permute-done | bytes 131104 | tf_op jit(solution)/shard_map/ppermute | solution.py:313
  28.0 1.9 %forward.3 = (bf16[1024,128]{1,0:T(8,128)(2,1)S(1)}, bf16[1024,128]{1,0:T(8,128)(2,1)S(1)}, f32[256,128]{1,0:T(8,128)S(1)}, f32[8,128]{1,0:T(8,128)S(1)}, bf16[2...) custom-call(bf16[24,2,128,128]{3,2,1,0:T(8,128)(2,1)S(1)} %bitcast.9, ...), custom_call_target="tpu_custom_call" | custom-call | tf_op jit(solution)/shard_map/forward/pallas_call | solution.py:25
  29.9 2.0 %collective-permute-start.8 = (bf16[272,128]{1,0:T(8,128)(2,1)S(1)}, bf16[272,128]{1,0:T(8,128)(2,1)S(1)}, u32[]{:S(2)}, u32[]{:S(2)}) collective-permute-start(bf16[272,128]{1,0:T(8,128)(2,1)S(1)} %get-tuple-element.79), channel_id=1, source_target_pairs={{0,2},{1,3},{2,0},{3,1},{4,6},{5,7},{6,4},{7,5},{8,10},{9,11},{10,... | collective-permute-start | bytes 208904 | tf_op jit(solution)/shard_map/ppermute | solution.py:313
  31.9 2.6 %collective-permute-start.9 = (bf16[272,128]{1,0:T(8,128)(2,1)S(1)}, bf16[272,128]{1,0:T(8,128)(2,1)S(1)}, u32[]{:S(2)}, u32[]{:S(2)}) collective-permute-start(bf16[272,128]{1,0:T(8,128)(2,1)S(1)} %get-tuple-element.80), channel_id=1, source_target_pairs={{0,4},{1,5},{2,6},{3,7},{4,0},{5,1},{6,2},{7,3},{8,12},{9,13},{10,... | collective-permute-start | bytes 208904 | tf_op jit(solution)/shard_map/ppermute | solution.py:313
  34.7 3.9 %collective-permute-done.9.refs_1_ = bf16[272,128]{1,0:T(8,128)(2,1)S(1)} collective-permute-done((bf16[272,128]{1,0:T(8,128)(2,1)S(1)}, bf16[272,128]{1,0:T(8,128)(2,1)S(1)}, u32[]{:S(2)}, u32[]{:S(2)}) %collective-permute-start.9) | collective-permute-done | bytes 69664 | tf_op jit(solution)/shard_map/ppermute | solution.py:313
  38.6 2.1 %collective-permute-done.10.refs_2_ = bf16[272,128]{1,0:T(8,128)(2,1)S(1)} collective-permute-done((bf16[272,128]{1,0:T(8,128)(2,1)S(1)}, bf16[272,128]{1,0:T(8,128)(2,1)S(1)}, u32[]{:S(2)}, u32[]{:S(2)}) %collective-permute-start.10) | collective-permute-done | bytes 69664 | tf_op jit(solution)/shard_map/ppermute | solution.py:313
  41.6 3.6 %collective-permute-start.11 = (bf16[256,128]{1,0:T(8,128)(2,1)S(1)}, bf16[256,128]{1,0:T(8,128)(2,1)S(1)}, u32[]{:S(2)}, u32[]{:S(2)}) collective-permute-start(bf16[256,128]{1,0:T(8,128)(2,1)S(1)} %get-tuple-element.82.refs_4_), channel_id=1, source_target_pairs={{0,2},{1,3},{2,0},{3,1},{4,6},{5,7},{6,4},{7,5},{8,10},{9,11},{10,... | collective-permute-start | bytes 196616 | tf_op jit(solution)/shard_map/ppermute | solution.py:313
  45.2 1.8 %collective-permute-done.13.refs_7_ = bf16[256,128]{1,0:T(8,128)(2,1)S(1)} collective-permute-done((bf16[256,128]{1,0:T(8,128)(2,1)S(1)}, bf16[256,128]{1,0:T(8,128)(2,1)S(1)}, u32[]{:S(2)}, u32[]{:S(2)}) %collective-permute-start.13) | collective-permute-done | bytes 65568 | tf_op jit(solution)/shard_map/ppermute | solution.py:313
  48.2 1.8 %adjoint.2 = (bf16[1024,128]{1,0:T(8,128)(2,1)S(1)}, f32[512,128]{1,0:T(8,128)S(1)}, f32[8,128]{1,0:T(8,128)S(1)}, bf16[528,128]{1,0:T(8,128)(2,1)S(1)}, bf16[52...) custom-call(bf16[24,128,256]{2,1,0:T(8,128)(2,1)S(1)} %get-tuple-element.67.refs_0_, ...), custom_call_target="tpu_custom_call" | custom-call | tf_op jit(solution)/shard_map/adjoint/pallas_call | solution.py:25
  50.0 2.2 %collective-permute-start.14 = (bf16[528,128]{1,0:T(8,128)(2,1)S(1)}, bf16[528,128]{1,0:T(8,128)(2,1)S(1)}, u32[]{:S(2)}, u32[]{:S(2)}) collective-permute-start(bf16[528,128]{1,0:T(8,128)(2,1)S(1)} %get-tuple-element.85), channel_id=1, source_target_pairs={{0,8},{8,0},{16,24},{24,16},{1,9},{9,1},{17,25},{25,17},{2,10},{10... | collective-permute-start | bytes 405512 | tf_op jit(solution)/shard_map/ppermute | solution.py:313
  55.7 2.7 %collective-permute-done.15.refs_1_ = bf16[528,128]{1,0:T(8,128)(2,1)S(1)} collective-permute-done((bf16[528,128]{1,0:T(8,128)(2,1)S(1)}, bf16[528,128]{1,0:T(8,128)(2,1)S(1)}, u32[]{:S(2)}, u32[]{:S(2)}) %collective-permute-start.15) | collective-permute-done | bytes 135200 | tf_op jit(solution)/shard_map/ppermute | solution.py:313
  60.3 1.8 %collective-permute-start.19 = (bf16[512,128]{1,0:T(8,128)(2,1)S(1)}, bf16[512,128]{1,0:T(8,128)(2,1)S(1)}, u32[]{:S(2)}, u32[]{:S(2)}) collective-permute-start(bf16[512,128]{1,0:T(8,128)(2,1)S(1)} %get-tuple-element.90.refs_4_), channel_id=1, source_target_pairs={{0,24},{8,16},{16,8},{24,0},{1,25},{9,17},{17,9},{25,1},{2,26},{10... | collective-permute-start | bytes 393224 | tf_op jit(solution)/shard_map/ppermute | solution.py:313
  63.8 3.1 %collective-permute-done.19.refs_7_ = bf16[512,128]{1,0:T(8,128)(2,1)S(1)} collective-permute-done((bf16[512,128]{1,0:T(8,128)(2,1)S(1)}, bf16[512,128]{1,0:T(8,128)(2,1)S(1)}, u32[]{:S(2)}, u32[]{:S(2)}) %collective-permute-start.19) | collective-permute-done | bytes 131104 | tf_op jit(solution)/shard_map/ppermute | solution.py:313
  68.1 1.9 %forward.4 = (bf16[1024,128]{1,0:T(8,128)(2,1)S(1)}, bf16[1024,128]{1,0:T(8,128)(2,1)S(1)}, f32[256,128]{1,0:T(8,128)S(1)}, f32[8,128]{1,0:T(8,128)S(1)}, bf16[2...) custom-call(bf16[24,2,128,128]{3,2,1,0:T(8,128)(2,1)S(1)} %bitcast.10, ...), custom_call_target="tpu_custom_call" | custom-call | tf_op jit(solution)/shard_map/forward/pallas_call | solution.py:25
  70.5 3.2 %collective-permute-start.21 = (bf16[272,128]{1,0:T(8,128)(2,1)S(1)}, bf16[272,128]{1,0:T(8,128)(2,1)S(1)}, u32[]{:S(2)}, u32[]{:S(2)}) collective-permute-start(bf16[272,128]{1,0:T(8,128)(2,1)S(1)} %get-tuple-element.94), channel_id=1, source_target_pairs={{0,4},{1,5},{2,6},{3,7},{4,0},{5,1},{6,2},{7,3},{8,12},{9,13},{10,... | collective-permute-start | bytes 208904 | tf_op jit(solution)/shard_map/ppermute | solution.py:313
  76.0 3.8 %collective-permute-done.22.refs_2_ = bf16[272,128]{1,0:T(8,128)(2,1)S(1)} collective-permute-done((bf16[272,128]{1,0:T(8,128)(2,1)S(1)}, bf16[272,128]{1,0:T(8,128)(2,1)S(1)}, u32[]{:S(2)}, u32[]{:S(2)}) %collective-permute-start.22) | collective-permute-done | bytes 69664 | tf_op jit(solution)/shard_map/ppermute | solution.py:313
  81.1 3.2 %collective-permute-start.23 = (bf16[256,128]{1,0:T(8,128)(2,1)S(1)}, bf16[256,128]{1,0:T(8,128)(2,1)S(1)}, u32[]{:S(2)}, u32[]{:S(2)}) collective-permute-start(bf16[256,128]{1,0:T(8,128)(2,1)S(1)} %get-tuple-element.97.refs_4_), channel_id=1, source_target_pairs={{0,2},{1,3},{2,0},{3,1},{4,6},{5,7},{6,4},{7,5},{8,10},{9,11},{10,... | collective-permute-start | bytes 196616 | tf_op jit(solution)/shard_map/ppermute | solution.py:313
  84.3 1.8 %collective-permute-done.25.refs_7_ = bf16[256,128]{1,0:T(8,128)(2,1)S(1)} collective-permute-done((bf16[256,128]{1,0:T(8,128)(2,1)S(1)}, bf16[256,128]{1,0:T(8,128)(2,1)S(1)}, u32[]{:S(2)}, u32[]{:S(2)}) %collective-permute-start.25) | collective-permute-done | bytes 65568 | tf_op jit(solution)/shard_map/ppermute | solution.py:313
  87.3 1.8 %adjoint.3 = (bf16[1024,128]{1,0:T(8,128)(2,1)S(1)}, f32[512,128]{1,0:T(8,128)S(1)}, f32[8,128]{1,0:T(8,128)S(1)}, bf16[528,128]{1,0:T(8,128)(2,1)S(1)}, bf16[52...) custom-call(bf16[24,128,256]{2,1,0:T(8,128)(2,1)S(1)} %get-tuple-element.67.refs_0_, ...), custom_call_target="tpu_custom_call" | custom-call | tf_op jit(solution)/shard_map/adjoint/pallas_call | solution.py:25
  89.1 2.2 %collective-permute-start.26 = (bf16[528,128]{1,0:T(8,128)(2,1)S(1)}, bf16[528,128]{1,0:T(8,128)(2,1)S(1)}, u32[]{:S(2)}, u32[]{:S(2)}) collective-permute-start(bf16[528,128]{1,0:T(8,128)(2,1)S(1)} %get-tuple-element.100), channel_id=1, source_target_pairs={{0,8},{8,0},{16,24},{24,16},{1,9},{9,1},{17,25},{25,17},{2,10},{10... | collective-permute-start | bytes 405512 | tf_op jit(solution)/shard_map/ppermute | solution.py:313
  94.3 2.0 %collective-permute-done.27.refs_1_ = bf16[528,128]{1,0:T(8,128)(2,1)S(1)} collective-permute-done((bf16[528,128]{1,0:T(8,128)(2,1)S(1)}, bf16[528,128]{1,0:T(8,128)(2,1)S(1)}, u32[]{:S(2)}, u32[]{:S(2)}) %collective-permute-start.27) | collective-permute-done | bytes 135200 | tf_op jit(solution)/shard_map/ppermute | solution.py:313
  96.4 2.1 %collective-permute-done.28.refs_2_ = bf16[528,128]{1,0:T(8,128)(2,1)S(1)} collective-permute-done((bf16[528,128]{1,0:T(8,128)(2,1)S(1)}, bf16[528,128]{1,0:T(8,128)(2,1)S(1)}, u32[]{:S(2)}, u32[]{:S(2)}) %collective-permute-start.28) | collective-permute-done | bytes 135200 | tf_op jit(solution)/shard_map/ppermute | solution.py:313
  99.3 2.3 %collective-permute-start.31 = (bf16[512,128]{1,0:T(8,128)(2,1)S(1)}, bf16[512,128]{1,0:T(8,128)(2,1)S(1)}, u32[]{:S(2)}, u32[]{:S(2)}) collective-permute-start(bf16[512,128]{1,0:T(8,128)(2,1)S(1)} %get-tuple-element.105.refs_4_), channel_id=1, source_target_pairs={{0,24},{8,16},{16,8},{24,0},{1,25},{9,17},{17,9},{25,1},{2,26},{10... | collective-permute-start | bytes 393224 | tf_op jit(solution)/shard_map/ppermute | solution.py:313
  102.9 2.2 %collective-permute-done.31.refs_7_ = bf16[512,128]{1,0:T(8,128)(2,1)S(1)} collective-permute-done((bf16[512,128]{1,0:T(8,128)(2,1)S(1)}, bf16[512,128]{1,0:T(8,128)(2,1)S(1)}, u32[]{:S(2)}, u32[]{:S(2)}) %collective-permute-start.31) | collective-permute-done | bytes 131104 | tf_op jit(solution)/shard_map/ppermute | solution.py:313
  107.9 1.9 %forward.5 = (bf16[1024,128]{1,0:T(8,128)(2,1)S(1)}, bf16[1024,128]{1,0:T(8,128)(2,1)S(1)}, f32[256,128]{1,0:T(8,128)S(1)}, f32[8,128]{1,0:T(8,128)S(1)}, bf16[2...) custom-call(bf16[24,2,128,128]{3,2,1,0:T(8,128)(2,1)S(1)} %bitcast.11, ...), custom_call_target="tpu_custom_call" | custom-call | tf_op jit(solution)/shard_map/forward/pallas_call | solution.py:25
  111.5 2.7 %collective-permute-start.34 = (bf16[272,128]{1,0:T(8,128)(2,1)S(1)}, bf16[272,128]{1,0:T(8,128)(2,1)S(1)}, u32[]{:S(2)}, u32[]{:S(2)}) collective-permute-start(bf16[272,128]{1,0:T(8,128)(2,1)S(1)} %get-tuple-element.110), channel_id=1, source_target_pairs={{0,6},{1,7},{2,4},{3,5},{4,2},{5,3},{6,0},{7,1},{8,14},{9,15},{10,... | collective-permute-start | bytes 208904 | tf_op jit(solution)/shard_map/ppermute | solution.py:313
  114.2 5.2 %collective-permute-done.33.refs_1_ = bf16[272,128]{1,0:T(8,128)(2,1)S(1)} collective-permute-done((bf16[272,128]{1,0:T(8,128)(2,1)S(1)}, bf16[272,128]{1,0:T(8,128)(2,1)S(1)}, u32[]{:S(2)}, u32[]{:S(2)}) %collective-permute-start.33) | collective-permute-done | bytes 69664 | tf_op jit(solution)/shard_map/ppermute | solution.py:313
  136.8 1.8 %unpack.1 = (f32[2,1024,128]{2,1,0:T(8,128)}, f32[2,1024,128]{2,1,0:T(8,128)}) custom-call(f32[1024,128]{1,0:T(8,128)S(1)} %get-tuple-element.128.own_x, f32[1024,128]{1,0:T(8,128)S(1)} %get-tuple-element.129.own_r, bf16[1024,128]{1,0:T(8,128)(2,1)S(1)} %collective-permute-done.41.pair_x, bf16[1024,128]{1,0:T(8,128)(2,1)S(1)} %collective-permute-done.42.pair_r), custom_call_target="tpu_custom_call" | custom-call | tf_op jit(solution)/shard_map/unpack/pallas_call | solution.py:25
  (80 shorter events, 54.4 us)
Async XLA Ops:
  0.6 6.5 %collective-permute-start = (bf16[24,2,128,128]{3,2,1,0:T(8,128)(2,1)}, bf16[24,2,128,128]{3,2,1,0:T(8,128)(2,1)S(1)}, u32[]{:S(2)}, u32[]{:S(2)}) collective-permute-start(bf16[24,2,128,128]{3,2,1,0:T(8,128)(2,1)} %bitcast.7), channel_id=1, source_target_pairs={{0,1},{1,0},{2,3},{3,2},{4,5},{5,4},{6,7},{7,6},{8,9},{9,8},{10,11... | collective-permute-start | bytes 4718600 | tf_op jit(solution)/shard_map/ppermute | solution.py:313
  8.2 7.6 %collective-permute-start.2 = (bf16[512,128]{1,0:T(8,128)(2,1)S(1)}, bf16[512,128]{1,0:T(8,128)(2,1)S(1)}, u32[]{:S(2)}, u32[]{:S(2)}) collective-permute-start(bf16[512,128]{1,0:T(8,128)(2,1)S(1)} %get-tuple-element.73), channel_id=1, source_target_pairs={{0,8},{8,0},{16,24},{24,16},{1,9},{9,1},{17,25},{25,17},{2,10},{10... | collective-permute-start | bytes 393224 | tf_op jit(solution)/shard_map/ppermute | solution.py:313
  11.9 7.9 %collective-permute-start.3 = (bf16[512,128]{1,0:T(8,128)(2,1)S(1)}, bf16[512,128]{1,0:T(8,128)(2,1)S(1)}, u32[]{:S(2)}, u32[]{:S(2)}) collective-permute-start(bf16[512,128]{1,0:T(8,128)(2,1)S(1)} %get-tuple-element.74), channel_id=1, source_target_pairs={{0,16},{8,24},{16,0},{24,8},{1,17},{9,25},{17,1},{25,9},{2,18},{10... | collective-permute-start | bytes 393224 | tf_op jit(solution)/shard_map/ppermute | solution.py:313
  12.7 7.1 %collective-permute-start.4 = (bf16[512,128]{1,0:T(8,128)(2,1)S(1)}, bf16[512,128]{1,0:T(8,128)(2,1)S(1)}, u32[]{:S(2)}, u32[]{:S(2)}) collective-permute-start(bf16[512,128]{1,0:T(8,128)(2,1)S(1)} %get-tuple-element.75), channel_id=1, source_target_pairs={{0,24},{8,16},{16,8},{24,0},{1,25},{9,17},{17,9},{25,1},{2,26},{10... | collective-permute-start | bytes 393224 | tf_op jit(solution)/shard_map/ppermute | solution.py:313
  19.9 6.8 %collective-permute-start.7 = (bf16[512,128]{1,0:T(8,128)(2,1)S(1)}, bf16[512,128]{1,0:T(8,128)(2,1)S(1)}, u32[]{:S(2)}, u32[]{:S(2)}) collective-permute-start(bf16[512,128]{1,0:T(8,128)(2,1)S(1)} %get-tuple-element.76.refs_4_), channel_id=1, source_target_pairs={{0,24},{8,16},{16,8},{24,0},{1,25},{9,17},{17,9},{25,1},{2,26},{10... | collective-permute-start | bytes 393224 | tf_op jit(solution)/shard_map/ppermute | solution.py:313
  21.5 6.5 %collective-permute-start.6 = (bf16[512,128]{1,0:T(8,128)(2,1)S(1)}, bf16[512,128]{1,0:T(8,128)(2,1)S(1)}, u32[]{:S(2)}, u32[]{:S(2)}) collective-permute-start(bf16[512,128]{1,0:T(8,128)(2,1)S(1)} %get-tuple-element.76.refs_4_), channel_id=1, source_target_pairs={{0,16},{8,24},{16,0},{24,8},{1,17},{9,25},{17,1},{25,9},{2,18},{10... | collective-permute-start | bytes 393224 | tf_op jit(solution)/shard_map/ppermute | solution.py:313
  22.0 6.0 %collective-permute-start.5 = (bf16[512,128]{1,0:T(8,128)(2,1)S(1)}, bf16[512,128]{1,0:T(8,128)(2,1)S(1)}, u32[]{:S(2)}, u32[]{:S(2)}) collective-permute-start(bf16[512,128]{1,0:T(8,128)(2,1)S(1)} %get-tuple-element.76.refs_4_), channel_id=1, source_target_pairs={{0,8},{8,0},{16,24},{24,16},{1,9},{9,1},{17,25},{25,17},{2,10},{10... | collective-permute-start | bytes 393224 | tf_op jit(solution)/shard_map/ppermute | solution.py:313
  31.9 6.7 %collective-permute-start.9 = (bf16[272,128]{1,0:T(8,128)(2,1)S(1)}, bf16[272,128]{1,0:T(8,128)(2,1)S(1)}, u32[]{:S(2)}, u32[]{:S(2)}) collective-permute-start(bf16[272,128]{1,0:T(8,128)(2,1)S(1)} %get-tuple-element.80), channel_id=1, source_target_pairs={{0,4},{1,5},{2,6},{3,7},{4,0},{5,1},{6,2},{7,3},{8,12},{9,13},{10,... | collective-permute-start | bytes 208904 | tf_op jit(solution)/shard_map/ppermute | solution.py:313
  34.5 6.2 %collective-permute-start.10 = (bf16[272,128]{1,0:T(8,128)(2,1)S(1)}, bf16[272,128]{1,0:T(8,128)(2,1)S(1)}, u32[]{:S(2)}, u32[]{:S(2)}) collective-permute-start(bf16[272,128]{1,0:T(8,128)(2,1)S(1)} %get-tuple-element.81), channel_id=1, source_target_pairs={{0,6},{1,7},{2,4},{3,5},{4,2},{5,3},{6,0},{7,1},{8,14},{9,15},{10,... | collective-permute-start | bytes 208904 | tf_op jit(solution)/shard_map/ppermute | solution.py:313
  40.8 6.3 %collective-permute-start.13 = (bf16[256,128]{1,0:T(8,128)(2,1)S(1)}, bf16[256,128]{1,0:T(8,128)(2,1)S(1)}, u32[]{:S(2)}, u32[]{:S(2)}) collective-permute-start(bf16[256,128]{1,0:T(8,128)(2,1)S(1)} %get-tuple-element.82.refs_4_), channel_id=1, source_target_pairs={{0,6},{1,7},{2,4},{3,5},{4,2},{5,3},{6,0},{7,1},{8,14},{9,15},{10,... | collective-permute-start | bytes 196616 | tf_op jit(solution)/shard_map/ppermute | solution.py:313
  41.6 6.6 %collective-permute-start.12 = (bf16[256,128]{1,0:T(8,128)(2,1)S(1)}, bf16[256,128]{1,0:T(8,128)(2,1)S(1)}, u32[]{:S(2)}, u32[]{:S(2)}) collective-permute-start(bf16[256,128]{1,0:T(8,128)(2,1)S(1)} %get-tuple-element.82.refs_4_), channel_id=1, source_target_pairs={{0,4},{1,5},{2,6},{3,7},{4,0},{5,1},{6,2},{7,3},{8,12},{9,13},{10,... | collective-permute-start | bytes 196616 | tf_op jit(solution)/shard_map/ppermute | solution.py:313
  41.6 6.5 %collective-permute-start.11 = (bf16[256,128]{1,0:T(8,128)(2,1)S(1)}, bf16[256,128]{1,0:T(8,128)(2,1)S(1)}, u32[]{:S(2)}, u32[]{:S(2)}) collective-permute-start(bf16[256,128]{1,0:T(8,128)(2,1)S(1)} %get-tuple-element.82.refs_4_), channel_id=1, source_target_pairs={{0,2},{1,3},{2,0},{3,1},{4,6},{5,7},{6,4},{7,5},{8,10},{9,11},{10,... | collective-permute-start | bytes 196616 | tf_op jit(solution)/shard_map/ppermute | solution.py:313
  50.0 5.7 %collective-permute-start.14 = (bf16[528,128]{1,0:T(8,128)(2,1)S(1)}, bf16[528,128]{1,0:T(8,128)(2,1)S(1)}, u32[]{:S(2)}, u32[]{:S(2)}) collective-permute-start(bf16[528,128]{1,0:T(8,128)(2,1)S(1)} %get-tuple-element.85), channel_id=1, source_target_pairs={{0,8},{8,0},{16,24},{24,16},{1,9},{9,1},{17,25},{25,17},{2,10},{10... | collective-permute-start | bytes 405512 | tf_op jit(solution)/shard_map/ppermute | solution.py:313
  52.1 6.2 %collective-permute-start.15 = (bf16[528,128]{1,0:T(8,128)(2,1)S(1)}, bf16[528,128]{1,0:T(8,128)(2,1)S(1)}, u32[]{:S(2)}, u32[]{:S(2)}) collective-permute-start(bf16[528,128]{1,0:T(8,128)(2,1)S(1)} %get-tuple-element.86), channel_id=1, source_target_pairs={{0,16},{8,24},{16,0},{24,8},{1,17},{9,25},{17,1},{25,9},{2,18},{10... | collective-permute-start | bytes 405512 | tf_op jit(solution)/shard_map/ppermute | solution.py:313
  52.8 7.4 %collective-permute-start.16 = (bf16[528,128]{1,0:T(8,128)(2,1)S(1)}, bf16[528,128]{1,0:T(8,128)(2,1)S(1)}, u32[]{:S(2)}, u32[]{:S(2)}) collective-permute-start(bf16[528,128]{1,0:T(8,128)(2,1)S(1)} %get-tuple-element.87), channel_id=1, source_target_pairs={{0,24},{8,16},{16,8},{24,0},{1,25},{9,17},{17,9},{25,1},{2,26},{10... | collective-permute-start | bytes 405512 | tf_op jit(solution)/shard_map/ppermute | solution.py:313
  60.3 6.7 %collective-permute-start.19 = (bf16[512,128]{1,0:T(8,128)(2,1)S(1)}, bf16[512,128]{1,0:T(8,128)(2,1)S(1)}, u32[]{:S(2)}, u32[]{:S(2)}) collective-permute-start(bf16[512,128]{1,0:T(8,128)(2,1)S(1)} %get-tuple-element.90.refs_4_), channel_id=1, source_target_pairs={{0,24},{8,16},{16,8},{24,0},{1,25},{9,17},{17,9},{25,1},{2,26},{10... | collective-permute-start | bytes 393224 | tf_op jit(solution)/shard_map/ppermute | solution.py:313
  62.1 6.0 %collective-permute-start.18 = (bf16[512,128]{1,0:T(8,128)(2,1)S(1)}, bf16[512,128]{1,0:T(8,128)(2,1)S(1)}, u32[]{:S(2)}, u32[]{:S(2)}) collective-permute-start(bf16[512,128]{1,0:T(8,128)(2,1)S(1)} %get-tuple-element.90.refs_4_), channel_id=1, source_target_pairs={{0,16},{8,24},{16,0},{24,8},{1,17},{9,25},{17,1},{25,9},{2,18},{10... | collective-permute-start | bytes 393224 | tf_op jit(solution)/shard_map/ppermute | solution.py:313
  62.4 5.8 %collective-permute-start.17 = (bf16[512,128]{1,0:T(8,128)(2,1)S(1)}, bf16[512,128]{1,0:T(8,128)(2,1)S(1)}, u32[]{:S(2)}, u32[]{:S(2)}) collective-permute-start(bf16[512,128]{1,0:T(8,128)(2,1)S(1)} %get-tuple-element.90.refs_4_), channel_id=1, source_target_pairs={{0,8},{8,0},{16,24},{24,16},{1,9},{9,1},{17,25},{25,17},{2,10},{10... | collective-permute-start | bytes 393224 | tf_op jit(solution)/shard_map/ppermute | solution.py:313
  70.5 5.4 %collective-permute-start.21 = (bf16[272,128]{1,0:T(8,128)(2,1)S(1)}, bf16[272,128]{1,0:T(8,128)(2,1)S(1)}, u32[]{:S(2)}, u32[]{:S(2)}) collective-permute-start(bf16[272,128]{1,0:T(8,128)(2,1)S(1)} %get-tuple-element.94), channel_id=1, source_target_pairs={{0,4},{1,5},{2,6},{3,7},{4,0},{5,1},{6,2},{7,3},{8,12},{9,13},{10,... | collective-permute-start | bytes 208904 | tf_op jit(solution)/shard_map/ppermute | solution.py:313
  73.7 6.1 %collective-permute-start.22 = (bf16[272,128]{1,0:T(8,128)(2,1)S(1)}, bf16[272,128]{1,0:T(8,128)(2,1)S(1)}, u32[]{:S(2)}, u32[]{:S(2)}) collective-permute-start(bf16[272,128]{1,0:T(8,128)(2,1)S(1)} %get-tuple-element.95), channel_id=1, source_target_pairs={{0,6},{1,7},{2,4},{3,5},{4,2},{5,3},{6,0},{7,1},{8,14},{9,15},{10,... | collective-permute-start | bytes 208904 | tf_op jit(solution)/shard_map/ppermute | solution.py:313
  79.8 6.3 %collective-permute-start.25 = (bf16[256,128]{1,0:T(8,128)(2,1)S(1)}, bf16[256,128]{1,0:T(8,128)(2,1)S(1)}, u32[]{:S(2)}, u32[]{:S(2)}) collective-permute-start(bf16[256,128]{1,0:T(8,128)(2,1)S(1)} %get-tuple-element.97.refs_4_), channel_id=1, source_target_pairs={{0,6},{1,7},{2,4},{3,5},{4,2},{5,3},{6,0},{7,1},{8,14},{9,15},{10,... | collective-permute-start | bytes 196616 | tf_op jit(solution)/shard_map/ppermute | solution.py:313
  80.7 6.6 %collective-permute-start.24 = (bf16[256,128]{1,0:T(8,128)(2,1)S(1)}, bf16[256,128]{1,0:T(8,128)(2,1)S(1)}, u32[]{:S(2)}, u32[]{:S(2)}) collective-permute-start(bf16[256,128]{1,0:T(8,128)(2,1)S(1)} %get-tuple-element.97.refs_4_), channel_id=1, source_target_pairs={{0,4},{1,5},{2,6},{3,7},{4,0},{5,1},{6,2},{7,3},{8,12},{9,13},{10,... | collective-permute-start | bytes 196616 | tf_op jit(solution)/shard_map/ppermute | solution.py:313
  81.1 6.3 %collective-permute-start.23 = (bf16[256,128]{1,0:T(8,128)(2,1)S(1)}, bf16[256,128]{1,0:T(8,128)(2,1)S(1)}, u32[]{:S(2)}, u32[]{:S(2)}) collective-permute-start(bf16[256,128]{1,0:T(8,128)(2,1)S(1)} %get-tuple-element.97.refs_4_), channel_id=1, source_target_pairs={{0,2},{1,3},{2,0},{3,1},{4,6},{5,7},{6,4},{7,5},{8,10},{9,11},{10,... | collective-permute-start | bytes 196616 | tf_op jit(solution)/shard_map/ppermute | solution.py:313
  89.1 5.2 %collective-permute-start.26 = (bf16[528,128]{1,0:T(8,128)(2,1)S(1)}, bf16[528,128]{1,0:T(8,128)(2,1)S(1)}, u32[]{:S(2)}, u32[]{:S(2)}) collective-permute-start(bf16[528,128]{1,0:T(8,128)(2,1)S(1)} %get-tuple-element.100), channel_id=1, source_target_pairs={{0,8},{8,0},{16,24},{24,16},{1,9},{9,1},{17,25},{25,17},{2,10},{10... | collective-permute-start | bytes 405512 | tf_op jit(solution)/shard_map/ppermute | solution.py:313
  91.3 5.0 %collective-permute-start.27 = (bf16[528,128]{1,0:T(8,128)(2,1)S(1)}, bf16[528,128]{1,0:T(8,128)(2,1)S(1)}, u32[]{:S(2)}, u32[]{:S(2)}) collective-permute-start(bf16[528,128]{1,0:T(8,128)(2,1)S(1)} %get-tuple-element.101), channel_id=1, source_target_pairs={{0,16},{8,24},{16,0},{24,8},{1,17},{9,25},{17,1},{25,9},{2,18},{10... | collective-permute-start | bytes 405512 | tf_op jit(solution)/shard_map/ppermute | solution.py:313
  91.8 6.6 %collective-permute-start.28 = (bf16[528,128]{1,0:T(8,128)(2,1)S(1)}, bf16[528,128]{1,0:T(8,128)(2,1)S(1)}, u32[]{:S(2)}, u32[]{:S(2)}) collective-permute-start(bf16[528,128]{1,0:T(8,128)(2,1)S(1)} %get-tuple-element.102), channel_id=1, source_target_pairs={{0,24},{8,16},{16,8},{24,0},{1,25},{9,17},{17,9},{25,1},{2,26},{10... | collective-permute-start | bytes 405512 | tf_op jit(solution)/shard_map/ppermute | solution.py:313
  99.3 5.9 %collective-permute-start.31 = (bf16[512,128]{1,0:T(8,128)(2,1)S(1)}, bf16[512,128]{1,0:T(8,128)(2,1)S(1)}, u32[]{:S(2)}, u32[]{:S(2)}) collective-permute-start(bf16[512,128]{1,0:T(8,128)(2,1)S(1)} %get-tuple-element.105.refs_4_), channel_id=1, source_target_pairs={{0,24},{8,16},{16,8},{24,0},{1,25},{9,17},{17,9},{25,1},{2,26},{10... | collective-permute-start | bytes 393224 | tf_op jit(solution)/shard_map/ppermute | solution.py:313
  101.6 5.0 %collective-permute-start.30 = (bf16[512,128]{1,0:T(8,128)(2,1)S(1)}, bf16[512,128]{1,0:T(8,128)(2,1)S(1)}, u32[]{:S(2)}, u32[]{:S(2)}) collective-permute-start(bf16[512,128]{1,0:T(8,128)(2,1)S(1)} %get-tuple-element.105.refs_4_), channel_id=1, source_target_pairs={{0,16},{8,24},{16,0},{24,8},{1,17},{9,25},{17,1},{25,9},{2,18},{10... | collective-permute-start | bytes 393224 | tf_op jit(solution)/shard_map/ppermute | solution.py:313
  111.1 8.3 %collective-permute-start.33 = (bf16[272,128]{1,0:T(8,128)(2,1)S(1)}, bf16[272,128]{1,0:T(8,128)(2,1)S(1)}, u32[]{:S(2)}, u32[]{:S(2)}) collective-permute-start(bf16[272,128]{1,0:T(8,128)(2,1)S(1)} %get-tuple-element.109), channel_id=1, source_target_pairs={{0,4},{1,5},{2,6},{3,7},{4,0},{5,1},{6,2},{7,3},{8,12},{9,13},{10,... | collective-permute-start | bytes 208904 | tf_op jit(solution)/shard_map/ppermute | solution.py:313
  111.5 7.9 %collective-permute-start.34 = (bf16[272,128]{1,0:T(8,128)(2,1)S(1)}, bf16[272,128]{1,0:T(8,128)(2,1)S(1)}, u32[]{:S(2)}, u32[]{:S(2)}) collective-permute-start(bf16[272,128]{1,0:T(8,128)(2,1)S(1)} %get-tuple-element.110), channel_id=1, source_target_pairs={{0,6},{1,7},{2,4},{3,5},{4,2},{5,3},{6,0},{7,1},{8,14},{9,15},{10,... | collective-permute-start | bytes 208904 | tf_op jit(solution)/shard_map/ppermute | solution.py:313
  120.1 6.1 %collective-permute-start.37 = (bf16[256,128]{1,0:T(8,128)(2,1)S(1)}, bf16[256,128]{1,0:T(8,128)(2,1)S(1)}, u32[]{:S(2)}, u32[]{:S(2)}) collective-permute-start(bf16[256,128]{1,0:T(8,128)(2,1)S(1)} %get-tuple-element.113.refs_0_), channel_id=1, source_target_pairs={{0,6},{1,7},{2,4},{3,5},{4,2},{5,3},{6,0},{7,1},{8,14},{9,15},{10,... | collective-permute-start | bytes 196616 | tf_op jit(solution)/shard_map/ppermute | solution.py:313
  121.6 6.1 %collective-permute-start.36 = (bf16[256,128]{1,0:T(8,128)(2,1)S(1)}, bf16[256,128]{1,0:T(8,128)(2,1)S(1)}, u32[]{:S(2)}, u32[]{:S(2)}) collective-permute-start(bf16[256,128]{1,0:T(8,128)(2,1)S(1)} %get-tuple-element.113.refs_0_), channel_id=1, source_target_pairs={{0,4},{1,5},{2,6},{3,7},{4,0},{5,1},{6,2},{7,3},{8,12},{9,13},{10,... | collective-permute-start | bytes 196616 | tf_op jit(solution)/shard_map/ppermute | solution.py:313
  (15 other events, 101.9 us)

commit v3 on v2

v3 whole, which is shorter than its diff:
```python
import functools

import jax
import jax.numpy as jnp
from jax import lax
from jax.experimental import pallas as pl
from jax.experimental.pallas import tpu as pltpu
from jax.sharding import PartitionSpec as P

SRC_DEV = 512
ITERS = 3
EPSILON = 1e-06
GROUP = 8
TAIL = 16
VMEM_BYTES = 16 << 20

F32 = jnp.float32
BF16 = jnp.bfloat16


def call(kernel, name, outs, scratch, *ins, away=0):
    def space(place, dtype):
        if place < away:
            return pltpu.HBM
        return pltpu.SMEM if dtype == jnp.int32 else pltpu.VMEM

    def room(shape, dtype):
        if dtype is pltpu.SemaphoreType.DMA:
            return dtype((shape,))
        return (pltpu.SMEM if dtype == jnp.int32 else pltpu.VMEM)(shape, dtype)

    return pl.pallas_call(
        kernel,
        name=name,
        out_shape=[jax.ShapeDtypeStruct(s, d) for s, d in outs],
        in_specs=[pl.BlockSpec(memory_space=space(i, a.dtype)) for i, a in enumerate(ins)],
        out_specs=[pl.BlockSpec(memory_space=pltpu.VMEM) for _ in outs],
        scratch_shapes=[room(s, d) for s, d in scratch],
        compiler_params=pltpu.CompilerParams(vmem_limit_bytes=VMEM_BYTES),
    )(*ins)


def low_half(shape):
    return lax.broadcasted_iota(jnp.int32, shape, len(shape) - 1) < shape[-1] // 2


def turn(value):
    return pltpu.roll(value, value.shape[-1] // 2, value.ndim - 1)


def times_i(value, sign):
    rolled = turn(value)
    return jnp.where(low_half(value.shape), -sign * rolled, sign * rolled)


def both_parts(row):
    return row + turn(row)


def fold_squares(value):
    return jnp.sum((value * value).reshape(-1, 8, value.shape[-1]), axis=0)


def rows_of_norm(folded):
    row = both_parts(jnp.sum(folded, axis=0, keepdims=True))
    return jnp.broadcast_to(row, (8, folded.shape[-1]))


def norm_tail(norm):
    row = jnp.broadcast_to(norm[:1], (TAIL, norm.shape[-1]))
    high = row.astype(BF16).astype(F32)
    at = lax.broadcasted_iota(jnp.int32, row.shape, 0)
    return jnp.where(at == 0, high, jnp.where(at == 1, row - high, 0.0)).astype(BF16)


def norm_from(tail):
    tail = tail.astype(F32)
    return jnp.broadcast_to(tail[:1] + tail[1:2], (8, tail.shape[-1]))


def spans(size, count):
    return pl.ds(pl.multiple_of(count * size, size), size)


def slots(index_ref, step):
    used = index_ref[2, 0]

    def turn_of(group, carry):
        for lane in range(GROUP):
            slot = group * GROUP + lane
            step(slot, slot < used, index_ref[0, slot], index_ref[1, slot])
        return carry

    lax.fori_loop(0, (used + GROUP - 1) // GROUP, turn_of, 0)


def add_tile(acc_ref, weights, plain_ref, turned_ref, source, target):
    size = weights.shape[0]
    right = jnp.concatenate([plain_ref[spans(size, source), :], turned_ref[spans(size, source), :]], axis=0)
    at = spans(size, target)
    acc_ref[at, :] = acc_ref[at, :] + jnp.dot(weights, right, preferred_element_type=F32)


def put_chunk(chunk, plain_ref, turned_ref, at, sign):
    wide = chunk.astype(F32)
    plain_ref[at, :] = chunk
    turned_ref[at, :] = times_i(wide, sign).astype(BF16)
    return fold_squares(wide)


def packed_record(core, real, imag):
    first = jnp.where(core == 0, real, turn(real))
    second = jnp.where(core == 0, turn(imag), imag)
    return jnp.where(low_half(real.shape), first, second)


def pack_kernel(core_axis, tiles, record_ref, tile_ref, index_ref, turned_tile_ref, total_ref, plain_ref, turned_ref):
    core = lax.rem(lax.axis_index(core_axis), 2)
    for at in range(0, plain_ref.shape[0], 128):
        span = pl.ds(at, 128)
        packed = packed_record(core, record_ref[0, span, :], record_ref[1, span, :])
        put_chunk(packed.astype(BF16), plain_ref, turned_ref, span, -1.0)
    total_ref[...] = jnp.zeros_like(total_ref)
    slots(index_ref, turn_step(tiles, tile_ref, turned_tile_ref, total_ref, plain_ref, turned_ref))


def turn_step(tiles, tile_ref, turned_tile_ref, total_ref, plain_ref, turned_ref):
    def step(slot, valid, row, col):
        weights = jnp.concatenate([tile_ref[slot, 0].T, tile_ref[slot, 1].T], axis=1)
        turned_tile_ref[slot] = weights
        add_tile(total_ref, weights, plain_ref, turned_ref, row, jnp.where(valid, col, tiles))

    return step


def first_adjoint_kernel(hyd_axis, order, tiles, tile_ref, index_ref, own_total_ref, plain_ref, turned_ref, *refs):
    turned_tile_ref, own_ref, sends, total_ref = refs[0], refs[1], refs[2:-1], refs[-1]
    total_ref[...] = jnp.zeros_like(total_ref)
    slots(index_ref, turn_step(tiles, tile_ref, turned_tile_ref, total_ref, plain_ref, turned_ref))
    give_columns(hyd_axis, order, own_total_ref, total_ref, own_ref, sends, None)


def give_columns(hyd_axis, order, first_ref, second_ref, own_ref, sends, tail):
    here = lax.axis_index(hyd_axis)
    part = own_ref.shape[0] // 2
    own_ref[:part, :] = first_ref[spans(part, here), :]
    own_ref[part:, :] = second_ref[spans(part, here), :]
    for send, offset in zip(sends, order):
        there = here ^ offset
        send[:part, :] = first_ref[spans(part, there), :].astype(BF16)
        send[part : 2 * part, :] = second_ref[spans(part, there), :].astype(BF16)
        if tail is not None:
            send[2 * part :, :] = tail


def adjoint_kernel(hyd_axis, core_axis, order, z_order, tiles, *refs):
    tile_a, tile_b, index_a, index_b = refs[:4]
    zs, hyds, refs = len(z_order) + 1, len(order) + 1, refs[4:]
    chunks = refs[:zs]
    plain_ref, own_ref, norm_ref = refs[zs : 3 + zs]
    sends = refs[3 + zs : 2 + zs + hyds]
    turned_ref, first_ref, second_ref = refs[2 + zs + hyds :]
    here = lax.axis_index(core_axis) // 2
    rows = chunks[0].shape[0]
    folded = jnp.zeros((8, plain_ref.shape[-1]), F32)
    for chunk, offset in zip(chunks, (0, *z_order)):
        folded += put_chunk(chunk[...], plain_ref, turned_ref, spans(rows, here ^ offset), -1.0)
    norm = rows_of_norm(folded)
    norm_ref[...] = norm
    for index, tile_ref, total_ref in ((index_a, tile_a, first_ref), (index_b, tile_b, second_ref)):
        total_ref[...] = jnp.zeros_like(total_ref)

        def step(slot, valid, row, col):
            add_tile(total_ref, tile_ref[slot], plain_ref, turned_ref, row, jnp.where(valid, col, tiles))

        slots(index, step)
    give_columns(hyd_axis, order, first_ref, second_ref, own_ref, sends, norm_tail(norm))


def forward_kernel(hyd_axis, core_axis, order, z_order, tiles, *refs):
    tile_a, tile_b, index_a, index_b = refs[:4]
    zs, hyds, refs = len(z_order) + 1, len(order) + 1, refs[4:]
    chunks = refs[:hyds]
    plain_a, plain_b, own_ref, norm_ref = refs[hyds : 4 + hyds]
    sends = refs[4 + hyds : 3 + hyds + zs]
    turned_a, turned_b, total_ref = refs[3 + hyds + zs :]
    here = lax.axis_index(hyd_axis)
    part = chunks[0].shape[0] // 2
    folded = jnp.zeros((8, plain_a.shape[-1]), F32)
    for chunk, offset in zip(chunks, (0, *order)):
        at = spans(part, here ^ offset)
        folded += put_chunk(chunk[:part, :], plain_a, turned_a, at, 1.0)
        folded += put_chunk(chunk[part:, :], plain_b, turned_b, at, 1.0)
    norm = rows_of_norm(folded)
    norm_ref[...] = norm
    total_ref[...] = jnp.zeros_like(total_ref)
    for index, tile_ref, plain_ref, turned_ref in (
        (index_a, tile_a, plain_a, turned_a),
        (index_b, tile_b, plain_b, turned_b),
    ):

        def step(slot, valid, row, col):
            weights = jnp.concatenate([tile_ref[slot, 0], tile_ref[slot, 1]], axis=1)
            add_tile(total_ref, weights, plain_ref, turned_ref, col, jnp.where(valid, row, tiles))

        slots(index, step)
    here = lax.axis_index(core_axis) // 2
    rows = own_ref.shape[0]
    own_ref[...] = total_ref[spans(rows, here), :]
    tail = norm_tail(norm)
    for send, offset in zip(sends, z_order):
        send[:rows, :] = total_ref[spans(rows, here ^ offset), :].astype(BF16)
        send[rows:, :] = tail


def summed(own_ref, others):
    value = own_ref[...]
    for other in others:
        value = value + other[: own_ref.shape[0], :].astype(F32)
    return value


def norm_sum(own_norm, others, size):
    norm = own_norm
    for other in others:
        norm = norm + norm_from(other[size:, :])
    return norm


def start_kernel(others, own_ref, *refs):
    gradient = summed(own_ref, refs[:others])
    refs[-2][...] = gradient
    refs[-1][...] = gradient.astype(BF16)


def image_kernel(others, later, last, own_ref, norm_ref, *refs):
    ins, refs = refs[:others], refs[others:]
    image = summed(own_ref, ins)
    gamma = norm_sum(norm_ref[...], ins, own_ref.shape[0])
    if later:
        before_ref, gamma_ref = refs[:2]
        beta = gamma / (gamma_ref[...] + EPSILON)
        image = image + beta[:1] * before_ref[...]
        refs = refs[2:]
        refs[2][...] = beta
    refs[0][...] = image.astype(BF16)
    refs[1][...] = gamma
    if not last:
        refs[-1][...] = image


def gradient_kernel(others, own_ref, norm_ref, *refs):
    ins, (before_ref, gamma_ref, narrow_ref, alpha_ref, *wide) = refs[:others], refs[others:]
    change = summed(own_ref, ins)
    alpha = gamma_ref[...] / (norm_sum(norm_ref[...], ins, own_ref.shape[0]) + EPSILON)
    gradient = before_ref[...] - alpha[:1] * change
    narrow_ref[...] = gradient.astype(BF16)
    alpha_ref[...] = alpha
    for wide_ref in wide:
        wide_ref[...] = gradient


def gather_kernel(core_axis, z_order, *refs):
    chunks, (plain_ref, norm_ref) = refs[:-2], refs[-2:]
    here = lax.axis_index(core_axis) // 2
    rows = chunks[0].shape[0]
    folded = jnp.zeros((8, plain_ref.shape[-1]), F32)
    for chunk, offset in zip(chunks, (0, *z_order)):
        chunk = chunk[...]
        plain_ref[spans(rows, here ^ offset), :] = chunk
        folded += fold_squares(chunk.astype(F32))
    norm_ref[...] = rows_of_norm(folded)


def answer_kernel(core_axis, norms, record_ref, gamma_ref, *refs):
    norm = refs[0][...]
    for other in refs[1:norms]:
        norm = norm + other[...]
    refs = refs[norms:]
    alphas = [ref[...] for ref in refs[: ITERS - 1]] + [gamma_ref[...] / (norm + EPSILON)]
    refs = refs[ITERS - 1 :]
    betas = [ref[...] for ref in refs[: ITERS - 1]]
    refs = refs[ITERS - 1 :]
    own_g, pair_g, images = refs[:ITERS], refs[ITERS : 2 * ITERS], refs[2 * ITERS : 3 * ITERS]
    own_x, pair_x, wide_r, narrow_r = refs[3 * ITERS :]
    weights = [None] * ITERS
    weights[-1] = alphas[-1]
    for k in range(ITERS - 2, -1, -1):
        weights[k] = alphas[k] + betas[k] * weights[k + 1]
    core = lax.rem(lax.axis_index(core_axis), 2)
    for at in range(0, own_x.shape[0], 128):
        span = pl.ds(at, 128)
        own_x[span, :] = sum(w[:1] * g[span, :].astype(F32) for w, g in zip(weights, own_g))
        pair_x[span, :] = sum(w[:1] * g[span, :].astype(F32) for w, g in zip(weights, pair_g)).astype(BF16)
    for at in range(0, wide_r.shape[0], 128):
        span = pl.ds(at, 128)
        residual = packed_record(core, record_ref[0, span, :], record_ref[1, span, :])
        for alpha, image in zip(alphas, images):
            residual = residual - alpha[:1] * image[span, :].astype(F32)
        wide_r[span, :] = residual
        narrow_r[span, :] = residual.astype(BF16)


def unpack_kernel(core_axis, own_x, own_r, pair_x, pair_r, x_ref, r_ref):
    core = lax.rem(lax.axis_index(core_axis), 2)
    for own, pair, out in ((own_x, pair_x, x_ref), (own_r, pair_r, r_ref)):
        for at in range(0, own.shape[0], 128):
            span = pl.ds(at, 128)
            mine, theirs = own[span, :], pair[span, :].astype(F32)
            first = jnp.where(core == 0, mine, theirs)
            second = jnp.where(core == 0, theirs, mine)
            low = low_half(mine.shape)
            out[0, span, :] = jnp.where(low, first, turn(second))
            out[1, span, :] = jnp.where(low, turn(first), second)


def solution(mesh):
    hyds, srcs = mesh.shape["hyd"], mesh.shape["src"]
    zs = srcs // 2

    def swap(value, axis, size, offset):
        return lax.ppermute(value, axis, [(i, i ^ offset) for i in range(size)])

    hyd_order = tuple(range(1, hyds))
    z_order = (zs - 1, *range(1, zs - 1))

    def over_hyd(values, order):
        return [swap(v, "hyd", hyds, o) for v, o in zip(values, order)]

    def over_z(values, order):
        return [swap(v, "src", srcs, 2 * o) for v, o in zip(values, order)]

    hyd_back, z_back = hyd_order[::-1], z_order[::-1]

    def body(record, tile_data, tile_rows, tile_cols, tile_counts):
        own_tiles = tile_data[0, 0]
        slot_count, _, size, _ = own_tiles.shape
        rows, shots = record.shape[1:]
        cols = 2 * SRC_DEV
        row_tiles, col_tiles = rows // size, cols // size
        row_part, col_part = rows // zs, cols // hyds
        norm = ((8, shots), F32)
        row_sends = [((row_part + TAIL, shots), BF16)] * (zs - 1)
        col_sends = [((2 * col_part + TAIL, shots), BF16)] * (hyds - 1)
        row_total, col_total = ((rows + size, shots), F32), ((cols + size, shots), F32)
        vector = lambda n, dtype: ((n, shots), dtype)

        pair_tiles = swap(own_tiles, "src", srcs, 1)
        index = jnp.stack([tile_rows[0, 0], tile_cols[0, 0], jnp.broadcast_to(tile_counts[0, 0], (slot_count,))])
        pair_index = swap(index, "src", srcs, 1)
        turned_shape = ((slot_count, size, 2 * size), BF16)
        turned_own, total, plain, turned = call(
            functools.partial(pack_kernel, "src", col_tiles), "pack",
            [turned_shape, col_total, vector(rows, BF16), vector(rows, BF16)],
            [],
            record, own_tiles, index,
        )
        turned_pair, own, *sends = call(
            functools.partial(first_adjoint_kernel, "hyd", hyd_order, col_tiles), "first_adjoint",
            [turned_shape, vector(2 * col_part, F32)] + [vector(2 * col_part, BF16)] * (hyds - 1), [col_total],
            pair_tiles, pair_index, total, plain, turned,
        )
        gradient, narrow = call(
            functools.partial(start_kernel, hyds - 1), "start",
            [vector(2 * col_part, F32), vector(2 * col_part, BF16)], [],
            own, *over_hyd(sends, hyd_order),
        )

        alphas, betas, own_g, pair_g, images = [], [], [], [], []
        image = gamma = None
        for step in range(ITERS):
            last = step + 1 == ITERS
            plain_a, plain_b, own, own_norm, *sends = call(
                functools.partial(forward_kernel, "hyd", "src", hyd_back, z_order, row_tiles), "forward",
                [vector(cols, BF16), vector(cols, BF16), vector(row_part, F32), norm] + row_sends,
                [vector(cols, BF16), vector(cols, BF16), row_total],
                own_tiles, pair_tiles, index, pair_index, narrow, *over_hyd([narrow] * (hyds - 1), hyd_back),
            )
            own_g.append(plain_a)
            pair_g.append(plain_b)
            narrow, gamma, *more = call(
                functools.partial(image_kernel, zs - 1, step > 0, last), "image",
                [vector(row_part, BF16), norm] + [norm] * (step > 0) + [vector(row_part, F32)] * (not last), [],
                own, own_norm, *over_z(sends, z_order), *([image, gamma] if step else []),
            )
            image = None if last else more.pop()
            betas += more
            chunks = [narrow] + over_z([narrow] * (zs - 1), z_back)
            if last:
                break
            plain, own, own_norm, *sends = call(
                functools.partial(adjoint_kernel, "hyd", "src", hyd_order, z_back, col_tiles), "adjoint",
                [vector(rows, BF16), vector(2 * col_part, F32), norm] + col_sends,
                [vector(rows, BF16), col_total, col_total],
                turned_own, turned_pair, index, pair_index, *chunks,
            )
            images.append(plain)
            more_steps = step + 2 < ITERS
            narrow, alpha, *wide = call(
                functools.partial(gradient_kernel, hyds - 1), "gradient",
                [vector(2 * col_part, BF16), norm] + [vector(2 * col_part, F32)] * more_steps, [],
                own, own_norm, *over_hyd(sends, hyd_order), gradient, gamma,
            )
            gradient = wide[0] if more_steps else None
            alphas.append(alpha)

        plain, own_norm = call(functools.partial(gather_kernel, "src", z_back), "gather", [vector(rows, BF16), norm], [], *chunks)
        images.append(plain)
        norms = [own_norm] + over_hyd([own_norm] * (hyds - 1), hyd_back)
        own_x, pair_x, wide_r, narrow_r = call(
            functools.partial(answer_kernel, "src", hyds), "answer",
            [vector(cols, F32), vector(cols, BF16), vector(rows, F32), vector(rows, BF16)], [],
            record, gamma, *norms, *alphas, *betas, *own_g, *pair_g, *images,
        )
        return call(
            functools.partial(unpack_kernel, "src"), "unpack",
            [((2, cols, shots), F32), ((2, rows, shots), F32)], [],
            own_x, wide_r, swap(pair_x, "src", srcs, 1), swap(narrow_r, "src", srcs, 1),
        )

    in_specs = (
        P(None, "hyd", None),
        P("hyd", "src", None, None, None, None),
        P("hyd", "src", None),
        P("hyd", "src", None),
        P("hyd", "src"),
    )
    out_specs = (P(None, "src", None), P(None, "hyd", None))
    return jax.shard_map(body, mesh=mesh, in_specs=in_specs, out_specs=out_specs, check_vma=False)
```

time: 137 us -> 134 us (0.978); the launches traced: 139 us -> 132 us
  waiting for transfers between devices: 61.9 us -> 57.5 us
  Pallas kernels: 16.5 us -> 15.1 us
    ppermute x43, waiting for transfers between devices: 61.9 us -> 57.5 us  [swap(): return lax.ppermute(value, axis, [(i, i ^ offset) for i in range(size)])]
    pallas_call x16, Pallas kernels: 16.5 us -> 15.1 us  [call(): pl.pallas_call(kernel, name=name, out_shape=[jax.ShapeDtypeStruct(s, d) f...]
  transfers between devices with their start and end apart: 43 -> 43, of which waited for: 34 -> 40; matrix products, arithmetic and copies ran while one was open for 1% -> 1% of each run, Pallas kernels for 1% -> 1%
where the time goes in v3:
time: 134 us; the launch traced here: 132 us
  waiting for transfers between devices  57.5 us (43%)
  starting transfers between devices  55 us (41%)
  Pallas kernels  15.1 us (11%)
  local copies, waits for them, and re-layouts  2.72 us (2%)
  between operations  1.44 us (1%)
    ppermute x43, waiting for transfers between devices, swap(): return lax.ppermute(value, axis, [(i, i ^ offset) for i in range(size)])  57.5 us
    ppermute x43, starting transfers between devices, swap(): return lax.ppermute(value, axis, [(i, i ^ offset) for i in range(size)])  55 us
    pallas_call x16, Pallas kernels, call(): pl.pallas_call(kernel, name=name, out_shape=[jax.ShapeDtypeStruct(s, d) f...  15.1 us
  transfers between devices with their start and end apart: 43, of which 40 were waited for; matrix products, arithmetic and copies ran while one was open for 1% of the time, Pallas kernels for 1%

profile of v3, /device:TPU:0, one launch (start us, length us, event | category | flops | bytes accessed | tf_op | source)
XLA Modules:
  0.0 132.4 jit_solution(15894039152059196339)
XLA Ops:
  5.3 1.8 %pack.1 = (bf16[24,128,256]{2,1,0:T(8,128)(2,1)S(1)}, f32[1152,128]{1,0:T(8,128)S(1)}, bf16[1024,128]{1,0:T(8,128)(2,1)S(1)}, bf16[1024,128]{1,0:T(8,128)(2,1)S(1)}) custom-call(f32[2,1024,128]{2,1,0:T(8,128)S(1)} %copy-done.2, bf16[24,2,128,128]{3,2,1,0:T(8,128)(2,1)S(1)} %bitcast.8, s32[3,24]{1,0:T(4,128)S(1)} %add_add_fusion.index_ref.refs_2_), custom_call_target="tpu_custom_call" | custom-call | tf_op jit(solution)/shard_map/pack/pallas_call | solution.py:32
  8.2 3.0 %collective-permute-start.2 = (bf16[512,128]{1,0:T(8,128)(2,1)S(1)}, bf16[512,128]{1,0:T(8,128)(2,1)S(1)}, u32[]{:S(2)}, u32[]{:S(2)}) collective-permute-start(bf16[512,128]{1,0:T(8,128)(2,1)S(1)} %get-tuple-element.73), channel_id=1, source_target_pairs={{0,8},{8,0},{16,24},{24,16},{1,9},{9,1},{17,25},{25,17},{2,10},{10... | collective-permute-start | bytes 393224 | tf_op jit(solution)/shard_map/ppermute | solution.py:322
  13.1 2.0 %collective-permute-done.2.refs_0_ = bf16[512,128]{1,0:T(8,128)(2,1)S(1)} collective-permute-done((bf16[512,128]{1,0:T(8,128)(2,1)S(1)}, bf16[512,128]{1,0:T(8,128)(2,1)S(1)}, u32[]{:S(2)}, u32[]{:S(2)}) %collective-permute-start.2) | collective-permute-done | bytes 131104 | tf_op jit(solution)/shard_map/ppermute | solution.py:322
  15.1 3.1 %collective-permute-done.3.refs_1_ = bf16[512,128]{1,0:T(8,128)(2,1)S(1)} collective-permute-done((bf16[512,128]{1,0:T(8,128)(2,1)S(1)}, bf16[512,128]{1,0:T(8,128)(2,1)S(1)}, u32[]{:S(2)}, u32[]{:S(2)}) %collective-permute-start.3) | collective-permute-done | bytes 131104 | tf_op jit(solution)/shard_map/ppermute | solution.py:322
  22.9 2.7 %collective-permute-done.7.refs_7_ = bf16[512,128]{1,0:T(8,128)(2,1)S(1)} collective-permute-done((bf16[512,128]{1,0:T(8,128)(2,1)S(1)}, bf16[512,128]{1,0:T(8,128)(2,1)S(1)}, u32[]{:S(2)}, u32[]{:S(2)}) %collective-permute-start.7) | collective-permute-done | bytes 131104 | tf_op jit(solution)/shard_map/ppermute | solution.py:322
  27.6 1.9 %forward.3 = (bf16[1024,128]{1,0:T(8,128)(2,1)S(1)}, bf16[1024,128]{1,0:T(8,128)(2,1)S(1)}, f32[256,128]{1,0:T(8,128)S(1)}, f32[8,128]{1,0:T(8,128)S(1)}, bf16[2...) custom-call(bf16[24,2,128,128]{3,2,1,0:T(8,128)(2,1)S(1)} %bitcast.9, ...), custom_call_target="tpu_custom_call" | custom-call | tf_op jit(solution)/shard_map/forward/pallas_call | solution.py:32
  29.5 3.9 %collective-permute-start.8 = (bf16[272,128]{1,0:T(8,128)(2,1)S(1)}, bf16[272,128]{1,0:T(8,128)(2,1)S(1)}, u32[]{:S(2)}, u32[]{:S(2)}) collective-permute-start(bf16[272,128]{1,0:T(8,128)(2,1)S(1)} %get-tuple-element.79), channel_id=1, source_target_pairs={{0,6},{1,7},{2,4},{3,5},{4,2},{5,3},{6,0},{7,1},{8,14},{9,15},{10,... | collective-permute-start | bytes 208904 | tf_op jit(solution)/shard_map/ppermute | solution.py:322
  34.0 1.8 %collective-permute-done.8.refs_0_ = bf16[272,128]{1,0:T(8,128)(2,1)S(1)} collective-permute-done((bf16[272,128]{1,0:T(8,128)(2,1)S(1)}, bf16[272,128]{1,0:T(8,128)(2,1)S(1)}, u32[]{:S(2)}, u32[]{:S(2)}) %collective-permute-start.8) | collective-permute-done | bytes 69664 | tf_op jit(solution)/shard_map/ppermute | solution.py:322
  35.8 2.0 %collective-permute-done.9.refs_1_ = bf16[272,128]{1,0:T(8,128)(2,1)S(1)} collective-permute-done((bf16[272,128]{1,0:T(8,128)(2,1)S(1)}, bf16[272,128]{1,0:T(8,128)(2,1)S(1)}, u32[]{:S(2)}, u32[]{:S(2)}) %collective-permute-start.9) | collective-permute-done | bytes 69664 | tf_op jit(solution)/shard_map/ppermute | solution.py:322
  40.9 2.4 %collective-permute-start.11 = (bf16[256,128]{1,0:T(8,128)(2,1)S(1)}, bf16[256,128]{1,0:T(8,128)(2,1)S(1)}, u32[]{:S(2)}, u32[]{:S(2)}) collective-permute-start(bf16[256,128]{1,0:T(8,128)(2,1)S(1)} %get-tuple-element.82.refs_4_), channel_id=1, source_target_pairs={{0,4},{1,5},{2,6},{3,7},{4,0},{5,1},{6,2},{7,3},{8,12},{9,13},{10,... | collective-permute-start | bytes 196616 | tf_op jit(solution)/shard_map/ppermute | solution.py:322
  46.0 1.8 %adjoint.2 = (bf16[1024,128]{1,0:T(8,128)(2,1)S(1)}, f32[512,128]{1,0:T(8,128)S(1)}, f32[8,128]{1,0:T(8,128)S(1)}, bf16[528,128]{1,0:T(8,128)(2,1)S(1)}, bf16[52...) custom-call(bf16[24,128,256]{2,1,0:T(8,128)(2,1)S(1)} %get-tuple-element.67.refs_0_, ...), custom_call_target="tpu_custom_call" | custom-call | tf_op jit(solution)/shard_map/adjoint/pallas_call | solution.py:32
  47.8 2.0 %collective-permute-start.14 = (bf16[528,128]{1,0:T(8,128)(2,1)S(1)}, bf16[528,128]{1,0:T(8,128)(2,1)S(1)}, u32[]{:S(2)}, u32[]{:S(2)}) collective-permute-start(bf16[528,128]{1,0:T(8,128)(2,1)S(1)} %get-tuple-element.85), channel_id=1, source_target_pairs={{0,8},{8,0},{16,24},{24,16},{1,9},{9,1},{17,25},{25,17},{2,10},{10... | collective-permute-start | bytes 405512 | tf_op jit(solution)/shard_map/ppermute | solution.py:322
  52.9 1.9 %collective-permute-done.15.refs_1_ = bf16[528,128]{1,0:T(8,128)(2,1)S(1)} collective-permute-done((bf16[528,128]{1,0:T(8,128)(2,1)S(1)}, bf16[528,128]{1,0:T(8,128)(2,1)S(1)}, u32[]{:S(2)}, u32[]{:S(2)}) %collective-permute-start.15) | collective-permute-done | bytes 135200 | tf_op jit(solution)/shard_map/ppermute | solution.py:322
  54.8 3.0 %collective-permute-done.16.refs_2_ = bf16[528,128]{1,0:T(8,128)(2,1)S(1)} collective-permute-done((bf16[528,128]{1,0:T(8,128)(2,1)S(1)}, bf16[528,128]{1,0:T(8,128)(2,1)S(1)}, u32[]{:S(2)}, u32[]{:S(2)}) %collective-permute-start.16) | collective-permute-done | bytes 135200 | tf_op jit(solution)/shard_map/ppermute | solution.py:322
  59.6 2.0 %collective-permute-start.17 = (bf16[512,128]{1,0:T(8,128)(2,1)S(1)}, bf16[512,128]{1,0:T(8,128)(2,1)S(1)}, u32[]{:S(2)}, u32[]{:S(2)}) collective-permute-start(bf16[512,128]{1,0:T(8,128)(2,1)S(1)} %get-tuple-element.90.refs_4_), channel_id=1, source_target_pairs={{0,24},{8,16},{16,8},{24,0},{1,25},{9,17},{17,9},{25,1},{2,26},{10... | collective-permute-start | bytes 393224 | tf_op jit(solution)/shard_map/ppermute | solution.py:322
  63.0 2.9 %collective-permute-done.18.refs_6_ = bf16[512,128]{1,0:T(8,128)(2,1)S(1)} collective-permute-done((bf16[512,128]{1,0:T(8,128)(2,1)S(1)}, bf16[512,128]{1,0:T(8,128)(2,1)S(1)}, u32[]{:S(2)}, u32[]{:S(2)}) %collective-permute-start.18) | collective-permute-done | bytes 131104 | tf_op jit(solution)/shard_map/ppermute | solution.py:322
  66.0 1.9 %forward.4 = (bf16[1024,128]{1,0:T(8,128)(2,1)S(1)}, bf16[1024,128]{1,0:T(8,128)(2,1)S(1)}, f32[256,128]{1,0:T(8,128)S(1)}, f32[8,128]{1,0:T(8,128)S(1)}, bf16[2...) custom-call(bf16[24,2,128,128]{3,2,1,0:T(8,128)(2,1)S(1)} %bitcast.10, ...), custom_call_target="tpu_custom_call" | custom-call | tf_op jit(solution)/shard_map/forward/pallas_call | solution.py:32
  67.8 4.3 %collective-permute-start.20 = (bf16[272,128]{1,0:T(8,128)(2,1)S(1)}, bf16[272,128]{1,0:T(8,128)(2,1)S(1)}, u32[]{:S(2)}, u32[]{:S(2)}) collective-permute-start(bf16[272,128]{1,0:T(8,128)(2,1)S(1)} %get-tuple-element.93), channel_id=1, source_target_pairs={{0,6},{1,7},{2,4},{3,5},{4,2},{5,3},{6,0},{7,1},{8,14},{9,15},{10,... | collective-permute-start | bytes 208904 | tf_op jit(solution)/shard_map/ppermute | solution.py:322
  74.8 1.9 %collective-permute-done.21.refs_1_ = bf16[272,128]{1,0:T(8,128)(2,1)S(1)} collective-permute-done((bf16[272,128]{1,0:T(8,128)(2,1)S(1)}, bf16[272,128]{1,0:T(8,128)(2,1)S(1)}, u32[]{:S(2)}, u32[]{:S(2)}) %collective-permute-start.21) | collective-permute-done | bytes 69664 | tf_op jit(solution)/shard_map/ppermute | solution.py:322
  77.5 3.1 %collective-permute-start.25 = (bf16[256,128]{1,0:T(8,128)(2,1)S(1)}, bf16[256,128]{1,0:T(8,128)(2,1)S(1)}, u32[]{:S(2)}, u32[]{:S(2)}) collective-permute-start(bf16[256,128]{1,0:T(8,128)(2,1)S(1)} %get-tuple-element.97.refs_4_), channel_id=1, source_target_pairs={{0,6},{1,7},{2,4},{3,5},{4,2},{5,3},{6,0},{7,1},{8,14},{9,15},{10,... | collective-permute-start | bytes 196616 | tf_op jit(solution)/shard_map/ppermute | solution.py:322
  81.9 1.8 %collective-permute-done.25.refs_7_ = bf16[256,128]{1,0:T(8,128)(2,1)S(1)} collective-permute-done((bf16[256,128]{1,0:T(8,128)(2,1)S(1)}, bf16[256,128]{1,0:T(8,128)(2,1)S(1)}, u32[]{:S(2)}, u32[]{:S(2)}) %collective-permute-start.25) | collective-permute-done | bytes 65568 | tf_op jit(solution)/shard_map/ppermute | solution.py:322
  85.8 1.8 %adjoint.3 = (bf16[1024,128]{1,0:T(8,128)(2,1)S(1)}, f32[512,128]{1,0:T(8,128)S(1)}, f32[8,128]{1,0:T(8,128)S(1)}, bf16[528,128]{1,0:T(8,128)(2,1)S(1)}, bf16[52...) custom-call(bf16[24,128,256]{2,1,0:T(8,128)(2,1)S(1)} %get-tuple-element.67.refs_0_, ...), custom_call_target="tpu_custom_call" | custom-call | tf_op jit(solution)/shard_map/adjoint/pallas_call | solution.py:32
  89.0 2.1 %collective-permute-start.28 = (bf16[528,128]{1,0:T(8,128)(2,1)S(1)}, bf16[528,128]{1,0:T(8,128)(2,1)S(1)}, u32[]{:S(2)}, u32[]{:S(2)}) collective-permute-start(bf16[528,128]{1,0:T(8,128)(2,1)S(1)} %get-tuple-element.102), channel_id=1, source_target_pairs={{0,24},{8,16},{16,8},{24,0},{1,25},{9,17},{17,9},{25,1},{2,26},{10... | collective-permute-start | bytes 405512 | tf_op jit(solution)/shard_map/ppermute | solution.py:322
  92.9 2.1 %collective-permute-done.28.refs_2_ = bf16[528,128]{1,0:T(8,128)(2,1)S(1)} collective-permute-done((bf16[528,128]{1,0:T(8,128)(2,1)S(1)}, bf16[528,128]{1,0:T(8,128)(2,1)S(1)}, u32[]{:S(2)}, u32[]{:S(2)}) %collective-permute-start.28) | collective-permute-done | bytes 135200 | tf_op jit(solution)/shard_map/ppermute | solution.py:322
  101.5 2.1 %collective-permute-done.29.refs_5_ = bf16[512,128]{1,0:T(8,128)(2,1)S(1)} collective-permute-done((bf16[512,128]{1,0:T(8,128)(2,1)S(1)}, bf16[512,128]{1,0:T(8,128)(2,1)S(1)}, u32[]{:S(2)}, u32[]{:S(2)}) %collective-permute-start.29) | collective-permute-done | bytes 131104 | tf_op jit(solution)/shard_map/ppermute | solution.py:322
  103.6 1.9 %forward.5 = (bf16[1024,128]{1,0:T(8,128)(2,1)S(1)}, bf16[1024,128]{1,0:T(8,128)(2,1)S(1)}, f32[256,128]{1,0:T(8,128)S(1)}, f32[8,128]{1,0:T(8,128)S(1)}, bf16[2...) custom-call(bf16[24,2,128,128]{3,2,1,0:T(8,128)(2,1)S(1)} %bitcast.11, ...), custom_call_target="tpu_custom_call" | custom-call | tf_op jit(solution)/shard_map/forward/pallas_call | solution.py:32
  105.5 2.6 %collective-permute-start.32 = (bf16[272,128]{1,0:T(8,128)(2,1)S(1)}, bf16[272,128]{1,0:T(8,128)(2,1)S(1)}, u32[]{:S(2)}, u32[]{:S(2)}) collective-permute-start(bf16[272,128]{1,0:T(8,128)(2,1)S(1)} %get-tuple-element.108), channel_id=1, source_target_pairs={{0,6},{1,7},{2,4},{3,5},{4,2},{5,3},{6,0},{7,1},{8,14},{9,15},{10,... | collective-permute-start | bytes 208904 | tf_op jit(solution)/shard_map/ppermute | solution.py:322
  110.0 1.9 %collective-permute-done.32.refs_0_ = bf16[272,128]{1,0:T(8,128)(2,1)S(1)} collective-permute-done((bf16[272,128]{1,0:T(8,128)(2,1)S(1)}, bf16[272,128]{1,0:T(8,128)(2,1)S(1)}, u32[]{:S(2)}, u32[]{:S(2)}) %collective-permute-start.32) | collective-permute-done | bytes 69664 | tf_op jit(solution)/shard_map/ppermute | solution.py:322
  113.6 3.4 %collective-permute-start.37 = (bf16[256,128]{1,0:T(8,128)(2,1)S(1)}, bf16[256,128]{1,0:T(8,128)(2,1)S(1)}, u32[]{:S(2)}, u32[]{:S(2)}) collective-permute-start(bf16[256,128]{1,0:T(8,128)(2,1)S(1)} %get-tuple-element.113.refs_0_), channel_id=1, source_target_pairs={{0,6},{1,7},{2,4},{3,5},{4,2},{5,3},{6,0},{7,1},{8,14},{9,15},{10,... | collective-permute-start | bytes 196616 | tf_op jit(solution)/shard_map/ppermute | solution.py:322
  118.0 1.8 %collective-permute-done.37.refs_3_ = bf16[256,128]{1,0:T(8,128)(2,1)S(1)} collective-permute-done((bf16[256,128]{1,0:T(8,128)(2,1)S(1)}, bf16[256,128]{1,0:T(8,128)(2,1)S(1)}, u32[]{:S(2)}, u32[]{:S(2)}) %collective-permute-start.37) | collective-permute-done | bytes 65568 | tf_op jit(solution)/shard_map/ppermute | solution.py:322
  123.5 2.3 %collective-permute-start.38 = (f32[8,128]{1,0:T(8,128)S(1)}, f32[8,128]{1,0:T(8,128)S(1)}, u32[]{:S(2)}, u32[]{:S(2)}) collective-permute-start(f32[8,128]{1,0:T(8,128)S(1)} %get-tuple-element.114.refs_0_), channel_id=1, source_target_pairs={{0,24},{8,16},{16,8},{24,0},{1,25},{9,17},{17,9},{25,1},{2,26},{10... | collective-permute-start | bytes 12296 | tf_op jit(solution)/shard_map/ppermute | solution.py:322
  130.6 1.8 %unpack.1 = (f32[2,1024,128]{2,1,0:T(8,128)}, f32[2,1024,128]{2,1,0:T(8,128)}) custom-call(f32[1024,128]{1,0:T(8,128)S(1)} %get-tuple-element.128.own_x, f32[1024,128]{1,0:T(8,128)S(1)} %get-tuple-element.129.own_r, bf16[1024,128]{1,0:T(8,128)(2,1)S(1)} %collective-permute-done.41.pair_x, bf16[1024,128]{1,0:T(8,128)(2,1)S(1)} %collective-permute-done.42.pair_r), custom_call_target="tpu_custom_call" | custom-call | tf_op jit(solution)/shard_map/unpack/pallas_call | solution.py:32
  (80 shorter events, 56.1 us)
Async XLA Ops:
  0.6 6.5 %collective-permute-start = (bf16[24,2,128,128]{3,2,1,0:T(8,128)(2,1)}, bf16[24,2,128,128]{3,2,1,0:T(8,128)(2,1)S(1)}, u32[]{:S(2)}, u32[]{:S(2)}) collective-permute-start(bf16[24,2,128,128]{3,2,1,0:T(8,128)(2,1)} %bitcast.7), channel_id=1, source_target_pairs={{0,1},{1,0},{2,3},{3,2},{4,5},{5,4},{6,7},{7,6},{8,9},{9,8},{10,11... | collective-permute-start | bytes 4718600 | tf_op jit(solution)/shard_map/ppermute | solution.py:322
  8.2 6.9 %collective-permute-start.2 = (bf16[512,128]{1,0:T(8,128)(2,1)S(1)}, bf16[512,128]{1,0:T(8,128)(2,1)S(1)}, u32[]{:S(2)}, u32[]{:S(2)}) collective-permute-start(bf16[512,128]{1,0:T(8,128)(2,1)S(1)} %get-tuple-element.73), channel_id=1, source_target_pairs={{0,8},{8,0},{16,24},{24,16},{1,9},{9,1},{17,25},{25,17},{2,10},{10... | collective-permute-start | bytes 393224 | tf_op jit(solution)/shard_map/ppermute | solution.py:322
  11.2 7.0 %collective-permute-start.3 = (bf16[512,128]{1,0:T(8,128)(2,1)S(1)}, bf16[512,128]{1,0:T(8,128)(2,1)S(1)}, u32[]{:S(2)}, u32[]{:S(2)}) collective-permute-start(bf16[512,128]{1,0:T(8,128)(2,1)S(1)} %get-tuple-element.74), channel_id=1, source_target_pairs={{0,16},{8,24},{16,0},{24,8},{1,17},{9,25},{17,1},{25,9},{2,18},{10... | collective-permute-start | bytes 393224 | tf_op jit(solution)/shard_map/ppermute | solution.py:322
  12.8 6.5 %collective-permute-start.4 = (bf16[512,128]{1,0:T(8,128)(2,1)S(1)}, bf16[512,128]{1,0:T(8,128)(2,1)S(1)}, u32[]{:S(2)}, u32[]{:S(2)}) collective-permute-start(bf16[512,128]{1,0:T(8,128)(2,1)S(1)} %get-tuple-element.75), channel_id=1, source_target_pairs={{0,24},{8,16},{16,8},{24,0},{1,25},{9,17},{17,9},{25,1},{2,26},{10... | collective-permute-start | bytes 393224 | tf_op jit(solution)/shard_map/ppermute | solution.py:322
  19.3 6.2 %collective-permute-start.7 = (bf16[512,128]{1,0:T(8,128)(2,1)S(1)}, bf16[512,128]{1,0:T(8,128)(2,1)S(1)}, u32[]{:S(2)}, u32[]{:S(2)}) collective-permute-start(bf16[512,128]{1,0:T(8,128)(2,1)S(1)} %get-tuple-element.76.refs_4_), channel_id=1, source_target_pairs={{0,8},{8,0},{16,24},{24,16},{1,9},{9,1},{17,25},{25,17},{2,10},{10... | collective-permute-start | bytes 393224 | tf_op jit(solution)/shard_map/ppermute | solution.py:322
  20.5 6.2 %collective-permute-start.6 = (bf16[512,128]{1,0:T(8,128)(2,1)S(1)}, bf16[512,128]{1,0:T(8,128)(2,1)S(1)}, u32[]{:S(2)}, u32[]{:S(2)}) collective-permute-start(bf16[512,128]{1,0:T(8,128)(2,1)S(1)} %get-tuple-element.76.refs_4_), channel_id=1, source_target_pairs={{0,16},{8,24},{16,0},{24,8},{1,17},{9,25},{17,1},{25,9},{2,18},{10... | collective-permute-start | bytes 393224 | tf_op jit(solution)/shard_map/ppermute | solution.py:322
  21.7 5.9 %collective-permute-start.5 = (bf16[512,128]{1,0:T(8,128)(2,1)S(1)}, bf16[512,128]{1,0:T(8,128)(2,1)S(1)}, u32[]{:S(2)}, u32[]{:S(2)}) collective-permute-start(bf16[512,128]{1,0:T(8,128)(2,1)S(1)} %get-tuple-element.76.refs_4_), channel_id=1, source_target_pairs={{0,24},{8,16},{16,8},{24,0},{1,25},{9,17},{17,9},{25,1},{2,26},{10... | collective-permute-start | bytes 393224 | tf_op jit(solution)/shard_map/ppermute | solution.py:322
  29.5 6.3 %collective-permute-start.8 = (bf16[272,128]{1,0:T(8,128)(2,1)S(1)}, bf16[272,128]{1,0:T(8,128)(2,1)S(1)}, u32[]{:S(2)}, u32[]{:S(2)}) collective-permute-start(bf16[272,128]{1,0:T(8,128)(2,1)S(1)} %get-tuple-element.79), channel_id=1, source_target_pairs={{0,6},{1,7},{2,4},{3,5},{4,2},{5,3},{6,0},{7,1},{8,14},{9,15},{10,... | collective-permute-start | bytes 208904 | tf_op jit(solution)/shard_map/ppermute | solution.py:322
  33.6 5.2 %collective-permute-start.10 = (bf16[272,128]{1,0:T(8,128)(2,1)S(1)}, bf16[272,128]{1,0:T(8,128)(2,1)S(1)}, u32[]{:S(2)}, u32[]{:S(2)}) collective-permute-start(bf16[272,128]{1,0:T(8,128)(2,1)S(1)} %get-tuple-element.81), channel_id=1, source_target_pairs={{0,4},{1,5},{2,6},{3,7},{4,0},{5,1},{6,2},{7,3},{8,12},{9,13},{10,... | collective-permute-start | bytes 208904 | tf_op jit(solution)/shard_map/ppermute | solution.py:322
  38.8 6.2 %collective-permute-start.13 = (bf16[256,128]{1,0:T(8,128)(2,1)S(1)}, bf16[256,128]{1,0:T(8,128)(2,1)S(1)}, u32[]{:S(2)}, u32[]{:S(2)}) collective-permute-start(bf16[256,128]{1,0:T(8,128)(2,1)S(1)} %get-tuple-element.82.refs_4_), channel_id=1, source_target_pairs={{0,6},{1,7},{2,4},{3,5},{4,2},{5,3},{6,0},{7,1},{8,14},{9,15},{10,... | collective-permute-start | bytes 196616 | tf_op jit(solution)/shard_map/ppermute | solution.py:322
  40.3 5.0 %collective-permute-start.12 = (bf16[256,128]{1,0:T(8,128)(2,1)S(1)}, bf16[256,128]{1,0:T(8,128)(2,1)S(1)}, u32[]{:S(2)}, u32[]{:S(2)}) collective-permute-start(bf16[256,128]{1,0:T(8,128)(2,1)S(1)} %get-tuple-element.82.refs_4_), channel_id=1, source_target_pairs={{0,2},{1,3},{2,0},{3,1},{4,6},{5,7},{6,4},{7,5},{8,10},{9,11},{10,... | collective-permute-start | bytes 196616 | tf_op jit(solution)/shard_map/ppermute | solution.py:322
  40.9 5.2 %collective-permute-start.11 = (bf16[256,128]{1,0:T(8,128)(2,1)S(1)}, bf16[256,128]{1,0:T(8,128)(2,1)S(1)}, u32[]{:S(2)}, u32[]{:S(2)}) collective-permute-start(bf16[256,128]{1,0:T(8,128)(2,1)S(1)} %get-tuple-element.82.refs_4_), channel_id=1, source_target_pairs={{0,4},{1,5},{2,6},{3,7},{4,0},{5,1},{6,2},{7,3},{8,12},{9,13},{10,... | collective-permute-start | bytes 196616 | tf_op jit(solution)/shard_map/ppermute | solution.py:322
  47.8 5.1 %collective-permute-start.14 = (bf16[528,128]{1,0:T(8,128)(2,1)S(1)}, bf16[528,128]{1,0:T(8,128)(2,1)S(1)}, u32[]{:S(2)}, u32[]{:S(2)}) collective-permute-start(bf16[528,128]{1,0:T(8,128)(2,1)S(1)} %get-tuple-element.85), channel_id=1, source_target_pairs={{0,8},{8,0},{16,24},{24,16},{1,9},{9,1},{17,25},{25,17},{2,10},{10... | collective-permute-start | bytes 405512 | tf_op jit(solution)/shard_map/ppermute | solution.py:322
  49.8 5.0 %collective-permute-start.15 = (bf16[528,128]{1,0:T(8,128)(2,1)S(1)}, bf16[528,128]{1,0:T(8,128)(2,1)S(1)}, u32[]{:S(2)}, u32[]{:S(2)}) collective-permute-start(bf16[528,128]{1,0:T(8,128)(2,1)S(1)} %get-tuple-element.86), channel_id=1, source_target_pairs={{0,16},{8,24},{16,0},{24,8},{1,17},{9,25},{17,1},{25,9},{2,18},{10... | collective-permute-start | bytes 405512 | tf_op jit(solution)/shard_map/ppermute | solution.py:322
  50.4 7.5 %collective-permute-start.16 = (bf16[528,128]{1,0:T(8,128)(2,1)S(1)}, bf16[528,128]{1,0:T(8,128)(2,1)S(1)}, u32[]{:S(2)}, u32[]{:S(2)}) collective-permute-start(bf16[528,128]{1,0:T(8,128)(2,1)S(1)} %get-tuple-element.87), channel_id=1, source_target_pairs={{0,24},{8,16},{16,8},{24,0},{1,25},{9,17},{17,9},{25,1},{2,26},{10... | collective-permute-start | bytes 405512 | tf_op jit(solution)/shard_map/ppermute | solution.py:322
  58.0 5.0 %collective-permute-start.19 = (bf16[512,128]{1,0:T(8,128)(2,1)S(1)}, bf16[512,128]{1,0:T(8,128)(2,1)S(1)}, u32[]{:S(2)}, u32[]{:S(2)}) collective-permute-start(bf16[512,128]{1,0:T(8,128)(2,1)S(1)} %get-tuple-element.90.refs_4_), channel_id=1, source_target_pairs={{0,8},{8,0},{16,24},{24,16},{1,9},{9,1},{17,25},{25,17},{2,10},{10... | collective-permute-start | bytes 393224 | tf_op jit(solution)/shard_map/ppermute | solution.py:322
  59.6 6.4 %collective-permute-start.18 = (bf16[512,128]{1,0:T(8,128)(2,1)S(1)}, bf16[512,128]{1,0:T(8,128)(2,1)S(1)}, u32[]{:S(2)}, u32[]{:S(2)}) collective-permute-start(bf16[512,128]{1,0:T(8,128)(2,1)S(1)} %get-tuple-element.90.refs_4_), channel_id=1, source_target_pairs={{0,16},{8,24},{16,0},{24,8},{1,17},{9,25},{17,1},{25,9},{2,18},{10... | collective-permute-start | bytes 393224 | tf_op jit(solution)/shard_map/ppermute | solution.py:322
  59.6 6.4 %collective-permute-start.17 = (bf16[512,128]{1,0:T(8,128)(2,1)S(1)}, bf16[512,128]{1,0:T(8,128)(2,1)S(1)}, u32[]{:S(2)}, u32[]{:S(2)}) collective-permute-start(bf16[512,128]{1,0:T(8,128)(2,1)S(1)} %get-tuple-element.90.refs_4_), channel_id=1, source_target_pairs={{0,24},{8,16},{16,8},{24,0},{1,25},{9,17},{17,9},{25,1},{2,26},{10... | collective-permute-start | bytes 393224 | tf_op jit(solution)/shard_map/ppermute | solution.py:322
  67.8 6.9 %collective-permute-start.20 = (bf16[272,128]{1,0:T(8,128)(2,1)S(1)}, bf16[272,128]{1,0:T(8,128)(2,1)S(1)}, u32[]{:S(2)}, u32[]{:S(2)}) collective-permute-start(bf16[272,128]{1,0:T(8,128)(2,1)S(1)} %get-tuple-element.93), channel_id=1, source_target_pairs={{0,6},{1,7},{2,4},{3,5},{4,2},{5,3},{6,0},{7,1},{8,14},{9,15},{10,... | collective-permute-start | bytes 208904 | tf_op jit(solution)/shard_map/ppermute | solution.py:322
  72.1 5.3 %collective-permute-start.22 = (bf16[272,128]{1,0:T(8,128)(2,1)S(1)}, bf16[272,128]{1,0:T(8,128)(2,1)S(1)}, u32[]{:S(2)}, u32[]{:S(2)}) collective-permute-start(bf16[272,128]{1,0:T(8,128)(2,1)S(1)} %get-tuple-element.95), channel_id=1, source_target_pairs={{0,4},{1,5},{2,6},{3,7},{4,0},{5,1},{6,2},{7,3},{8,12},{9,13},{10,... | collective-permute-start | bytes 208904 | tf_op jit(solution)/shard_map/ppermute | solution.py:322
  77.5 6.2 %collective-permute-start.25 = (bf16[256,128]{1,0:T(8,128)(2,1)S(1)}, bf16[256,128]{1,0:T(8,128)(2,1)S(1)}, u32[]{:S(2)}, u32[]{:S(2)}) collective-permute-start(bf16[256,128]{1,0:T(8,128)(2,1)S(1)} %get-tuple-element.97.refs_4_), channel_id=1, source_target_pairs={{0,6},{1,7},{2,4},{3,5},{4,2},{5,3},{6,0},{7,1},{8,14},{9,15},{10,... | collective-permute-start | bytes 196616 | tf_op jit(solution)/shard_map/ppermute | solution.py:322
  80.6 5.2 %collective-permute-start.23 = (bf16[256,128]{1,0:T(8,128)(2,1)S(1)}, bf16[256,128]{1,0:T(8,128)(2,1)S(1)}, u32[]{:S(2)}, u32[]{:S(2)}) collective-permute-start(bf16[256,128]{1,0:T(8,128)(2,1)S(1)} %get-tuple-element.97.refs_4_), channel_id=1, source_target_pairs={{0,4},{1,5},{2,6},{3,7},{4,0},{5,1},{6,2},{7,3},{8,12},{9,13},{10,... | collective-permute-start | bytes 196616 | tf_op jit(solution)/shard_map/ppermute | solution.py:322
  87.6 5.1 %collective-permute-start.26 = (bf16[528,128]{1,0:T(8,128)(2,1)S(1)}, bf16[528,128]{1,0:T(8,128)(2,1)S(1)}, u32[]{:S(2)}, u32[]{:S(2)}) collective-permute-start(bf16[528,128]{1,0:T(8,128)(2,1)S(1)} %get-tuple-element.100), channel_id=1, source_target_pairs={{0,8},{8,0},{16,24},{24,16},{1,9},{9,1},{17,25},{25,17},{2,10},{10... | collective-permute-start | bytes 405512 | tf_op jit(solution)/shard_map/ppermute | solution.py:322
  87.9 5.0 %collective-permute-start.27 = (bf16[528,128]{1,0:T(8,128)(2,1)S(1)}, bf16[528,128]{1,0:T(8,128)(2,1)S(1)}, u32[]{:S(2)}, u32[]{:S(2)}) collective-permute-start(bf16[528,128]{1,0:T(8,128)(2,1)S(1)} %get-tuple-element.101), channel_id=1, source_target_pairs={{0,16},{8,24},{16,0},{24,8},{1,17},{9,25},{17,1},{25,9},{2,18},{10... | collective-permute-start | bytes 405512 | tf_op jit(solution)/shard_map/ppermute | solution.py:322
  89.0 5.9 %collective-permute-start.28 = (bf16[528,128]{1,0:T(8,128)(2,1)S(1)}, bf16[528,128]{1,0:T(8,128)(2,1)S(1)}, u32[]{:S(2)}, u32[]{:S(2)}) collective-permute-start(bf16[528,128]{1,0:T(8,128)(2,1)S(1)} %get-tuple-element.102), channel_id=1, source_target_pairs={{0,24},{8,16},{16,8},{24,0},{1,25},{9,17},{17,9},{25,1},{2,26},{10... | collective-permute-start | bytes 405512 | tf_op jit(solution)/shard_map/ppermute | solution.py:322
  95.1 5.0 %collective-permute-start.31 = (bf16[512,128]{1,0:T(8,128)(2,1)S(1)}, bf16[512,128]{1,0:T(8,128)(2,1)S(1)}, u32[]{:S(2)}, u32[]{:S(2)}) collective-permute-start(bf16[512,128]{1,0:T(8,128)(2,1)S(1)} %get-tuple-element.105.refs_4_), channel_id=1, source_target_pairs={{0,8},{8,0},{16,24},{24,16},{1,9},{9,1},{17,25},{25,17},{2,10},{10... | collective-permute-start | bytes 393224 | tf_op jit(solution)/shard_map/ppermute | solution.py:322
  96.6 5.0 %collective-permute-start.30 = (bf16[512,128]{1,0:T(8,128)(2,1)S(1)}, bf16[512,128]{1,0:T(8,128)(2,1)S(1)}, u32[]{:S(2)}, u32[]{:S(2)}) collective-permute-start(bf16[512,128]{1,0:T(8,128)(2,1)S(1)} %get-tuple-element.105.refs_4_), channel_id=1, source_target_pairs={{0,16},{8,24},{16,0},{24,8},{1,17},{9,25},{17,1},{25,9},{2,18},{10... | collective-permute-start | bytes 393224 | tf_op jit(solution)/shard_map/ppermute | solution.py:322
  97.8 5.9 %collective-permute-start.29 = (bf16[512,128]{1,0:T(8,128)(2,1)S(1)}, bf16[512,128]{1,0:T(8,128)(2,1)S(1)}, u32[]{:S(2)}, u32[]{:S(2)}) collective-permute-start(bf16[512,128]{1,0:T(8,128)(2,1)S(1)} %get-tuple-element.105.refs_4_), channel_id=1, source_target_pairs={{0,24},{8,16},{16,8},{24,0},{1,25},{9,17},{17,9},{25,1},{2,26},{10... | collective-permute-start | bytes 393224 | tf_op jit(solution)/shard_map/ppermute | solution.py:322
  105.5 6.3 %collective-permute-start.32 = (bf16[272,128]{1,0:T(8,128)(2,1)S(1)}, bf16[272,128]{1,0:T(8,128)(2,1)S(1)}, u32[]{:S(2)}, u32[]{:S(2)}) collective-permute-start(bf16[272,128]{1,0:T(8,128)(2,1)S(1)} %get-tuple-element.108), channel_id=1, source_target_pairs={{0,6},{1,7},{2,4},{3,5},{4,2},{5,3},{6,0},{7,1},{8,14},{9,15},{10,... | collective-permute-start | bytes 208904 | tf_op jit(solution)/shard_map/ppermute | solution.py:322
  108.3 5.2 %collective-permute-start.34 = (bf16[272,128]{1,0:T(8,128)(2,1)S(1)}, bf16[272,128]{1,0:T(8,128)(2,1)S(1)}, u32[]{:S(2)}, u32[]{:S(2)}) collective-permute-start(bf16[272,128]{1,0:T(8,128)(2,1)S(1)} %get-tuple-element.110), channel_id=1, source_target_pairs={{0,4},{1,5},{2,6},{3,7},{4,0},{5,1},{6,2},{7,3},{8,12},{9,13},{10,... | collective-permute-start | bytes 208904 | tf_op jit(solution)/shard_map/ppermute | solution.py:322
  113.6 6.2 %collective-permute-start.37 = (bf16[256,128]{1,0:T(8,128)(2,1)S(1)}, bf16[256,128]{1,0:T(8,128)(2,1)S(1)}, u32[]{:S(2)}, u32[]{:S(2)}) collective-permute-start(bf16[256,128]{1,0:T(8,128)(2,1)S(1)} %get-tuple-element.113.refs_0_), channel_id=1, source_target_pairs={{0,6},{1,7},{2,4},{3,5},{4,2},{5,3},{6,0},{7,1},{8,14},{9,15},{10,... | collective-permute-start | bytes 196616 | tf_op jit(solution)/shard_map/ppermute | solution.py:322
  117.0 5.2 %collective-permute-start.35 = (bf16[256,128]{1,0:T(8,128)(2,1)S(1)}, bf16[256,128]{1,0:T(8,128)(2,1)S(1)}, u32[]{:S(2)}, u32[]{:S(2)}) collective-permute-start(bf16[256,128]{1,0:T(8,128)(2,1)S(1)} %get-tuple-element.113.refs_0_), channel_id=1, source_target_pairs={{0,4},{1,5},{2,6},{3,7},{4,0},{5,1},{6,2},{7,3},{8,12},{9,13},{10,... | collective-permute-start | bytes 196616 | tf_op jit(solution)/shard_map/ppermute | solution.py:322
  (15 other events, 97.6 us)

commit v4 on v3

--- a/solution.py
+++ b/solution.py
@@ -1,4 +1,5 @@
 import functools
+from typing import NamedTuple
 
 import jax
 import jax.numpy as jnp
@@ -16,26 +17,38 @@
 
 F32 = jnp.float32
 BF16 = jnp.bfloat16
-
-
-def call(kernel, name, outs, scratch, *ins, away=0):
-    def space(place, dtype):
-        if place < away:
-            return pltpu.HBM
-        return pltpu.SMEM if dtype == jnp.int32 else pltpu.VMEM
-
-    def room(shape, dtype):
-        if dtype is pltpu.SemaphoreType.DMA:
-            return dtype((shape,))
-        return (pltpu.SMEM if dtype == jnp.int32 else pltpu.VMEM)(shape, dtype)
+F32_INDEX = jnp.int32
+
+
+class Way(NamedTuple):
+    source: int
+    sign: float
+    size: int
+    part: int
+    halves: int
+    length: int
+    target_part: int
+    target_begins: tuple
+    target_shift: int
+    spare: int
+    send_order: tuple
+    source_place: object
+    target_place: object
+    weights: object
+
+
+def call(kernel, name, outs, scratch, *ins, vector=False, alias=None):
+    def space(dtype):
+        return pltpu.SMEM if dtype == jnp.int32 and not vector else pltpu.VMEM
 
     return pl.pallas_call(
         kernel,
         name=name,
         out_shape=[jax.ShapeDtypeStruct(s, d) for s, d in outs],
-        in_specs=[pl.BlockSpec(memory_space=space(i, a.dtype)) for i, a in enumerate(ins)],
+        in_specs=[pl.BlockSpec(memory_space=space(a.dtype)) for a in ins],
         out_specs=[pl.BlockSpec(memory_space=pltpu.VMEM) for _ in outs],
-        scratch_shapes=[room(s, d) for s, d in scratch],
+        scratch_shapes=[pltpu.VMEM(s, d) for s, d in scratch],
+        input_output_aliases=alias or {},
         compiler_params=pltpu.CompilerParams(vmem_limit_bytes=VMEM_BYTES),
     )(*ins)
 
@@ -153,64 +166,91 @@
             send[2 * part :, :] = tail
 
 
-def adjoint_kernel(hyd_axis, core_axis, order, z_order, tiles, *refs):
-    tile_a, tile_b, index_a, index_b = refs[:4]
-    zs, hyds, refs = len(z_order) + 1, len(order) + 1, refs[4:]
-    chunks = refs[:zs]
-    plain_ref, own_ref, norm_ref = refs[zs : 3 + zs]
-    sends = refs[3 + zs : 2 + zs + hyds]
-    turned_ref, first_ref, second_ref = refs[2 + zs + hyds :]
-    here = lax.axis_index(core_axis) // 2
-    rows = chunks[0].shape[0]
-    folded = jnp.zeros((8, plain_ref.shape[-1]), F32)
-    for chunk, offset in zip(chunks, (0, *z_order)):
-        folded += put_chunk(chunk[...], plain_ref, turned_ref, spans(rows, here ^ offset), -1.0)
+def list_kernel(keys, index_a, index_b, *lists):
+    slot_count = index_a.shape[1]
+    down = lax.broadcasted_iota(F32_INDEX, (slot_count, slot_count), 0)
+    along = lax.broadcasted_iota(F32_INDEX, (slot_count, slot_count), 1)
+    for list_ref, (row, width, buckets) in zip(lists, keys):
+        down_f, wide = down.astype(F32), lax.broadcasted_iota(F32_INDEX, (slot_count, list_ref.shape[1]), 1).astype(F32)
+        slot_f = lax.broadcasted_iota(F32_INDEX, wide.shape, 0).astype(F32)
+        for k, index_ref in enumerate((index_a, index_b)):
+            bucket = index_ref[row : row + 1, :] // width
+            used = along[:1, :] < index_ref[2:3, :]
+            key = jnp.broadcast_to(jnp.where(used, bucket, buckets).astype(F32), down.shape)
+            order_along = key * slot_count + along.astype(F32)
+            here = down == along
+            key_down = jnp.sum(jnp.where(here, key, 0.0), axis=1, keepdims=True)
+            order_down = key_down * slot_count + down_f[:, :1]
+            rank = jnp.sum(jnp.where(order_along < order_down, 1.0, 0.0), axis=1, keepdims=True)
+            order = jnp.sum(jnp.where(rank == wide, slot_f, 0.0), axis=0, keepdims=True)
+            begin = jnp.sum(jnp.where(key_down < wide, 1.0, 0.0), axis=0, keepdims=True)
+            list_ref[k : k + 1, :] = order.astype(jnp.int32)
+            list_ref[k + 2 : k + 3, :] = begin.astype(jnp.int32)
+
+
+def step_kernel(way, pick, first, last, *refs):
+    (tile_a, tile_b, index_a, index_b, list_ref), refs = refs[:5], refs[5:]
+    chunks, refs = refs[: len(pick)], refs[len(pick) :]
+    if not first:
+        folded, refs = refs[1][...], refs[2:]
+    total_ref, refs = refs[0], refs[1:]
+    here, there = way.source_place(), way.target_place()
+    single = len(pick) == 1
+    if first:
+        total_ref[...] = jnp.zeros_like(total_ref)
+        folded = jnp.zeros((8, total_ref.shape[-1]), F32)
+    if single:
+        turned_ref, plain_ref = refs[-1], chunks[0]
+        wide = plain_ref[...].astype(F32)
+        turned_ref[...] = times_i(wide, way.sign).astype(BF16)
+        folded += fold_squares(wide)
+    else:
+        plain_ref, turned_ref = refs[-2:]
+        for chunk, offset in zip(chunks, pick):
+            for half in range(way.halves):
+                at = pl.ds(pl.multiple_of((here ^ offset) * way.part + half * way.length, way.part), way.part)
+                folded += put_chunk(chunk[half * way.part : (half + 1) * way.part, :], plain_ref, turned_ref, at, way.sign)
+    place = here ^ pick[0]
+    base = place * (way.part // way.size) if single else 0
+    stride = plain_ref.shape[0] // way.halves
+    width = 4 if single else GROUP
+    for k, (tile_ref, index_ref) in enumerate(((tile_a, index_a), (tile_b, index_b))):
+        low = list_ref[k + 2, place] if single else 0
+        high = list_ref[k + 2, place + 1] if single else index_ref[2, 0]
+
+        def turn_of(group, carry):
+            for lane in range(width):
+                at = low + group * width + lane
+                valid = at < high
+                slot = list_ref[k, at] if single else at
+                source = jnp.where(valid, index_ref[way.source, slot] - base, 0)
+                target = jnp.where(valid, index_ref[1 - way.source, slot] + k * way.target_shift, way.spare)
+                start = pl.multiple_of(source * way.size + k * (way.halves - 1) * stride, way.size)
+                span = pl.ds(start, way.size)
+                right = jnp.concatenate([plain_ref[span, :], turned_ref[span, :]], axis=0)
+                goal = spans(way.size, target)
+                product = jnp.dot(way.weights(tile_ref, slot), right, preferred_element_type=F32)
+                total_ref[goal, :] = total_ref[goal, :] + product
+            return carry
+
+        lax.fori_loop(0, (high - low + width - 1) // width, turn_of, 0)
+    if not last:
+        refs[0][...] = folded
+        return
+    own_ref, norm_ref, sends = refs[0], refs[1], refs[2 : 2 + len(way.send_order)]
     norm = rows_of_norm(folded)
     norm_ref[...] = norm
-    for index, tile_ref, total_ref in ((index_a, tile_a, first_ref), (index_b, tile_b, second_ref)):
-        total_ref[...] = jnp.zeros_like(total_ref)
-
-        def step(slot, valid, row, col):
-            add_tile(total_ref, tile_ref[slot], plain_ref, turned_ref, row, jnp.where(valid, col, tiles))
-
-        slots(index, step)
-    give_columns(hyd_axis, order, first_ref, second_ref, own_ref, sends, norm_tail(norm))
-
-
-def forward_kernel(hyd_axis, core_axis, order, z_order, tiles, *refs):
-    tile_a, tile_b, index_a, index_b = refs[:4]
-    zs, hyds, refs = len(z_order) + 1, len(order) + 1, refs[4:]
-    chunks = refs[:hyds]
-    plain_a, plain_b, own_ref, norm_ref = refs[hyds : 4 + hyds]
-    sends = refs[4 + hyds : 3 + hyds + zs]
-    turned_a, turned_b, total_ref = refs[3 + hyds + zs :]
-    here = lax.axis_index(hyd_axis)
-    part = chunks[0].shape[0] // 2
-    folded = jnp.zeros((8, plain_a.shape[-1]), F32)
-    for chunk, offset in zip(chunks, (0, *order)):
-        at = spans(part, here ^ offset)
-        folded += put_chunk(chunk[:part, :], plain_a, turned_a, at, 1.0)
-        folded += put_chunk(chunk[part:, :], plain_b, turned_b, at, 1.0)
-    norm = rows_of_norm(folded)
-    norm_ref[...] = norm
-    total_ref[...] = jnp.zeros_like(total_ref)
-    for index, tile_ref, plain_ref, turned_ref in (
-        (index_a, tile_a, plain_a, turned_a),
-        (index_b, tile_b, plain_b, turned_b),
-    ):
-
-        def step(slot, valid, row, col):
-            weights = jnp.concatenate([tile_ref[slot, 0], tile_ref[slot, 1]], axis=1)
-            add_tile(total_ref, weights, plain_ref, turned_ref, col, jnp.where(valid, row, tiles))
-
-        slots(index, step)
-    here = lax.axis_index(core_axis) // 2
-    rows = own_ref.shape[0]
-    own_ref[...] = total_ref[spans(rows, here), :]
     tail = norm_tail(norm)
-    for send, offset in zip(sends, z_order):
-        send[:rows, :] = total_ref[spans(rows, here ^ offset), :].astype(BF16)
-        send[rows:, :] = tail
+    part = way.target_part
+    for j, begin in enumerate(way.target_begins):
+        def piece(position):
+            return total_ref[pl.ds(pl.multiple_of(position * part + begin, part), part), :]
+
+        own_ref[j * part : (j + 1) * part, :] = piece(there)
+        for send, offset in zip(sends, way.send_order):
+            send[j * part : (j + 1) * part, :] = piece(there ^ offset).astype(BF16)
+    for send in sends:
+        send[len(way.target_begins) * part :, :] = tail
 
 
 def summed(own_ref, others):
@@ -260,19 +300,13 @@
         wide_ref[...] = gradient
 
 
-def gather_kernel(core_axis, z_order, *refs):
-    chunks, (plain_ref, norm_ref) = refs[:-2], refs[-2:]
-    here = lax.axis_index(core_axis) // 2
-    rows = chunks[0].shape[0]
-    folded = jnp.zeros((8, plain_ref.shape[-1]), F32)
-    for chunk, offset in zip(chunks, (0, *z_order)):
-        chunk = chunk[...]
-        plain_ref[spans(rows, here ^ offset), :] = chunk
-        folded += fold_squares(chunk.astype(F32))
-    norm_ref[...] = rows_of_norm(folded)
-
-
-def answer_kernel(core_axis, norms, record_ref, gamma_ref, *refs):
+def norm_kernel(*refs):
+    folded = sum(fold_squares(chunk[...].astype(F32)) for chunk in refs[:-1])
+    refs[-1][...] = rows_of_norm(folded)
+
+
+def answer_kernel(hyd_axis, core_axis, g_order, image_order, record_ref, gamma_ref, *refs):
+    norms = len(g_order)
     norm = refs[0][...]
     for other in refs[1:norms]:
         norm = norm + other[...]
@@ -281,22 +315,27 @@
     refs = refs[ITERS - 1 :]
     betas = [ref[...] for ref in refs[: ITERS - 1]]
     refs = refs[ITERS - 1 :]
-    own_g, pair_g, images = refs[:ITERS], refs[ITERS : 2 * ITERS], refs[2 * ITERS : 3 * ITERS]
-    own_x, pair_x, wide_r, narrow_r = refs[3 * ITERS :]
+    g_count, image_count = ITERS * len(g_order), ITERS * len(image_order)
+    g_chunks, images, (own_x, pair_x, wide_r, narrow_r) = refs[:g_count], refs[g_count : g_count + image_count], refs[g_count + image_count :]
     weights = [None] * ITERS
     weights[-1] = alphas[-1]
     for k in range(ITERS - 2, -1, -1):
         weights[k] = alphas[k] + betas[k] * weights[k + 1]
     core = lax.rem(lax.axis_index(core_axis), 2)
-    for at in range(0, own_x.shape[0], 128):
-        span = pl.ds(at, 128)
-        own_x[span, :] = sum(w[:1] * g[span, :].astype(F32) for w, g in zip(weights, own_g))
-        pair_x[span, :] = sum(w[:1] * g[span, :].astype(F32) for w, g in zip(weights, pair_g)).astype(BF16)
-    for at in range(0, wide_r.shape[0], 128):
-        span = pl.ds(at, 128)
+    here = lax.axis_index(hyd_axis)
+    for at, offset in enumerate(g_order):
+        mine = g_chunks[at :: len(g_order)]
+        part = mine[0].shape[0] // 2
+        span = spans(part, here ^ offset)
+        own_x[span, :] = sum(w[:1] * g[:part, :].astype(F32) for w, g in zip(weights, mine))
+        pair_x[span, :] = sum(w[:1] * g[part:, :].astype(F32) for w, g in zip(weights, mine)).astype(BF16)
+    here = lax.axis_index(core_axis) // 2
+    for at, offset in enumerate(image_order):
+        mine = images[at :: len(image_order)]
+        span = spans(mine[0].shape[0], here ^ offset)
         residual = packed_record(core, record_ref[0, span, :], record_ref[1, span, :])
-        for alpha, image in zip(alphas, images):
-            residual = residual - alpha[:1] * image[span, :].astype(F32)
+        for alpha, image in zip(alphas, mine):
+            residual = residual - alpha[:1] * image[...].astype(F32)
         wide_r[span, :] = residual
         narrow_r[span, :] = residual.astype(BF16)
 
@@ -342,7 +381,7 @@
         norm = ((8, shots), F32)
         row_sends = [((row_part + TAIL, shots), BF16)] * (zs - 1)
         col_sends = [((2 * col_part + TAIL, shots), BF16)] * (hyds - 1)
-        row_total, col_total = ((rows + size, shots), F32), ((cols + size, shots), F32)
+        col_total = ((cols + size, shots), F32)
         vector = lambda n, dtype: ((n, shots), dtype)
 
         pair_tiles = swap(own_tiles, "src", srcs, 1)
@@ -366,18 +405,45 @@
             own, *over_hyd(sends, hyd_order),
         )
 
-        alphas, betas, own_g, pair_g, images = [], [], [], [], []
+        hyd_place = lambda: lax.axis_index("hyd")
+        z_place = lambda: lax.axis_index("src") // 2
+        flat = lambda tile_ref, slot: jnp.concatenate([tile_ref[slot, 0], tile_ref[slot, 1]], axis=1)
+        forward = Way(1, 1.0, size, col_part, 2, cols, row_part, (0,), 0, row_tiles, z_order, hyd_place, z_place, flat)
+        adjoint = Way(
+            0, -1.0, size, row_part, 1, rows, col_part, (0, cols), col_tiles, 2 * col_tiles, hyd_order,
+            z_place, hyd_place, lambda tile_ref, slot: tile_ref[slot],
+        )
+        lists = call(
+            functools.partial(list_kernel, [(w.source, max(w.part // size, 1), w.length // w.part) for w in (forward, adjoint)]),
+            "lists", [((8, 128), jnp.int32)] * 2, [], index, pair_index, vector=True,
+        )
+
+        def apply(way, name, tiles, slot_list, chunks, order, outs):
+            picks = [(k,) for k in range(len(order))] if way.part % size == 0 else [tuple(range(len(order)))]
+            total = (((len(way.target_begins) * (way.spare // len(way.target_begins)) + 1) * size, shots), F32)
+            carry = []
+            for at, pick in enumerate(picks):
+                last = at + 1 == len(picks)
+                length = sum(chunks[k].shape[0] for k in pick)
+                carry = call(
+                    functools.partial(step_kernel, way, tuple(order[k] for k in pick), at == 0, last), name,
+                    [total] + (outs if last else [norm]),
+                    [vector(length, BF16)] * (1 if len(pick) == 1 else 2),
+                    *tiles, index, pair_index, slot_list, *(chunks[k] for k in pick), *carry,
+                    alias={6: 0} if at else None,
+                )
+            return carry[1:]
+
+        alphas, betas, g_chunks, images = [], [], [], []
         image = gamma = None
+        g_order, image_order = (0, *hyd_back), (0, *z_back)
         for step in range(ITERS):
             last = step + 1 == ITERS
-            plain_a, plain_b, own, own_norm, *sends = call(
-                functools.partial(forward_kernel, "hyd", "src", hyd_back, z_order, row_tiles), "forward",
-                [vector(cols, BF16), vector(cols, BF16), vector(row_part, F32), norm] + row_sends,
-                [vector(cols, BF16), vector(cols, BF16), row_total],
-                own_tiles, pair_tiles, index, pair_index, narrow, *over_hyd([narrow] * (hyds - 1), hyd_back),
+            chunks = [narrow, *over_hyd([narrow] * (hyds - 1), hyd_back)]
+            g_chunks += chunks
+            own, own_norm, *sends = apply(
+                forward, "forward", (own_tiles, pair_tiles), lists[0], chunks, g_order, [vector(row_part, F32), norm] + row_sends
             )
-            own_g.append(plain_a)
-            pair_g.append(plain_b)
             narrow, gamma, *more = call(
                 functools.partial(image_kernel, zs - 1, step > 0, last), "image",
                 [vector(row_part, BF16), norm] + [norm] * (step > 0) + [vector(row_part, F32)] * (not last), [],
@@ -385,16 +451,13 @@
             )
             image = None if last else more.pop()
             betas += more
-            chunks = [narrow] + over_z([narrow] * (zs - 1), z_back)
+            chunks = [narrow, *over_z([narrow] * (zs - 1), z_back)]
+            images += chunks
             if last:
                 break
-            plain, own, own_norm, *sends = call(
-                functools.partial(adjoint_kernel, "hyd", "src", hyd_order, z_back, col_tiles), "adjoint",
-                [vector(rows, BF16), vector(2 * col_part, F32), norm] + col_sends,
-                [vector(rows, BF16), col_total, col_total],
-                turned_own, turned_pair, index, pair_index, *chunks,
+            own, own_norm, *sends = apply(
+                adjoint, "adjoint", (turned_own, turned_pair), lists[1], chunks, image_order, [vector(2 * col_part, F32), norm] + col_sends
             )
-            images.append(plain)
             more_steps = step + 2 < ITERS
             narrow, alpha, *wide = call(
                 functools.partial(gradient_kernel, hyds - 1), "gradient",
@@ -404,13 +467,12 @@
             gradient = wide[0] if more_steps else None
             alphas.append(alpha)
 
-        plain, own_norm = call(functools.partial(gather_kernel, "src", z_back), "gather", [vector(rows, BF16), norm], [], *chunks)
-        images.append(plain)
+        (own_norm,) = call(norm_kernel, "norm", [norm], [], *chunks)
         norms = [own_norm] + over_hyd([own_norm] * (hyds - 1), hyd_back)
         own_x, pair_x, wide_r, narrow_r = call(
-            functools.partial(answer_kernel, "src", hyds), "answer",
+            functools.partial(answer_kernel, "hyd", "src", g_order, image_order), "answer",
             [vector(cols, F32), vector(cols, BF16), vector(rows, F32), vector(rows, BF16)], [],
-            record, gamma, *norms, *alphas, *betas, *own_g, *pair_g, *images,
+            record, gamma, *norms, *alphas, *betas, *g_chunks, *images,
         )
         return call(
             functools.partial(unpack_kernel, "src"), "unpack",

time: 134 us -> 135 us (level); the launches traced: 132 us -> 135 us
  Pallas kernels: 15.1 us -> 33.6 us
  waiting for transfers between devices: 57.5 us -> 41.9 us
    pallas_call x16 -> x32, Pallas kernels: 15.1 us -> 33.6 us  [call(): pl.pallas_call(kernel, name=name, out_shape=[jax.ShapeDtypeStruct(s, d) f...]
    ppermute x43, waiting for transfers between devices: 57.5 us -> 41.9 us  [swap(): return lax.ppermute(value, axis, [(i, i ^ offset) for i in range(size)])]
  transfers between devices with their start and end apart: 43 -> 43, of which waited for: 40 -> 30; matrix products, arithmetic and copies ran while one was open for 1% -> 1% of each run, Pallas kernels for 1% -> 16%
where the time goes in v4:
time: 135 us
  starting transfers between devices  54.7 us (41%)
  waiting for transfers between devices  41.9 us (31%)
  Pallas kernels  33.6 us (25%)
  local copies, waits for them, and re-layouts  2.72 us (2%)
  between operations  1.61 us (1%)
    ppermute x43, starting transfers between devices, swap(): return lax.ppermute(value, axis, [(i, i ^ offset) for i in range(size)])  54.7 us
    ppermute x43, waiting for transfers between devices, swap(): return lax.ppermute(value, axis, [(i, i ^ offset) for i in range(size)])  41.9 us
    pallas_call x32, Pallas kernels, call(): pl.pallas_call(kernel, name=name, out_shape=[jax.ShapeDtypeStruct(s, d) f...  33.6 us
  transfers between devices with their start and end apart: 43, of which 30 were waited for; matrix products, arithmetic and copies ran while one was open for 1% of the time, Pallas kernels for 16%

profile of v4, /device:TPU:0, one launch (start us, length us, event | category | flops | bytes accessed | tf_op | source)
XLA Modules:
  0.0 135.2 jit_solution(7368831014663351113)
XLA Ops:
  5.3 1.8 %pack.1 = (bf16[24,128,256]{2,1,0:T(8,128)(2,1)S(1)}, f32[1152,128]{1,0:T(8,128)S(1)}, bf16[1024,128]{1,0:T(8,128)(2,1)S(1)}, bf16[1024,128]{1,0:T(8,128)(2,1)S(1)}) custom-call(f32[2,1024,128]{2,1,0:T(8,128)S(1)} %copy-done.2, bf16[24,2,128,128]{3,2,1,0:T(8,128)(2,1)S(1)} %bitcast.8, s32[3,24]{1,0:T(4,128)S(1)} %add_add_fusion.index_a.index_ref.refs_2_), custom_call_target="tpu_custom_call" | custom-call | tf_op jit(solution)/shard_map/pack/pallas_call | solution.py:44
  8.5 2.7 %collective-permute-start.2 = (bf16[512,128]{1,0:T(8,128)(2,1)S(1)}, bf16[512,128]{1,0:T(8,128)(2,1)S(1)}, u32[]{:S(2)}, u32[]{:S(2)}) collective-permute-start(bf16[512,128]{1,0:T(8,128)(2,1)S(1)} %get-tuple-element.97), channel_id=1, source_target_pairs={{0,8},{8,0},{16,24},{24,16},{1,9},{9,1},{17,25},{25,17},{2,10},{10... | collective-permute-start | bytes 393224 | tf_op jit(solution)/shard_map/ppermute | solution.py:361
  11.2 2.2 %collective-permute-start.3 = (bf16[512,128]{1,0:T(8,128)(2,1)S(1)}, bf16[512,128]{1,0:T(8,128)(2,1)S(1)}, u32[]{:S(2)}, u32[]{:S(2)}) collective-permute-start(bf16[512,128]{1,0:T(8,128)(2,1)S(1)} %get-tuple-element.98), channel_id=1, source_target_pairs={{0,16},{8,24},{16,0},{24,8},{1,17},{9,25},{17,1},{25,9},{2,18},{10... | collective-permute-start | bytes 393224 | tf_op jit(solution)/shard_map/ppermute | solution.py:361
  15.0 4.6 %collective-permute-done.3.refs_1_ = bf16[512,128]{1,0:T(8,128)(2,1)S(1)} collective-permute-done((bf16[512,128]{1,0:T(8,128)(2,1)S(1)}, bf16[512,128]{1,0:T(8,128)(2,1)S(1)}, u32[]{:S(2)}, u32[]{:S(2)}) %collective-permute-start.3) | collective-permute-done | bytes 131104 | tf_op jit(solution)/shard_map/ppermute | solution.py:361
  24.7 2.0 %collective-permute-done.7.refs_5_.refs_9_ = bf16[512,128]{1,0:T(8,128)(2,1)S(1)} collective-permute-done((bf16[512,128]{1,0:T(8,128)(2,1)S(1)}, bf16[512,128]{1,0:T(8,128)(2,1)S(1)}, u32[]{:S(2)}, u32[]{:S(2)}) %collective-permute-start.7) | collective-permute-done | bytes 131104 | tf_op jit(solution)/shard_map/ppermute | solution.py:361
  30.9 4.1 %collective-permute-start.8 = (bf16[272,128]{1,0:T(8,128)(2,1)S(1)}, bf16[272,128]{1,0:T(8,128)(2,1)S(1)}, u32[]{:S(2)}, u32[]{:S(2)}) collective-permute-start(bf16[272,128]{1,0:T(8,128)(2,1)S(1)} %get-tuple-element.109), channel_id=1, source_target_pairs={{0,6},{1,7},{2,4},{3,5},{4,2},{5,3},{6,0},{7,1},{8,14},{9,15},{10,... | collective-permute-start | bytes 208904 | tf_op jit(solution)/shard_map/ppermute | solution.py:361
  35.7 1.7 %collective-permute-done.8.refs_0_ = bf16[272,128]{1,0:T(8,128)(2,1)S(1)} collective-permute-done((bf16[272,128]{1,0:T(8,128)(2,1)S(1)}, bf16[272,128]{1,0:T(8,128)(2,1)S(1)}, u32[]{:S(2)}, u32[]{:S(2)}) %collective-permute-start.8) | collective-permute-done | bytes 69664 | tf_op jit(solution)/shard_map/ppermute | solution.py:361
  37.4 1.9 %collective-permute-done.9.refs_1_ = bf16[272,128]{1,0:T(8,128)(2,1)S(1)} collective-permute-done((bf16[272,128]{1,0:T(8,128)(2,1)S(1)}, bf16[272,128]{1,0:T(8,128)(2,1)S(1)}, u32[]{:S(2)}, u32[]{:S(2)}) %collective-permute-start.9) | collective-permute-done | bytes 69664 | tf_op jit(solution)/shard_map/ppermute | solution.py:361
  40.3 1.7 %collective-permute-start.13 = (bf16[256,128]{1,0:T(8,128)(2,1)S(1)}, bf16[256,128]{1,0:T(8,128)(2,1)S(1)}, u32[]{:S(2)}, u32[]{:S(2)}) collective-permute-start(bf16[256,128]{1,0:T(8,128)(2,1)S(1)} %get-tuple-element.112.refs_5_.refs_20_), channel_id=1, source_target_pairs={{0,4},{1,5},{2,6},{3,7},{4,0},{5,1},{6,2},{7,3},{8,12},{9,13},{10,... | collective-permute-start | bytes 196616 | tf_op jit(solution)/shard_map/ppermute | solution.py:361
  41.9 1.7 %collective-permute-start.12 = (bf16[256,128]{1,0:T(8,128)(2,1)S(1)}, bf16[256,128]{1,0:T(8,128)(2,1)S(1)}, u32[]{:S(2)}, u32[]{:S(2)}) collective-permute-start(bf16[256,128]{1,0:T(8,128)(2,1)S(1)} %get-tuple-element.112.refs_5_.refs_20_), channel_id=1, source_target_pairs={{0,2},{1,3},{2,0},{3,1},{4,6},{5,7},{6,4},{7,5},{8,10},{9,11},{10,... | collective-permute-start | bytes 196616 | tf_op jit(solution)/shard_map/ppermute | solution.py:361
  53.0 1.8 %collective-permute-start.16 = (bf16[528,128]{1,0:T(8,128)(2,1)S(1)}, bf16[528,128]{1,0:T(8,128)(2,1)S(1)}, u32[]{:S(2)}, u32[]{:S(2)}) collective-permute-start(bf16[528,128]{1,0:T(8,128)(2,1)S(1)} %get-tuple-element.123), channel_id=1, source_target_pairs={{0,24},{8,16},{16,8},{24,0},{1,25},{9,17},{17,9},{25,1},{2,26},{10... | collective-permute-start | bytes 405512 | tf_op jit(solution)/shard_map/ppermute | solution.py:361
  56.6 2.8 %collective-permute-done.16.refs_2_ = bf16[528,128]{1,0:T(8,128)(2,1)S(1)} collective-permute-done((bf16[528,128]{1,0:T(8,128)(2,1)S(1)}, bf16[528,128]{1,0:T(8,128)(2,1)S(1)}, u32[]{:S(2)}, u32[]{:S(2)}) %collective-permute-start.16) | collective-permute-done | bytes 135200 | tf_op jit(solution)/shard_map/ppermute | solution.py:361
  59.5 1.8 %collective-permute-start.19 = (bf16[512,128]{1,0:T(8,128)(2,1)S(1)}, bf16[512,128]{1,0:T(8,128)(2,1)S(1)}, u32[]{:S(2)}, u32[]{:S(2)}) collective-permute-start(bf16[512,128]{1,0:T(8,128)(2,1)S(1)} %get-tuple-element.126.refs_5_.refs_12_), channel_id=1, source_target_pairs={{0,24},{8,16},{16,8},{24,0},{1,25},{9,17},{17,9},{25,1},{2,26},{10... | collective-permute-start | bytes 393224 | tf_op jit(solution)/shard_map/ppermute | solution.py:361
  61.3 1.9 %collective-permute-start.18 = (bf16[512,128]{1,0:T(8,128)(2,1)S(1)}, bf16[512,128]{1,0:T(8,128)(2,1)S(1)}, u32[]{:S(2)}, u32[]{:S(2)}) collective-permute-start(bf16[512,128]{1,0:T(8,128)(2,1)S(1)} %get-tuple-element.126.refs_5_.refs_12_), channel_id=1, source_target_pairs={{0,16},{8,24},{16,0},{24,8},{1,17},{9,25},{17,1},{25,9},{2,18},{10... | collective-permute-start | bytes 393224 | tf_op jit(solution)/shard_map/ppermute | solution.py:361
  69.8 4.0 %collective-permute-start.20 = (bf16[272,128]{1,0:T(8,128)(2,1)S(1)}, bf16[272,128]{1,0:T(8,128)(2,1)S(1)}, u32[]{:S(2)}, u32[]{:S(2)}) collective-permute-start(bf16[272,128]{1,0:T(8,128)(2,1)S(1)} %get-tuple-element.135), channel_id=1, source_target_pairs={{0,6},{1,7},{2,4},{3,5},{4,2},{5,3},{6,0},{7,1},{8,14},{9,15},{10,... | collective-permute-start | bytes 208904 | tf_op jit(solution)/shard_map/ppermute | solution.py:361
  74.4 2.2 %collective-permute-done.20.refs_0_ = bf16[272,128]{1,0:T(8,128)(2,1)S(1)} collective-permute-done((bf16[272,128]{1,0:T(8,128)(2,1)S(1)}, bf16[272,128]{1,0:T(8,128)(2,1)S(1)}, u32[]{:S(2)}, u32[]{:S(2)}) %collective-permute-start.20) | collective-permute-done | bytes 69664 | tf_op jit(solution)/shard_map/ppermute | solution.py:361
  79.8 1.6 %collective-permute-start.25 = (bf16[256,128]{1,0:T(8,128)(2,1)S(1)}, bf16[256,128]{1,0:T(8,128)(2,1)S(1)}, u32[]{:S(2)}, u32[]{:S(2)}) collective-permute-start(bf16[256,128]{1,0:T(8,128)(2,1)S(1)} %get-tuple-element.139.refs_5_.refs_24_), channel_id=1, source_target_pairs={{0,4},{1,5},{2,6},{3,7},{4,0},{5,1},{6,2},{7,3},{8,12},{9,13},{10,... | collective-permute-start | bytes 196616 | tf_op jit(solution)/shard_map/ppermute | solution.py:361
  82.1 2.1 %collective-permute-start.23 = (bf16[256,128]{1,0:T(8,128)(2,1)S(1)}, bf16[256,128]{1,0:T(8,128)(2,1)S(1)}, u32[]{:S(2)}, u32[]{:S(2)}) collective-permute-start(bf16[256,128]{1,0:T(8,128)(2,1)S(1)} %get-tuple-element.139.refs_5_.refs_24_), channel_id=1, source_target_pairs={{0,6},{1,7},{2,4},{3,5},{4,2},{5,3},{6,0},{7,1},{8,14},{9,15},{10,... | collective-permute-start | bytes 196616 | tf_op jit(solution)/shard_map/ppermute | solution.py:361
  89.8 2.1 %collective-permute-start.26 = (bf16[528,128]{1,0:T(8,128)(2,1)S(1)}, bf16[528,128]{1,0:T(8,128)(2,1)S(1)}, u32[]{:S(2)}, u32[]{:S(2)}) collective-permute-start(bf16[528,128]{1,0:T(8,128)(2,1)S(1)} %get-tuple-element.148), channel_id=1, source_target_pairs={{0,8},{8,0},{16,24},{24,16},{1,9},{9,1},{17,25},{25,17},{2,10},{10... | collective-permute-start | bytes 405512 | tf_op jit(solution)/shard_map/ppermute | solution.py:361
  93.4 1.6 %collective-permute-done.26.refs_0_ = bf16[528,128]{1,0:T(8,128)(2,1)S(1)} collective-permute-done((bf16[528,128]{1,0:T(8,128)(2,1)S(1)}, bf16[528,128]{1,0:T(8,128)(2,1)S(1)}, u32[]{:S(2)}, u32[]{:S(2)}) %collective-permute-start.26) | collective-permute-done | bytes 135200 | tf_op jit(solution)/shard_map/ppermute | solution.py:361
  95.0 1.8 %collective-permute-done.27.refs_1_ = bf16[528,128]{1,0:T(8,128)(2,1)S(1)} collective-permute-done((bf16[528,128]{1,0:T(8,128)(2,1)S(1)}, bf16[528,128]{1,0:T(8,128)(2,1)S(1)}, u32[]{:S(2)}, u32[]{:S(2)}) %collective-permute-start.27) | collective-permute-done | bytes 135200 | tf_op jit(solution)/shard_map/ppermute | solution.py:361
  96.9 1.7 %collective-permute-done.28.refs_2_ = bf16[528,128]{1,0:T(8,128)(2,1)S(1)} collective-permute-done((bf16[528,128]{1,0:T(8,128)(2,1)S(1)}, bf16[528,128]{1,0:T(8,128)(2,1)S(1)}, u32[]{:S(2)}, u32[]{:S(2)}) %collective-permute-start.28) | collective-permute-done | bytes 135200 | tf_op jit(solution)/shard_map/ppermute | solution.py:361
  104.7 1.7 %forward.21 = (f32[1152,128]{1,0:T(8,128)S(1)}, f32[8,128]{1,0:T(8,128)S(1)}) custom-call(bf16[24,2,128,128]{3,2,1,0:T(8,128)(2,1)S(1)} %bitcast.18, bf16[24,2,128,128]{3,2,1,0:T(8,128)(2,1)S(1)} %collective-permute-done.tile_ref.refs_1_, s32[3,24]{1,0:T(4,128)S(1)} %add_add_fusion.index_a.index_ref.refs_2_, ...), custom_call_target="tpu_custom_call", output_to_operand_aliasing={{0}: (6, {})} | custom-call | tf_op jit(solution)/shard_map/forward/pallas_call | solution.py:44
  109.0 2.8 %collective-permute-start.32 = (bf16[272,128]{1,0:T(8,128)(2,1)S(1)}, bf16[272,128]{1,0:T(8,128)(2,1)S(1)}, u32[]{:S(2)}, u32[]{:S(2)}) collective-permute-start(bf16[272,128]{1,0:T(8,128)(2,1)S(1)} %get-tuple-element.162), channel_id=1, source_target_pairs={{0,6},{1,7},{2,4},{3,5},{4,2},{5,3},{6,0},{7,1},{8,14},{9,15},{10,... | collective-permute-start | bytes 208904 | tf_op jit(solution)/shard_map/ppermute | solution.py:361
  111.8 1.7 %collective-permute-start.34 = (bf16[272,128]{1,0:T(8,128)(2,1)S(1)}, bf16[272,128]{1,0:T(8,128)(2,1)S(1)}, u32[]{:S(2)}, u32[]{:S(2)}) collective-permute-start(bf16[272,128]{1,0:T(8,128)(2,1)S(1)} %get-tuple-element.164), channel_id=1, source_target_pairs={{0,4},{1,5},{2,6},{3,7},{4,0},{5,1},{6,2},{7,3},{8,12},{9,13},{10,... | collective-permute-start | bytes 208904 | tf_op jit(solution)/shard_map/ppermute | solution.py:361
  113.5 1.7 %collective-permute-done.32.refs_0_ = bf16[272,128]{1,0:T(8,128)(2,1)S(1)} collective-permute-done((bf16[272,128]{1,0:T(8,128)(2,1)S(1)}, bf16[272,128]{1,0:T(8,128)(2,1)S(1)}, u32[]{:S(2)}, u32[]{:S(2)}) %collective-permute-start.32) | collective-permute-done | bytes 69664 | tf_op jit(solution)/shard_map/ppermute | solution.py:361
  117.1 1.7 %collective-permute-start.37 = (bf16[256,128]{1,0:T(8,128)(2,1)S(1)}, bf16[256,128]{1,0:T(8,128)(2,1)S(1)}, u32[]{:S(2)}, u32[]{:S(2)}) collective-permute-start(bf16[256,128]{1,0:T(8,128)(2,1)S(1)} %get-tuple-element.167.refs_0_.refs_28_), channel_id=1, source_target_pairs={{0,6},{1,7},{2,4},{3,5},{4,2},{5,3},{6,0},{7,1},{8,14},{9,15},{10,... | collective-permute-start | bytes 196616 | tf_op jit(solution)/shard_map/ppermute | solution.py:361
  119.3 2.2 %collective-permute-start.35 = (bf16[256,128]{1,0:T(8,128)(2,1)S(1)}, bf16[256,128]{1,0:T(8,128)(2,1)S(1)}, u32[]{:S(2)}, u32[]{:S(2)}) collective-permute-start(bf16[256,128]{1,0:T(8,128)(2,1)S(1)} %get-tuple-element.167.refs_0_.refs_28_), channel_id=1, source_target_pairs={{0,4},{1,5},{2,6},{3,7},{4,0},{5,1},{6,2},{7,3},{8,12},{9,13},{10,... | collective-permute-start | bytes 196616 | tf_op jit(solution)/shard_map/ppermute | solution.py:361
  121.5 1.8 %collective-permute-done.37.refs_3_.refs_31_ = bf16[256,128]{1,0:T(8,128)(2,1)S(1)} collective-permute-done((bf16[256,128]{1,0:T(8,128)(2,1)S(1)}, bf16[256,128]{1,0:T(8,128)(2,1)S(1)}, u32[]{:S(2)}, u32[]{:S(2)}) %collective-permute-start.37) | collective-permute-done | bytes 65568 | tf_op jit(solution)/shard_map/ppermute | solution.py:361
  126.3 1.8 %collective-permute-start.38 = (f32[8,128]{1,0:T(8,128)S(1)}, f32[8,128]{1,0:T(8,128)S(1)}, u32[]{:S(2)}, u32[]{:S(2)}) collective-permute-start(f32[8,128]{1,0:T(8,128)S(1)} %norm.1.refs_0_), channel_id=1, source_target_pairs={{0,24},{8,16},{16,8},{24,0},{1,25},{9,17},{17,9},{25,1},{2,26},{10... | collective-permute-start | bytes 12296 | tf_op jit(solution)/shard_map/ppermute | solution.py:361
  128.5 2.3 %collective-permute-done.38.refs_1_ = f32[8,128]{1,0:T(8,128)S(1)} collective-permute-done((f32[8,128]{1,0:T(8,128)S(1)}, f32[8,128]{1,0:T(8,128)S(1)}, u32[]{:S(2)}, u32[]{:S(2)}) %collective-permute-start.38) | collective-permute-done | bytes 4128 | tf_op jit(solution)/shard_map/ppermute | solution.py:361
  133.4 1.8 %unpack.1 = (f32[2,1024,128]{2,1,0:T(8,128)}, f32[2,1024,128]{2,1,0:T(8,128)}) custom-call(f32[1024,128]{1,0:T(8,128)S(1)} %get-tuple-element.172.own_x, f32[1024,128]{1,0:T(8,128)S(1)} %get-tuple-element.173.own_r, bf16[1024,128]{1,0:T(8,128)(2,1)S(1)} %collective-permute-done.41.pair_x, bf16[1024,128]{1,0:T(8,128)(2,1)S(1)} %collective-permute-done.42.pair_r), custom_call_target="tpu_custom_call" | custom-call | tf_op jit(solution)/shard_map/unpack/pallas_call | solution.py:44
  (96 shorter events, 64.1 us)
Async XLA Ops:
  0.6 6.5 %collective-permute-start = (bf16[24,2,128,128]{3,2,1,0:T(8,128)(2,1)}, bf16[24,2,128,128]{3,2,1,0:T(8,128)(2,1)S(1)}, u32[]{:S(2)}, u32[]{:S(2)}) collective-permute-start(bf16[24,2,128,128]{3,2,1,0:T(8,128)(2,1)} %bitcast.7), channel_id=1, source_target_pairs={{0,1},{1,0},{2,3},{3,2},{4,5},{5,4},{6,7},{7,6},{8,9},{9,8},{10,11... | collective-permute-start | bytes 4718600 | tf_op jit(solution)/shard_map/ppermute | solution.py:361
  8.5 6.5 %collective-permute-start.2 = (bf16[512,128]{1,0:T(8,128)(2,1)S(1)}, bf16[512,128]{1,0:T(8,128)(2,1)S(1)}, u32[]{:S(2)}, u32[]{:S(2)}) collective-permute-start(bf16[512,128]{1,0:T(8,128)(2,1)S(1)} %get-tuple-element.97), channel_id=1, source_target_pairs={{0,8},{8,0},{16,24},{24,16},{1,9},{9,1},{17,25},{25,17},{2,10},{10... | collective-permute-start | bytes 393224 | tf_op jit(solution)/shard_map/ppermute | solution.py:361
  11.2 8.4 %collective-permute-start.3 = (bf16[512,128]{1,0:T(8,128)(2,1)S(1)}, bf16[512,128]{1,0:T(8,128)(2,1)S(1)}, u32[]{:S(2)}, u32[]{:S(2)}) collective-permute-start(bf16[512,128]{1,0:T(8,128)(2,1)S(1)} %get-tuple-element.98), channel_id=1, source_target_pairs={{0,16},{8,24},{16,0},{24,8},{1,17},{9,25},{17,1},{25,9},{2,18},{10... | collective-permute-start | bytes 393224 | tf_op jit(solution)/shard_map/ppermute | solution.py:361
  13.4 6.2 %collective-permute-start.4 = (bf16[512,128]{1,0:T(8,128)(2,1)S(1)}, bf16[512,128]{1,0:T(8,128)(2,1)S(1)}, u32[]{:S(2)}, u32[]{:S(2)}) collective-permute-start(bf16[512,128]{1,0:T(8,128)(2,1)S(1)} %get-tuple-element.99), channel_id=1, source_target_pairs={{0,24},{8,16},{16,8},{24,0},{1,25},{9,17},{17,9},{25,1},{2,26},{10... | collective-permute-start | bytes 393224 | tf_op jit(solution)/shard_map/ppermute | solution.py:361
  19.7 7.0 %collective-permute-start.7 = (bf16[512,128]{1,0:T(8,128)(2,1)S(1)}, bf16[512,128]{1,0:T(8,128)(2,1)S(1)}, u32[]{:S(2)}, u32[]{:S(2)}) collective-permute-start(bf16[512,128]{1,0:T(8,128)(2,1)S(1)} %get-tuple-element.100.refs_5_.refs_8_), channel_id=1, source_target_pairs={{0,24},{8,16},{16,8},{24,0},{1,25},{9,17},{17,9},{25,1},{2,26},{10... | collective-permute-start | bytes 393224 | tf_op jit(solution)/shard_map/ppermute | solution.py:361
  21.3 6.9 %collective-permute-start.6 = (bf16[512,128]{1,0:T(8,128)(2,1)S(1)}, bf16[512,128]{1,0:T(8,128)(2,1)S(1)}, u32[]{:S(2)}, u32[]{:S(2)}) collective-permute-start(bf16[512,128]{1,0:T(8,128)(2,1)S(1)} %get-tuple-element.100.refs_5_.refs_8_), channel_id=1, source_target_pairs={{0,16},{8,24},{16,0},{24,8},{1,17},{9,25},{17,1},{25,9},{2,18},{10... | collective-permute-start | bytes 393224 | tf_op jit(solution)/shard_map/ppermute | solution.py:361
  22.7 6.6 %collective-permute-start.5 = (bf16[512,128]{1,0:T(8,128)(2,1)S(1)}, bf16[512,128]{1,0:T(8,128)(2,1)S(1)}, u32[]{:S(2)}, u32[]{:S(2)}) collective-permute-start(bf16[512,128]{1,0:T(8,128)(2,1)S(1)} %get-tuple-element.100.refs_5_.refs_8_), channel_id=1, source_target_pairs={{0,8},{8,0},{16,24},{24,16},{1,9},{9,1},{17,25},{25,17},{2,10},{10... | collective-permute-start | bytes 393224 | tf_op jit(solution)/shard_map/ppermute | solution.py:361
  30.9 6.5 %collective-permute-start.8 = (bf16[272,128]{1,0:T(8,128)(2,1)S(1)}, bf16[272,128]{1,0:T(8,128)(2,1)S(1)}, u32[]{:S(2)}, u32[]{:S(2)}) collective-permute-start(bf16[272,128]{1,0:T(8,128)(2,1)S(1)} %get-tuple-element.109), channel_id=1, source_target_pairs={{0,6},{1,7},{2,4},{3,5},{4,2},{5,3},{6,0},{7,1},{8,14},{9,15},{10,... | collective-permute-start | bytes 208904 | tf_op jit(solution)/shard_map/ppermute | solution.py:361
  35.0 5.2 %collective-permute-start.10 = (bf16[272,128]{1,0:T(8,128)(2,1)S(1)}, bf16[272,128]{1,0:T(8,128)(2,1)S(1)}, u32[]{:S(2)}, u32[]{:S(2)}) collective-permute-start(bf16[272,128]{1,0:T(8,128)(2,1)S(1)} %get-tuple-element.111), channel_id=1, source_target_pairs={{0,4},{1,5},{2,6},{3,7},{4,0},{5,1},{6,2},{7,3},{8,12},{9,13},{10,... | collective-permute-start | bytes 208904 | tf_op jit(solution)/shard_map/ppermute | solution.py:361
  40.3 5.7 %collective-permute-start.13 = (bf16[256,128]{1,0:T(8,128)(2,1)S(1)}, bf16[256,128]{1,0:T(8,128)(2,1)S(1)}, u32[]{:S(2)}, u32[]{:S(2)}) collective-permute-start(bf16[256,128]{1,0:T(8,128)(2,1)S(1)} %get-tuple-element.112.refs_5_.refs_20_), channel_id=1, source_target_pairs={{0,4},{1,5},{2,6},{3,7},{4,0},{5,1},{6,2},{7,3},{8,12},{9,13},{10,... | collective-permute-start | bytes 196616 | tf_op jit(solution)/shard_map/ppermute | solution.py:361
  41.9 5.3 %collective-permute-start.12 = (bf16[256,128]{1,0:T(8,128)(2,1)S(1)}, bf16[256,128]{1,0:T(8,128)(2,1)S(1)}, u32[]{:S(2)}, u32[]{:S(2)}) collective-permute-start(bf16[256,128]{1,0:T(8,128)(2,1)S(1)} %get-tuple-element.112.refs_5_.refs_20_), channel_id=1, source_target_pairs={{0,2},{1,3},{2,0},{3,1},{4,6},{5,7},{6,4},{7,5},{8,10},{9,11},{10,... | collective-permute-start | bytes 196616 | tf_op jit(solution)/shard_map/ppermute | solution.py:361
  43.6 6.1 %collective-permute-start.11 = (bf16[256,128]{1,0:T(8,128)(2,1)S(1)}, bf16[256,128]{1,0:T(8,128)(2,1)S(1)}, u32[]{:S(2)}, u32[]{:S(2)}) collective-permute-start(bf16[256,128]{1,0:T(8,128)(2,1)S(1)} %get-tuple-element.112.refs_5_.refs_20_), channel_id=1, source_target_pairs={{0,6},{1,7},{2,4},{3,5},{4,2},{5,3},{6,0},{7,1},{8,14},{9,15},{10,... | collective-permute-start | bytes 196616 | tf_op jit(solution)/shard_map/ppermute | solution.py:361
  51.2 5.1 %collective-permute-start.14 = (bf16[528,128]{1,0:T(8,128)(2,1)S(1)}, bf16[528,128]{1,0:T(8,128)(2,1)S(1)}, u32[]{:S(2)}, u32[]{:S(2)}) collective-permute-start(bf16[528,128]{1,0:T(8,128)(2,1)S(1)} %get-tuple-element.121), channel_id=1, source_target_pairs={{0,8},{8,0},{16,24},{24,16},{1,9},{9,1},{17,25},{25,17},{2,10},{10... | collective-permute-start | bytes 405512 | tf_op jit(solution)/shard_map/ppermute | solution.py:361
  51.6 5.0 %collective-permute-start.15 = (bf16[528,128]{1,0:T(8,128)(2,1)S(1)}, bf16[528,128]{1,0:T(8,128)(2,1)S(1)}, u32[]{:S(2)}, u32[]{:S(2)}) collective-permute-start(bf16[528,128]{1,0:T(8,128)(2,1)S(1)} %get-tuple-element.122), channel_id=1, source_target_pairs={{0,16},{8,24},{16,0},{24,8},{1,17},{9,25},{17,1},{25,9},{2,18},{10... | collective-permute-start | bytes 405512 | tf_op jit(solution)/shard_map/ppermute | solution.py:361
  53.0 6.5 %collective-permute-start.16 = (bf16[528,128]{1,0:T(8,128)(2,1)S(1)}, bf16[528,128]{1,0:T(8,128)(2,1)S(1)}, u32[]{:S(2)}, u32[]{:S(2)}) collective-permute-start(bf16[528,128]{1,0:T(8,128)(2,1)S(1)} %get-tuple-element.123), channel_id=1, source_target_pairs={{0,24},{8,16},{16,8},{24,0},{1,25},{9,17},{17,9},{25,1},{2,26},{10... | collective-permute-start | bytes 405512 | tf_op jit(solution)/shard_map/ppermute | solution.py:361
  59.5 6.0 %collective-permute-start.19 = (bf16[512,128]{1,0:T(8,128)(2,1)S(1)}, bf16[512,128]{1,0:T(8,128)(2,1)S(1)}, u32[]{:S(2)}, u32[]{:S(2)}) collective-permute-start(bf16[512,128]{1,0:T(8,128)(2,1)S(1)} %get-tuple-element.126.refs_5_.refs_12_), channel_id=1, source_target_pairs={{0,24},{8,16},{16,8},{24,0},{1,25},{9,17},{17,9},{25,1},{2,26},{10... | collective-permute-start | bytes 393224 | tf_op jit(solution)/shard_map/ppermute | solution.py:361
  61.3 5.7 %collective-permute-start.18 = (bf16[512,128]{1,0:T(8,128)(2,1)S(1)}, bf16[512,128]{1,0:T(8,128)(2,1)S(1)}, u32[]{:S(2)}, u32[]{:S(2)}) collective-permute-start(bf16[512,128]{1,0:T(8,128)(2,1)S(1)} %get-tuple-element.126.refs_5_.refs_12_), channel_id=1, source_target_pairs={{0,16},{8,24},{16,0},{24,8},{1,17},{9,25},{17,1},{25,9},{2,18},{10... | collective-permute-start | bytes 393224 | tf_op jit(solution)/shard_map/ppermute | solution.py:361
  69.8 6.9 %collective-permute-start.20 = (bf16[272,128]{1,0:T(8,128)(2,1)S(1)}, bf16[272,128]{1,0:T(8,128)(2,1)S(1)}, u32[]{:S(2)}, u32[]{:S(2)}) collective-permute-start(bf16[272,128]{1,0:T(8,128)(2,1)S(1)} %get-tuple-element.135), channel_id=1, source_target_pairs={{0,6},{1,7},{2,4},{3,5},{4,2},{5,3},{6,0},{7,1},{8,14},{9,15},{10,... | collective-permute-start | bytes 208904 | tf_op jit(solution)/shard_map/ppermute | solution.py:361
  73.8 5.9 %collective-permute-start.22 = (bf16[272,128]{1,0:T(8,128)(2,1)S(1)}, bf16[272,128]{1,0:T(8,128)(2,1)S(1)}, u32[]{:S(2)}, u32[]{:S(2)}) collective-permute-start(bf16[272,128]{1,0:T(8,128)(2,1)S(1)} %get-tuple-element.137), channel_id=1, source_target_pairs={{0,4},{1,5},{2,6},{3,7},{4,0},{5,1},{6,2},{7,3},{8,12},{9,13},{10,... | collective-permute-start | bytes 208904 | tf_op jit(solution)/shard_map/ppermute | solution.py:361
  79.8 5.7 %collective-permute-start.25 = (bf16[256,128]{1,0:T(8,128)(2,1)S(1)}, bf16[256,128]{1,0:T(8,128)(2,1)S(1)}, u32[]{:S(2)}, u32[]{:S(2)}) collective-permute-start(bf16[256,128]{1,0:T(8,128)(2,1)S(1)} %get-tuple-element.139.refs_5_.refs_24_), channel_id=1, source_target_pairs={{0,4},{1,5},{2,6},{3,7},{4,0},{5,1},{6,2},{7,3},{8,12},{9,13},{10,... | collective-permute-start | bytes 196616 | tf_op jit(solution)/shard_map/ppermute | solution.py:361
  81.4 5.3 %collective-permute-start.24 = (bf16[256,128]{1,0:T(8,128)(2,1)S(1)}, bf16[256,128]{1,0:T(8,128)(2,1)S(1)}, u32[]{:S(2)}, u32[]{:S(2)}) collective-permute-start(bf16[256,128]{1,0:T(8,128)(2,1)S(1)} %get-tuple-element.139.refs_5_.refs_24_), channel_id=1, source_target_pairs={{0,2},{1,3},{2,0},{3,1},{4,6},{5,7},{6,4},{7,5},{8,10},{9,11},{10,... | collective-permute-start | bytes 196616 | tf_op jit(solution)/shard_map/ppermute | solution.py:361
  82.1 6.1 %collective-permute-start.23 = (bf16[256,128]{1,0:T(8,128)(2,1)S(1)}, bf16[256,128]{1,0:T(8,128)(2,1)S(1)}, u32[]{:S(2)}, u32[]{:S(2)}) collective-permute-start(bf16[256,128]{1,0:T(8,128)(2,1)S(1)} %get-tuple-element.139.refs_5_.refs_24_), channel_id=1, source_target_pairs={{0,6},{1,7},{2,4},{3,5},{4,2},{5,3},{6,0},{7,1},{8,14},{9,15},{10,... | collective-permute-start | bytes 196616 | tf_op jit(solution)/shard_map/ppermute | solution.py:361
  89.8 5.3 %collective-permute-start.26 = (bf16[528,128]{1,0:T(8,128)(2,1)S(1)}, bf16[528,128]{1,0:T(8,128)(2,1)S(1)}, u32[]{:S(2)}, u32[]{:S(2)}) collective-permute-start(bf16[528,128]{1,0:T(8,128)(2,1)S(1)} %get-tuple-element.148), channel_id=1, source_target_pairs={{0,8},{8,0},{16,24},{24,16},{1,9},{9,1},{17,25},{25,17},{2,10},{10... | collective-permute-start | bytes 405512 | tf_op jit(solution)/shard_map/ppermute | solution.py:361
  91.9 5.0 %collective-permute-start.27 = (bf16[528,128]{1,0:T(8,128)(2,1)S(1)}, bf16[528,128]{1,0:T(8,128)(2,1)S(1)}, u32[]{:S(2)}, u32[]{:S(2)}) collective-permute-start(bf16[528,128]{1,0:T(8,128)(2,1)S(1)} %get-tuple-element.149), channel_id=1, source_target_pairs={{0,16},{8,24},{16,0},{24,8},{1,17},{9,25},{17,1},{25,9},{2,18},{10... | collective-permute-start | bytes 405512 | tf_op jit(solution)/shard_map/ppermute | solution.py:361
  92.7 5.9 %collective-permute-start.28 = (bf16[528,128]{1,0:T(8,128)(2,1)S(1)}, bf16[528,128]{1,0:T(8,128)(2,1)S(1)}, u32[]{:S(2)}, u32[]{:S(2)}) collective-permute-start(bf16[528,128]{1,0:T(8,128)(2,1)S(1)} %get-tuple-element.150), channel_id=1, source_target_pairs={{0,24},{8,16},{16,8},{24,0},{1,25},{9,17},{17,9},{25,1},{2,26},{10... | collective-permute-start | bytes 405512 | tf_op jit(solution)/shard_map/ppermute | solution.py:361
  98.7 6.0 %collective-permute-start.31 = (bf16[512,128]{1,0:T(8,128)(2,1)S(1)}, bf16[512,128]{1,0:T(8,128)(2,1)S(1)}, u32[]{:S(2)}, u32[]{:S(2)}) collective-permute-start(bf16[512,128]{1,0:T(8,128)(2,1)S(1)} %get-tuple-element.153.refs_5_.refs_16_), channel_id=1, source_target_pairs={{0,24},{8,16},{16,8},{24,0},{1,25},{9,17},{17,9},{25,1},{2,26},{10... | collective-permute-start | bytes 393224 | tf_op jit(solution)/shard_map/ppermute | solution.py:361
  99.5 6.9 %collective-permute-start.30 = (bf16[512,128]{1,0:T(8,128)(2,1)S(1)}, bf16[512,128]{1,0:T(8,128)(2,1)S(1)}, u32[]{:S(2)}, u32[]{:S(2)}) collective-permute-start(bf16[512,128]{1,0:T(8,128)(2,1)S(1)} %get-tuple-element.153.refs_5_.refs_16_), channel_id=1, source_target_pairs={{0,16},{8,24},{16,0},{24,8},{1,17},{9,25},{17,1},{25,9},{2,18},{10... | collective-permute-start | bytes 393224 | tf_op jit(solution)/shard_map/ppermute | solution.py:361
  101.0 6.4 %collective-permute-start.29 = (bf16[512,128]{1,0:T(8,128)(2,1)S(1)}, bf16[512,128]{1,0:T(8,128)(2,1)S(1)}, u32[]{:S(2)}, u32[]{:S(2)}) collective-permute-start(bf16[512,128]{1,0:T(8,128)(2,1)S(1)} %get-tuple-element.153.refs_5_.refs_16_), channel_id=1, source_target_pairs={{0,8},{8,0},{16,24},{24,16},{1,9},{9,1},{17,25},{25,17},{2,10},{10... | collective-permute-start | bytes 393224 | tf_op jit(solution)/shard_map/ppermute | solution.py:361
  109.0 6.1 %collective-permute-start.32 = (bf16[272,128]{1,0:T(8,128)(2,1)S(1)}, bf16[272,128]{1,0:T(8,128)(2,1)S(1)}, u32[]{:S(2)}, u32[]{:S(2)}) collective-permute-start(bf16[272,128]{1,0:T(8,128)(2,1)S(1)} %get-tuple-element.162), channel_id=1, source_target_pairs={{0,6},{1,7},{2,4},{3,5},{4,2},{5,3},{6,0},{7,1},{8,14},{9,15},{10,... | collective-permute-start | bytes 208904 | tf_op jit(solution)/shard_map/ppermute | solution.py:361
  111.8 5.2 %collective-permute-start.34 = (bf16[272,128]{1,0:T(8,128)(2,1)S(1)}, bf16[272,128]{1,0:T(8,128)(2,1)S(1)}, u32[]{:S(2)}, u32[]{:S(2)}) collective-permute-start(bf16[272,128]{1,0:T(8,128)(2,1)S(1)} %get-tuple-element.164), channel_id=1, source_target_pairs={{0,4},{1,5},{2,6},{3,7},{4,0},{5,1},{6,2},{7,3},{8,12},{9,13},{10,... | collective-permute-start | bytes 208904 | tf_op jit(solution)/shard_map/ppermute | solution.py:361
  117.1 6.2 %collective-permute-start.37 = (bf16[256,128]{1,0:T(8,128)(2,1)S(1)}, bf16[256,128]{1,0:T(8,128)(2,1)S(1)}, u32[]{:S(2)}, u32[]{:S(2)}) collective-permute-start(bf16[256,128]{1,0:T(8,128)(2,1)S(1)} %get-tuple-element.167.refs_0_.refs_28_), channel_id=1, source_target_pairs={{0,6},{1,7},{2,4},{3,5},{4,2},{5,3},{6,0},{7,1},{8,14},{9,15},{10,... | collective-permute-start | bytes 196616 | tf_op jit(solution)/shard_map/ppermute | solution.py:361
  119.3 5.2 %collective-permute-start.35 = (bf16[256,128]{1,0:T(8,128)(2,1)S(1)}, bf16[256,128]{1,0:T(8,128)(2,1)S(1)}, u32[]{:S(2)}, u32[]{:S(2)}) collective-permute-start(bf16[256,128]{1,0:T(8,128)(2,1)S(1)} %get-tuple-element.167.refs_0_.refs_28_), channel_id=1, source_target_pairs={{0,4},{1,5},{2,6},{3,7},{4,0},{5,1},{6,2},{7,3},{8,12},{9,13},{10,... | collective-permute-start | bytes 196616 | tf_op jit(solution)/shard_map/ppermute | solution.py:361
  (15 other events, 84.9 us)

commit v5 on v4

--- a/solution.py
+++ b/solution.py
@@ -17,7 +17,6 @@
 
 F32 = jnp.float32
 BF16 = jnp.bfloat16
-F32_INDEX = jnp.int32
 
 
 class Way(NamedTuple):
@@ -166,19 +165,24 @@
             send[2 * part :, :] = tail
 
 
-def list_kernel(keys, index_a, index_b, *lists):
+def list_kernel(plans, index_a, index_b, *lists):
     slot_count = index_a.shape[1]
-    down = lax.broadcasted_iota(F32_INDEX, (slot_count, slot_count), 0)
-    along = lax.broadcasted_iota(F32_INDEX, (slot_count, slot_count), 1)
-    for list_ref, (row, width, buckets) in zip(lists, keys):
-        down_f, wide = down.astype(F32), lax.broadcasted_iota(F32_INDEX, (slot_count, list_ref.shape[1]), 1).astype(F32)
-        slot_f = lax.broadcasted_iota(F32_INDEX, wide.shape, 0).astype(F32)
+    square = (slot_count, slot_count)
+    down, along = (lax.broadcasted_iota(jnp.int32, square, k) for k in (0, 1))
+    down_f, along_f, here = down.astype(F32), along.astype(F32), down == along
+    for list_ref, (way, groups) in zip(lists, plans):
+        wide = lax.broadcasted_iota(jnp.int32, (slot_count, list_ref.shape[1]), 1).astype(F32)
+        slot_f = lax.broadcasted_iota(jnp.int32, wide.shape, 0).astype(F32)
+        place = way.source_place()
         for k, index_ref in enumerate((index_a, index_b)):
-            bucket = index_ref[row : row + 1, :] // width
-            used = along[:1, :] < index_ref[2:3, :]
-            key = jnp.broadcast_to(jnp.where(used, bucket, buckets).astype(F32), down.shape)
-            order_along = key * slot_count + along.astype(F32)
-            here = down == along
+            offset = (index_ref[way.source : way.source + 1, :] * way.size // way.part) ^ place
+            bucket = jnp.zeros(offset.shape, F32)
+            for at, group in enumerate(groups):
+                for member in group:
+                    bucket = jnp.where(offset == member, float(at), bucket)
+            bucket = jnp.where(along[:1, :] < index_ref[2:3, :], bucket, float(len(groups)))
+            key = jnp.broadcast_to(bucket, square)
+            order_along = key * slot_count + along_f
             key_down = jnp.sum(jnp.where(here, key, 0.0), axis=1, keepdims=True)
             order_down = key_down * slot_count + down_f[:, :1]
             rank = jnp.sum(jnp.where(order_along < order_down, 1.0, 0.0), axis=1, keepdims=True)
@@ -188,52 +192,38 @@
             list_ref[k + 2 : k + 3, :] = begin.astype(jnp.int32)
 
 
-def step_kernel(way, pick, first, last, *refs):
+def step_kernel(way, pick, at_group, last, *refs):
     (tile_a, tile_b, index_a, index_b, list_ref), refs = refs[:5], refs[5:]
     chunks, refs = refs[: len(pick)], refs[len(pick) :]
-    if not first:
+    if at_group:
         folded, refs = refs[1][...], refs[2:]
     total_ref, refs = refs[0], refs[1:]
     here, there = way.source_place(), way.target_place()
-    single = len(pick) == 1
-    if first:
+    if not at_group:
         total_ref[...] = jnp.zeros_like(total_ref)
         folded = jnp.zeros((8, total_ref.shape[-1]), F32)
-    if single:
-        turned_ref, plain_ref = refs[-1], chunks[0]
-        wide = plain_ref[...].astype(F32)
-        turned_ref[...] = times_i(wide, way.sign).astype(BF16)
-        folded += fold_squares(wide)
-    else:
-        plain_ref, turned_ref = refs[-2:]
-        for chunk, offset in zip(chunks, pick):
-            for half in range(way.halves):
-                at = pl.ds(pl.multiple_of((here ^ offset) * way.part + half * way.length, way.part), way.part)
-                folded += put_chunk(chunk[half * way.part : (half + 1) * way.part, :], plain_ref, turned_ref, at, way.sign)
-    place = here ^ pick[0]
-    base = place * (way.part // way.size) if single else 0
-    stride = plain_ref.shape[0] // way.halves
-    width = 4 if single else GROUP
+    plain_ref, turned_ref = refs[-2:]
+    for chunk, offset in zip(chunks, pick):
+        for half in range(way.halves):
+            at = pl.ds(pl.multiple_of((here ^ offset) * way.part + half * way.length, way.part), way.part)
+            folded += put_chunk(chunk[half * way.part : (half + 1) * way.part, :], plain_ref, turned_ref, at, way.sign)
     for k, (tile_ref, index_ref) in enumerate(((tile_a, index_a), (tile_b, index_b))):
-        low = list_ref[k + 2, place] if single else 0
-        high = list_ref[k + 2, place + 1] if single else index_ref[2, 0]
+        low, high = list_ref[k + 2, at_group], list_ref[k + 2, at_group + 1]
 
         def turn_of(group, carry):
-            for lane in range(width):
-                at = low + group * width + lane
-                valid = at < high
-                slot = list_ref[k, at] if single else at
-                source = jnp.where(valid, index_ref[way.source, slot] - base, 0)
-                target = jnp.where(valid, index_ref[1 - way.source, slot] + k * way.target_shift, way.spare)
-                start = pl.multiple_of(source * way.size + k * (way.halves - 1) * stride, way.size)
-                span = pl.ds(start, way.size)
+            for lane in range(GROUP):
+                at = low + group * GROUP + lane
+                slot = list_ref[k, at]
+                source = index_ref[way.source, slot]
+                target = jnp.where(at < high, index_ref[1 - way.source, slot] + k * way.target_shift, way.spare)
+                span = pl.ds(pl.multiple_of(source * way.size + k * (way.halves - 1) * way.length, way.size), way.size)
                 right = jnp.concatenate([plain_ref[span, :], turned_ref[span, :]], axis=0)
                 goal = spans(way.size, target)
                 product = jnp.dot(way.weights(tile_ref, slot), right, preferred_element_type=F32)
                 total_ref[goal, :] = total_ref[goal, :] + product
             return carry
 
-        lax.fori_loop(0, (high - low + width - 1) // width, turn_of, 0)
+        lax.fori_loop(0, (high - low + GROUP - 1) // GROUP, turn_of, 0)
     if not last:
         refs[0][...] = folded
         return
@@ -369,7 +359,9 @@
     def over_z(values, order):
         return [swap(v, "src", srcs, 2 * o) for v, o in zip(values, order)]
 
-    hyd_back, z_back = hyd_order[::-1], z_order[::-1]
+    def groups_of(order, way):
+        half = len(order) // 2
+        return (order[:half], order[half:]) if way.part % way.size == 0 else (order,)
 
     def body(record, tile_data, tile_rows, tile_cols, tile_counts):
         own_tiles = tile_data[0, 0]
@@ -413,36 +405,35 @@
             0, -1.0, size, row_part, 1, rows, col_part, (0, cols), col_tiles, 2 * col_tiles, hyd_order,
             z_place, hyd_place, lambda tile_ref, slot: tile_ref[slot],
         )
+        g_order, image_order = ((0, *o[: len(o) // 2], *o[len(o) // 2 :][::-1]) for o in (hyd_order, z_order))
+        g_groups, image_groups = (groups_of(order, w) for order, w in ((g_order, forward), (image_order, adjoint)))
         lists = call(
-            functools.partial(list_kernel, [(w.source, max(w.part // size, 1), w.length // w.part) for w in (forward, adjoint)]),
+            functools.partial(list_kernel, ((forward, g_groups), (adjoint, image_groups))),
             "lists", [((8, 128), jnp.int32)] * 2, [], index, pair_index, vector=True,
         )
 
-        def apply(way, name, tiles, slot_list, chunks, order, outs):
-            picks = [(k,) for k in range(len(order))] if way.part % size == 0 else [tuple(range(len(order)))]
+        def apply(way, name, tiles, slot_list, chunks, groups, outs):
             total = (((len(way.target_begins) * (way.spare // len(way.target_begins)) + 1) * size, shots), F32)
-            carry = []
-            for at, pick in enumerate(picks):
-                last = at + 1 == len(picks)
-                length = sum(chunks[k].shape[0] for k in pick)
+            carry, at = [], 0
+            for k, group in enumerate(groups):
+                last = k + 1 == len(groups)
                 carry = call(
-                    functools.partial(step_kernel, way, tuple(order[k] for k in pick), at == 0, last), name,
-                    [total] + (outs if last else [norm]),
-                    [vector(length, BF16)] * (1 if len(pick) == 1 else 2),
-                    *tiles, index, pair_index, slot_list, *(chunks[k] for k in pick), *carry,
-                    alias={6: 0} if at else None,
+                    functools.partial(step_kernel, way, group, k, last), name,
+                    [total] + (outs if last else [norm]), [vector(way.halves * way.length, BF16)] * 2,
+                    *tiles, index, pair_index, slot_list, *chunks[at : at + len(group)], *carry,
+                    alias={5 + len(group): 0} if k else None,
                 )
+                at += len(group)
             return carry[1:]
 
         alphas, betas, g_chunks, images = [], [], [], []
         image = gamma = None
-        g_order, image_order = (0, *hyd_back), (0, *z_back)
         for step in range(ITERS):
             last = step + 1 == ITERS
-            chunks = [narrow, *over_hyd([narrow] * (hyds - 1), hyd_back)]
+            chunks = [narrow, *over_hyd([narrow] * (hyds - 1), g_order[1:])]
             g_chunks += chunks
             own, own_norm, *sends = apply(
-                forward, "forward", (own_tiles, pair_tiles), lists[0], chunks, g_order, [vector(row_part, F32), norm] + row_sends
+                forward, "forward", (own_tiles, pair_tiles), lists[0], chunks, g_groups, [vector(row_part, F32), norm] + row_sends
             )
             narrow, gamma, *more = call(
                 functools.partial(image_kernel, zs - 1, step > 0, last), "image",
@@ -451,12 +442,17 @@
             )
             image = None if last else more.pop()
             betas += more
-            chunks = [narrow, *over_z([narrow] * (zs - 1), z_back)]
+            if last:
+                issued = z_order[::-1]
+                arrived = dict(zip(issued, over_z([narrow] * (zs - 1), issued)))
+                chunks = [narrow, *(arrived[o] for o in image_order[1:])]
+            else:
+                chunks = [narrow, *over_z([narrow] * (zs - 1), image_order[1:])]
             images += chunks
             if last:
                 break
             own, own_norm, *sends = apply(
-                adjoint, "adjoint", (turned_own, turned_pair), lists[1], chunks, image_order, [vector(2 * col_part, F32), norm] + col_sends
+                adjoint, "adjoint", (turned_own, turned_pair), lists[1], chunks, image_groups, [vector(2 * col_part, F32), norm] + col_sends
             )
             more_steps = step + 2 < ITERS
             narrow, alpha, *wide = call(
@@ -468,7 +464,7 @@
             alphas.append(alpha)
 
         (own_norm,) = call(norm_kernel, "norm", [norm], [], *chunks)
-        norms = [own_norm] + over_hyd([own_norm] * (hyds - 1), hyd_back)
+        norms = [own_norm] + over_hyd([own_norm] * (hyds - 1), hyd_order[::-1])
         own_x, pair_x, wide_r, narrow_r = call(
             functools.partial(answer_kernel, "hyd", "src", g_order, image_order), "answer",
             [vector(cols, F32), vector(cols, BF16), vector(rows, F32), vector(rows, BF16)], [],

time: 135 us -> 132 us (0.978)
  Pallas kernels: 33.6 us -> 23.9 us
  waiting for transfers between devices: 41.9 us -> 49.3 us
    pallas_call x32 -> x22, Pallas kernels: 33.6 us -> 23.9 us  [call(): pl.pallas_call(kernel, name=name, out_shape=[jax.ShapeDtypeStruct(s, d) f...]
    ppermute x43, waiting for transfers between devices: 41.9 us -> 49.3 us  [swap(): return lax.ppermute(value, axis, [(i, i ^ offset) for i in range(size)])]
  transfers between devices with their start and end apart: 43 -> 43, of which waited for: 30 -> 30; matrix products, arithmetic and copies ran while one was open for 1% -> 1% of each run, Pallas kernels for 16% -> 8%
where the time goes in v5:
time: 132 us
  starting transfers between devices  53.5 us (41%)
  waiting for transfers between devices  49.3 us (37%)
  Pallas kernels  23.9 us (18%)
  local copies, waits for them, and re-layouts  2.72 us (2%)
  between operations  1.49 us (1%)
    ppermute x43, starting transfers between devices, swap(): return lax.ppermute(value, axis, [(i, i ^ offset) for i in range(size)])  53.5 us
    ppermute x43, waiting for transfers between devices, swap(): return lax.ppermute(value, axis, [(i, i ^ offset) for i in range(size)])  49.3 us
    pallas_call x22, Pallas kernels, call(): pl.pallas_call(kernel, name=name, out_shape=[jax.ShapeDtypeStruct(s, d) f...  23.9 us
    unnamed x8, local copies, waits for them, and re-layouts  2.64 us
  transfers between devices with their start and end apart: 43, of which 30 were waited for; matrix products, arithmetic and copies ran while one was open for 1% of the time, Pallas kernels for 8%

profile of v5, /device:TPU:0, one launch (start us, length us, event | category | flops | bytes accessed | tf_op | source)
XLA Modules:
  0.0 131.7 jit_solution(15480671198685949344)
XLA Ops:
  5.3 2.2 %pack.1 = (bf16[24,128,256]{2,1,0:T(8,128)(2,1)S(1)}, f32[1152,128]{1,0:T(8,128)S(1)}, bf16[1024,128]{1,0:T(8,128)(2,1)S(1)}, bf16[1024,128]{1,0:T(8,128)(2,1)S(1)}) custom-call(f32[2,1024,128]{2,1,0:T(8,128)S(1)} %copy-done.2, bf16[24,2,128,128]{3,2,1,0:T(8,128)(2,1)S(1)} %bitcast.8, s32[3,24]{1,0:T(4,128)S(1)} %add_add_fusion.index_a.index_ref.refs_2_), custom_call_target="tpu_custom_call" | custom-call | tf_op jit(solution)/shard_map/pack/pallas_call | solution.py:43
  8.9 2.7 %collective-permute-start.2 = (bf16[512,128]{1,0:T(8,128)(2,1)S(1)}, bf16[512,128]{1,0:T(8,128)(2,1)S(1)}, u32[]{:S(2)}, u32[]{:S(2)}) collective-permute-start(bf16[512,128]{1,0:T(8,128)(2,1)S(1)} %get-tuple-element.77), channel_id=1, source_target_pairs={{0,8},{8,0},{16,24},{24,16},{1,9},{9,1},{17,25},{25,17},{2,10},{10... | collective-permute-start | bytes 393224 | tf_op jit(solution)/shard_map/ppermute | solution.py:351
  11.6 1.9 %collective-permute-start.3 = (bf16[512,128]{1,0:T(8,128)(2,1)S(1)}, bf16[512,128]{1,0:T(8,128)(2,1)S(1)}, u32[]{:S(2)}, u32[]{:S(2)}) collective-permute-start(bf16[512,128]{1,0:T(8,128)(2,1)S(1)} %get-tuple-element.78), channel_id=1, source_target_pairs={{0,16},{8,24},{16,0},{24,8},{1,17},{9,25},{17,1},{25,9},{2,18},{10... | collective-permute-start | bytes 393224 | tf_op jit(solution)/shard_map/ppermute | solution.py:351
  13.4 2.0 %collective-permute-done.2.refs_0_ = bf16[512,128]{1,0:T(8,128)(2,1)S(1)} collective-permute-done((bf16[512,128]{1,0:T(8,128)(2,1)S(1)}, bf16[512,128]{1,0:T(8,128)(2,1)S(1)}, u32[]{:S(2)}, u32[]{:S(2)}) %collective-permute-start.2) | collective-permute-done | bytes 131104 | tf_op jit(solution)/shard_map/ppermute | solution.py:351
  15.5 4.2 %collective-permute-done.3.refs_1_ = bf16[512,128]{1,0:T(8,128)(2,1)S(1)} collective-permute-done((bf16[512,128]{1,0:T(8,128)(2,1)S(1)}, bf16[512,128]{1,0:T(8,128)(2,1)S(1)}, u32[]{:S(2)}, u32[]{:S(2)}) %collective-permute-start.3) | collective-permute-done | bytes 131104 | tf_op jit(solution)/shard_map/ppermute | solution.py:351
  23.5 2.1 %collective-permute-done.7.refs_6_.refs_9_ = bf16[512,128]{1,0:T(8,128)(2,1)S(1)} collective-permute-done((bf16[512,128]{1,0:T(8,128)(2,1)S(1)}, bf16[512,128]{1,0:T(8,128)(2,1)S(1)}, u32[]{:S(2)}, u32[]{:S(2)}) %collective-permute-start.7) | collective-permute-done | bytes 131104 | tf_op jit(solution)/shard_map/ppermute | solution.py:351
  28.4 1.9 %forward.7 = (f32[1152,128]{1,0:T(8,128)S(1)}, f32[256,128]{1,0:T(8,128)S(1)}, f32[8,128]{1,0:T(8,128)S(1)}, bf16[272,128]{1,0:T(8,128)(2,1)S(1)}, bf16[272,128]...) custom-call(bf16[24,2,128,128]{3,2,1,0:T(8,128)(2,1)S(1)} %bitcast.10, ...), custom_call_target="tpu_custom_call", output_to_operand_aliasing={{0}: (7, {})} | custom-call | tf_op jit(solution)/shard_map/forward/pallas_call | solution.py:43
  30.2 3.1 %collective-permute-start.8 = (bf16[272,128]{1,0:T(8,128)(2,1)S(1)}, bf16[272,128]{1,0:T(8,128)(2,1)S(1)}, u32[]{:S(2)}, u32[]{:S(2)}) collective-permute-start(bf16[272,128]{1,0:T(8,128)(2,1)S(1)} %get-tuple-element.85), channel_id=1, source_target_pairs={{0,6},{1,7},{2,4},{3,5},{4,2},{5,3},{6,0},{7,1},{8,14},{9,15},{10,... | collective-permute-start | bytes 208904 | tf_op jit(solution)/shard_map/ppermute | solution.py:351
  34.6 2.2 %collective-permute-done.8.refs_0_ = bf16[272,128]{1,0:T(8,128)(2,1)S(1)} collective-permute-done((bf16[272,128]{1,0:T(8,128)(2,1)S(1)}, bf16[272,128]{1,0:T(8,128)(2,1)S(1)}, u32[]{:S(2)}, u32[]{:S(2)}) %collective-permute-start.8) | collective-permute-done | bytes 69664 | tf_op jit(solution)/shard_map/ppermute | solution.py:351
  36.8 1.9 %collective-permute-done.9.refs_1_ = bf16[272,128]{1,0:T(8,128)(2,1)S(1)} collective-permute-done((bf16[272,128]{1,0:T(8,128)(2,1)S(1)}, bf16[272,128]{1,0:T(8,128)(2,1)S(1)}, u32[]{:S(2)}, u32[]{:S(2)}) %collective-permute-start.9) | collective-permute-done | bytes 69664 | tf_op jit(solution)/shard_map/ppermute | solution.py:351
  38.8 2.6 %collective-permute-start.13 = (bf16[256,128]{1,0:T(8,128)(2,1)S(1)}, bf16[256,128]{1,0:T(8,128)(2,1)S(1)}, u32[]{:S(2)}, u32[]{:S(2)}) collective-permute-start(bf16[256,128]{1,0:T(8,128)(2,1)S(1)} %get-tuple-element.88.refs_5_.refs_20_), channel_id=1, source_target_pairs={{0,6},{1,7},{2,4},{3,5},{4,2},{5,3},{6,0},{7,1},{8,14},{9,15},{10,... | collective-permute-start | bytes 196616 | tf_op jit(solution)/shard_map/ppermute | solution.py:351
  41.4 1.9 %collective-permute-start.11 = (bf16[256,128]{1,0:T(8,128)(2,1)S(1)}, bf16[256,128]{1,0:T(8,128)(2,1)S(1)}, u32[]{:S(2)}, u32[]{:S(2)}) collective-permute-start(bf16[256,128]{1,0:T(8,128)(2,1)S(1)} %get-tuple-element.88.refs_5_.refs_20_), channel_id=1, source_target_pairs={{0,4},{1,5},{2,6},{3,7},{4,0},{5,1},{6,2},{7,3},{8,12},{9,13},{10,... | collective-permute-start | bytes 196616 | tf_op jit(solution)/shard_map/ppermute | solution.py:351
  43.2 2.5 %collective-permute-done.13.refs_6_.refs_21_ = bf16[256,128]{1,0:T(8,128)(2,1)S(1)} collective-permute-done((bf16[256,128]{1,0:T(8,128)(2,1)S(1)}, bf16[256,128]{1,0:T(8,128)(2,1)S(1)}, u32[]{:S(2)}, u32[]{:S(2)}) %collective-permute-start.13) | collective-permute-done | bytes 65568 | tf_op jit(solution)/shard_map/ppermute | solution.py:351
  50.3 2.1 %collective-permute-start.16 = (bf16[528,128]{1,0:T(8,128)(2,1)S(1)}, bf16[528,128]{1,0:T(8,128)(2,1)S(1)}, u32[]{:S(2)}, u32[]{:S(2)}) collective-permute-start(bf16[528,128]{1,0:T(8,128)(2,1)S(1)} %get-tuple-element.95), channel_id=1, source_target_pairs={{0,24},{8,16},{16,8},{24,0},{1,25},{9,17},{17,9},{25,1},{2,26},{10... | collective-permute-start | bytes 405512 | tf_op jit(solution)/shard_map/ppermute | solution.py:351
  54.1 3.1 %collective-permute-done.16.refs_2_ = bf16[528,128]{1,0:T(8,128)(2,1)S(1)} collective-permute-done((bf16[528,128]{1,0:T(8,128)(2,1)S(1)}, bf16[528,128]{1,0:T(8,128)(2,1)S(1)}, u32[]{:S(2)}, u32[]{:S(2)}) %collective-permute-start.16) | collective-permute-done | bytes 135200 | tf_op jit(solution)/shard_map/ppermute | solution.py:351
  58.1 2.3 %collective-permute-start.18 = (bf16[512,128]{1,0:T(8,128)(2,1)S(1)}, bf16[512,128]{1,0:T(8,128)(2,1)S(1)}, u32[]{:S(2)}, u32[]{:S(2)}) collective-permute-start(bf16[512,128]{1,0:T(8,128)(2,1)S(1)} %get-tuple-element.98.refs_5_.refs_12_), channel_id=1, source_target_pairs={{0,16},{8,24},{16,0},{24,8},{1,17},{9,25},{17,1},{25,9},{2,18},{10... | collective-permute-start | bytes 393224 | tf_op jit(solution)/shard_map/ppermute | solution.py:351
  64.3 1.9 %collective-permute-done.17.refs_5_.refs_14_ = bf16[512,128]{1,0:T(8,128)(2,1)S(1)} collective-permute-done((bf16[512,128]{1,0:T(8,128)(2,1)S(1)}, bf16[512,128]{1,0:T(8,128)(2,1)S(1)}, u32[]{:S(2)}, u32[]{:S(2)}) %collective-permute-start.17) | collective-permute-done | bytes 131104 | tf_op jit(solution)/shard_map/ppermute | solution.py:351
  66.2 1.9 %forward.9 = (f32[1152,128]{1,0:T(8,128)S(1)}, f32[256,128]{1,0:T(8,128)S(1)}, f32[8,128]{1,0:T(8,128)S(1)}, bf16[272,128]{1,0:T(8,128)(2,1)S(1)}, bf16[272,128]...) custom-call(bf16[24,2,128,128]{3,2,1,0:T(8,128)(2,1)S(1)} %bitcast.12, ...), custom_call_target="tpu_custom_call", output_to_operand_aliasing={{0}: (7, {})} | custom-call | tf_op jit(solution)/shard_map/forward/pallas_call | solution.py:43
  69.4 3.0 %collective-permute-start.22 = (bf16[272,128]{1,0:T(8,128)(2,1)S(1)}, bf16[272,128]{1,0:T(8,128)(2,1)S(1)}, u32[]{:S(2)}, u32[]{:S(2)}) collective-permute-start(bf16[272,128]{1,0:T(8,128)(2,1)S(1)} %get-tuple-element.105), channel_id=1, source_target_pairs={{0,4},{1,5},{2,6},{3,7},{4,0},{5,1},{6,2},{7,3},{8,12},{9,13},{10,... | collective-permute-start | bytes 208904 | tf_op jit(solution)/shard_map/ppermute | solution.py:351
  72.5 2.1 %collective-permute-done.20.refs_0_ = bf16[272,128]{1,0:T(8,128)(2,1)S(1)} collective-permute-done((bf16[272,128]{1,0:T(8,128)(2,1)S(1)}, bf16[272,128]{1,0:T(8,128)(2,1)S(1)}, u32[]{:S(2)}, u32[]{:S(2)}) %collective-permute-start.20) | collective-permute-done | bytes 69664 | tf_op jit(solution)/shard_map/ppermute | solution.py:351
  75.3 2.1 %collective-permute-done.22.refs_2_ = bf16[272,128]{1,0:T(8,128)(2,1)S(1)} collective-permute-done((bf16[272,128]{1,0:T(8,128)(2,1)S(1)}, bf16[272,128]{1,0:T(8,128)(2,1)S(1)}, u32[]{:S(2)}, u32[]{:S(2)}) %collective-permute-start.22) | collective-permute-done | bytes 69664 | tf_op jit(solution)/shard_map/ppermute | solution.py:351
  79.0 2.9 %collective-permute-start.23 = (bf16[256,128]{1,0:T(8,128)(2,1)S(1)}, bf16[256,128]{1,0:T(8,128)(2,1)S(1)}, u32[]{:S(2)}, u32[]{:S(2)}) collective-permute-start(bf16[256,128]{1,0:T(8,128)(2,1)S(1)} %get-tuple-element.107.refs_5_.refs_24_), channel_id=1, source_target_pairs={{0,4},{1,5},{2,6},{3,7},{4,0},{5,1},{6,2},{7,3},{8,12},{9,13},{10,... | collective-permute-start | bytes 196616 | tf_op jit(solution)/shard_map/ppermute | solution.py:351
  81.9 1.8 %collective-permute-done.25.refs_6_.refs_25_ = bf16[256,128]{1,0:T(8,128)(2,1)S(1)} collective-permute-done((bf16[256,128]{1,0:T(8,128)(2,1)S(1)}, bf16[256,128]{1,0:T(8,128)(2,1)S(1)}, u32[]{:S(2)}, u32[]{:S(2)}) %collective-permute-start.25) | collective-permute-done | bytes 65568 | tf_op jit(solution)/shard_map/ppermute | solution.py:351
  87.9 2.6 %collective-permute-start.28 = (bf16[528,128]{1,0:T(8,128)(2,1)S(1)}, bf16[528,128]{1,0:T(8,128)(2,1)S(1)}, u32[]{:S(2)}, u32[]{:S(2)}) collective-permute-start(bf16[528,128]{1,0:T(8,128)(2,1)S(1)} %get-tuple-element.114), channel_id=1, source_target_pairs={{0,24},{8,16},{16,8},{24,0},{1,25},{9,17},{17,9},{25,1},{2,26},{10... | collective-permute-start | bytes 405512 | tf_op jit(solution)/shard_map/ppermute | solution.py:351
  90.5 2.0 %collective-permute-done.26.refs_0_ = bf16[528,128]{1,0:T(8,128)(2,1)S(1)} collective-permute-done((bf16[528,128]{1,0:T(8,128)(2,1)S(1)}, bf16[528,128]{1,0:T(8,128)(2,1)S(1)}, u32[]{:S(2)}, u32[]{:S(2)}) %collective-permute-start.26) | collective-permute-done | bytes 135200 | tf_op jit(solution)/shard_map/ppermute | solution.py:351
  92.5 2.3 %collective-permute-done.27.refs_1_ = bf16[528,128]{1,0:T(8,128)(2,1)S(1)} collective-permute-done((bf16[528,128]{1,0:T(8,128)(2,1)S(1)}, bf16[528,128]{1,0:T(8,128)(2,1)S(1)}, u32[]{:S(2)}, u32[]{:S(2)}) %collective-permute-start.27) | collective-permute-done | bytes 135200 | tf_op jit(solution)/shard_map/ppermute | solution.py:351
  103.0 1.9 %forward.11 = (f32[1152,128]{1,0:T(8,128)S(1)}, f32[256,128]{1,0:T(8,128)S(1)}, f32[8,128]{1,0:T(8,128)S(1)}, bf16[272,128]{1,0:T(8,128)(2,1)S(1)}, bf16[272,128...) custom-call(bf16[24,2,128,128]{3,2,1,0:T(8,128)(2,1)S(1)} %bitcast.14, ...), custom_call_target="tpu_custom_call", output_to_operand_aliasing={{0}: (7, {})} | custom-call | tf_op jit(solution)/shard_map/forward/pallas_call | solution.py:43
  106.8 2.5 %collective-permute-start.34 = (bf16[272,128]{1,0:T(8,128)(2,1)S(1)}, bf16[272,128]{1,0:T(8,128)(2,1)S(1)}, u32[]{:S(2)}, u32[]{:S(2)}) collective-permute-start(bf16[272,128]{1,0:T(8,128)(2,1)S(1)} %get-tuple-element.124), channel_id=1, source_target_pairs={{0,4},{1,5},{2,6},{3,7},{4,0},{5,1},{6,2},{7,3},{8,12},{9,13},{10,... | collective-permute-start | bytes 208904 | tf_op jit(solution)/shard_map/ppermute | solution.py:351
  114.7 2.6 %collective-permute-start.35 = (bf16[256,128]{1,0:T(8,128)(2,1)S(1)}, bf16[256,128]{1,0:T(8,128)(2,1)S(1)}, u32[]{:S(2)}, u32[]{:S(2)}) collective-permute-start(bf16[256,128]{1,0:T(8,128)(2,1)S(1)} %get-tuple-element.127.refs_0_.refs_28_), channel_id=1, source_target_pairs={{0,6},{1,7},{2,4},{3,5},{4,2},{5,3},{6,0},{7,1},{8,14},{9,15},{10,... | collective-permute-start | bytes 196616 | tf_op jit(solution)/shard_map/ppermute | solution.py:351
  118.5 2.3 %collective-permute-done.35.refs_1_.refs_29_ = bf16[256,128]{1,0:T(8,128)(2,1)S(1)} collective-permute-done((bf16[256,128]{1,0:T(8,128)(2,1)S(1)}, bf16[256,128]{1,0:T(8,128)(2,1)S(1)}, u32[]{:S(2)}, u32[]{:S(2)}) %collective-permute-start.35) | collective-permute-done | bytes 65568 | tf_op jit(solution)/shard_map/ppermute | solution.py:351
  125.0 2.3 %collective-permute-done.38.refs_1_ = f32[8,128]{1,0:T(8,128)S(1)} collective-permute-done((f32[8,128]{1,0:T(8,128)S(1)}, f32[8,128]{1,0:T(8,128)S(1)}, u32[]{:S(2)}, u32[]{:S(2)}) %collective-permute-start.38) | collective-permute-done | bytes 4128 | tf_op jit(solution)/shard_map/ppermute | solution.py:351
  129.9 1.8 %unpack.1 = (f32[2,1024,128]{2,1,0:T(8,128)}, f32[2,1024,128]{2,1,0:T(8,128)}) custom-call(f32[1024,128]{1,0:T(8,128)S(1)} %get-tuple-element.132.own_x, f32[1024,128]{1,0:T(8,128)S(1)} %get-tuple-element.133.own_r, bf16[1024,128]{1,0:T(8,128)(2,1)S(1)} %collective-permute-done.41.pair_x, bf16[1024,128]{1,0:T(8,128)(2,1)S(1)} %collective-permute-done.42.pair_r), custom_call_target="tpu_custom_call" | custom-call | tf_op jit(solution)/shard_map/unpack/pallas_call | solution.py:43
  (86 shorter events, 55.8 us)
Async XLA Ops:
  0.6 6.9 %collective-permute-start = (bf16[24,2,128,128]{3,2,1,0:T(8,128)(2,1)}, bf16[24,2,128,128]{3,2,1,0:T(8,128)(2,1)S(1)}, u32[]{:S(2)}, u32[]{:S(2)}) collective-permute-start(bf16[24,2,128,128]{3,2,1,0:T(8,128)(2,1)} %bitcast.7), channel_id=1, source_target_pairs={{0,1},{1,0},{2,3},{3,2},{4,5},{5,4},{6,7},{7,6},{8,9},{9,8},{10,11... | collective-permute-start | bytes 4718600 | tf_op jit(solution)/shard_map/ppermute | solution.py:351
  8.9 6.6 %collective-permute-start.2 = (bf16[512,128]{1,0:T(8,128)(2,1)S(1)}, bf16[512,128]{1,0:T(8,128)(2,1)S(1)}, u32[]{:S(2)}, u32[]{:S(2)}) collective-permute-start(bf16[512,128]{1,0:T(8,128)(2,1)S(1)} %get-tuple-element.77), channel_id=1, source_target_pairs={{0,8},{8,0},{16,24},{24,16},{1,9},{9,1},{17,25},{25,17},{2,10},{10... | collective-permute-start | bytes 393224 | tf_op jit(solution)/shard_map/ppermute | solution.py:351
  11.6 8.1 %collective-permute-start.3 = (bf16[512,128]{1,0:T(8,128)(2,1)S(1)}, bf16[512,128]{1,0:T(8,128)(2,1)S(1)}, u32[]{:S(2)}, u32[]{:S(2)}) collective-permute-start(bf16[512,128]{1,0:T(8,128)(2,1)S(1)} %get-tuple-element.78), channel_id=1, source_target_pairs={{0,16},{8,24},{16,0},{24,8},{1,17},{9,25},{17,1},{25,9},{2,18},{10... | collective-permute-start | bytes 393224 | tf_op jit(solution)/shard_map/ppermute | solution.py:351
  13.4 6.2 %collective-permute-start.4 = (bf16[512,128]{1,0:T(8,128)(2,1)S(1)}, bf16[512,128]{1,0:T(8,128)(2,1)S(1)}, u32[]{:S(2)}, u32[]{:S(2)}) collective-permute-start(bf16[512,128]{1,0:T(8,128)(2,1)S(1)} %get-tuple-element.79), channel_id=1, source_target_pairs={{0,24},{8,16},{16,8},{24,0},{1,25},{9,17},{17,9},{25,1},{2,26},{10... | collective-permute-start | bytes 393224 | tf_op jit(solution)/shard_map/ppermute | solution.py:351
  19.7 5.9 %collective-permute-start.7 = (bf16[512,128]{1,0:T(8,128)(2,1)S(1)}, bf16[512,128]{1,0:T(8,128)(2,1)S(1)}, u32[]{:S(2)}, u32[]{:S(2)}) collective-permute-start(bf16[512,128]{1,0:T(8,128)(2,1)S(1)} %get-tuple-element.80.refs_5_.refs_8_), channel_id=1, source_target_pairs={{0,8},{8,0},{16,24},{24,16},{1,9},{9,1},{17,25},{25,17},{2,10},{10... | collective-permute-start | bytes 393224 | tf_op jit(solution)/shard_map/ppermute | solution.py:351
  21.2 7.1 %collective-permute-start.6 = (bf16[512,128]{1,0:T(8,128)(2,1)S(1)}, bf16[512,128]{1,0:T(8,128)(2,1)S(1)}, u32[]{:S(2)}, u32[]{:S(2)}) collective-permute-start(bf16[512,128]{1,0:T(8,128)(2,1)S(1)} %get-tuple-element.80.refs_5_.refs_8_), channel_id=1, source_target_pairs={{0,16},{8,24},{16,0},{24,8},{1,17},{9,25},{17,1},{25,9},{2,18},{10... | collective-permute-start | bytes 393224 | tf_op jit(solution)/shard_map/ppermute | solution.py:351
  21.9 6.5 %collective-permute-start.5 = (bf16[512,128]{1,0:T(8,128)(2,1)S(1)}, bf16[512,128]{1,0:T(8,128)(2,1)S(1)}, u32[]{:S(2)}, u32[]{:S(2)}) collective-permute-start(bf16[512,128]{1,0:T(8,128)(2,1)S(1)} %get-tuple-element.80.refs_5_.refs_8_), channel_id=1, source_target_pairs={{0,24},{8,16},{16,8},{24,0},{1,25},{9,17},{17,9},{25,1},{2,26},{10... | collective-permute-start | bytes 393224 | tf_op jit(solution)/shard_map/ppermute | solution.py:351
  30.2 6.6 %collective-permute-start.8 = (bf16[272,128]{1,0:T(8,128)(2,1)S(1)}, bf16[272,128]{1,0:T(8,128)(2,1)S(1)}, u32[]{:S(2)}, u32[]{:S(2)}) collective-permute-start(bf16[272,128]{1,0:T(8,128)(2,1)S(1)} %get-tuple-element.85), channel_id=1, source_target_pairs={{0,6},{1,7},{2,4},{3,5},{4,2},{5,3},{6,0},{7,1},{8,14},{9,15},{10,... | collective-permute-start | bytes 208904 | tf_op jit(solution)/shard_map/ppermute | solution.py:351
  33.4 5.4 %collective-permute-start.9 = (bf16[272,128]{1,0:T(8,128)(2,1)S(1)}, bf16[272,128]{1,0:T(8,128)(2,1)S(1)}, u32[]{:S(2)}, u32[]{:S(2)}) collective-permute-start(bf16[272,128]{1,0:T(8,128)(2,1)S(1)} %get-tuple-element.86), channel_id=1, source_target_pairs={{0,2},{1,3},{2,0},{3,1},{4,6},{5,7},{6,4},{7,5},{8,10},{9,11},{10,... | collective-permute-start | bytes 208904 | tf_op jit(solution)/shard_map/ppermute | solution.py:351
  33.4 5.4 %collective-permute-start.10 = (bf16[272,128]{1,0:T(8,128)(2,1)S(1)}, bf16[272,128]{1,0:T(8,128)(2,1)S(1)}, u32[]{:S(2)}, u32[]{:S(2)}) collective-permute-start(bf16[272,128]{1,0:T(8,128)(2,1)S(1)} %get-tuple-element.87), channel_id=1, source_target_pairs={{0,4},{1,5},{2,6},{3,7},{4,0},{5,1},{6,2},{7,3},{8,12},{9,13},{10,... | collective-permute-start | bytes 208904 | tf_op jit(solution)/shard_map/ppermute | solution.py:351
  38.8 6.9 %collective-permute-start.13 = (bf16[256,128]{1,0:T(8,128)(2,1)S(1)}, bf16[256,128]{1,0:T(8,128)(2,1)S(1)}, u32[]{:S(2)}, u32[]{:S(2)}) collective-permute-start(bf16[256,128]{1,0:T(8,128)(2,1)S(1)} %get-tuple-element.88.refs_5_.refs_20_), channel_id=1, source_target_pairs={{0,6},{1,7},{2,4},{3,5},{4,2},{5,3},{6,0},{7,1},{8,14},{9,15},{10,... | collective-permute-start | bytes 196616 | tf_op jit(solution)/shard_map/ppermute | solution.py:351
  41.4 5.8 %collective-permute-start.12 = (bf16[256,128]{1,0:T(8,128)(2,1)S(1)}, bf16[256,128]{1,0:T(8,128)(2,1)S(1)}, u32[]{:S(2)}, u32[]{:S(2)}) collective-permute-start(bf16[256,128]{1,0:T(8,128)(2,1)S(1)} %get-tuple-element.88.refs_5_.refs_20_), channel_id=1, source_target_pairs={{0,2},{1,3},{2,0},{3,1},{4,6},{5,7},{6,4},{7,5},{8,10},{9,11},{10,... | collective-permute-start | bytes 196616 | tf_op jit(solution)/shard_map/ppermute | solution.py:351
  41.4 5.8 %collective-permute-start.11 = (bf16[256,128]{1,0:T(8,128)(2,1)S(1)}, bf16[256,128]{1,0:T(8,128)(2,1)S(1)}, u32[]{:S(2)}, u32[]{:S(2)}) collective-permute-start(bf16[256,128]{1,0:T(8,128)(2,1)S(1)} %get-tuple-element.88.refs_5_.refs_20_), channel_id=1, source_target_pairs={{0,4},{1,5},{2,6},{3,7},{4,0},{5,1},{6,2},{7,3},{8,12},{9,13},{10,... | collective-permute-start | bytes 196616 | tf_op jit(solution)/shard_map/ppermute | solution.py:351
  50.3 6.8 %collective-permute-start.16 = (bf16[528,128]{1,0:T(8,128)(2,1)S(1)}, bf16[528,128]{1,0:T(8,128)(2,1)S(1)}, u32[]{:S(2)}, u32[]{:S(2)}) collective-permute-start(bf16[528,128]{1,0:T(8,128)(2,1)S(1)} %get-tuple-element.95), channel_id=1, source_target_pairs={{0,24},{8,16},{16,8},{24,0},{1,25},{9,17},{17,9},{25,1},{2,26},{10... | collective-permute-start | bytes 405512 | tf_op jit(solution)/shard_map/ppermute | solution.py:351
  58.1 6.2 %collective-permute-start.18 = (bf16[512,128]{1,0:T(8,128)(2,1)S(1)}, bf16[512,128]{1,0:T(8,128)(2,1)S(1)}, u32[]{:S(2)}, u32[]{:S(2)}) collective-permute-start(bf16[512,128]{1,0:T(8,128)(2,1)S(1)} %get-tuple-element.98.refs_5_.refs_12_), channel_id=1, source_target_pairs={{0,16},{8,24},{16,0},{24,8},{1,17},{9,25},{17,1},{25,9},{2,18},{10... | collective-permute-start | bytes 393224 | tf_op jit(solution)/shard_map/ppermute | solution.py:351
  60.3 5.9 %collective-permute-start.17 = (bf16[512,128]{1,0:T(8,128)(2,1)S(1)}, bf16[512,128]{1,0:T(8,128)(2,1)S(1)}, u32[]{:S(2)}, u32[]{:S(2)}) collective-permute-start(bf16[512,128]{1,0:T(8,128)(2,1)S(1)} %get-tuple-element.98.refs_5_.refs_12_), channel_id=1, source_target_pairs={{0,24},{8,16},{16,8},{24,0},{1,25},{9,17},{17,9},{25,1},{2,26},{10... | collective-permute-start | bytes 393224 | tf_op jit(solution)/shard_map/ppermute | solution.py:351
  68.1 6.6 %collective-permute-start.20 = (bf16[272,128]{1,0:T(8,128)(2,1)S(1)}, bf16[272,128]{1,0:T(8,128)(2,1)S(1)}, u32[]{:S(2)}, u32[]{:S(2)}) collective-permute-start(bf16[272,128]{1,0:T(8,128)(2,1)S(1)} %get-tuple-element.103), channel_id=1, source_target_pairs={{0,6},{1,7},{2,4},{3,5},{4,2},{5,3},{6,0},{7,1},{8,14},{9,15},{10,... | collective-permute-start | bytes 208904 | tf_op jit(solution)/shard_map/ppermute | solution.py:351
  69.4 5.9 %collective-permute-start.21 = (bf16[272,128]{1,0:T(8,128)(2,1)S(1)}, bf16[272,128]{1,0:T(8,128)(2,1)S(1)}, u32[]{:S(2)}, u32[]{:S(2)}) collective-permute-start(bf16[272,128]{1,0:T(8,128)(2,1)S(1)} %get-tuple-element.104), channel_id=1, source_target_pairs={{0,2},{1,3},{2,0},{3,1},{4,6},{5,7},{6,4},{7,5},{8,10},{9,11},{10,... | collective-permute-start | bytes 208904 | tf_op jit(solution)/shard_map/ppermute | solution.py:351
  69.4 8.0 %collective-permute-start.22 = (bf16[272,128]{1,0:T(8,128)(2,1)S(1)}, bf16[272,128]{1,0:T(8,128)(2,1)S(1)}, u32[]{:S(2)}, u32[]{:S(2)}) collective-permute-start(bf16[272,128]{1,0:T(8,128)(2,1)S(1)} %get-tuple-element.105), channel_id=1, source_target_pairs={{0,4},{1,5},{2,6},{3,7},{4,0},{5,1},{6,2},{7,3},{8,12},{9,13},{10,... | collective-permute-start | bytes 208904 | tf_op jit(solution)/shard_map/ppermute | solution.py:351
  77.5 6.2 %collective-permute-start.25 = (bf16[256,128]{1,0:T(8,128)(2,1)S(1)}, bf16[256,128]{1,0:T(8,128)(2,1)S(1)}, u32[]{:S(2)}, u32[]{:S(2)}) collective-permute-start(bf16[256,128]{1,0:T(8,128)(2,1)S(1)} %get-tuple-element.107.refs_5_.refs_24_), channel_id=1, source_target_pairs={{0,6},{1,7},{2,4},{3,5},{4,2},{5,3},{6,0},{7,1},{8,14},{9,15},{10,... | collective-permute-start | bytes 196616 | tf_op jit(solution)/shard_map/ppermute | solution.py:351
  79.0 6.1 %collective-permute-start.24 = (bf16[256,128]{1,0:T(8,128)(2,1)S(1)}, bf16[256,128]{1,0:T(8,128)(2,1)S(1)}, u32[]{:S(2)}, u32[]{:S(2)}) collective-permute-start(bf16[256,128]{1,0:T(8,128)(2,1)S(1)} %get-tuple-element.107.refs_5_.refs_24_), channel_id=1, source_target_pairs={{0,2},{1,3},{2,0},{3,1},{4,6},{5,7},{6,4},{7,5},{8,10},{9,11},{10,... | collective-permute-start | bytes 196616 | tf_op jit(solution)/shard_map/ppermute | solution.py:351
  79.0 6.1 %collective-permute-start.23 = (bf16[256,128]{1,0:T(8,128)(2,1)S(1)}, bf16[256,128]{1,0:T(8,128)(2,1)S(1)}, u32[]{:S(2)}, u32[]{:S(2)}) collective-permute-start(bf16[256,128]{1,0:T(8,128)(2,1)S(1)} %get-tuple-element.107.refs_5_.refs_24_), channel_id=1, source_target_pairs={{0,4},{1,5},{2,6},{3,7},{4,0},{5,1},{6,2},{7,3},{8,12},{9,13},{10,... | collective-permute-start | bytes 196616 | tf_op jit(solution)/shard_map/ppermute | solution.py:351
  86.9 5.5 %collective-permute-start.26 = (bf16[528,128]{1,0:T(8,128)(2,1)S(1)}, bf16[528,128]{1,0:T(8,128)(2,1)S(1)}, u32[]{:S(2)}, u32[]{:S(2)}) collective-permute-start(bf16[528,128]{1,0:T(8,128)(2,1)S(1)} %get-tuple-element.112), channel_id=1, source_target_pairs={{0,8},{8,0},{16,24},{24,16},{1,9},{9,1},{17,25},{25,17},{2,10},{10... | collective-permute-start | bytes 405512 | tf_op jit(solution)/shard_map/ppermute | solution.py:351
  87.0 7.7 %collective-permute-start.27 = (bf16[528,128]{1,0:T(8,128)(2,1)S(1)}, bf16[528,128]{1,0:T(8,128)(2,1)S(1)}, u32[]{:S(2)}, u32[]{:S(2)}) collective-permute-start(bf16[528,128]{1,0:T(8,128)(2,1)S(1)} %get-tuple-element.113), channel_id=1, source_target_pairs={{0,16},{8,24},{16,0},{24,8},{1,17},{9,25},{17,1},{25,9},{2,18},{10... | collective-permute-start | bytes 405512 | tf_op jit(solution)/shard_map/ppermute | solution.py:351
  87.9 6.8 %collective-permute-start.28 = (bf16[528,128]{1,0:T(8,128)(2,1)S(1)}, bf16[528,128]{1,0:T(8,128)(2,1)S(1)}, u32[]{:S(2)}, u32[]{:S(2)}) collective-permute-start(bf16[528,128]{1,0:T(8,128)(2,1)S(1)} %get-tuple-element.114), channel_id=1, source_target_pairs={{0,24},{8,16},{16,8},{24,0},{1,25},{9,17},{17,9},{25,1},{2,26},{10... | collective-permute-start | bytes 405512 | tf_op jit(solution)/shard_map/ppermute | solution.py:351
  96.1 5.6 %collective-permute-start.30 = (bf16[512,128]{1,0:T(8,128)(2,1)S(1)}, bf16[512,128]{1,0:T(8,128)(2,1)S(1)}, u32[]{:S(2)}, u32[]{:S(2)}) collective-permute-start(bf16[512,128]{1,0:T(8,128)(2,1)S(1)} %get-tuple-element.117.refs_5_.refs_16_), channel_id=1, source_target_pairs={{0,16},{8,24},{16,0},{24,8},{1,17},{9,25},{17,1},{25,9},{2,18},{10... | collective-permute-start | bytes 393224 | tf_op jit(solution)/shard_map/ppermute | solution.py:351
  97.1 5.9 %collective-permute-start.29 = (bf16[512,128]{1,0:T(8,128)(2,1)S(1)}, bf16[512,128]{1,0:T(8,128)(2,1)S(1)}, u32[]{:S(2)}, u32[]{:S(2)}) collective-permute-start(bf16[512,128]{1,0:T(8,128)(2,1)S(1)} %get-tuple-element.117.refs_5_.refs_16_), channel_id=1, source_target_pairs={{0,24},{8,16},{16,8},{24,0},{1,25},{9,17},{17,9},{25,1},{2,26},{10... | collective-permute-start | bytes 393224 | tf_op jit(solution)/shard_map/ppermute | solution.py:351
  104.8 6.1 %collective-permute-start.32 = (bf16[272,128]{1,0:T(8,128)(2,1)S(1)}, bf16[272,128]{1,0:T(8,128)(2,1)S(1)}, u32[]{:S(2)}, u32[]{:S(2)}) collective-permute-start(bf16[272,128]{1,0:T(8,128)(2,1)S(1)} %get-tuple-element.122), channel_id=1, source_target_pairs={{0,6},{1,7},{2,4},{3,5},{4,2},{5,3},{6,0},{7,1},{8,14},{9,15},{10,... | collective-permute-start | bytes 208904 | tf_op jit(solution)/shard_map/ppermute | solution.py:351
  105.9 5.1 %collective-permute-start.33 = (bf16[272,128]{1,0:T(8,128)(2,1)S(1)}, bf16[272,128]{1,0:T(8,128)(2,1)S(1)}, u32[]{:S(2)}, u32[]{:S(2)}) collective-permute-start(bf16[272,128]{1,0:T(8,128)(2,1)S(1)} %get-tuple-element.123), channel_id=1, source_target_pairs={{0,2},{1,3},{2,0},{3,1},{4,6},{5,7},{6,4},{7,5},{8,10},{9,11},{10,... | collective-permute-start | bytes 208904 | tf_op jit(solution)/shard_map/ppermute | solution.py:351
  106.8 6.0 %collective-permute-start.34 = (bf16[272,128]{1,0:T(8,128)(2,1)S(1)}, bf16[272,128]{1,0:T(8,128)(2,1)S(1)}, u32[]{:S(2)}, u32[]{:S(2)}) collective-permute-start(bf16[272,128]{1,0:T(8,128)(2,1)S(1)} %get-tuple-element.124), channel_id=1, source_target_pairs={{0,4},{1,5},{2,6},{3,7},{4,0},{5,1},{6,2},{7,3},{8,12},{9,13},{10,... | collective-permute-start | bytes 208904 | tf_op jit(solution)/shard_map/ppermute | solution.py:351
  113.3 5.2 %collective-permute-start.36 = (bf16[256,128]{1,0:T(8,128)(2,1)S(1)}, bf16[256,128]{1,0:T(8,128)(2,1)S(1)}, u32[]{:S(2)}, u32[]{:S(2)}) collective-permute-start(bf16[256,128]{1,0:T(8,128)(2,1)S(1)} %get-tuple-element.127.refs_0_.refs_28_), channel_id=1, source_target_pairs={{0,4},{1,5},{2,6},{3,7},{4,0},{5,1},{6,2},{7,3},{8,12},{9,13},{10,... | collective-permute-start | bytes 196616 | tf_op jit(solution)/shard_map/ppermute | solution.py:351
  114.7 6.2 %collective-permute-start.35 = (bf16[256,128]{1,0:T(8,128)(2,1)S(1)}, bf16[256,128]{1,0:T(8,128)(2,1)S(1)}, u32[]{:S(2)}, u32[]{:S(2)}) collective-permute-start(bf16[256,128]{1,0:T(8,128)(2,1)S(1)} %get-tuple-element.127.refs_0_.refs_28_), channel_id=1, source_target_pairs={{0,6},{1,7},{2,4},{3,5},{4,2},{5,3},{6,0},{7,1},{8,14},{9,15},{10,... | collective-permute-start | bytes 196616 | tf_op jit(solution)/shard_map/ppermute | solution.py:351
  (15 other events, 89.8 us)

commit v6 on v5

--- a/solution.py
+++ b/solution.py
@@ -36,20 +36,27 @@
     weights: object
 
 
-def call(kernel, name, outs, scratch, *ins, vector=False, alias=None):
-    def space(dtype):
+def call(kernel, name, outs, scratch, *ins, vector=False, alias=None, away=0):
+    def space(place, dtype):
+        if place < away:
+            return pltpu.HBM
         return pltpu.SMEM if dtype == jnp.int32 and not vector else pltpu.VMEM
+
+    def room(shape, dtype):
+        if dtype is pltpu.SemaphoreType.DMA:
+            return dtype((shape,))
+        return (pltpu.SMEM if dtype == jnp.int32 else pltpu.VMEM)(shape, dtype)
 
     return pl.pallas_call(
         kernel,
         name=name,
         out_shape=[jax.ShapeDtypeStruct(s, d) for s, d in outs],
-        in_specs=[pl.BlockSpec(memory_space=space(a.dtype)) for a in ins],
+        in_specs=[pl.BlockSpec(memory_space=space(i, a.dtype)) for i, a in enumerate(ins)],
         out_specs=[pl.BlockSpec(memory_space=pltpu.VMEM) for _ in outs],
-        scratch_shapes=[pltpu.VMEM(s, d) for s, d in scratch],
+        scratch_shapes=[room(s, d) for s, d in scratch],
         input_output_aliases=alias or {},
         compiler_params=pltpu.CompilerParams(vmem_limit_bytes=VMEM_BYTES),
-    )(*ins)
+    )(*[pltpu.with_memory_space_constraint(a, pltpu.HBM) if i < away else a for i, a in enumerate(ins)])
 
 
 def low_half(shape):
@@ -94,16 +101,18 @@
     return pl.ds(pl.multiple_of(count * size, size), size)
 
 
-def slots(index_ref, step):
-    used = index_ref[2, 0]
-
+def group_of(index, group, step):
+    for lane in range(GROUP):
+        slot = group * GROUP + lane
+        step(slot, slot < index[2][0], index[0][slot], index[1][slot])
+
+
+def slots(index, step):
     def turn_of(group, carry):
-        for lane in range(GROUP):
-            slot = group * GROUP + lane
-            step(slot, slot < used, index_ref[0, slot], index_ref[1, slot])
+        group_of(index, group, step)
         return carry
 
-    lax.fori_loop(0, (used + GROUP - 1) // GROUP, turn_of, 0)
+    lax.fori_loop(0, (index[2][0] + GROUP - 1) // GROUP, turn_of, 0)
 
 
 def add_tile(acc_ref, weights, plain_ref, turned_ref, source, target):
@@ -126,14 +135,46 @@
     return jnp.where(low_half(real.shape), first, second)
 
 
-def pack_kernel(core_axis, tiles, record_ref, tile_ref, index_ref, turned_tile_ref, total_ref, plain_ref, turned_ref):
+def pack_kernel(core_axis, tiles, record_hbm, tile_hbm, row_hbm, col_hbm, used_ref, *refs):
+    turned_tile_ref, total_ref, plain_ref, turned_ref, record_ref, tile_ref, row_ref, col_ref, record_sem, tile_sem, index_sem = refs
     core = lax.rem(lax.axis_index(core_axis), 2)
-    for at in range(0, plain_ref.shape[0], 128):
-        span = pl.ds(at, 128)
+    rows, slot_count = plain_ref.shape[0], tile_ref.shape[0]
+    pieces = record_sem.shape[0]
+    piece, groups = rows // pieces, slot_count // GROUP
+
+    def record_copy(k):
+        span = pl.ds(k * piece, piece)
+        return pltpu.make_async_copy(record_hbm.at[:, span, :], record_ref.at[:, span, :], record_sem.at[k])
+
+    def tile_copy(k):
+        span = pl.ds(k * GROUP, GROUP)
+        return pltpu.make_async_copy(tile_hbm.at[span], tile_ref.at[span], tile_sem.at[k])
+
+    index_copies = [
+        pltpu.make_async_copy(source, target, index_sem.at[k])
+        for k, (source, target) in enumerate(((row_hbm, row_ref), (col_hbm, col_ref)))
+    ]
+    for k in range(pieces):
+        record_copy(k).start()
+    for copy in index_copies:
+        copy.start()
+    for k in range(groups):
+        tile_copy(k).start()
+    total_ref[...] = jnp.zeros_like(total_ref)
+    for k in range(pieces):
+        record_copy(k).wait()
+        span = pl.ds(k * piece, piece)
         packed = packed_record(core, record_ref[0, span, :], record_ref[1, span, :])
         put_chunk(packed.astype(BF16), plain_ref, turned_ref, span, -1.0)
-    total_ref[...] = jnp.zeros_like(total_ref)
-    slots(index_ref, turn_step(tiles, tile_ref, turned_tile_ref, total_ref, plain_ref, turned_ref))
+    for copy in index_copies:
+        copy.wait()
+    step = turn_step(tiles, tile_ref, turned_tile_ref, total_ref, plain_ref, turned_ref)
+    for k in range(groups):
+        tile_copy(k).wait()
+
+        @pl.when(k * GROUP < used_ref[0, 0])
+        def _():
+            group_of((row_ref.at[0], col_ref.at[0], used_ref.at[0]), k, step)
 
 
 def turn_step(tiles, tile_ref, turned_tile_ref, total_ref, plain_ref, turned_ref):
@@ -145,10 +186,10 @@
     return step
 
 
-def first_adjoint_kernel(hyd_axis, order, tiles, tile_ref, index_ref, own_total_ref, plain_ref, turned_ref, *refs):
+def first_adjoint_kernel(hyd_axis, order, tiles, tile_ref, row_ref, col_ref, used_ref, own_total_ref, plain_ref, turned_ref, *refs):
     turned_tile_ref, own_ref, sends, total_ref = refs[0], refs[1], refs[2:-1], refs[-1]
     total_ref[...] = jnp.zeros_like(total_ref)
-    slots(index_ref, turn_step(tiles, tile_ref, turned_tile_ref, total_ref, plain_ref, turned_ref))
+    slots((row_ref.at[0], col_ref.at[0], used_ref.at[0]), turn_step(tiles, tile_ref, turned_tile_ref, total_ref, plain_ref, turned_ref))
     give_columns(hyd_axis, order, own_total_ref, total_ref, own_ref, sends, None)
 
 
@@ -165,8 +206,9 @@
             send[2 * part :, :] = tail
 
 
-def list_kernel(plans, index_a, index_b, *lists):
-    slot_count = index_a.shape[1]
+def list_kernel(plans, *refs):
+    indices, lists = (refs[:3], refs[3:6]), refs[6:]
+    slot_count = refs[0].shape[1]
     square = (slot_count, slot_count)
     down, along = (lax.broadcasted_iota(jnp.int32, square, k) for k in (0, 1))
     down_f, along_f, here = down.astype(F32), along.astype(F32), down == along
@@ -174,13 +216,13 @@
         wide = lax.broadcasted_iota(jnp.int32, (slot_count, list_ref.shape[1]), 1).astype(F32)
         slot_f = lax.broadcasted_iota(jnp.int32, wide.shape, 0).astype(F32)
         place = way.source_place()
-        for k, index_ref in enumerate((index_a, index_b)):
-            offset = (index_ref[way.source : way.source + 1, :] * way.size // way.part) ^ place
+        for k, index in enumerate(indices):
+            offset = (index[way.source][...] * way.size // way.part) ^ place
             bucket = jnp.zeros(offset.shape, F32)
             for at, group in enumerate(groups):
                 for member in group:
                     bucket = jnp.where(offset == member, float(at), bucket)
-            bucket = jnp.where(along[:1, :] < index_ref[2:3, :], bucket, float(len(groups)))
+            bucket = jnp.where(along[:1, :] < jnp.broadcast_to(index[2][...], (1, slot_count)), bucket, float(len(groups)))
             key = jnp.broadcast_to(bucket, square)
             order_along = key * slot_count + along_f
             key_down = jnp.sum(jnp.where(here, key, 0.0), axis=1, keepdims=True)
@@ -188,12 +230,18 @@
             rank = jnp.sum(jnp.where(order_along < order_down, 1.0, 0.0), axis=1, keepdims=True)
             order = jnp.sum(jnp.where(rank == wide, slot_f, 0.0), axis=0, keepdims=True)
             begin = jnp.sum(jnp.where(key_down < wide, 1.0, 0.0), axis=0, keepdims=True)
-            list_ref[k : k + 1, :] = order.astype(jnp.int32)
-            list_ref[k + 2 : k + 3, :] = begin.astype(jnp.int32)
+            ordered = rank == wide
+            rows = [order, begin]
+            for which in (way.source, 1 - way.source):
+                value = jnp.broadcast_to(index[which][...].astype(F32), square)
+                value_down = jnp.sum(jnp.where(here, value, 0.0), axis=1, keepdims=True)
+                rows.append(jnp.sum(jnp.where(ordered, value_down, 0.0), axis=0, keepdims=True))
+            for at, row in enumerate(rows):
+                list_ref[2 * at + k : 2 * at + k + 1, :] = row.astype(jnp.int32)
 
 
 def step_kernel(way, pick, at_group, last, *refs):
-    (tile_a, tile_b, index_a, index_b, list_ref), refs = refs[:5], refs[5:]
+    (tile_a, tile_b, list_ref), refs = refs[:3], refs[3:]
     chunks, refs = refs[: len(pick)], refs[len(pick) :]
     if at_group:
         folded, refs = refs[1][...], refs[2:]
@@ -207,15 +255,15 @@
         for half in range(way.halves):
             at = pl.ds(pl.multiple_of((here ^ offset) * way.part + half * way.length, way.part), way.part)
             folded += put_chunk(chunk[half * way.part : (half + 1) * way.part, :], plain_ref, turned_ref, at, way.sign)
-    for k, (tile_ref, index_ref) in enumerate(((tile_a, index_a), (tile_b, index_b))):
+    for k, tile_ref in enumerate((tile_a, tile_b)):
         low, high = list_ref[k + 2, at_group], list_ref[k + 2, at_group + 1]
 
         def turn_of(group, carry):
             for lane in range(GROUP):
                 at = low + group * GROUP + lane
                 slot = list_ref[k, at]
-                source = index_ref[way.source, slot]
-                target = jnp.where(at < high, index_ref[1 - way.source, slot] + k * way.target_shift, way.spare)
+                source = list_ref[k + 4, at]
+                target = jnp.where(at < high, list_ref[k + 6, at] + k * way.target_shift, way.spare)
                 span = pl.ds(pl.multiple_of(source * way.size + k * (way.halves - 1) * way.length, way.size), way.size)
                 right = jnp.concatenate([plain_ref[span, :], turned_ref[span, :]], axis=0)
                 goal = spans(way.size, target)
@@ -377,19 +425,21 @@
         vector = lambda n, dtype: ((n, shots), dtype)
 
         pair_tiles = swap(own_tiles, "src", srcs, 1)
-        index = jnp.stack([tile_rows[0, 0], tile_cols[0, 0], jnp.broadcast_to(tile_counts[0, 0], (slot_count,))])
-        pair_index = swap(index, "src", srcs, 1)
+        index = (tile_rows[0], tile_cols[0], tile_counts)
+        pair_index = tuple(swap(v, "src", srcs, 1) for v in index)
+        pieces, groups = 4, slot_count // GROUP
         turned_shape = ((slot_count, size, 2 * size), BF16)
         turned_own, total, plain, turned = call(
             functools.partial(pack_kernel, "src", col_tiles), "pack",
             [turned_shape, col_total, vector(rows, BF16), vector(rows, BF16)],
-            [],
-            record, own_tiles, index,
+            [(record.shape, F32), (own_tiles.shape, BF16), (index[0].shape, jnp.int32), (index[1].shape, jnp.int32)]
+            + [(n, pltpu.SemaphoreType.DMA) for n in (pieces, groups, 2)],
+            record, own_tiles, *index, away=4,
         )
         turned_pair, own, *sends = call(
             functools.partial(first_adjoint_kernel, "hyd", hyd_order, col_tiles), "first_adjoint",
             [turned_shape, vector(2 * col_part, F32)] + [vector(2 * col_part, BF16)] * (hyds - 1), [col_total],
-            pair_tiles, pair_index, total, plain, turned,
+            pair_tiles, *pair_index, total, plain, turned,
         )
         gradient, narrow = call(
             functools.partial(start_kernel, hyds - 1), "start",
@@ -409,7 +459,7 @@
         g_groups, image_groups = (groups_of(order, w) for order, w in ((g_order, forward), (image_order, adjoint)))
         lists = call(
             functools.partial(list_kernel, ((forward, g_groups), (adjoint, image_groups))),
-            "lists", [((8, 128), jnp.int32)] * 2, [], index, pair_index, vector=True,
+            "lists", [((8, 128), jnp.int32)] * 2, [], *index, *pair_index, vector=True,
         )
 
         def apply(way, name, tiles, slot_list, chunks, groups, outs):
@@ -420,8 +470,8 @@
                 carry = call(
                     functools.partial(step_kernel, way, group, k, last), name,
                     [total] + (outs if last else [norm]), [vector(way.halves * way.length, BF16)] * 2,
-                    *tiles, index, pair_index, slot_list, *chunks[at : at + len(group)], *carry,
-                    alias={5 + len(group): 0} if k else None,
+                    *tiles, slot_list, *chunks[at : at + len(group)], *carry,
+                    alias={3 + len(group): 0} if k else None,
                 )
                 at += len(group)
             return carry[1:]

time: 132 us -> 132 us (level)
  local copies, waits for them, and re-layouts: 2.72 us -> 0.02 us
  starting transfers between devices: 53.5 us -> 55.3 us
    unnamed x8, local copies, waits for them, and re-layouts: 2.64 us -> 0.02 us
    ppermute x43 -> x45, starting transfers between devices: 53.5 us -> 55.3 us  [swap(): return lax.ppermute(value, axis, [(i, i ^ offset) for i in range(size)])]
    ppermute x43 -> x45, waiting for transfers between devices: 49.3 us -> 50.3 us  [swap(): return lax.ppermute(value, axis, [(i, i ^ offset) for i in range(size)])]
  transfers between devices with their start and end apart: 43 -> 45, of which waited for: 30 -> 35; matrix products, arithmetic and copies ran while one was open for 1% -> 0% of each run, Pallas kernels for 8% -> 8%
where the time goes in v6:
time: 132 us; the launch traced here: 131 us
  starting transfers between devices  55.3 us (42%)
  waiting for transfers between devices  50.3 us (38%)
  Pallas kernels  23.9 us (18%)
  between operations  1.51 us (1%)
    ppermute x45, starting transfers between devices, swap(): return lax.ppermute(value, axis, [(i, i ^ offset) for i in range(size)])  55.3 us
    ppermute x45, waiting for transfers between devices, swap(): return lax.ppermute(value, axis, [(i, i ^ offset) for i in range(size)])  50.3 us
    pallas_call x22, Pallas kernels, call(): pl.pallas_call(kernel, name=name, out_shape=[jax.ShapeDtypeStruct(s, d) f...  23.9 us
  transfers between devices with their start and end apart: 45, of which 35 were waited for; matrix products, arithmetic and copies ran while one was open for 0% of the time, Pallas kernels for 8%

profile of v6, /device:TPU:0, one launch (start us, length us, event | category | flops | bytes accessed | tf_op | source)
XLA Modules:
  0.0 131.1 jit_solution(6318737993831363259)
XLA Ops:
  2.4 2.8 %pack.1 = (bf16[24,128,256]{2,1,0:T(8,128)(2,1)S(1)}, f32[1152,128]{1,0:T(8,128)S(1)}, bf16[1024,128]{1,0:T(8,128)(2,1)S(1)}, bf16[1024,128]{1,0:T(8,128)(2,1)S(1)}) custom-call(f32[2,1024,128]{2,1,0:T(8,128)} %record_ref.1, bf16[24,2,128,128]{3,2,1,0:T(8,128)(2,1)} %bitcast.4, s32[1,24]{1,0:T(1,128)} %bitcast.12, s32[1,24]{1,0:T(1,128)} %bitcast.15, ...), custom_call_target="tpu_custom_call" | custom-call | tf_op jit(solution)/shard_map/pack/pallas_call | solution.py:50
  5.3 2.1 %first_adjoint.1 = (bf16[24,128,256]{2,1,0:T(8,128)(2,1)S(1)}, f32[512,128]{1,0:T(8,128)S(1)}, bf16[512,128]{1,0:T(8,128)(2,1)S(1)}, bf16[512,128]{1,0:T(8,128)(2,1)S(1)}, bf16[512,128]{1,0:T(8,128)(2,1)S(1)}) custom-call(bf16[24,2,128,128]{3,2,1,0:T(8,128)(2,1)S(1)} %collective-permute-done.tile_ref.refs_1_, ...), custom_call_target="tpu_custom_call" | custom-call | tf_op jit(solution)/shard_map/first_adjoint/pallas_call | solution.py:50
  7.5 2.6 %collective-permute-start.4 = (bf16[512,128]{1,0:T(8,128)(2,1)S(1)}, bf16[512,128]{1,0:T(8,128)(2,1)S(1)}, u32[]{:S(2)}, u32[]{:S(2)}) collective-permute-start(bf16[512,128]{1,0:T(8,128)(2,1)S(1)} %get-tuple-element.77), channel_id=1, source_target_pairs={{0,8},{8,0},{16,24},{24,16},{1,9},{9,1},{17,25},{25,17},{2,10},{10... | collective-permute-start | bytes 393224 | tf_op jit(solution)/shard_map/ppermute | solution.py:399
  12.3 1.7 %collective-permute-done.4.refs_0_ = bf16[512,128]{1,0:T(8,128)(2,1)S(1)} collective-permute-done((bf16[512,128]{1,0:T(8,128)(2,1)S(1)}, bf16[512,128]{1,0:T(8,128)(2,1)S(1)}, u32[]{:S(2)}, u32[]{:S(2)}) %collective-permute-start.4) | collective-permute-done | bytes 131104 | tf_op jit(solution)/shard_map/ppermute | solution.py:399
  14.0 3.1 %collective-permute-done.5.refs_1_ = bf16[512,128]{1,0:T(8,128)(2,1)S(1)} collective-permute-done((bf16[512,128]{1,0:T(8,128)(2,1)S(1)}, bf16[512,128]{1,0:T(8,128)(2,1)S(1)}, u32[]{:S(2)}, u32[]{:S(2)}) %collective-permute-start.5) | collective-permute-done | bytes 131104 | tf_op jit(solution)/shard_map/ppermute | solution.py:399
  23.1 1.8 %collective-permute-done.9.refs_4_.refs_9_ = bf16[512,128]{1,0:T(8,128)(2,1)S(1)} collective-permute-done((bf16[512,128]{1,0:T(8,128)(2,1)S(1)}, bf16[512,128]{1,0:T(8,128)(2,1)S(1)}, u32[]{:S(2)}, u32[]{:S(2)}) %collective-permute-start.9) | collective-permute-done | bytes 131104 | tf_op jit(solution)/shard_map/ppermute | solution.py:399
  28.3 4.0 %collective-permute-start.10 = (bf16[272,128]{1,0:T(8,128)(2,1)S(1)}, bf16[272,128]{1,0:T(8,128)(2,1)S(1)}, u32[]{:S(2)}, u32[]{:S(2)}) collective-permute-start(bf16[272,128]{1,0:T(8,128)(2,1)S(1)} %get-tuple-element.85), channel_id=1, source_target_pairs={{0,6},{1,7},{2,4},{3,5},{4,2},{5,3},{6,0},{7,1},{8,14},{9,15},{10,... | collective-permute-start | bytes 208904 | tf_op jit(solution)/shard_map/ppermute | solution.py:399
  33.0 1.7 %collective-permute-done.10.refs_0_ = bf16[272,128]{1,0:T(8,128)(2,1)S(1)} collective-permute-done((bf16[272,128]{1,0:T(8,128)(2,1)S(1)}, bf16[272,128]{1,0:T(8,128)(2,1)S(1)}, u32[]{:S(2)}, u32[]{:S(2)}) %collective-permute-start.10) | collective-permute-done | bytes 69664 | tf_op jit(solution)/shard_map/ppermute | solution.py:399
  34.7 1.9 %collective-permute-done.11.refs_1_ = bf16[272,128]{1,0:T(8,128)(2,1)S(1)} collective-permute-done((bf16[272,128]{1,0:T(8,128)(2,1)S(1)}, bf16[272,128]{1,0:T(8,128)(2,1)S(1)}, u32[]{:S(2)}, u32[]{:S(2)}) %collective-permute-start.11) | collective-permute-done | bytes 69664 | tf_op jit(solution)/shard_map/ppermute | solution.py:399
  37.6 2.7 %collective-permute-start.15 = (bf16[256,128]{1,0:T(8,128)(2,1)S(1)}, bf16[256,128]{1,0:T(8,128)(2,1)S(1)}, u32[]{:S(2)}, u32[]{:S(2)}) collective-permute-start(bf16[256,128]{1,0:T(8,128)(2,1)S(1)} %get-tuple-element.88.refs_3_.refs_20_), channel_id=1, source_target_pairs={{0,6},{1,7},{2,4},{3,5},{4,2},{5,3},{6,0},{7,1},{8,14},{9,15},{10,... | collective-permute-start | bytes 196616 | tf_op jit(solution)/shard_map/ppermute | solution.py:399
  40.3 1.7 %collective-permute-start.13 = (bf16[256,128]{1,0:T(8,128)(2,1)S(1)}, bf16[256,128]{1,0:T(8,128)(2,1)S(1)}, u32[]{:S(2)}, u32[]{:S(2)}) collective-permute-start(bf16[256,128]{1,0:T(8,128)(2,1)S(1)} %get-tuple-element.88.refs_3_.refs_20_), channel_id=1, source_target_pairs={{0,4},{1,5},{2,6},{3,7},{4,0},{5,1},{6,2},{7,3},{8,12},{9,13},{10,... | collective-permute-start | bytes 196616 | tf_op jit(solution)/shard_map/ppermute | solution.py:399
  42.1 1.8 %collective-permute-done.15.refs_4_.refs_21_ = bf16[256,128]{1,0:T(8,128)(2,1)S(1)} collective-permute-done((bf16[256,128]{1,0:T(8,128)(2,1)S(1)}, bf16[256,128]{1,0:T(8,128)(2,1)S(1)}, u32[]{:S(2)}, u32[]{:S(2)}) %collective-permute-start.15) | collective-permute-done | bytes 65568 | tf_op jit(solution)/shard_map/ppermute | solution.py:399
  45.5 1.7 %adjoint.5 = (f32[2176,128]{1,0:T(8,128)S(1)}, f32[512,128]{1,0:T(8,128)S(1)}, f32[8,128]{1,0:T(8,128)S(1)}, bf16[528,128]{1,0:T(8,128)(2,1)S(1)}, bf16[528,128]...) custom-call(bf16[24,128,256]{2,1,0:T(8,128)(2,1)S(1)} %get-tuple-element.70.refs_0_, ...), custom_call_target="tpu_custom_call", output_to_operand_aliasing={{0}: (5, {})} | custom-call | tf_op jit(solution)/shard_map/adjoint/pallas_call | solution.py:50
  49.0 1.8 %collective-permute-start.18 = (bf16[528,128]{1,0:T(8,128)(2,1)S(1)}, bf16[528,128]{1,0:T(8,128)(2,1)S(1)}, u32[]{:S(2)}, u32[]{:S(2)}) collective-permute-start(bf16[528,128]{1,0:T(8,128)(2,1)S(1)} %get-tuple-element.95), channel_id=1, source_target_pairs={{0,24},{8,16},{16,8},{24,0},{1,25},{9,17},{17,9},{25,1},{2,26},{10... | collective-permute-start | bytes 405512 | tf_op jit(solution)/shard_map/ppermute | solution.py:399
  53.3 3.0 %collective-permute-done.18.refs_2_ = bf16[528,128]{1,0:T(8,128)(2,1)S(1)} collective-permute-done((bf16[528,128]{1,0:T(8,128)(2,1)S(1)}, bf16[528,128]{1,0:T(8,128)(2,1)S(1)}, u32[]{:S(2)}, u32[]{:S(2)}) %collective-permute-start.18) | collective-permute-done | bytes 135200 | tf_op jit(solution)/shard_map/ppermute | solution.py:399
  56.3 2.1 %collective-permute-start.21 = (bf16[512,128]{1,0:T(8,128)(2,1)S(1)}, bf16[512,128]{1,0:T(8,128)(2,1)S(1)}, u32[]{:S(2)}, u32[]{:S(2)}) collective-permute-start(bf16[512,128]{1,0:T(8,128)(2,1)S(1)} %get-tuple-element.98.refs_3_.refs_12_), channel_id=1, source_target_pairs={{0,8},{8,0},{16,24},{24,16},{1,9},{9,1},{17,25},{25,17},{2,10},{10... | collective-permute-start | bytes 393224 | tf_op jit(solution)/shard_map/ppermute | solution.py:399
  66.3 4.4 %collective-permute-start.22 = (bf16[272,128]{1,0:T(8,128)(2,1)S(1)}, bf16[272,128]{1,0:T(8,128)(2,1)S(1)}, u32[]{:S(2)}, u32[]{:S(2)}) collective-permute-start(bf16[272,128]{1,0:T(8,128)(2,1)S(1)} %get-tuple-element.103), channel_id=1, source_target_pairs={{0,6},{1,7},{2,4},{3,5},{4,2},{5,3},{6,0},{7,1},{8,14},{9,15},{10,... | collective-permute-start | bytes 208904 | tf_op jit(solution)/shard_map/ppermute | solution.py:399
  71.3 1.8 %collective-permute-done.22.refs_0_ = bf16[272,128]{1,0:T(8,128)(2,1)S(1)} collective-permute-done((bf16[272,128]{1,0:T(8,128)(2,1)S(1)}, bf16[272,128]{1,0:T(8,128)(2,1)S(1)}, u32[]{:S(2)}, u32[]{:S(2)}) %collective-permute-start.22) | collective-permute-done | bytes 69664 | tf_op jit(solution)/shard_map/ppermute | solution.py:399
  73.2 1.9 %collective-permute-done.23.refs_1_ = bf16[272,128]{1,0:T(8,128)(2,1)S(1)} collective-permute-done((bf16[272,128]{1,0:T(8,128)(2,1)S(1)}, bf16[272,128]{1,0:T(8,128)(2,1)S(1)}, u32[]{:S(2)}, u32[]{:S(2)}) %collective-permute-start.23) | collective-permute-done | bytes 69664 | tf_op jit(solution)/shard_map/ppermute | solution.py:399
  75.9 1.7 %collective-permute-start.27 = (bf16[256,128]{1,0:T(8,128)(2,1)S(1)}, bf16[256,128]{1,0:T(8,128)(2,1)S(1)}, u32[]{:S(2)}, u32[]{:S(2)}) collective-permute-start(bf16[256,128]{1,0:T(8,128)(2,1)S(1)} %get-tuple-element.107.refs_3_.refs_24_), channel_id=1, source_target_pairs={{0,6},{1,7},{2,4},{3,5},{4,2},{5,3},{6,0},{7,1},{8,14},{9,15},{10,... | collective-permute-start | bytes 196616 | tf_op jit(solution)/shard_map/ppermute | solution.py:399
  78.1 2.3 %collective-permute-start.25 = (bf16[256,128]{1,0:T(8,128)(2,1)S(1)}, bf16[256,128]{1,0:T(8,128)(2,1)S(1)}, u32[]{:S(2)}, u32[]{:S(2)}) collective-permute-start(bf16[256,128]{1,0:T(8,128)(2,1)S(1)} %get-tuple-element.107.refs_3_.refs_24_), channel_id=1, source_target_pairs={{0,4},{1,5},{2,6},{3,7},{4,0},{5,1},{6,2},{7,3},{8,12},{9,13},{10,... | collective-permute-start | bytes 196616 | tf_op jit(solution)/shard_map/ppermute | solution.py:399
  80.4 1.8 %collective-permute-done.27.refs_4_.refs_25_ = bf16[256,128]{1,0:T(8,128)(2,1)S(1)} collective-permute-done((bf16[256,128]{1,0:T(8,128)(2,1)S(1)}, bf16[256,128]{1,0:T(8,128)(2,1)S(1)}, u32[]{:S(2)}, u32[]{:S(2)}) %collective-permute-start.27) | collective-permute-done | bytes 65568 | tf_op jit(solution)/shard_map/ppermute | solution.py:399
  83.6 1.7 %adjoint.7 = (f32[2176,128]{1,0:T(8,128)S(1)}, f32[512,128]{1,0:T(8,128)S(1)}, f32[8,128]{1,0:T(8,128)S(1)}, bf16[528,128]{1,0:T(8,128)(2,1)S(1)}, bf16[528,128]...) custom-call(bf16[24,128,256]{2,1,0:T(8,128)(2,1)S(1)} %get-tuple-element.70.refs_0_, ...), custom_call_target="tpu_custom_call", output_to_operand_aliasing={{0}: (5, {})} | custom-call | tf_op jit(solution)/shard_map/adjoint/pallas_call | solution.py:50
  86.9 1.9 %collective-permute-start.30 = (bf16[528,128]{1,0:T(8,128)(2,1)S(1)}, bf16[528,128]{1,0:T(8,128)(2,1)S(1)}, u32[]{:S(2)}, u32[]{:S(2)}) collective-permute-start(bf16[528,128]{1,0:T(8,128)(2,1)S(1)} %get-tuple-element.114), channel_id=1, source_target_pairs={{0,24},{8,16},{16,8},{24,0},{1,25},{9,17},{17,9},{25,1},{2,26},{10... | collective-permute-start | bytes 405512 | tf_op jit(solution)/shard_map/ppermute | solution.py:399
  99.6 1.8 %collective-permute-done.31.refs_3_.refs_18_ = bf16[512,128]{1,0:T(8,128)(2,1)S(1)} collective-permute-done((bf16[512,128]{1,0:T(8,128)(2,1)S(1)}, bf16[512,128]{1,0:T(8,128)(2,1)S(1)}, u32[]{:S(2)}, u32[]{:S(2)}) %collective-permute-start.31) | collective-permute-done | bytes 131104 | tf_op jit(solution)/shard_map/ppermute | solution.py:399
  102.8 3.0 %collective-permute-start.34 = (bf16[272,128]{1,0:T(8,128)(2,1)S(1)}, bf16[272,128]{1,0:T(8,128)(2,1)S(1)}, u32[]{:S(2)}, u32[]{:S(2)}) collective-permute-start(bf16[272,128]{1,0:T(8,128)(2,1)S(1)} %get-tuple-element.122), channel_id=1, source_target_pairs={{0,6},{1,7},{2,4},{3,5},{4,2},{5,3},{6,0},{7,1},{8,14},{9,15},{10,... | collective-permute-start | bytes 208904 | tf_op jit(solution)/shard_map/ppermute | solution.py:399
  107.3 1.7 %collective-permute-done.34.refs_0_ = bf16[272,128]{1,0:T(8,128)(2,1)S(1)} collective-permute-done((bf16[272,128]{1,0:T(8,128)(2,1)S(1)}, bf16[272,128]{1,0:T(8,128)(2,1)S(1)}, u32[]{:S(2)}, u32[]{:S(2)}) %collective-permute-start.34) | collective-permute-done | bytes 69664 | tf_op jit(solution)/shard_map/ppermute | solution.py:399
  111.1 2.1 %collective-permute-start.39 = (bf16[256,128]{1,0:T(8,128)(2,1)S(1)}, bf16[256,128]{1,0:T(8,128)(2,1)S(1)}, u32[]{:S(2)}, u32[]{:S(2)}) collective-permute-start(bf16[256,128]{1,0:T(8,128)(2,1)S(1)} %get-tuple-element.127.refs_0_.refs_28_), channel_id=1, source_target_pairs={{0,2},{1,3},{2,0},{3,1},{4,6},{5,7},{6,4},{7,5},{8,10},{9,11},{10,... | collective-permute-start | bytes 196616 | tf_op jit(solution)/shard_map/ppermute | solution.py:399
  113.3 2.3 %collective-permute-start.37 = (bf16[256,128]{1,0:T(8,128)(2,1)S(1)}, bf16[256,128]{1,0:T(8,128)(2,1)S(1)}, u32[]{:S(2)}, u32[]{:S(2)}) collective-permute-start(bf16[256,128]{1,0:T(8,128)(2,1)S(1)} %get-tuple-element.127.refs_0_.refs_28_), channel_id=1, source_target_pairs={{0,6},{1,7},{2,4},{3,5},{4,2},{5,3},{6,0},{7,1},{8,14},{9,15},{10,... | collective-permute-start | bytes 196616 | tf_op jit(solution)/shard_map/ppermute | solution.py:399
  115.6 2.9 %collective-permute-done.38.refs_2_.refs_30_ = bf16[256,128]{1,0:T(8,128)(2,1)S(1)} collective-permute-done((bf16[256,128]{1,0:T(8,128)(2,1)S(1)}, bf16[256,128]{1,0:T(8,128)(2,1)S(1)}, u32[]{:S(2)}, u32[]{:S(2)}) %collective-permute-start.38) | collective-permute-done | bytes 65568 | tf_op jit(solution)/shard_map/ppermute | solution.py:399
  124.2 2.5 %collective-permute-done.40.refs_1_ = f32[8,128]{1,0:T(8,128)S(1)} collective-permute-done((f32[8,128]{1,0:T(8,128)S(1)}, f32[8,128]{1,0:T(8,128)S(1)}, u32[]{:S(2)}, u32[]{:S(2)}) %collective-permute-start.40) | collective-permute-done | bytes 4128 | tf_op jit(solution)/shard_map/ppermute | solution.py:399
  129.3 1.8 %unpack.1 = (f32[2,1024,128]{2,1,0:T(8,128)}, f32[2,1024,128]{2,1,0:T(8,128)}) custom-call(f32[1024,128]{1,0:T(8,128)S(1)} %get-tuple-element.132.own_x, f32[1024,128]{1,0:T(8,128)S(1)} %get-tuple-element.133.own_r, bf16[1024,128]{1,0:T(8,128)(2,1)S(1)} %collective-permute-done.43.pair_x, bf16[1024,128]{1,0:T(8,128)(2,1)S(1)} %collective-permute-done.44.pair_r), custom_call_target="tpu_custom_call" | custom-call | tf_op jit(solution)/shard_map/unpack/pallas_call | solution.py:50
  (88 shorter events, 57.3 us)
Async XLA Ops:
  7.5 6.5 %collective-permute-start.4 = (bf16[512,128]{1,0:T(8,128)(2,1)S(1)}, bf16[512,128]{1,0:T(8,128)(2,1)S(1)}, u32[]{:S(2)}, u32[]{:S(2)}) collective-permute-start(bf16[512,128]{1,0:T(8,128)(2,1)S(1)} %get-tuple-element.77), channel_id=1, source_target_pairs={{0,8},{8,0},{16,24},{24,16},{1,9},{9,1},{17,25},{25,17},{2,10},{10... | collective-permute-start | bytes 393224 | tf_op jit(solution)/shard_map/ppermute | solution.py:399
  10.1 7.0 %collective-permute-start.5 = (bf16[512,128]{1,0:T(8,128)(2,1)S(1)}, bf16[512,128]{1,0:T(8,128)(2,1)S(1)}, u32[]{:S(2)}, u32[]{:S(2)}) collective-permute-start(bf16[512,128]{1,0:T(8,128)(2,1)S(1)} %get-tuple-element.78), channel_id=1, source_target_pairs={{0,16},{8,24},{16,0},{24,8},{1,17},{9,25},{17,1},{25,9},{2,18},{10... | collective-permute-start | bytes 393224 | tf_op jit(solution)/shard_map/ppermute | solution.py:399
  11.6 6.9 %collective-permute-start.6 = (bf16[512,128]{1,0:T(8,128)(2,1)S(1)}, bf16[512,128]{1,0:T(8,128)(2,1)S(1)}, u32[]{:S(2)}, u32[]{:S(2)}) collective-permute-start(bf16[512,128]{1,0:T(8,128)(2,1)S(1)} %get-tuple-element.79), channel_id=1, source_target_pairs={{0,24},{8,16},{16,8},{24,0},{1,25},{9,17},{17,9},{25,1},{2,26},{10... | collective-permute-start | bytes 393224 | tf_op jit(solution)/shard_map/ppermute | solution.py:399
  18.6 6.3 %collective-permute-start.9 = (bf16[512,128]{1,0:T(8,128)(2,1)S(1)}, bf16[512,128]{1,0:T(8,128)(2,1)S(1)}, u32[]{:S(2)}, u32[]{:S(2)}) collective-permute-start(bf16[512,128]{1,0:T(8,128)(2,1)S(1)} %get-tuple-element.80.refs_3_.refs_8_), channel_id=1, source_target_pairs={{0,8},{8,0},{16,24},{24,16},{1,9},{9,1},{17,25},{25,17},{2,10},{10... | collective-permute-start | bytes 393224 | tf_op jit(solution)/shard_map/ppermute | solution.py:399
  19.5 6.9 %collective-permute-start.8 = (bf16[512,128]{1,0:T(8,128)(2,1)S(1)}, bf16[512,128]{1,0:T(8,128)(2,1)S(1)}, u32[]{:S(2)}, u32[]{:S(2)}) collective-permute-start(bf16[512,128]{1,0:T(8,128)(2,1)S(1)} %get-tuple-element.80.refs_3_.refs_8_), channel_id=1, source_target_pairs={{0,16},{8,24},{16,0},{24,8},{1,17},{9,25},{17,1},{25,9},{2,18},{10... | collective-permute-start | bytes 393224 | tf_op jit(solution)/shard_map/ppermute | solution.py:399
  21.0 5.9 %collective-permute-start.7 = (bf16[512,128]{1,0:T(8,128)(2,1)S(1)}, bf16[512,128]{1,0:T(8,128)(2,1)S(1)}, u32[]{:S(2)}, u32[]{:S(2)}) collective-permute-start(bf16[512,128]{1,0:T(8,128)(2,1)S(1)} %get-tuple-element.80.refs_3_.refs_8_), channel_id=1, source_target_pairs={{0,24},{8,16},{16,8},{24,0},{1,25},{9,17},{17,9},{25,1},{2,26},{10... | collective-permute-start | bytes 393224 | tf_op jit(solution)/shard_map/ppermute | solution.py:399
  28.3 6.4 %collective-permute-start.10 = (bf16[272,128]{1,0:T(8,128)(2,1)S(1)}, bf16[272,128]{1,0:T(8,128)(2,1)S(1)}, u32[]{:S(2)}, u32[]{:S(2)}) collective-permute-start(bf16[272,128]{1,0:T(8,128)(2,1)S(1)} %get-tuple-element.85), channel_id=1, source_target_pairs={{0,6},{1,7},{2,4},{3,5},{4,2},{5,3},{6,0},{7,1},{8,14},{9,15},{10,... | collective-permute-start | bytes 208904 | tf_op jit(solution)/shard_map/ppermute | solution.py:399
  32.3 5.2 %collective-permute-start.12 = (bf16[272,128]{1,0:T(8,128)(2,1)S(1)}, bf16[272,128]{1,0:T(8,128)(2,1)S(1)}, u32[]{:S(2)}, u32[]{:S(2)}) collective-permute-start(bf16[272,128]{1,0:T(8,128)(2,1)S(1)} %get-tuple-element.87), channel_id=1, source_target_pairs={{0,4},{1,5},{2,6},{3,7},{4,0},{5,1},{6,2},{7,3},{8,12},{9,13},{10,... | collective-permute-start | bytes 208904 | tf_op jit(solution)/shard_map/ppermute | solution.py:399
  37.6 6.2 %collective-permute-start.15 = (bf16[256,128]{1,0:T(8,128)(2,1)S(1)}, bf16[256,128]{1,0:T(8,128)(2,1)S(1)}, u32[]{:S(2)}, u32[]{:S(2)}) collective-permute-start(bf16[256,128]{1,0:T(8,128)(2,1)S(1)} %get-tuple-element.88.refs_3_.refs_20_), channel_id=1, source_target_pairs={{0,6},{1,7},{2,4},{3,5},{4,2},{5,3},{6,0},{7,1},{8,14},{9,15},{10,... | collective-permute-start | bytes 196616 | tf_op jit(solution)/shard_map/ppermute | solution.py:399
  40.3 4.9 %collective-permute-start.14 = (bf16[256,128]{1,0:T(8,128)(2,1)S(1)}, bf16[256,128]{1,0:T(8,128)(2,1)S(1)}, u32[]{:S(2)}, u32[]{:S(2)}) collective-permute-start(bf16[256,128]{1,0:T(8,128)(2,1)S(1)} %get-tuple-element.88.refs_3_.refs_20_), channel_id=1, source_target_pairs={{0,2},{1,3},{2,0},{3,1},{4,6},{5,7},{6,4},{7,5},{8,10},{9,11},{10,... | collective-permute-start | bytes 196616 | tf_op jit(solution)/shard_map/ppermute | solution.py:399
  40.3 5.2 %collective-permute-start.13 = (bf16[256,128]{1,0:T(8,128)(2,1)S(1)}, bf16[256,128]{1,0:T(8,128)(2,1)S(1)}, u32[]{:S(2)}, u32[]{:S(2)}) collective-permute-start(bf16[256,128]{1,0:T(8,128)(2,1)S(1)} %get-tuple-element.88.refs_3_.refs_20_), channel_id=1, source_target_pairs={{0,4},{1,5},{2,6},{3,7},{4,0},{5,1},{6,2},{7,3},{8,12},{9,13},{10,... | collective-permute-start | bytes 196616 | tf_op jit(solution)/shard_map/ppermute | solution.py:399
  47.2 5.1 %collective-permute-start.16 = (bf16[528,128]{1,0:T(8,128)(2,1)S(1)}, bf16[528,128]{1,0:T(8,128)(2,1)S(1)}, u32[]{:S(2)}, u32[]{:S(2)}) collective-permute-start(bf16[528,128]{1,0:T(8,128)(2,1)S(1)} %get-tuple-element.93), channel_id=1, source_target_pairs={{0,8},{8,0},{16,24},{24,16},{1,9},{9,1},{17,25},{25,17},{2,10},{10... | collective-permute-start | bytes 405512 | tf_op jit(solution)/shard_map/ppermute | solution.py:399
  48.3 5.0 %collective-permute-start.17 = (bf16[528,128]{1,0:T(8,128)(2,1)S(1)}, bf16[528,128]{1,0:T(8,128)(2,1)S(1)}, u32[]{:S(2)}, u32[]{:S(2)}) collective-permute-start(bf16[528,128]{1,0:T(8,128)(2,1)S(1)} %get-tuple-element.94), channel_id=1, source_target_pairs={{0,16},{8,24},{16,0},{24,8},{1,17},{9,25},{17,1},{25,9},{2,18},{10... | collective-permute-start | bytes 405512 | tf_op jit(solution)/shard_map/ppermute | solution.py:399
  49.0 7.3 %collective-permute-start.18 = (bf16[528,128]{1,0:T(8,128)(2,1)S(1)}, bf16[528,128]{1,0:T(8,128)(2,1)S(1)}, u32[]{:S(2)}, u32[]{:S(2)}) collective-permute-start(bf16[528,128]{1,0:T(8,128)(2,1)S(1)} %get-tuple-element.95), channel_id=1, source_target_pairs={{0,24},{8,16},{16,8},{24,0},{1,25},{9,17},{17,9},{25,1},{2,26},{10... | collective-permute-start | bytes 405512 | tf_op jit(solution)/shard_map/ppermute | solution.py:399
  56.3 5.0 %collective-permute-start.21 = (bf16[512,128]{1,0:T(8,128)(2,1)S(1)}, bf16[512,128]{1,0:T(8,128)(2,1)S(1)}, u32[]{:S(2)}, u32[]{:S(2)}) collective-permute-start(bf16[512,128]{1,0:T(8,128)(2,1)S(1)} %get-tuple-element.98.refs_3_.refs_12_), channel_id=1, source_target_pairs={{0,8},{8,0},{16,24},{24,16},{1,9},{9,1},{17,25},{25,17},{2,10},{10... | collective-permute-start | bytes 393224 | tf_op jit(solution)/shard_map/ppermute | solution.py:399
  58.4 5.0 %collective-permute-start.20 = (bf16[512,128]{1,0:T(8,128)(2,1)S(1)}, bf16[512,128]{1,0:T(8,128)(2,1)S(1)}, u32[]{:S(2)}, u32[]{:S(2)}) collective-permute-start(bf16[512,128]{1,0:T(8,128)(2,1)S(1)} %get-tuple-element.98.refs_3_.refs_12_), channel_id=1, source_target_pairs={{0,16},{8,24},{16,0},{24,8},{1,17},{9,25},{17,1},{25,9},{2,18},{10... | collective-permute-start | bytes 393224 | tf_op jit(solution)/shard_map/ppermute | solution.py:399
  58.9 5.9 %collective-permute-start.19 = (bf16[512,128]{1,0:T(8,128)(2,1)S(1)}, bf16[512,128]{1,0:T(8,128)(2,1)S(1)}, u32[]{:S(2)}, u32[]{:S(2)}) collective-permute-start(bf16[512,128]{1,0:T(8,128)(2,1)S(1)} %get-tuple-element.98.refs_3_.refs_12_), channel_id=1, source_target_pairs={{0,24},{8,16},{16,8},{24,0},{1,25},{9,17},{17,9},{25,1},{2,26},{10... | collective-permute-start | bytes 393224 | tf_op jit(solution)/shard_map/ppermute | solution.py:399
  66.3 6.9 %collective-permute-start.22 = (bf16[272,128]{1,0:T(8,128)(2,1)S(1)}, bf16[272,128]{1,0:T(8,128)(2,1)S(1)}, u32[]{:S(2)}, u32[]{:S(2)}) collective-permute-start(bf16[272,128]{1,0:T(8,128)(2,1)S(1)} %get-tuple-element.103), channel_id=1, source_target_pairs={{0,6},{1,7},{2,4},{3,5},{4,2},{5,3},{6,0},{7,1},{8,14},{9,15},{10,... | collective-permute-start | bytes 208904 | tf_op jit(solution)/shard_map/ppermute | solution.py:399
  70.7 5.2 %collective-permute-start.24 = (bf16[272,128]{1,0:T(8,128)(2,1)S(1)}, bf16[272,128]{1,0:T(8,128)(2,1)S(1)}, u32[]{:S(2)}, u32[]{:S(2)}) collective-permute-start(bf16[272,128]{1,0:T(8,128)(2,1)S(1)} %get-tuple-element.105), channel_id=1, source_target_pairs={{0,4},{1,5},{2,6},{3,7},{4,0},{5,1},{6,2},{7,3},{8,12},{9,13},{10,... | collective-permute-start | bytes 208904 | tf_op jit(solution)/shard_map/ppermute | solution.py:399
  75.9 6.2 %collective-permute-start.27 = (bf16[256,128]{1,0:T(8,128)(2,1)S(1)}, bf16[256,128]{1,0:T(8,128)(2,1)S(1)}, u32[]{:S(2)}, u32[]{:S(2)}) collective-permute-start(bf16[256,128]{1,0:T(8,128)(2,1)S(1)} %get-tuple-element.107.refs_3_.refs_24_), channel_id=1, source_target_pairs={{0,6},{1,7},{2,4},{3,5},{4,2},{5,3},{6,0},{7,1},{8,14},{9,15},{10,... | collective-permute-start | bytes 196616 | tf_op jit(solution)/shard_map/ppermute | solution.py:399
  77.7 5.9 %collective-permute-start.26 = (bf16[256,128]{1,0:T(8,128)(2,1)S(1)}, bf16[256,128]{1,0:T(8,128)(2,1)S(1)}, u32[]{:S(2)}, u32[]{:S(2)}) collective-permute-start(bf16[256,128]{1,0:T(8,128)(2,1)S(1)} %get-tuple-element.107.refs_3_.refs_24_), channel_id=1, source_target_pairs={{0,2},{1,3},{2,0},{3,1},{4,6},{5,7},{6,4},{7,5},{8,10},{9,11},{10,... | collective-permute-start | bytes 196616 | tf_op jit(solution)/shard_map/ppermute | solution.py:399
  78.1 5.4 %collective-permute-start.25 = (bf16[256,128]{1,0:T(8,128)(2,1)S(1)}, bf16[256,128]{1,0:T(8,128)(2,1)S(1)}, u32[]{:S(2)}, u32[]{:S(2)}) collective-permute-start(bf16[256,128]{1,0:T(8,128)(2,1)S(1)} %get-tuple-element.107.refs_3_.refs_24_), channel_id=1, source_target_pairs={{0,4},{1,5},{2,6},{3,7},{4,0},{5,1},{6,2},{7,3},{8,12},{9,13},{10,... | collective-permute-start | bytes 196616 | tf_op jit(solution)/shard_map/ppermute | solution.py:399
  85.3 5.1 %collective-permute-start.28 = (bf16[528,128]{1,0:T(8,128)(2,1)S(1)}, bf16[528,128]{1,0:T(8,128)(2,1)S(1)}, u32[]{:S(2)}, u32[]{:S(2)}) collective-permute-start(bf16[528,128]{1,0:T(8,128)(2,1)S(1)} %get-tuple-element.112), channel_id=1, source_target_pairs={{0,8},{8,0},{16,24},{24,16},{1,9},{9,1},{17,25},{25,17},{2,10},{10... | collective-permute-start | bytes 405512 | tf_op jit(solution)/shard_map/ppermute | solution.py:399
  86.3 5.0 %collective-permute-start.29 = (bf16[528,128]{1,0:T(8,128)(2,1)S(1)}, bf16[528,128]{1,0:T(8,128)(2,1)S(1)}, u32[]{:S(2)}, u32[]{:S(2)}) collective-permute-start(bf16[528,128]{1,0:T(8,128)(2,1)S(1)} %get-tuple-element.113), channel_id=1, source_target_pairs={{0,16},{8,24},{16,0},{24,8},{1,17},{9,25},{17,1},{25,9},{2,18},{10... | collective-permute-start | bytes 405512 | tf_op jit(solution)/shard_map/ppermute | solution.py:399
  86.9 5.9 %collective-permute-start.30 = (bf16[528,128]{1,0:T(8,128)(2,1)S(1)}, bf16[528,128]{1,0:T(8,128)(2,1)S(1)}, u32[]{:S(2)}, u32[]{:S(2)}) collective-permute-start(bf16[528,128]{1,0:T(8,128)(2,1)S(1)} %get-tuple-element.114), channel_id=1, source_target_pairs={{0,24},{8,16},{16,8},{24,0},{1,25},{9,17},{17,9},{25,1},{2,26},{10... | collective-permute-start | bytes 405512 | tf_op jit(solution)/shard_map/ppermute | solution.py:399
  92.9 5.0 %collective-permute-start.33 = (bf16[512,128]{1,0:T(8,128)(2,1)S(1)}, bf16[512,128]{1,0:T(8,128)(2,1)S(1)}, u32[]{:S(2)}, u32[]{:S(2)}) collective-permute-start(bf16[512,128]{1,0:T(8,128)(2,1)S(1)} %get-tuple-element.117.refs_3_.refs_16_), channel_id=1, source_target_pairs={{0,8},{8,0},{16,24},{24,16},{1,9},{9,1},{17,25},{25,17},{2,10},{10... | collective-permute-start | bytes 393224 | tf_op jit(solution)/shard_map/ppermute | solution.py:399
  94.6 5.0 %collective-permute-start.32 = (bf16[512,128]{1,0:T(8,128)(2,1)S(1)}, bf16[512,128]{1,0:T(8,128)(2,1)S(1)}, u32[]{:S(2)}, u32[]{:S(2)}) collective-permute-start(bf16[512,128]{1,0:T(8,128)(2,1)S(1)} %get-tuple-element.117.refs_3_.refs_16_), channel_id=1, source_target_pairs={{0,16},{8,24},{16,0},{24,8},{1,17},{9,25},{17,1},{25,9},{2,18},{10... | collective-permute-start | bytes 393224 | tf_op jit(solution)/shard_map/ppermute | solution.py:399
  95.5 5.9 %collective-permute-start.31 = (bf16[512,128]{1,0:T(8,128)(2,1)S(1)}, bf16[512,128]{1,0:T(8,128)(2,1)S(1)}, u32[]{:S(2)}, u32[]{:S(2)}) collective-permute-start(bf16[512,128]{1,0:T(8,128)(2,1)S(1)} %get-tuple-element.117.refs_3_.refs_16_), channel_id=1, source_target_pairs={{0,24},{8,16},{16,8},{24,0},{1,25},{9,17},{17,9},{25,1},{2,26},{10... | collective-permute-start | bytes 393224 | tf_op jit(solution)/shard_map/ppermute | solution.py:399
  102.8 6.1 %collective-permute-start.34 = (bf16[272,128]{1,0:T(8,128)(2,1)S(1)}, bf16[272,128]{1,0:T(8,128)(2,1)S(1)}, u32[]{:S(2)}, u32[]{:S(2)}) collective-permute-start(bf16[272,128]{1,0:T(8,128)(2,1)S(1)} %get-tuple-element.122), channel_id=1, source_target_pairs={{0,6},{1,7},{2,4},{3,5},{4,2},{5,3},{6,0},{7,1},{8,14},{9,15},{10,... | collective-permute-start | bytes 208904 | tf_op jit(solution)/shard_map/ppermute | solution.py:399
  105.8 5.2 %collective-permute-start.36 = (bf16[272,128]{1,0:T(8,128)(2,1)S(1)}, bf16[272,128]{1,0:T(8,128)(2,1)S(1)}, u32[]{:S(2)}, u32[]{:S(2)}) collective-permute-start(bf16[272,128]{1,0:T(8,128)(2,1)S(1)} %get-tuple-element.124), channel_id=1, source_target_pairs={{0,4},{1,5},{2,6},{3,7},{4,0},{5,1},{6,2},{7,3},{8,12},{9,13},{10,... | collective-permute-start | bytes 208904 | tf_op jit(solution)/shard_map/ppermute | solution.py:399
  113.2 5.4 %collective-permute-start.38 = (bf16[256,128]{1,0:T(8,128)(2,1)S(1)}, bf16[256,128]{1,0:T(8,128)(2,1)S(1)}, u32[]{:S(2)}, u32[]{:S(2)}) collective-permute-start(bf16[256,128]{1,0:T(8,128)(2,1)S(1)} %get-tuple-element.127.refs_0_.refs_28_), channel_id=1, source_target_pairs={{0,4},{1,5},{2,6},{3,7},{4,0},{5,1},{6,2},{7,3},{8,12},{9,13},{10,... | collective-permute-start | bytes 196616 | tf_op jit(solution)/shard_map/ppermute | solution.py:399
  113.3 6.2 %collective-permute-start.37 = (bf16[256,128]{1,0:T(8,128)(2,1)S(1)}, bf16[256,128]{1,0:T(8,128)(2,1)S(1)}, u32[]{:S(2)}, u32[]{:S(2)}) collective-permute-start(bf16[256,128]{1,0:T(8,128)(2,1)S(1)} %get-tuple-element.127.refs_0_.refs_28_), channel_id=1, source_target_pairs={{0,6},{1,7},{2,4},{3,5},{4,2},{5,3},{6,0},{7,1},{8,14},{9,15},{10,... | collective-permute-start | bytes 196616 | tf_op jit(solution)/shard_map/ppermute | solution.py:399
  (17 other events, 127.8 us)

commit v7 on v6

--- a/solution.py
+++ b/solution.py
@@ -36,7 +36,7 @@
     weights: object
 
 
-def call(kernel, name, outs, scratch, *ins, vector=False, alias=None, away=0):
+def call(kernel, name, outs, scratch, *ins, vector=False, alias=None, away=0, out_space=pltpu.VMEM):
     def space(place, dtype):
         if place < away:
             return pltpu.HBM
@@ -44,7 +44,7 @@
 
     def room(shape, dtype):
         if dtype is pltpu.SemaphoreType.DMA:
-            return dtype((shape,))
+            return dtype(shape if isinstance(shape, tuple) else (shape,))
         return (pltpu.SMEM if dtype == jnp.int32 else pltpu.VMEM)(shape, dtype)
 
     return pl.pallas_call(
@@ -52,7 +52,7 @@
         name=name,
         out_shape=[jax.ShapeDtypeStruct(s, d) for s, d in outs],
         in_specs=[pl.BlockSpec(memory_space=space(i, a.dtype)) for i, a in enumerate(ins)],
-        out_specs=[pl.BlockSpec(memory_space=pltpu.VMEM) for _ in outs],
+        out_specs=[pl.BlockSpec(memory_space=out_space) for _ in outs],
         scratch_shapes=[room(s, d) for s, d in scratch],
         input_output_aliases=alias or {},
         compiler_params=pltpu.CompilerParams(vmem_limit_bytes=VMEM_BYTES),
@@ -186,14 +186,23 @@
     return step
 
 
-def first_adjoint_kernel(hyd_axis, order, tiles, tile_ref, row_ref, col_ref, used_ref, own_total_ref, plain_ref, turned_ref, *refs):
-    turned_tile_ref, own_ref, sends, total_ref = refs[0], refs[1], refs[2:-1], refs[-1]
+def first_adjoint_kernel(hyd_axis, order, tiles, tile_ref, row_vmem, col_vmem, used_vmem, own_total_ref, plain_ref, turned_ref, *refs):
+    turned_tile_ref, own_ref, sends = refs[0], refs[1], refs[2:-5]
+    total_ref, *index, index_sem = refs[-5:]
+    copies = [
+        pltpu.make_async_copy(source, target, index_sem.at[k])
+        for k, (source, target) in enumerate(zip((row_vmem, col_vmem, used_vmem), index))
+    ]
+    for copy in copies:
+        copy.start()
     total_ref[...] = jnp.zeros_like(total_ref)
-    slots((row_ref.at[0], col_ref.at[0], used_ref.at[0]), turn_step(tiles, tile_ref, turned_tile_ref, total_ref, plain_ref, turned_ref))
-    give_columns(hyd_axis, order, own_total_ref, total_ref, own_ref, sends, None)
-
-
-def give_columns(hyd_axis, order, first_ref, second_ref, own_ref, sends, tail):
+    for copy in copies:
+        copy.wait()
+    slots([ref.at[0] for ref in index], turn_step(tiles, tile_ref, turned_tile_ref, total_ref, plain_ref, turned_ref))
+    give_columns(hyd_axis, order, own_total_ref, total_ref, own_ref, sends)
+
+
+def give_columns(hyd_axis, order, first_ref, second_ref, own_ref, sends):
     here = lax.axis_index(hyd_axis)
     part = own_ref.shape[0] // 2
     own_ref[:part, :] = first_ref[spans(part, here), :]
@@ -202,8 +211,6 @@
         there = here ^ offset
         send[:part, :] = first_ref[spans(part, there), :].astype(BF16)
         send[part : 2 * part, :] = second_ref[spans(part, there), :].astype(BF16)
-        if tail is not None:
-            send[2 * part :, :] = tail
 
 
 def list_kernel(plans, *refs):
@@ -378,17 +385,23 @@
         narrow_r[span, :] = residual.astype(BF16)
 
 
-def unpack_kernel(core_axis, own_x, own_r, pair_x, pair_r, x_ref, r_ref):
+def unpack_kernel(core_axis, own_x, own_r, pair_x, pair_r, x_hbm, r_hbm, x_ref, r_ref, sems):
     core = lax.rem(lax.axis_index(core_axis), 2)
-    for own, pair, out in ((own_x, pair_x, x_ref), (own_r, pair_r, r_ref)):
-        for at in range(0, own.shape[0], 128):
-            span = pl.ds(at, 128)
+    copies = []
+    for k, (own, pair, out, target) in enumerate(((own_x, pair_x, x_ref, x_hbm), (own_r, pair_r, r_ref, r_hbm))):
+        piece = own.shape[0] // sems.shape[1]
+        for j in range(sems.shape[1]):
+            span = pl.ds(j * piece, piece)
             mine, theirs = own[span, :], pair[span, :].astype(F32)
             first = jnp.where(core == 0, mine, theirs)
             second = jnp.where(core == 0, theirs, mine)
             low = low_half(mine.shape)
             out[0, span, :] = jnp.where(low, first, turn(second))
             out[1, span, :] = jnp.where(low, turn(first), second)
+            copies.append(pltpu.make_async_copy(out.at[:, span, :], target.at[:, span, :], sems.at[k, j]))
+            copies[-1].start()
+    for copy in copies:
+        copy.wait()
 
 
 def solution(mesh):
@@ -425,21 +438,23 @@
         vector = lambda n, dtype: ((n, shots), dtype)
 
         pair_tiles = swap(own_tiles, "src", srcs, 1)
-        index = (tile_rows[0], tile_cols[0], tile_counts)
+        index = (tile_rows[0], tile_cols[0], jnp.broadcast_to(tile_counts, tile_rows.shape[1:]))
         pair_index = tuple(swap(v, "src", srcs, 1) for v in index)
         pieces, groups = 4, slot_count // GROUP
+        table = [(v.shape, jnp.int32) for v in index]
         turned_shape = ((slot_count, size, 2 * size), BF16)
         turned_own, total, plain, turned = call(
             functools.partial(pack_kernel, "src", col_tiles), "pack",
             [turned_shape, col_total, vector(rows, BF16), vector(rows, BF16)],
-            [(record.shape, F32), (own_tiles.shape, BF16), (index[0].shape, jnp.int32), (index[1].shape, jnp.int32)]
+            [(record.shape, F32), (own_tiles.shape, BF16)] + table[:2]
             + [(n, pltpu.SemaphoreType.DMA) for n in (pieces, groups, 2)],
             record, own_tiles, *index, away=4,
         )
         turned_pair, own, *sends = call(
             functools.partial(first_adjoint_kernel, "hyd", hyd_order, col_tiles), "first_adjoint",
-            [turned_shape, vector(2 * col_part, F32)] + [vector(2 * col_part, BF16)] * (hyds - 1), [col_total],
-            pair_tiles, *pair_index, total, plain, turned,
+            [turned_shape, vector(2 * col_part, F32)] + [vector(2 * col_part, BF16)] * (hyds - 1),
+            [col_total] + table + [(len(table), pltpu.SemaphoreType.DMA)],
+            pair_tiles, *(pltpu.with_memory_space_constraint(v, pltpu.VMEM) for v in pair_index), total, plain, turned, vector=True,
         )
         gradient, narrow = call(
             functools.partial(start_kernel, hyds - 1), "start",
@@ -522,8 +537,9 @@
         )
         return call(
             functools.partial(unpack_kernel, "src"), "unpack",
-            [((2, cols, shots), F32), ((2, rows, shots), F32)], [],
-            own_x, wide_r, swap(pair_x, "src", srcs, 1), swap(narrow_r, "src", srcs, 1),
+            [((2, cols, shots), F32), ((2, rows, shots), F32)],
+            [((2, cols, shots), F32), ((2, rows, shots), F32), ((2, 4), pltpu.SemaphoreType.DMA)],
+            own_x, wide_r, swap(pair_x, "src", srcs, 1), swap(narrow_r, "src", srcs, 1), out_space=pltpu.HBM,
         )
 
     in_specs = (

time: 132 us -> 131 us (level)
  Pallas kernels: 23.9 us -> 21.8 us
  waiting for transfers between devices: 50.3 us -> 52 us
    pallas_call x22, Pallas kernels: 23.9 us -> 21.8 us  [call(): pl.pallas_call(kernel, name=name, out_shape=[jax.ShapeDtypeStruct(s, d) f...]
    ppermute x45, waiting for transfers between devices: 50.3 us -> 52 us  [swap(): return lax.ppermute(value, axis, [(i, i ^ offset) for i in range(size)])]
  transfers between devices with their start and end apart: 45 -> 45, of which waited for: 35 -> 32; matrix products, arithmetic and copies ran while one was open for 0% -> 0% of each run, Pallas kernels for 8% -> 8%
where the time goes in v7:
time: 131 us; the launch traced here: 130 us
  starting transfers between devices  54.1 us (41%)
  waiting for transfers between devices  52 us (40%)
  Pallas kernels  21.8 us (17%)
  between operations  1.68 us (1%)
    ppermute x45, starting transfers between devices, swap(): return lax.ppermute(value, axis, [(i, i ^ offset) for i in range(size)])  54.1 us
    ppermute x45, waiting for transfers between devices, swap(): return lax.ppermute(value, axis, [(i, i ^ offset) for i in range(size)])  52 us
    pallas_call x22, Pallas kernels, call(): pl.pallas_call(kernel, name=name, out_shape=[jax.ShapeDtypeStruct(s, d) f...  21.8 us
  transfers between devices with their start and end apart: 45, of which 32 were waited for; matrix products, arithmetic and copies ran while one was open for 0% of the time, Pallas kernels for 8%

profile of v7, /device:TPU:0, one launch (start us, length us, event | category | flops | bytes accessed | tf_op | source)
XLA Modules:
  0.0 129.7 jit_solution(4334161106719796139)
XLA Ops:
  2.5 3.2 %pack.1 = (bf16[24,128,256]{2,1,0:T(8,128)(2,1)S(1)}, f32[1152,128]{1,0:T(8,128)S(1)}, bf16[1024,128]{1,0:T(8,128)(2,1)S(1)}, bf16[1024,128]{1,0:T(8,128)(2,1)S(1)}) custom-call(f32[2,1024,128]{2,1,0:T(8,128)} %record_ref.1, bf16[24,2,128,128]{3,2,1,0:T(8,128)(2,1)} %bitcast.6, s32[1,24]{1,0:T(1,128)} %bitcast.14, s32[1,24]{1,0:T(1,128)} %bitcast.17, ...), custom_call_target="tpu_custom_call" | custom-call | tf_op jit(solution)/shard_map/pack/pallas_call | solution.py:50
  7.1 2.6 %collective-permute-start.4 = (bf16[512,128]{1,0:T(8,128)(2,1)S(1)}, bf16[512,128]{1,0:T(8,128)(2,1)S(1)}, u32[]{:S(2)}, u32[]{:S(2)}) collective-permute-start(bf16[512,128]{1,0:T(8,128)(2,1)S(1)} %get-tuple-element.77), channel_id=1, source_target_pairs={{0,8},{8,0},{16,24},{24,16},{1,9},{9,1},{17,25},{25,17},{2,10},{10... | collective-permute-start | bytes 393224 | tf_op jit(solution)/shard_map/ppermute | solution.py:412
  9.8 1.9 %collective-permute-start.5 = (bf16[512,128]{1,0:T(8,128)(2,1)S(1)}, bf16[512,128]{1,0:T(8,128)(2,1)S(1)}, u32[]{:S(2)}, u32[]{:S(2)}) collective-permute-start(bf16[512,128]{1,0:T(8,128)(2,1)S(1)} %get-tuple-element.78), channel_id=1, source_target_pairs={{0,16},{8,24},{16,0},{24,8},{1,17},{9,25},{17,1},{25,9},{2,18},{10... | collective-permute-start | bytes 393224 | tf_op jit(solution)/shard_map/ppermute | solution.py:412
  11.6 2.0 %collective-permute-done.4.refs_0_ = bf16[512,128]{1,0:T(8,128)(2,1)S(1)} collective-permute-done((bf16[512,128]{1,0:T(8,128)(2,1)S(1)}, bf16[512,128]{1,0:T(8,128)(2,1)S(1)}, u32[]{:S(2)}, u32[]{:S(2)}) %collective-permute-start.4) | collective-permute-done | bytes 131104 | tf_op jit(solution)/shard_map/ppermute | solution.py:412
  13.6 4.3 %collective-permute-done.5.refs_1_ = bf16[512,128]{1,0:T(8,128)(2,1)S(1)} collective-permute-done((bf16[512,128]{1,0:T(8,128)(2,1)S(1)}, bf16[512,128]{1,0:T(8,128)(2,1)S(1)}, u32[]{:S(2)}, u32[]{:S(2)}) %collective-permute-start.5) | collective-permute-done | bytes 131104 | tf_op jit(solution)/shard_map/ppermute | solution.py:412
  21.8 2.0 %collective-permute-done.9.refs_4_.refs_9_ = bf16[512,128]{1,0:T(8,128)(2,1)S(1)} collective-permute-done((bf16[512,128]{1,0:T(8,128)(2,1)S(1)}, bf16[512,128]{1,0:T(8,128)(2,1)S(1)}, u32[]{:S(2)}, u32[]{:S(2)}) %collective-permute-start.9) | collective-permute-done | bytes 131104 | tf_op jit(solution)/shard_map/ppermute | solution.py:412
  28.2 3.1 %collective-permute-start.10 = (bf16[272,128]{1,0:T(8,128)(2,1)S(1)}, bf16[272,128]{1,0:T(8,128)(2,1)S(1)}, u32[]{:S(2)}, u32[]{:S(2)}) collective-permute-start(bf16[272,128]{1,0:T(8,128)(2,1)S(1)} %get-tuple-element.85), channel_id=1, source_target_pairs={{0,6},{1,7},{2,4},{3,5},{4,2},{5,3},{6,0},{7,1},{8,14},{9,15},{10,... | collective-permute-start | bytes 208904 | tf_op jit(solution)/shard_map/ppermute | solution.py:412
  32.6 2.3 %collective-permute-done.10.refs_0_ = bf16[272,128]{1,0:T(8,128)(2,1)S(1)} collective-permute-done((bf16[272,128]{1,0:T(8,128)(2,1)S(1)}, bf16[272,128]{1,0:T(8,128)(2,1)S(1)}, u32[]{:S(2)}, u32[]{:S(2)}) %collective-permute-start.10) | collective-permute-done | bytes 69664 | tf_op jit(solution)/shard_map/ppermute | solution.py:412
  38.8 2.9 %collective-permute-start.13 = (bf16[256,128]{1,0:T(8,128)(2,1)S(1)}, bf16[256,128]{1,0:T(8,128)(2,1)S(1)}, u32[]{:S(2)}, u32[]{:S(2)}) collective-permute-start(bf16[256,128]{1,0:T(8,128)(2,1)S(1)} %get-tuple-element.88.refs_3_.refs_20_), channel_id=1, source_target_pairs={{0,4},{1,5},{2,6},{3,7},{4,0},{5,1},{6,2},{7,3},{8,12},{9,13},{10,... | collective-permute-start | bytes 196616 | tf_op jit(solution)/shard_map/ppermute | solution.py:412
  41.7 1.7 %collective-permute-done.15.refs_4_.refs_21_ = bf16[256,128]{1,0:T(8,128)(2,1)S(1)} collective-permute-done((bf16[256,128]{1,0:T(8,128)(2,1)S(1)}, bf16[256,128]{1,0:T(8,128)(2,1)S(1)}, u32[]{:S(2)}, u32[]{:S(2)}) %collective-permute-start.15) | collective-permute-done | bytes 65568 | tf_op jit(solution)/shard_map/ppermute | solution.py:412
  47.2 1.9 %collective-permute-start.17 = (bf16[528,128]{1,0:T(8,128)(2,1)S(1)}, bf16[528,128]{1,0:T(8,128)(2,1)S(1)}, u32[]{:S(2)}, u32[]{:S(2)}) collective-permute-start(bf16[528,128]{1,0:T(8,128)(2,1)S(1)} %get-tuple-element.94), channel_id=1, source_target_pairs={{0,16},{8,24},{16,0},{24,8},{1,17},{9,25},{17,1},{25,9},{2,18},{10... | collective-permute-start | bytes 405512 | tf_op jit(solution)/shard_map/ppermute | solution.py:412
  49.7 1.6 %collective-permute-done.16.refs_0_ = bf16[528,128]{1,0:T(8,128)(2,1)S(1)} collective-permute-done((bf16[528,128]{1,0:T(8,128)(2,1)S(1)}, bf16[528,128]{1,0:T(8,128)(2,1)S(1)}, u32[]{:S(2)}, u32[]{:S(2)}) %collective-permute-start.16) | collective-permute-done | bytes 135200 | tf_op jit(solution)/shard_map/ppermute | solution.py:412
  51.4 1.8 %collective-permute-done.17.refs_1_ = bf16[528,128]{1,0:T(8,128)(2,1)S(1)} collective-permute-done((bf16[528,128]{1,0:T(8,128)(2,1)S(1)}, bf16[528,128]{1,0:T(8,128)(2,1)S(1)}, u32[]{:S(2)}, u32[]{:S(2)}) %collective-permute-start.17) | collective-permute-done | bytes 135200 | tf_op jit(solution)/shard_map/ppermute | solution.py:412
  53.2 2.6 %collective-permute-done.18.refs_2_ = bf16[528,128]{1,0:T(8,128)(2,1)S(1)} collective-permute-done((bf16[528,128]{1,0:T(8,128)(2,1)S(1)}, bf16[528,128]{1,0:T(8,128)(2,1)S(1)}, u32[]{:S(2)}, u32[]{:S(2)}) %collective-permute-start.18) | collective-permute-done | bytes 135200 | tf_op jit(solution)/shard_map/ppermute | solution.py:412
  57.4 2.0 %collective-permute-start.19 = (bf16[512,128]{1,0:T(8,128)(2,1)S(1)}, bf16[512,128]{1,0:T(8,128)(2,1)S(1)}, u32[]{:S(2)}, u32[]{:S(2)}) collective-permute-start(bf16[512,128]{1,0:T(8,128)(2,1)S(1)} %get-tuple-element.98.refs_3_.refs_12_), channel_id=1, source_target_pairs={{0,24},{8,16},{16,8},{24,0},{1,25},{9,17},{17,9},{25,1},{2,26},{10... | collective-permute-start | bytes 393224 | tf_op jit(solution)/shard_map/ppermute | solution.py:412
  65.3 2.7 %collective-permute-start.22 = (bf16[272,128]{1,0:T(8,128)(2,1)S(1)}, bf16[272,128]{1,0:T(8,128)(2,1)S(1)}, u32[]{:S(2)}, u32[]{:S(2)}) collective-permute-start(bf16[272,128]{1,0:T(8,128)(2,1)S(1)} %get-tuple-element.103), channel_id=1, source_target_pairs={{0,6},{1,7},{2,4},{3,5},{4,2},{5,3},{6,0},{7,1},{8,14},{9,15},{10,... | collective-permute-start | bytes 208904 | tf_op jit(solution)/shard_map/ppermute | solution.py:412
  69.7 2.5 %collective-permute-done.22.refs_0_ = bf16[272,128]{1,0:T(8,128)(2,1)S(1)} collective-permute-done((bf16[272,128]{1,0:T(8,128)(2,1)S(1)}, bf16[272,128]{1,0:T(8,128)(2,1)S(1)}, u32[]{:S(2)}, u32[]{:S(2)}) %collective-permute-start.22) | collective-permute-done | bytes 69664 | tf_op jit(solution)/shard_map/ppermute | solution.py:412
  73.1 2.1 %collective-permute-done.24.refs_2_ = bf16[272,128]{1,0:T(8,128)(2,1)S(1)} collective-permute-done((bf16[272,128]{1,0:T(8,128)(2,1)S(1)}, bf16[272,128]{1,0:T(8,128)(2,1)S(1)}, u32[]{:S(2)}, u32[]{:S(2)}) %collective-permute-start.24) | collective-permute-done | bytes 69664 | tf_op jit(solution)/shard_map/ppermute | solution.py:412
  75.3 1.8 %collective-permute-start.27 = (bf16[256,128]{1,0:T(8,128)(2,1)S(1)}, bf16[256,128]{1,0:T(8,128)(2,1)S(1)}, u32[]{:S(2)}, u32[]{:S(2)}) collective-permute-start(bf16[256,128]{1,0:T(8,128)(2,1)S(1)} %get-tuple-element.107.refs_3_.refs_24_), channel_id=1, source_target_pairs={{0,6},{1,7},{2,4},{3,5},{4,2},{5,3},{6,0},{7,1},{8,14},{9,15},{10,... | collective-permute-start | bytes 196616 | tf_op jit(solution)/shard_map/ppermute | solution.py:412
  77.1 2.6 %collective-permute-start.25 = (bf16[256,128]{1,0:T(8,128)(2,1)S(1)}, bf16[256,128]{1,0:T(8,128)(2,1)S(1)}, u32[]{:S(2)}, u32[]{:S(2)}) collective-permute-start(bf16[256,128]{1,0:T(8,128)(2,1)S(1)} %get-tuple-element.107.refs_3_.refs_24_), channel_id=1, source_target_pairs={{0,4},{1,5},{2,6},{3,7},{4,0},{5,1},{6,2},{7,3},{8,12},{9,13},{10,... | collective-permute-start | bytes 196616 | tf_op jit(solution)/shard_map/ppermute | solution.py:412
  79.7 1.8 %collective-permute-done.27.refs_4_.refs_25_ = bf16[256,128]{1,0:T(8,128)(2,1)S(1)} collective-permute-done((bf16[256,128]{1,0:T(8,128)(2,1)S(1)}, bf16[256,128]{1,0:T(8,128)(2,1)S(1)}, u32[]{:S(2)}, u32[]{:S(2)}) %collective-permute-start.27) | collective-permute-done | bytes 65568 | tf_op jit(solution)/shard_map/ppermute | solution.py:412
  84.3 1.6 %collective-permute-start.28 = (bf16[528,128]{1,0:T(8,128)(2,1)S(1)}, bf16[528,128]{1,0:T(8,128)(2,1)S(1)}, u32[]{:S(2)}, u32[]{:S(2)}) collective-permute-start(bf16[528,128]{1,0:T(8,128)(2,1)S(1)} %get-tuple-element.112), channel_id=1, source_target_pairs={{0,8},{8,0},{16,24},{24,16},{1,9},{9,1},{17,25},{25,17},{2,10},{10... | collective-permute-start | bytes 405512 | tf_op jit(solution)/shard_map/ppermute | solution.py:412
  87.9 2.2 %collective-permute-done.28.refs_0_ = bf16[528,128]{1,0:T(8,128)(2,1)S(1)} collective-permute-done((bf16[528,128]{1,0:T(8,128)(2,1)S(1)}, bf16[528,128]{1,0:T(8,128)(2,1)S(1)}, u32[]{:S(2)}, u32[]{:S(2)}) %collective-permute-start.28) | collective-permute-done | bytes 135200 | tf_op jit(solution)/shard_map/ppermute | solution.py:412
  91.3 1.7 %collective-permute-done.30.refs_2_ = bf16[528,128]{1,0:T(8,128)(2,1)S(1)} collective-permute-done((bf16[528,128]{1,0:T(8,128)(2,1)S(1)}, bf16[528,128]{1,0:T(8,128)(2,1)S(1)}, u32[]{:S(2)}, u32[]{:S(2)}) %collective-permute-start.30) | collective-permute-done | bytes 135200 | tf_op jit(solution)/shard_map/ppermute | solution.py:412
  94.5 2.1 %collective-permute-start.31 = (bf16[512,128]{1,0:T(8,128)(2,1)S(1)}, bf16[512,128]{1,0:T(8,128)(2,1)S(1)}, u32[]{:S(2)}, u32[]{:S(2)}) collective-permute-start(bf16[512,128]{1,0:T(8,128)(2,1)S(1)} %get-tuple-element.117.refs_3_.refs_16_), channel_id=1, source_target_pairs={{0,24},{8,16},{16,8},{24,0},{1,25},{9,17},{17,9},{25,1},{2,26},{10... | collective-permute-start | bytes 393224 | tf_op jit(solution)/shard_map/ppermute | solution.py:412
  98.1 1.6 %forward.10 = (f32[1152,128]{1,0:T(8,128)S(1)}, f32[8,128]{1,0:T(8,128)S(1)}) custom-call(bf16[24,2,128,128]{3,2,1,0:T(8,128)(2,1)S(1)} %bitcast.11, bf16[24,2,128,128]{3,2,1,0:T(8,128)(2,1)S(1)} %collective-permute-done.tile_ref.refs_1_, s32[8,128]{1,0:T(8,128)S(1)} %get-tuple-element.69.refs_2_, bf16[512,128]{1,0:T(8,128)(2,1)S(1)} %get-tuple-element.117.refs_3_.refs_16_, ...), custom_call_target="tpu_custom_call" | custom-call | tf_op jit(solution)/shard_map/forward/pallas_call | solution.py:50
  101.9 2.0 %collective-permute-start.34 = (bf16[272,128]{1,0:T(8,128)(2,1)S(1)}, bf16[272,128]{1,0:T(8,128)(2,1)S(1)}, u32[]{:S(2)}, u32[]{:S(2)}) collective-permute-start(bf16[272,128]{1,0:T(8,128)(2,1)S(1)} %get-tuple-element.122), channel_id=1, source_target_pairs={{0,6},{1,7},{2,4},{3,5},{4,2},{5,3},{6,0},{7,1},{8,14},{9,15},{10,... | collective-permute-start | bytes 208904 | tf_op jit(solution)/shard_map/ppermute | solution.py:412
  106.3 1.8 %collective-permute-done.34.refs_0_ = bf16[272,128]{1,0:T(8,128)(2,1)S(1)} collective-permute-done((bf16[272,128]{1,0:T(8,128)(2,1)S(1)}, bf16[272,128]{1,0:T(8,128)(2,1)S(1)}, u32[]{:S(2)}, u32[]{:S(2)}) %collective-permute-start.34) | collective-permute-done | bytes 69664 | tf_op jit(solution)/shard_map/ppermute | solution.py:412
  108.8 2.2 %collective-permute-done.36.refs_2_ = bf16[272,128]{1,0:T(8,128)(2,1)S(1)} collective-permute-done((bf16[272,128]{1,0:T(8,128)(2,1)S(1)}, bf16[272,128]{1,0:T(8,128)(2,1)S(1)}, u32[]{:S(2)}, u32[]{:S(2)}) %collective-permute-start.36) | collective-permute-done | bytes 69664 | tf_op jit(solution)/shard_map/ppermute | solution.py:412
  112.2 3.3 %collective-permute-start.37 = (bf16[256,128]{1,0:T(8,128)(2,1)S(1)}, bf16[256,128]{1,0:T(8,128)(2,1)S(1)}, u32[]{:S(2)}, u32[]{:S(2)}) collective-permute-start(bf16[256,128]{1,0:T(8,128)(2,1)S(1)} %get-tuple-element.127.refs_0_.refs_28_), channel_id=1, source_target_pairs={{0,6},{1,7},{2,4},{3,5},{4,2},{5,3},{6,0},{7,1},{8,14},{9,15},{10,... | collective-permute-start | bytes 196616 | tf_op jit(solution)/shard_map/ppermute | solution.py:412
  116.5 2.0 %collective-permute-done.37.refs_1_.refs_29_ = bf16[256,128]{1,0:T(8,128)(2,1)S(1)} collective-permute-done((bf16[256,128]{1,0:T(8,128)(2,1)S(1)}, bf16[256,128]{1,0:T(8,128)(2,1)S(1)}, u32[]{:S(2)}, u32[]{:S(2)}) %collective-permute-start.37) | collective-permute-done | bytes 65568 | tf_op jit(solution)/shard_map/ppermute | solution.py:412
  123.2 2.2 %collective-permute-done.40.refs_1_ = f32[8,128]{1,0:T(8,128)S(1)} collective-permute-done((f32[8,128]{1,0:T(8,128)S(1)}, f32[8,128]{1,0:T(8,128)S(1)}, u32[]{:S(2)}, u32[]{:S(2)}) %collective-permute-start.40) | collective-permute-done | bytes 4128 | tf_op jit(solution)/shard_map/ppermute | solution.py:412
  (89 shorter events, 55.9 us)
Async XLA Ops:
  0.6 5.1 %collective-permute-start = (bf16[24,2,128,128]{3,2,1,0:T(8,128)(2,1)}, bf16[24,2,128,128]{3,2,1,0:T(8,128)(2,1)S(1)}, u32[]{:S(2)}, u32[]{:S(2)}) collective-permute-start(bf16[24,2,128,128]{3,2,1,0:T(8,128)(2,1)} %bitcast.5), channel_id=1, source_target_pairs={{0,1},{1,0},{2,3},{3,2},{4,5},{5,4},{6,7},{7,6},{8,9},{9,8},{10,11... | collective-permute-start | bytes 4718600 | tf_op jit(solution)/shard_map/ppermute | solution.py:412
  7.1 6.5 %collective-permute-start.4 = (bf16[512,128]{1,0:T(8,128)(2,1)S(1)}, bf16[512,128]{1,0:T(8,128)(2,1)S(1)}, u32[]{:S(2)}, u32[]{:S(2)}) collective-permute-start(bf16[512,128]{1,0:T(8,128)(2,1)S(1)} %get-tuple-element.77), channel_id=1, source_target_pairs={{0,8},{8,0},{16,24},{24,16},{1,9},{9,1},{17,25},{25,17},{2,10},{10... | collective-permute-start | bytes 393224 | tf_op jit(solution)/shard_map/ppermute | solution.py:412
  9.8 8.1 %collective-permute-start.5 = (bf16[512,128]{1,0:T(8,128)(2,1)S(1)}, bf16[512,128]{1,0:T(8,128)(2,1)S(1)}, u32[]{:S(2)}, u32[]{:S(2)}) collective-permute-start(bf16[512,128]{1,0:T(8,128)(2,1)S(1)} %get-tuple-element.78), channel_id=1, source_target_pairs={{0,16},{8,24},{16,0},{24,8},{1,17},{9,25},{17,1},{25,9},{2,18},{10... | collective-permute-start | bytes 393224 | tf_op jit(solution)/shard_map/ppermute | solution.py:412
  11.6 6.3 %collective-permute-start.6 = (bf16[512,128]{1,0:T(8,128)(2,1)S(1)}, bf16[512,128]{1,0:T(8,128)(2,1)S(1)}, u32[]{:S(2)}, u32[]{:S(2)}) collective-permute-start(bf16[512,128]{1,0:T(8,128)(2,1)S(1)} %get-tuple-element.79), channel_id=1, source_target_pairs={{0,24},{8,16},{16,8},{24,0},{1,25},{9,17},{17,9},{25,1},{2,26},{10... | collective-permute-start | bytes 393224 | tf_op jit(solution)/shard_map/ppermute | solution.py:412
  18.0 5.8 %collective-permute-start.9 = (bf16[512,128]{1,0:T(8,128)(2,1)S(1)}, bf16[512,128]{1,0:T(8,128)(2,1)S(1)}, u32[]{:S(2)}, u32[]{:S(2)}) collective-permute-start(bf16[512,128]{1,0:T(8,128)(2,1)S(1)} %get-tuple-element.80.refs_3_.refs_8_), channel_id=1, source_target_pairs={{0,8},{8,0},{16,24},{24,16},{1,9},{9,1},{17,25},{25,17},{2,10},{10... | collective-permute-start | bytes 393224 | tf_op jit(solution)/shard_map/ppermute | solution.py:412
  19.5 7.2 %collective-permute-start.8 = (bf16[512,128]{1,0:T(8,128)(2,1)S(1)}, bf16[512,128]{1,0:T(8,128)(2,1)S(1)}, u32[]{:S(2)}, u32[]{:S(2)}) collective-permute-start(bf16[512,128]{1,0:T(8,128)(2,1)S(1)} %get-tuple-element.80.refs_3_.refs_8_), channel_id=1, source_target_pairs={{0,16},{8,24},{16,0},{24,8},{1,17},{9,25},{17,1},{25,9},{2,18},{10... | collective-permute-start | bytes 393224 | tf_op jit(solution)/shard_map/ppermute | solution.py:412
  20.2 6.5 %collective-permute-start.7 = (bf16[512,128]{1,0:T(8,128)(2,1)S(1)}, bf16[512,128]{1,0:T(8,128)(2,1)S(1)}, u32[]{:S(2)}, u32[]{:S(2)}) collective-permute-start(bf16[512,128]{1,0:T(8,128)(2,1)S(1)} %get-tuple-element.80.refs_3_.refs_8_), channel_id=1, source_target_pairs={{0,24},{8,16},{16,8},{24,0},{1,25},{9,17},{17,9},{25,1},{2,26},{10... | collective-permute-start | bytes 393224 | tf_op jit(solution)/shard_map/ppermute | solution.py:412
  28.2 6.8 %collective-permute-start.10 = (bf16[272,128]{1,0:T(8,128)(2,1)S(1)}, bf16[272,128]{1,0:T(8,128)(2,1)S(1)}, u32[]{:S(2)}, u32[]{:S(2)}) collective-permute-start(bf16[272,128]{1,0:T(8,128)(2,1)S(1)} %get-tuple-element.85), channel_id=1, source_target_pairs={{0,6},{1,7},{2,4},{3,5},{4,2},{5,3},{6,0},{7,1},{8,14},{9,15},{10,... | collective-permute-start | bytes 208904 | tf_op jit(solution)/shard_map/ppermute | solution.py:412
  32.0 5.2 %collective-permute-start.12 = (bf16[272,128]{1,0:T(8,128)(2,1)S(1)}, bf16[272,128]{1,0:T(8,128)(2,1)S(1)}, u32[]{:S(2)}, u32[]{:S(2)}) collective-permute-start(bf16[272,128]{1,0:T(8,128)(2,1)S(1)} %get-tuple-element.87), channel_id=1, source_target_pairs={{0,4},{1,5},{2,6},{3,7},{4,0},{5,1},{6,2},{7,3},{8,12},{9,13},{10,... | collective-permute-start | bytes 208904 | tf_op jit(solution)/shard_map/ppermute | solution.py:412
  37.2 6.1 %collective-permute-start.15 = (bf16[256,128]{1,0:T(8,128)(2,1)S(1)}, bf16[256,128]{1,0:T(8,128)(2,1)S(1)}, u32[]{:S(2)}, u32[]{:S(2)}) collective-permute-start(bf16[256,128]{1,0:T(8,128)(2,1)S(1)} %get-tuple-element.88.refs_3_.refs_20_), channel_id=1, source_target_pairs={{0,6},{1,7},{2,4},{3,5},{4,2},{5,3},{6,0},{7,1},{8,14},{9,15},{10,... | collective-permute-start | bytes 196616 | tf_op jit(solution)/shard_map/ppermute | solution.py:412
  38.3 6.4 %collective-permute-start.14 = (bf16[256,128]{1,0:T(8,128)(2,1)S(1)}, bf16[256,128]{1,0:T(8,128)(2,1)S(1)}, u32[]{:S(2)}, u32[]{:S(2)}) collective-permute-start(bf16[256,128]{1,0:T(8,128)(2,1)S(1)} %get-tuple-element.88.refs_3_.refs_20_), channel_id=1, source_target_pairs={{0,2},{1,3},{2,0},{3,1},{4,6},{5,7},{6,4},{7,5},{8,10},{9,11},{10,... | collective-permute-start | bytes 196616 | tf_op jit(solution)/shard_map/ppermute | solution.py:412
  38.8 5.9 %collective-permute-start.13 = (bf16[256,128]{1,0:T(8,128)(2,1)S(1)}, bf16[256,128]{1,0:T(8,128)(2,1)S(1)}, u32[]{:S(2)}, u32[]{:S(2)}) collective-permute-start(bf16[256,128]{1,0:T(8,128)(2,1)S(1)} %get-tuple-element.88.refs_3_.refs_20_), channel_id=1, source_target_pairs={{0,4},{1,5},{2,6},{3,7},{4,0},{5,1},{6,2},{7,3},{8,12},{9,13},{10,... | collective-permute-start | bytes 196616 | tf_op jit(solution)/shard_map/ppermute | solution.py:412
  46.2 5.2 %collective-permute-start.16 = (bf16[528,128]{1,0:T(8,128)(2,1)S(1)}, bf16[528,128]{1,0:T(8,128)(2,1)S(1)}, u32[]{:S(2)}, u32[]{:S(2)}) collective-permute-start(bf16[528,128]{1,0:T(8,128)(2,1)S(1)} %get-tuple-element.93), channel_id=1, source_target_pairs={{0,8},{8,0},{16,24},{24,16},{1,9},{9,1},{17,25},{25,17},{2,10},{10... | collective-permute-start | bytes 405512 | tf_op jit(solution)/shard_map/ppermute | solution.py:412
  47.2 6.0 %collective-permute-start.17 = (bf16[528,128]{1,0:T(8,128)(2,1)S(1)}, bf16[528,128]{1,0:T(8,128)(2,1)S(1)}, u32[]{:S(2)}, u32[]{:S(2)}) collective-permute-start(bf16[528,128]{1,0:T(8,128)(2,1)S(1)} %get-tuple-element.94), channel_id=1, source_target_pairs={{0,16},{8,24},{16,0},{24,8},{1,17},{9,25},{17,1},{25,9},{2,18},{10... | collective-permute-start | bytes 405512 | tf_op jit(solution)/shard_map/ppermute | solution.py:412
  49.1 6.7 %collective-permute-start.18 = (bf16[528,128]{1,0:T(8,128)(2,1)S(1)}, bf16[528,128]{1,0:T(8,128)(2,1)S(1)}, u32[]{:S(2)}, u32[]{:S(2)}) collective-permute-start(bf16[528,128]{1,0:T(8,128)(2,1)S(1)} %get-tuple-element.95), channel_id=1, source_target_pairs={{0,24},{8,16},{16,8},{24,0},{1,25},{9,17},{17,9},{25,1},{2,26},{10... | collective-permute-start | bytes 405512 | tf_op jit(solution)/shard_map/ppermute | solution.py:412
  57.4 6.4 %collective-permute-start.20 = (bf16[512,128]{1,0:T(8,128)(2,1)S(1)}, bf16[512,128]{1,0:T(8,128)(2,1)S(1)}, u32[]{:S(2)}, u32[]{:S(2)}) collective-permute-start(bf16[512,128]{1,0:T(8,128)(2,1)S(1)} %get-tuple-element.98.refs_3_.refs_12_), channel_id=1, source_target_pairs={{0,16},{8,24},{16,0},{24,8},{1,17},{9,25},{17,1},{25,9},{2,18},{10... | collective-permute-start | bytes 393224 | tf_op jit(solution)/shard_map/ppermute | solution.py:412
  57.4 6.4 %collective-permute-start.19 = (bf16[512,128]{1,0:T(8,128)(2,1)S(1)}, bf16[512,128]{1,0:T(8,128)(2,1)S(1)}, u32[]{:S(2)}, u32[]{:S(2)}) collective-permute-start(bf16[512,128]{1,0:T(8,128)(2,1)S(1)} %get-tuple-element.98.refs_3_.refs_12_), channel_id=1, source_target_pairs={{0,24},{8,16},{16,8},{24,0},{1,25},{9,17},{17,9},{25,1},{2,26},{10... | collective-permute-start | bytes 393224 | tf_op jit(solution)/shard_map/ppermute | solution.py:412
  65.3 6.9 %collective-permute-start.22 = (bf16[272,128]{1,0:T(8,128)(2,1)S(1)}, bf16[272,128]{1,0:T(8,128)(2,1)S(1)}, u32[]{:S(2)}, u32[]{:S(2)}) collective-permute-start(bf16[272,128]{1,0:T(8,128)(2,1)S(1)} %get-tuple-element.103), channel_id=1, source_target_pairs={{0,6},{1,7},{2,4},{3,5},{4,2},{5,3},{6,0},{7,1},{8,14},{9,15},{10,... | collective-permute-start | bytes 208904 | tf_op jit(solution)/shard_map/ppermute | solution.py:412
  67.9 5.2 %collective-permute-start.23 = (bf16[272,128]{1,0:T(8,128)(2,1)S(1)}, bf16[272,128]{1,0:T(8,128)(2,1)S(1)}, u32[]{:S(2)}, u32[]{:S(2)}) collective-permute-start(bf16[272,128]{1,0:T(8,128)(2,1)S(1)} %get-tuple-element.104), channel_id=1, source_target_pairs={{0,2},{1,3},{2,0},{3,1},{4,6},{5,7},{6,4},{7,5},{8,10},{9,11},{10,... | collective-permute-start | bytes 208904 | tf_op jit(solution)/shard_map/ppermute | solution.py:412
  68.5 6.8 %collective-permute-start.24 = (bf16[272,128]{1,0:T(8,128)(2,1)S(1)}, bf16[272,128]{1,0:T(8,128)(2,1)S(1)}, u32[]{:S(2)}, u32[]{:S(2)}) collective-permute-start(bf16[272,128]{1,0:T(8,128)(2,1)S(1)} %get-tuple-element.105), channel_id=1, source_target_pairs={{0,4},{1,5},{2,6},{3,7},{4,0},{5,1},{6,2},{7,3},{8,12},{9,13},{10,... | collective-permute-start | bytes 208904 | tf_op jit(solution)/shard_map/ppermute | solution.py:412
  75.3 6.2 %collective-permute-start.27 = (bf16[256,128]{1,0:T(8,128)(2,1)S(1)}, bf16[256,128]{1,0:T(8,128)(2,1)S(1)}, u32[]{:S(2)}, u32[]{:S(2)}) collective-permute-start(bf16[256,128]{1,0:T(8,128)(2,1)S(1)} %get-tuple-element.107.refs_3_.refs_24_), channel_id=1, source_target_pairs={{0,6},{1,7},{2,4},{3,5},{4,2},{5,3},{6,0},{7,1},{8,14},{9,15},{10,... | collective-permute-start | bytes 196616 | tf_op jit(solution)/shard_map/ppermute | solution.py:412
  77.1 5.8 %collective-permute-start.26 = (bf16[256,128]{1,0:T(8,128)(2,1)S(1)}, bf16[256,128]{1,0:T(8,128)(2,1)S(1)}, u32[]{:S(2)}, u32[]{:S(2)}) collective-permute-start(bf16[256,128]{1,0:T(8,128)(2,1)S(1)} %get-tuple-element.107.refs_3_.refs_24_), channel_id=1, source_target_pairs={{0,2},{1,3},{2,0},{3,1},{4,6},{5,7},{6,4},{7,5},{8,10},{9,11},{10,... | collective-permute-start | bytes 196616 | tf_op jit(solution)/shard_map/ppermute | solution.py:412
  77.1 5.8 %collective-permute-start.25 = (bf16[256,128]{1,0:T(8,128)(2,1)S(1)}, bf16[256,128]{1,0:T(8,128)(2,1)S(1)}, u32[]{:S(2)}, u32[]{:S(2)}) collective-permute-start(bf16[256,128]{1,0:T(8,128)(2,1)S(1)} %get-tuple-element.107.refs_3_.refs_24_), channel_id=1, source_target_pairs={{0,4},{1,5},{2,6},{3,7},{4,0},{5,1},{6,2},{7,3},{8,12},{9,13},{10,... | collective-permute-start | bytes 196616 | tf_op jit(solution)/shard_map/ppermute | solution.py:412
  84.3 5.8 %collective-permute-start.28 = (bf16[528,128]{1,0:T(8,128)(2,1)S(1)}, bf16[528,128]{1,0:T(8,128)(2,1)S(1)}, u32[]{:S(2)}, u32[]{:S(2)}) collective-permute-start(bf16[528,128]{1,0:T(8,128)(2,1)S(1)} %get-tuple-element.112), channel_id=1, source_target_pairs={{0,8},{8,0},{16,24},{24,16},{1,9},{9,1},{17,25},{25,17},{2,10},{10... | collective-permute-start | bytes 405512 | tf_op jit(solution)/shard_map/ppermute | solution.py:412
  85.9 5.4 %collective-permute-start.29 = (bf16[528,128]{1,0:T(8,128)(2,1)S(1)}, bf16[528,128]{1,0:T(8,128)(2,1)S(1)}, u32[]{:S(2)}, u32[]{:S(2)}) collective-permute-start(bf16[528,128]{1,0:T(8,128)(2,1)S(1)} %get-tuple-element.113), channel_id=1, source_target_pairs={{0,16},{8,24},{16,0},{24,8},{1,17},{9,25},{17,1},{25,9},{2,18},{10... | collective-permute-start | bytes 405512 | tf_op jit(solution)/shard_map/ppermute | solution.py:412
  87.1 5.9 %collective-permute-start.30 = (bf16[528,128]{1,0:T(8,128)(2,1)S(1)}, bf16[528,128]{1,0:T(8,128)(2,1)S(1)}, u32[]{:S(2)}, u32[]{:S(2)}) collective-permute-start(bf16[528,128]{1,0:T(8,128)(2,1)S(1)} %get-tuple-element.114), channel_id=1, source_target_pairs={{0,24},{8,16},{16,8},{24,0},{1,25},{9,17},{17,9},{25,1},{2,26},{10... | collective-permute-start | bytes 405512 | tf_op jit(solution)/shard_map/ppermute | solution.py:412
  93.7 6.0 %collective-permute-start.32 = (bf16[512,128]{1,0:T(8,128)(2,1)S(1)}, bf16[512,128]{1,0:T(8,128)(2,1)S(1)}, u32[]{:S(2)}, u32[]{:S(2)}) collective-permute-start(bf16[512,128]{1,0:T(8,128)(2,1)S(1)} %get-tuple-element.117.refs_3_.refs_16_), channel_id=1, source_target_pairs={{0,16},{8,24},{16,0},{24,8},{1,17},{9,25},{17,1},{25,9},{2,18},{10... | collective-permute-start | bytes 393224 | tf_op jit(solution)/shard_map/ppermute | solution.py:412
  94.5 5.9 %collective-permute-start.31 = (bf16[512,128]{1,0:T(8,128)(2,1)S(1)}, bf16[512,128]{1,0:T(8,128)(2,1)S(1)}, u32[]{:S(2)}, u32[]{:S(2)}) collective-permute-start(bf16[512,128]{1,0:T(8,128)(2,1)S(1)} %get-tuple-element.117.refs_3_.refs_16_), channel_id=1, source_target_pairs={{0,24},{8,16},{16,8},{24,0},{1,25},{9,17},{17,9},{25,1},{2,26},{10... | collective-permute-start | bytes 393224 | tf_op jit(solution)/shard_map/ppermute | solution.py:412
  101.9 6.2 %collective-permute-start.34 = (bf16[272,128]{1,0:T(8,128)(2,1)S(1)}, bf16[272,128]{1,0:T(8,128)(2,1)S(1)}, u32[]{:S(2)}, u32[]{:S(2)}) collective-permute-start(bf16[272,128]{1,0:T(8,128)(2,1)S(1)} %get-tuple-element.122), channel_id=1, source_target_pairs={{0,6},{1,7},{2,4},{3,5},{4,2},{5,3},{6,0},{7,1},{8,14},{9,15},{10,... | collective-permute-start | bytes 208904 | tf_op jit(solution)/shard_map/ppermute | solution.py:412
  105.1 6.0 %collective-permute-start.36 = (bf16[272,128]{1,0:T(8,128)(2,1)S(1)}, bf16[272,128]{1,0:T(8,128)(2,1)S(1)}, u32[]{:S(2)}, u32[]{:S(2)}) collective-permute-start(bf16[272,128]{1,0:T(8,128)(2,1)S(1)} %get-tuple-element.124), channel_id=1, source_target_pairs={{0,4},{1,5},{2,6},{3,7},{4,0},{5,1},{6,2},{7,3},{8,12},{9,13},{10,... | collective-permute-start | bytes 208904 | tf_op jit(solution)/shard_map/ppermute | solution.py:412
  111.4 5.2 %collective-permute-start.38 = (bf16[256,128]{1,0:T(8,128)(2,1)S(1)}, bf16[256,128]{1,0:T(8,128)(2,1)S(1)}, u32[]{:S(2)}, u32[]{:S(2)}) collective-permute-start(bf16[256,128]{1,0:T(8,128)(2,1)S(1)} %get-tuple-element.127.refs_0_.refs_28_), channel_id=1, source_target_pairs={{0,4},{1,5},{2,6},{3,7},{4,0},{5,1},{6,2},{7,3},{8,12},{9,13},{10,... | collective-permute-start | bytes 196616 | tf_op jit(solution)/shard_map/ppermute | solution.py:412
  112.2 6.3 %collective-permute-start.37 = (bf16[256,128]{1,0:T(8,128)(2,1)S(1)}, bf16[256,128]{1,0:T(8,128)(2,1)S(1)}, u32[]{:S(2)}, u32[]{:S(2)}) collective-permute-start(bf16[256,128]{1,0:T(8,128)(2,1)S(1)} %get-tuple-element.127.refs_0_.refs_28_), channel_id=1, source_target_pairs={{0,6},{1,7},{2,4},{3,5},{4,2},{5,3},{6,0},{7,1},{8,14},{9,15},{10,... | collective-permute-start | bytes 196616 | tf_op jit(solution)/shard_map/ppermute | solution.py:412
  (17 other events, 126.2 us)

commit v8 on v7

--- a/solution.py
+++ b/solution.py
@@ -12,6 +12,7 @@
 ITERS = 3
 EPSILON = 1e-06
 GROUP = 8
+WIDTH = 4
 TAIL = 16
 VMEM_BYTES = 16 << 20
 
@@ -266,8 +267,8 @@
         low, high = list_ref[k + 2, at_group], list_ref[k + 2, at_group + 1]
 
         def turn_of(group, carry):
-            for lane in range(GROUP):
-                at = low + group * GROUP + lane
+            for lane in range(WIDTH):
+                at = low + group * WIDTH + lane
                 slot = list_ref[k, at]
                 source = list_ref[k + 4, at]
                 target = jnp.where(at < high, list_ref[k + 6, at] + k * way.target_shift, way.spare)
@@ -278,7 +279,7 @@
                 total_ref[goal, :] = total_ref[goal, :] + product
             return carry
 
-        lax.fori_loop(0, (high - low + GROUP - 1) // GROUP, turn_of, 0)
+        lax.fori_loop(0, (high - low + WIDTH - 1) // WIDTH, turn_of, 0)
     if not last:
         refs[0][...] = folded
         return
@@ -422,7 +423,7 @@
 
     def groups_of(order, way):
         half = len(order) // 2
-        return (order[:half], order[half:]) if way.part % way.size == 0 else (order,)
+        return (order[:1], order[1:half], order[half:]) if way.part % way.size == 0 else (order,)
 
     def body(record, tile_data, tile_rows, tile_cols, tile_counts):
         own_tiles = tile_data[0, 0]
@@ -507,12 +508,7 @@
             )
             image = None if last else more.pop()
             betas += more
-            if last:
-                issued = z_order[::-1]
-                arrived = dict(zip(issued, over_z([narrow] * (zs - 1), issued)))
-                chunks = [narrow, *(arrived[o] for o in image_order[1:])]
-            else:
-                chunks = [narrow, *over_z([narrow] * (zs - 1), image_order[1:])]
+            chunks = [narrow, *over_z([narrow] * (zs - 1), image_order[1:])]
             images += chunks
             if last:
                 break
@@ -528,6 +524,7 @@
             gradient = wide[0] if more_steps else None
             alphas.append(alpha)
 
+        chunks = [chunks[image_order.index(o)] for o in (0, *z_order[::-1])]
         (own_norm,) = call(norm_kernel, "norm", [norm], [], *chunks)
         norms = [own_norm] + over_hyd([own_norm] * (hyds - 1), hyd_order[::-1])
         own_x, pair_x, wide_r, narrow_r = call(

time: 131 us -> 130 us (level); the launches traced: 130 us -> 130 us
  waiting for transfers between devices: 52 us -> 43.3 us
  Pallas kernels: 21.8 us -> 30.3 us
    ppermute x45, waiting for transfers between devices: 52 us -> 43.3 us  [swap(): return lax.ppermute(value, axis, [(i, i ^ offset) for i in range(size)])]
    pallas_call x22 -> x27, Pallas kernels: 21.8 us -> 30.3 us  [call(): pl.pallas_call(kernel, name=name, out_shape=[jax.ShapeDtypeStruct(s, d) f...]
  transfers between devices with their start and end apart: 45 -> 45, of which waited for: 32 -> 28; matrix products, arithmetic and copies ran while one was open for 0% -> 0% of each run, Pallas kernels for 8% -> 13%
where the time goes in v8:
time: 130 us
  starting transfers between devices  55.1 us (42%)
  waiting for transfers between devices  43.3 us (33%)
  Pallas kernels  30.3 us (23%)
  between operations  1.58 us (1%)
    ppermute x45, starting transfers between devices, swap(): return lax.ppermute(value, axis, [(i, i ^ offset) for i in range(size)])  55.1 us
    ppermute x45, waiting for transfers between devices, swap(): return lax.ppermute(value, axis, [(i, i ^ offset) for i in range(size)])  43.3 us
    pallas_call x27, Pallas kernels, call(): pl.pallas_call(kernel, name=name, out_shape=[jax.ShapeDtypeStruct(s, d) f...  30.3 us
  transfers between devices with their start and end apart: 45, of which 28 were waited for; matrix products, arithmetic and copies ran while one was open for 0% of the time, Pallas kernels for 13%

profile of v8, /device:TPU:0, one launch (start us, length us, event | category | flops | bytes accessed | tf_op | source)
XLA Modules:
  0.0 130.3 jit_solution(12365764377991106489)
XLA Ops:
  2.5 3.5 %pack.1 = (bf16[24,128,256]{2,1,0:T(8,128)(2,1)S(1)}, f32[1152,128]{1,0:T(8,128)S(1)}, bf16[1024,128]{1,0:T(8,128)(2,1)S(1)}, bf16[1024,128]{1,0:T(8,128)(2,1)S(1)}) custom-call(f32[2,1024,128]{2,1,0:T(8,128)} %record_ref.1, bf16[24,2,128,128]{3,2,1,0:T(8,128)(2,1)} %bitcast.6, s32[1,24]{1,0:T(1,128)} %bitcast.17, s32[1,24]{1,0:T(1,128)} %bitcast.20, ...), custom_call_target="tpu_custom_call" | custom-call | tf_op jit(solution)/shard_map/pack/pallas_call | solution.py:51
  7.5 2.3 %collective-permute-start.4 = (bf16[512,128]{1,0:T(8,128)(2,1)S(1)}, bf16[512,128]{1,0:T(8,128)(2,1)S(1)}, u32[]{:S(2)}, u32[]{:S(2)}) collective-permute-start(bf16[512,128]{1,0:T(8,128)(2,1)S(1)} %get-tuple-element.87), channel_id=1, source_target_pairs={{0,8},{8,0},{16,24},{24,16},{1,9},{9,1},{17,25},{25,17},{2,10},{10... | collective-permute-start | bytes 393224 | tf_op jit(solution)/shard_map/ppermute | solution.py:413
  9.8 1.9 %collective-permute-start.5 = (bf16[512,128]{1,0:T(8,128)(2,1)S(1)}, bf16[512,128]{1,0:T(8,128)(2,1)S(1)}, u32[]{:S(2)}, u32[]{:S(2)}) collective-permute-start(bf16[512,128]{1,0:T(8,128)(2,1)S(1)} %get-tuple-element.88), channel_id=1, source_target_pairs={{0,16},{8,24},{16,0},{24,8},{1,17},{9,25},{17,1},{25,9},{2,18},{10... | collective-permute-start | bytes 393224 | tf_op jit(solution)/shard_map/ppermute | solution.py:413
  11.6 2.0 %collective-permute-done.4.refs_0_ = bf16[512,128]{1,0:T(8,128)(2,1)S(1)} collective-permute-done((bf16[512,128]{1,0:T(8,128)(2,1)S(1)}, bf16[512,128]{1,0:T(8,128)(2,1)S(1)}, u32[]{:S(2)}, u32[]{:S(2)}) %collective-permute-start.4) | collective-permute-done | bytes 131104 | tf_op jit(solution)/shard_map/ppermute | solution.py:413
  13.7 4.2 %collective-permute-done.5.refs_1_ = bf16[512,128]{1,0:T(8,128)(2,1)S(1)} collective-permute-done((bf16[512,128]{1,0:T(8,128)(2,1)S(1)}, bf16[512,128]{1,0:T(8,128)(2,1)S(1)}, u32[]{:S(2)}, u32[]{:S(2)}) %collective-permute-start.5) | collective-permute-done | bytes 131104 | tf_op jit(solution)/shard_map/ppermute | solution.py:413
  26.7 1.8 %forward.11 = (f32[1152,128]{1,0:T(8,128)S(1)}, f32[256,128]{1,0:T(8,128)S(1)}, f32[8,128]{1,0:T(8,128)S(1)}, bf16[272,128]{1,0:T(8,128)(2,1)S(1)}, bf16[272,128...) custom-call(bf16[24,2,128,128]{3,2,1,0:T(8,128)(2,1)S(1)} %bitcast.9, ...), custom_call_target="tpu_custom_call", output_to_operand_aliasing={{0}: (5, {})} | custom-call | tf_op jit(solution)/shard_map/forward/pallas_call | solution.py:51
  28.5 4.0 %collective-permute-start.10 = (bf16[272,128]{1,0:T(8,128)(2,1)S(1)}, bf16[272,128]{1,0:T(8,128)(2,1)S(1)}, u32[]{:S(2)}, u32[]{:S(2)}) collective-permute-start(bf16[272,128]{1,0:T(8,128)(2,1)S(1)} %get-tuple-element.97), channel_id=1, source_target_pairs={{0,6},{1,7},{2,4},{3,5},{4,2},{5,3},{6,0},{7,1},{8,14},{9,15},{10,... | collective-permute-start | bytes 208904 | tf_op jit(solution)/shard_map/ppermute | solution.py:413
  33.2 1.7 %collective-permute-done.10.refs_0_ = bf16[272,128]{1,0:T(8,128)(2,1)S(1)} collective-permute-done((bf16[272,128]{1,0:T(8,128)(2,1)S(1)}, bf16[272,128]{1,0:T(8,128)(2,1)S(1)}, u32[]{:S(2)}, u32[]{:S(2)}) %collective-permute-start.10) | collective-permute-done | bytes 69664 | tf_op jit(solution)/shard_map/ppermute | solution.py:413
  34.9 1.9 %collective-permute-done.11.refs_1_ = bf16[272,128]{1,0:T(8,128)(2,1)S(1)} collective-permute-done((bf16[272,128]{1,0:T(8,128)(2,1)S(1)}, bf16[272,128]{1,0:T(8,128)(2,1)S(1)}, u32[]{:S(2)}, u32[]{:S(2)}) %collective-permute-start.11) | collective-permute-done | bytes 69664 | tf_op jit(solution)/shard_map/ppermute | solution.py:413
  40.0 2.2 %collective-permute-start.13 = (bf16[256,128]{1,0:T(8,128)(2,1)S(1)}, bf16[256,128]{1,0:T(8,128)(2,1)S(1)}, u32[]{:S(2)}, u32[]{:S(2)}) collective-permute-start(bf16[256,128]{1,0:T(8,128)(2,1)S(1)} %get-tuple-element.100.refs_3_.refs_20_), channel_id=1, source_target_pairs={{0,4},{1,5},{2,6},{3,7},{4,0},{5,1},{6,2},{7,3},{8,12},{9,13},{10,... | collective-permute-start | bytes 196616 | tf_op jit(solution)/shard_map/ppermute | solution.py:413
  45.2 2.0 %adjoint.8 = (f32[2176,128]{1,0:T(8,128)S(1)}, f32[512,128]{1,0:T(8,128)S(1)}, f32[8,128]{1,0:T(8,128)S(1)}, bf16[528,128]{1,0:T(8,128)(2,1)S(1)}, bf16[528,128]...) custom-call(bf16[24,128,256]{2,1,0:T(8,128)(2,1)S(1)} %get-tuple-element.80.refs_0_, ...), custom_call_target="tpu_custom_call", output_to_operand_aliasing={{0}: (5, {})} | custom-call | tf_op jit(solution)/shard_map/adjoint/pallas_call | solution.py:51
  47.2 1.9 %collective-permute-start.16 = (bf16[528,128]{1,0:T(8,128)(2,1)S(1)}, bf16[528,128]{1,0:T(8,128)(2,1)S(1)}, u32[]{:S(2)}, u32[]{:S(2)}) collective-permute-start(bf16[528,128]{1,0:T(8,128)(2,1)S(1)} %get-tuple-element.107), channel_id=1, source_target_pairs={{0,8},{8,0},{16,24},{24,16},{1,9},{9,1},{17,25},{25,17},{2,10},{10... | collective-permute-start | bytes 405512 | tf_op jit(solution)/shard_map/ppermute | solution.py:413
  52.2 3.7 %collective-permute-done.17.refs_1_ = bf16[528,128]{1,0:T(8,128)(2,1)S(1)} collective-permute-done((bf16[528,128]{1,0:T(8,128)(2,1)S(1)}, bf16[528,128]{1,0:T(8,128)(2,1)S(1)}, u32[]{:S(2)}, u32[]{:S(2)}) %collective-permute-start.17) | collective-permute-done | bytes 135200 | tf_op jit(solution)/shard_map/ppermute | solution.py:413
  56.1 1.9 %collective-permute-start.21 = (bf16[512,128]{1,0:T(8,128)(2,1)S(1)}, bf16[512,128]{1,0:T(8,128)(2,1)S(1)}, u32[]{:S(2)}, u32[]{:S(2)}) collective-permute-start(bf16[512,128]{1,0:T(8,128)(2,1)S(1)} %get-tuple-element.112.refs_3_.refs_12_), channel_id=1, source_target_pairs={{0,8},{8,0},{16,24},{24,16},{1,9},{9,1},{17,25},{25,17},{2,10},{10... | collective-permute-start | bytes 393224 | tf_op jit(solution)/shard_map/ppermute | solution.py:413
  62.9 1.8 %collective-permute-done.19.refs_3_.refs_14_ = bf16[512,128]{1,0:T(8,128)(2,1)S(1)} collective-permute-done((bf16[512,128]{1,0:T(8,128)(2,1)S(1)}, bf16[512,128]{1,0:T(8,128)(2,1)S(1)}, u32[]{:S(2)}, u32[]{:S(2)}) %collective-permute-start.19) | collective-permute-done | bytes 131104 | tf_op jit(solution)/shard_map/ppermute | solution.py:413
  64.7 1.8 %forward.14 = (f32[1152,128]{1,0:T(8,128)S(1)}, f32[256,128]{1,0:T(8,128)S(1)}, f32[8,128]{1,0:T(8,128)S(1)}, bf16[272,128]{1,0:T(8,128)(2,1)S(1)}, bf16[272,128...) custom-call(bf16[24,2,128,128]{3,2,1,0:T(8,128)(2,1)S(1)} %bitcast.12, ...), custom_call_target="tpu_custom_call", output_to_operand_aliasing={{0}: (5, {})} | custom-call | tf_op jit(solution)/shard_map/forward/pallas_call | solution.py:51
  66.6 4.1 %collective-permute-start.22 = (bf16[272,128]{1,0:T(8,128)(2,1)S(1)}, bf16[272,128]{1,0:T(8,128)(2,1)S(1)}, u32[]{:S(2)}, u32[]{:S(2)}) collective-permute-start(bf16[272,128]{1,0:T(8,128)(2,1)S(1)} %get-tuple-element.119), channel_id=1, source_target_pairs={{0,6},{1,7},{2,4},{3,5},{4,2},{5,3},{6,0},{7,1},{8,14},{9,15},{10,... | collective-permute-start | bytes 208904 | tf_op jit(solution)/shard_map/ppermute | solution.py:413
  71.3 2.4 %collective-permute-done.22.refs_0_ = bf16[272,128]{1,0:T(8,128)(2,1)S(1)} collective-permute-done((bf16[272,128]{1,0:T(8,128)(2,1)S(1)}, bf16[272,128]{1,0:T(8,128)(2,1)S(1)}, u32[]{:S(2)}, u32[]{:S(2)}) %collective-permute-start.22) | collective-permute-done | bytes 69664 | tf_op jit(solution)/shard_map/ppermute | solution.py:413
  73.7 2.3 %collective-permute-done.23.refs_1_ = bf16[272,128]{1,0:T(8,128)(2,1)S(1)} collective-permute-done((bf16[272,128]{1,0:T(8,128)(2,1)S(1)}, bf16[272,128]{1,0:T(8,128)(2,1)S(1)}, u32[]{:S(2)}, u32[]{:S(2)}) %collective-permute-start.23) | collective-permute-done | bytes 69664 | tf_op jit(solution)/shard_map/ppermute | solution.py:413
  78.1 2.4 %collective-permute-start.25 = (bf16[256,128]{1,0:T(8,128)(2,1)S(1)}, bf16[256,128]{1,0:T(8,128)(2,1)S(1)}, u32[]{:S(2)}, u32[]{:S(2)}) collective-permute-start(bf16[256,128]{1,0:T(8,128)(2,1)S(1)} %get-tuple-element.123.refs_3_.refs_24_), channel_id=1, source_target_pairs={{0,4},{1,5},{2,6},{3,7},{4,0},{5,1},{6,2},{7,3},{8,12},{9,13},{10,... | collective-permute-start | bytes 196616 | tf_op jit(solution)/shard_map/ppermute | solution.py:413
  83.5 2.0 %adjoint.11 = (f32[2176,128]{1,0:T(8,128)S(1)}, f32[512,128]{1,0:T(8,128)S(1)}, f32[8,128]{1,0:T(8,128)S(1)}, bf16[528,128]{1,0:T(8,128)(2,1)S(1)}, bf16[528,128...) custom-call(bf16[24,128,256]{2,1,0:T(8,128)(2,1)S(1)} %get-tuple-element.80.refs_0_, ...), custom_call_target="tpu_custom_call", output_to_operand_aliasing={{0}: (5, {})} | custom-call | tf_op jit(solution)/shard_map/adjoint/pallas_call | solution.py:51
  86.4 1.8 %collective-permute-start.29 = (bf16[528,128]{1,0:T(8,128)(2,1)S(1)}, bf16[528,128]{1,0:T(8,128)(2,1)S(1)}, u32[]{:S(2)}, u32[]{:S(2)}) collective-permute-start(bf16[528,128]{1,0:T(8,128)(2,1)S(1)} %get-tuple-element.131), channel_id=1, source_target_pairs={{0,16},{8,24},{16,0},{24,8},{1,17},{9,25},{17,1},{25,9},{2,18},{10... | collective-permute-start | bytes 405512 | tf_op jit(solution)/shard_map/ppermute | solution.py:413
  92.2 1.9 %collective-permute-done.30.refs_2_ = bf16[528,128]{1,0:T(8,128)(2,1)S(1)} collective-permute-done((bf16[528,128]{1,0:T(8,128)(2,1)S(1)}, bf16[528,128]{1,0:T(8,128)(2,1)S(1)}, u32[]{:S(2)}, u32[]{:S(2)}) %collective-permute-start.30) | collective-permute-done | bytes 135200 | tf_op jit(solution)/shard_map/ppermute | solution.py:413
  95.7 2.1 %collective-permute-start.31 = (bf16[512,128]{1,0:T(8,128)(2,1)S(1)}, bf16[512,128]{1,0:T(8,128)(2,1)S(1)}, u32[]{:S(2)}, u32[]{:S(2)}) collective-permute-start(bf16[512,128]{1,0:T(8,128)(2,1)S(1)} %get-tuple-element.135.refs_3_.refs_16_), channel_id=1, source_target_pairs={{0,24},{8,16},{16,8},{24,0},{1,25},{9,17},{17,9},{25,1},{2,26},{10... | collective-permute-start | bytes 393224 | tf_op jit(solution)/shard_map/ppermute | solution.py:413
  101.5 1.8 %forward.17 = (f32[1152,128]{1,0:T(8,128)S(1)}, f32[256,128]{1,0:T(8,128)S(1)}, f32[8,128]{1,0:T(8,128)S(1)}, bf16[272,128]{1,0:T(8,128)(2,1)S(1)}, bf16[272,128...) custom-call(bf16[24,2,128,128]{3,2,1,0:T(8,128)(2,1)S(1)} %bitcast.15, ...), custom_call_target="tpu_custom_call", output_to_operand_aliasing={{0}: (5, {})} | custom-call | tf_op jit(solution)/shard_map/forward/pallas_call | solution.py:51
  103.3 4.0 %collective-permute-start.34 = (bf16[272,128]{1,0:T(8,128)(2,1)S(1)}, bf16[272,128]{1,0:T(8,128)(2,1)S(1)}, u32[]{:S(2)}, u32[]{:S(2)}) collective-permute-start(bf16[272,128]{1,0:T(8,128)(2,1)S(1)} %get-tuple-element.142), channel_id=1, source_target_pairs={{0,6},{1,7},{2,4},{3,5},{4,2},{5,3},{6,0},{7,1},{8,14},{9,15},{10,... | collective-permute-start | bytes 208904 | tf_op jit(solution)/shard_map/ppermute | solution.py:413
  108.0 1.7 %collective-permute-done.34.refs_0_ = bf16[272,128]{1,0:T(8,128)(2,1)S(1)} collective-permute-done((bf16[272,128]{1,0:T(8,128)(2,1)S(1)}, bf16[272,128]{1,0:T(8,128)(2,1)S(1)}, u32[]{:S(2)}, u32[]{:S(2)}) %collective-permute-start.34) | collective-permute-done | bytes 69664 | tf_op jit(solution)/shard_map/ppermute | solution.py:413
  109.8 1.9 %collective-permute-done.35.refs_1_ = bf16[272,128]{1,0:T(8,128)(2,1)S(1)} collective-permute-done((bf16[272,128]{1,0:T(8,128)(2,1)S(1)}, bf16[272,128]{1,0:T(8,128)(2,1)S(1)}, u32[]{:S(2)}, u32[]{:S(2)}) %collective-permute-start.35) | collective-permute-done | bytes 69664 | tf_op jit(solution)/shard_map/ppermute | solution.py:413
  114.8 2.3 %collective-permute-start.37 = (bf16[256,128]{1,0:T(8,128)(2,1)S(1)}, bf16[256,128]{1,0:T(8,128)(2,1)S(1)}, u32[]{:S(2)}, u32[]{:S(2)}) collective-permute-start(bf16[256,128]{1,0:T(8,128)(2,1)S(1)} %get-tuple-element.147.refs_0_.refs_28_), channel_id=1, source_target_pairs={{0,4},{1,5},{2,6},{3,7},{4,0},{5,1},{6,2},{7,3},{8,12},{9,13},{10,... | collective-permute-start | bytes 196616 | tf_op jit(solution)/shard_map/ppermute | solution.py:413
  117.1 1.8 %collective-permute-done.39.refs_3_.refs_29_ = bf16[256,128]{1,0:T(8,128)(2,1)S(1)} collective-permute-done((bf16[256,128]{1,0:T(8,128)(2,1)S(1)}, bf16[256,128]{1,0:T(8,128)(2,1)S(1)}, u32[]{:S(2)}, u32[]{:S(2)}) %collective-permute-start.39) | collective-permute-done | bytes 65568 | tf_op jit(solution)/shard_map/ppermute | solution.py:413
  121.7 1.9 %collective-permute-start.40 = (f32[8,128]{1,0:T(8,128)S(1)}, f32[8,128]{1,0:T(8,128)S(1)}, u32[]{:S(2)}, u32[]{:S(2)}) collective-permute-start(f32[8,128]{1,0:T(8,128)S(1)} %norm.1.refs_0_), channel_id=1, source_target_pairs={{0,24},{8,16},{16,8},{24,0},{1,25},{9,17},{17,9},{25,1},{2,26},{10... | collective-permute-start | bytes 12296 | tf_op jit(solution)/shard_map/ppermute | solution.py:413
  124.1 2.2 %collective-permute-done.40.refs_1_ = f32[8,128]{1,0:T(8,128)S(1)} collective-permute-done((f32[8,128]{1,0:T(8,128)S(1)}, f32[8,128]{1,0:T(8,128)S(1)}, u32[]{:S(2)}, u32[]{:S(2)}) %collective-permute-start.40) | collective-permute-done | bytes 4128 | tf_op jit(solution)/shard_map/ppermute | solution.py:413
  (94 shorter events, 53.3 us)
Async XLA Ops:
  0.6 5.4 %collective-permute-start = (bf16[24,2,128,128]{3,2,1,0:T(8,128)(2,1)}, bf16[24,2,128,128]{3,2,1,0:T(8,128)(2,1)S(1)}, u32[]{:S(2)}, u32[]{:S(2)}) collective-permute-start(bf16[24,2,128,128]{3,2,1,0:T(8,128)(2,1)} %bitcast.5), channel_id=1, source_target_pairs={{0,1},{1,0},{2,3},{3,2},{4,5},{5,4},{6,7},{7,6},{8,9},{9,8},{10,11... | collective-permute-start | bytes 4718600 | tf_op jit(solution)/shard_map/ppermute | solution.py:413
  7.5 6.2 %collective-permute-start.4 = (bf16[512,128]{1,0:T(8,128)(2,1)S(1)}, bf16[512,128]{1,0:T(8,128)(2,1)S(1)}, u32[]{:S(2)}, u32[]{:S(2)}) collective-permute-start(bf16[512,128]{1,0:T(8,128)(2,1)S(1)} %get-tuple-element.87), channel_id=1, source_target_pairs={{0,8},{8,0},{16,24},{24,16},{1,9},{9,1},{17,25},{25,17},{2,10},{10... | collective-permute-start | bytes 393224 | tf_op jit(solution)/shard_map/ppermute | solution.py:413
  9.8 8.1 %collective-permute-start.5 = (bf16[512,128]{1,0:T(8,128)(2,1)S(1)}, bf16[512,128]{1,0:T(8,128)(2,1)S(1)}, u32[]{:S(2)}, u32[]{:S(2)}) collective-permute-start(bf16[512,128]{1,0:T(8,128)(2,1)S(1)} %get-tuple-element.88), channel_id=1, source_target_pairs={{0,16},{8,24},{16,0},{24,8},{1,17},{9,25},{17,1},{25,9},{2,18},{10... | collective-permute-start | bytes 393224 | tf_op jit(solution)/shard_map/ppermute | solution.py:413
  11.6 6.3 %collective-permute-start.6 = (bf16[512,128]{1,0:T(8,128)(2,1)S(1)}, bf16[512,128]{1,0:T(8,128)(2,1)S(1)}, u32[]{:S(2)}, u32[]{:S(2)}) collective-permute-start(bf16[512,128]{1,0:T(8,128)(2,1)S(1)} %get-tuple-element.89), channel_id=1, source_target_pairs={{0,24},{8,16},{16,8},{24,0},{1,25},{9,17},{17,9},{25,1},{2,26},{10... | collective-permute-start | bytes 393224 | tf_op jit(solution)/shard_map/ppermute | solution.py:413
  18.0 5.8 %collective-permute-start.9 = (bf16[512,128]{1,0:T(8,128)(2,1)S(1)}, bf16[512,128]{1,0:T(8,128)(2,1)S(1)}, u32[]{:S(2)}, u32[]{:S(2)}) collective-permute-start(bf16[512,128]{1,0:T(8,128)(2,1)S(1)} %get-tuple-element.90.refs_3_.refs_8_), channel_id=1, source_target_pairs={{0,8},{8,0},{16,24},{24,16},{1,9},{9,1},{17,25},{25,17},{2,10},{10... | collective-permute-start | bytes 393224 | tf_op jit(solution)/shard_map/ppermute | solution.py:413
  19.5 7.2 %collective-permute-start.8 = (bf16[512,128]{1,0:T(8,128)(2,1)S(1)}, bf16[512,128]{1,0:T(8,128)(2,1)S(1)}, u32[]{:S(2)}, u32[]{:S(2)}) collective-permute-start(bf16[512,128]{1,0:T(8,128)(2,1)S(1)} %get-tuple-element.90.refs_3_.refs_8_), channel_id=1, source_target_pairs={{0,16},{8,24},{16,0},{24,8},{1,17},{9,25},{17,1},{25,9},{2,18},{10... | collective-permute-start | bytes 393224 | tf_op jit(solution)/shard_map/ppermute | solution.py:413
  20.1 6.5 %collective-permute-start.7 = (bf16[512,128]{1,0:T(8,128)(2,1)S(1)}, bf16[512,128]{1,0:T(8,128)(2,1)S(1)}, u32[]{:S(2)}, u32[]{:S(2)}) collective-permute-start(bf16[512,128]{1,0:T(8,128)(2,1)S(1)} %get-tuple-element.90.refs_3_.refs_8_), channel_id=1, source_target_pairs={{0,24},{8,16},{16,8},{24,0},{1,25},{9,17},{17,9},{25,1},{2,26},{10... | collective-permute-start | bytes 393224 | tf_op jit(solution)/shard_map/ppermute | solution.py:413
  28.5 6.4 %collective-permute-start.10 = (bf16[272,128]{1,0:T(8,128)(2,1)S(1)}, bf16[272,128]{1,0:T(8,128)(2,1)S(1)}, u32[]{:S(2)}, u32[]{:S(2)}) collective-permute-start(bf16[272,128]{1,0:T(8,128)(2,1)S(1)} %get-tuple-element.97), channel_id=1, source_target_pairs={{0,6},{1,7},{2,4},{3,5},{4,2},{5,3},{6,0},{7,1},{8,14},{9,15},{10,... | collective-permute-start | bytes 208904 | tf_op jit(solution)/shard_map/ppermute | solution.py:413
  32.5 5.2 %collective-permute-start.12 = (bf16[272,128]{1,0:T(8,128)(2,1)S(1)}, bf16[272,128]{1,0:T(8,128)(2,1)S(1)}, u32[]{:S(2)}, u32[]{:S(2)}) collective-permute-start(bf16[272,128]{1,0:T(8,128)(2,1)S(1)} %get-tuple-element.99), channel_id=1, source_target_pairs={{0,4},{1,5},{2,6},{3,7},{4,0},{5,1},{6,2},{7,3},{8,12},{9,13},{10,... | collective-permute-start | bytes 208904 | tf_op jit(solution)/shard_map/ppermute | solution.py:413
  37.8 6.2 %collective-permute-start.15 = (bf16[256,128]{1,0:T(8,128)(2,1)S(1)}, bf16[256,128]{1,0:T(8,128)(2,1)S(1)}, u32[]{:S(2)}, u32[]{:S(2)}) collective-permute-start(bf16[256,128]{1,0:T(8,128)(2,1)S(1)} %get-tuple-element.100.refs_3_.refs_20_), channel_id=1, source_target_pairs={{0,6},{1,7},{2,4},{3,5},{4,2},{5,3},{6,0},{7,1},{8,14},{9,15},{10,... | collective-permute-start | bytes 196616 | tf_op jit(solution)/shard_map/ppermute | solution.py:413
  39.5 5.7 %collective-permute-start.14 = (bf16[256,128]{1,0:T(8,128)(2,1)S(1)}, bf16[256,128]{1,0:T(8,128)(2,1)S(1)}, u32[]{:S(2)}, u32[]{:S(2)}) collective-permute-start(bf16[256,128]{1,0:T(8,128)(2,1)S(1)} %get-tuple-element.100.refs_3_.refs_20_), channel_id=1, source_target_pairs={{0,2},{1,3},{2,0},{3,1},{4,6},{5,7},{6,4},{7,5},{8,10},{9,11},{10,... | collective-permute-start | bytes 196616 | tf_op jit(solution)/shard_map/ppermute | solution.py:413
  49.1 6.9 %collective-permute-start.17 = (bf16[528,128]{1,0:T(8,128)(2,1)S(1)}, bf16[528,128]{1,0:T(8,128)(2,1)S(1)}, u32[]{:S(2)}, u32[]{:S(2)}) collective-permute-start(bf16[528,128]{1,0:T(8,128)(2,1)S(1)} %get-tuple-element.108), channel_id=1, source_target_pairs={{0,16},{8,24},{16,0},{24,8},{1,17},{9,25},{17,1},{25,9},{2,18},{10... | collective-permute-start | bytes 405512 | tf_op jit(solution)/shard_map/ppermute | solution.py:413
  49.1 6.9 %collective-permute-start.18 = (bf16[528,128]{1,0:T(8,128)(2,1)S(1)}, bf16[528,128]{1,0:T(8,128)(2,1)S(1)}, u32[]{:S(2)}, u32[]{:S(2)}) collective-permute-start(bf16[528,128]{1,0:T(8,128)(2,1)S(1)} %get-tuple-element.109), channel_id=1, source_target_pairs={{0,24},{8,16},{16,8},{24,0},{1,25},{9,17},{17,9},{25,1},{2,26},{10... | collective-permute-start | bytes 405512 | tf_op jit(solution)/shard_map/ppermute | solution.py:413
  56.1 5.7 %collective-permute-start.21 = (bf16[512,128]{1,0:T(8,128)(2,1)S(1)}, bf16[512,128]{1,0:T(8,128)(2,1)S(1)}, u32[]{:S(2)}, u32[]{:S(2)}) collective-permute-start(bf16[512,128]{1,0:T(8,128)(2,1)S(1)} %get-tuple-element.112.refs_3_.refs_12_), channel_id=1, source_target_pairs={{0,8},{8,0},{16,24},{24,16},{1,9},{9,1},{17,25},{25,17},{2,10},{10... | collective-permute-start | bytes 393224 | tf_op jit(solution)/shard_map/ppermute | solution.py:413
  58.9 5.9 %collective-permute-start.19 = (bf16[512,128]{1,0:T(8,128)(2,1)S(1)}, bf16[512,128]{1,0:T(8,128)(2,1)S(1)}, u32[]{:S(2)}, u32[]{:S(2)}) collective-permute-start(bf16[512,128]{1,0:T(8,128)(2,1)S(1)} %get-tuple-element.112.refs_3_.refs_12_), channel_id=1, source_target_pairs={{0,24},{8,16},{16,8},{24,0},{1,25},{9,17},{17,9},{25,1},{2,26},{10... | collective-permute-start | bytes 393224 | tf_op jit(solution)/shard_map/ppermute | solution.py:413
  66.6 7.1 %collective-permute-start.22 = (bf16[272,128]{1,0:T(8,128)(2,1)S(1)}, bf16[272,128]{1,0:T(8,128)(2,1)S(1)}, u32[]{:S(2)}, u32[]{:S(2)}) collective-permute-start(bf16[272,128]{1,0:T(8,128)(2,1)S(1)} %get-tuple-element.119), channel_id=1, source_target_pairs={{0,6},{1,7},{2,4},{3,5},{4,2},{5,3},{6,0},{7,1},{8,14},{9,15},{10,... | collective-permute-start | bytes 208904 | tf_op jit(solution)/shard_map/ppermute | solution.py:413
  70.7 5.4 %collective-permute-start.23 = (bf16[272,128]{1,0:T(8,128)(2,1)S(1)}, bf16[272,128]{1,0:T(8,128)(2,1)S(1)}, u32[]{:S(2)}, u32[]{:S(2)}) collective-permute-start(bf16[272,128]{1,0:T(8,128)(2,1)S(1)} %get-tuple-element.120), channel_id=1, source_target_pairs={{0,2},{1,3},{2,0},{3,1},{4,6},{5,7},{6,4},{7,5},{8,10},{9,11},{10,... | collective-permute-start | bytes 208904 | tf_op jit(solution)/shard_map/ppermute | solution.py:413
  70.7 5.4 %collective-permute-start.24 = (bf16[272,128]{1,0:T(8,128)(2,1)S(1)}, bf16[272,128]{1,0:T(8,128)(2,1)S(1)}, u32[]{:S(2)}, u32[]{:S(2)}) collective-permute-start(bf16[272,128]{1,0:T(8,128)(2,1)S(1)} %get-tuple-element.121), channel_id=1, source_target_pairs={{0,4},{1,5},{2,6},{3,7},{4,0},{5,1},{6,2},{7,3},{8,12},{9,13},{10,... | collective-permute-start | bytes 208904 | tf_op jit(solution)/shard_map/ppermute | solution.py:413
  76.1 6.2 %collective-permute-start.27 = (bf16[256,128]{1,0:T(8,128)(2,1)S(1)}, bf16[256,128]{1,0:T(8,128)(2,1)S(1)}, u32[]{:S(2)}, u32[]{:S(2)}) collective-permute-start(bf16[256,128]{1,0:T(8,128)(2,1)S(1)} %get-tuple-element.123.refs_3_.refs_24_), channel_id=1, source_target_pairs={{0,6},{1,7},{2,4},{3,5},{4,2},{5,3},{6,0},{7,1},{8,14},{9,15},{10,... | collective-permute-start | bytes 196616 | tf_op jit(solution)/shard_map/ppermute | solution.py:413
  77.7 5.8 %collective-permute-start.26 = (bf16[256,128]{1,0:T(8,128)(2,1)S(1)}, bf16[256,128]{1,0:T(8,128)(2,1)S(1)}, u32[]{:S(2)}, u32[]{:S(2)}) collective-permute-start(bf16[256,128]{1,0:T(8,128)(2,1)S(1)} %get-tuple-element.123.refs_3_.refs_24_), channel_id=1, source_target_pairs={{0,2},{1,3},{2,0},{3,1},{4,6},{5,7},{6,4},{7,5},{8,10},{9,11},{10,... | collective-permute-start | bytes 196616 | tf_op jit(solution)/shard_map/ppermute | solution.py:413
  78.1 5.4 %collective-permute-start.25 = (bf16[256,128]{1,0:T(8,128)(2,1)S(1)}, bf16[256,128]{1,0:T(8,128)(2,1)S(1)}, u32[]{:S(2)}, u32[]{:S(2)}) collective-permute-start(bf16[256,128]{1,0:T(8,128)(2,1)S(1)} %get-tuple-element.123.refs_3_.refs_24_), channel_id=1, source_target_pairs={{0,4},{1,5},{2,6},{3,7},{4,0},{5,1},{6,2},{7,3},{8,12},{9,13},{10,... | collective-permute-start | bytes 196616 | tf_op jit(solution)/shard_map/ppermute | solution.py:413
  85.5 5.2 %collective-permute-start.28 = (bf16[528,128]{1,0:T(8,128)(2,1)S(1)}, bf16[528,128]{1,0:T(8,128)(2,1)S(1)}, u32[]{:S(2)}, u32[]{:S(2)}) collective-permute-start(bf16[528,128]{1,0:T(8,128)(2,1)S(1)} %get-tuple-element.130), channel_id=1, source_target_pairs={{0,8},{8,0},{16,24},{24,16},{1,9},{9,1},{17,25},{25,17},{2,10},{10... | collective-permute-start | bytes 405512 | tf_op jit(solution)/shard_map/ppermute | solution.py:413
  86.4 5.8 %collective-permute-start.29 = (bf16[528,128]{1,0:T(8,128)(2,1)S(1)}, bf16[528,128]{1,0:T(8,128)(2,1)S(1)}, u32[]{:S(2)}, u32[]{:S(2)}) collective-permute-start(bf16[528,128]{1,0:T(8,128)(2,1)S(1)} %get-tuple-element.131), channel_id=1, source_target_pairs={{0,16},{8,24},{16,0},{24,8},{1,17},{9,25},{17,1},{25,9},{2,18},{10... | collective-permute-start | bytes 405512 | tf_op jit(solution)/shard_map/ppermute | solution.py:413
  88.2 5.9 %collective-permute-start.30 = (bf16[528,128]{1,0:T(8,128)(2,1)S(1)}, bf16[528,128]{1,0:T(8,128)(2,1)S(1)}, u32[]{:S(2)}, u32[]{:S(2)}) collective-permute-start(bf16[528,128]{1,0:T(8,128)(2,1)S(1)} %get-tuple-element.132), channel_id=1, source_target_pairs={{0,24},{8,16},{16,8},{24,0},{1,25},{9,17},{17,9},{25,1},{2,26},{10... | collective-permute-start | bytes 405512 | tf_op jit(solution)/shard_map/ppermute | solution.py:413
  94.2 5.2 %collective-permute-start.33 = (bf16[512,128]{1,0:T(8,128)(2,1)S(1)}, bf16[512,128]{1,0:T(8,128)(2,1)S(1)}, u32[]{:S(2)}, u32[]{:S(2)}) collective-permute-start(bf16[512,128]{1,0:T(8,128)(2,1)S(1)} %get-tuple-element.135.refs_3_.refs_16_), channel_id=1, source_target_pairs={{0,8},{8,0},{16,24},{24,16},{1,9},{9,1},{17,25},{25,17},{2,10},{10... | collective-permute-start | bytes 393224 | tf_op jit(solution)/shard_map/ppermute | solution.py:413
  94.7 5.9 %collective-permute-start.32 = (bf16[512,128]{1,0:T(8,128)(2,1)S(1)}, bf16[512,128]{1,0:T(8,128)(2,1)S(1)}, u32[]{:S(2)}, u32[]{:S(2)}) collective-permute-start(bf16[512,128]{1,0:T(8,128)(2,1)S(1)} %get-tuple-element.135.refs_3_.refs_16_), channel_id=1, source_target_pairs={{0,16},{8,24},{16,0},{24,8},{1,17},{9,25},{17,1},{25,9},{2,18},{10... | collective-permute-start | bytes 393224 | tf_op jit(solution)/shard_map/ppermute | solution.py:413
  95.7 5.9 %collective-permute-start.31 = (bf16[512,128]{1,0:T(8,128)(2,1)S(1)}, bf16[512,128]{1,0:T(8,128)(2,1)S(1)}, u32[]{:S(2)}, u32[]{:S(2)}) collective-permute-start(bf16[512,128]{1,0:T(8,128)(2,1)S(1)} %get-tuple-element.135.refs_3_.refs_16_), channel_id=1, source_target_pairs={{0,24},{8,16},{16,8},{24,0},{1,25},{9,17},{17,9},{25,1},{2,26},{10... | collective-permute-start | bytes 393224 | tf_op jit(solution)/shard_map/ppermute | solution.py:413
  103.3 6.4 %collective-permute-start.34 = (bf16[272,128]{1,0:T(8,128)(2,1)S(1)}, bf16[272,128]{1,0:T(8,128)(2,1)S(1)}, u32[]{:S(2)}, u32[]{:S(2)}) collective-permute-start(bf16[272,128]{1,0:T(8,128)(2,1)S(1)} %get-tuple-element.142), channel_id=1, source_target_pairs={{0,6},{1,7},{2,4},{3,5},{4,2},{5,3},{6,0},{7,1},{8,14},{9,15},{10,... | collective-permute-start | bytes 208904 | tf_op jit(solution)/shard_map/ppermute | solution.py:413
  107.4 5.2 %collective-permute-start.36 = (bf16[272,128]{1,0:T(8,128)(2,1)S(1)}, bf16[272,128]{1,0:T(8,128)(2,1)S(1)}, u32[]{:S(2)}, u32[]{:S(2)}) collective-permute-start(bf16[272,128]{1,0:T(8,128)(2,1)S(1)} %get-tuple-element.144), channel_id=1, source_target_pairs={{0,4},{1,5},{2,6},{3,7},{4,0},{5,1},{6,2},{7,3},{8,12},{9,13},{10,... | collective-permute-start | bytes 208904 | tf_op jit(solution)/shard_map/ppermute | solution.py:413
  112.6 6.2 %collective-permute-start.39 = (bf16[256,128]{1,0:T(8,128)(2,1)S(1)}, bf16[256,128]{1,0:T(8,128)(2,1)S(1)}, u32[]{:S(2)}, u32[]{:S(2)}) collective-permute-start(bf16[256,128]{1,0:T(8,128)(2,1)S(1)} %get-tuple-element.147.refs_0_.refs_28_), channel_id=1, source_target_pairs={{0,6},{1,7},{2,4},{3,5},{4,2},{5,3},{6,0},{7,1},{8,14},{9,15},{10,... | collective-permute-start | bytes 196616 | tf_op jit(solution)/shard_map/ppermute | solution.py:413
  114.3 5.7 %collective-permute-start.38 = (bf16[256,128]{1,0:T(8,128)(2,1)S(1)}, bf16[256,128]{1,0:T(8,128)(2,1)S(1)}, u32[]{:S(2)}, u32[]{:S(2)}) collective-permute-start(bf16[256,128]{1,0:T(8,128)(2,1)S(1)} %get-tuple-element.147.refs_0_.refs_28_), channel_id=1, source_target_pairs={{0,2},{1,3},{2,0},{3,1},{4,6},{5,7},{6,4},{7,5},{8,10},{9,11},{10,... | collective-permute-start | bytes 196616 | tf_op jit(solution)/shard_map/ppermute | solution.py:413
  114.8 5.2 %collective-permute-start.37 = (bf16[256,128]{1,0:T(8,128)(2,1)S(1)}, bf16[256,128]{1,0:T(8,128)(2,1)S(1)}, u32[]{:S(2)}, u32[]{:S(2)}) collective-permute-start(bf16[256,128]{1,0:T(8,128)(2,1)S(1)} %get-tuple-element.147.refs_0_.refs_28_), channel_id=1, source_target_pairs={{0,4},{1,5},{2,6},{3,7},{4,0},{5,1},{6,2},{7,3},{8,12},{9,13},{10,... | collective-permute-start | bytes 196616 | tf_op jit(solution)/shard_map/ppermute | solution.py:413
  (17 other events, 123.7 us)

commit v9 on v8

--- a/solution.py
+++ b/solution.py
@@ -12,7 +12,8 @@
 ITERS = 3
 EPSILON = 1e-06
 GROUP = 8
-WIDTH = 4
+WIDTH = 8
+LAST_WIDTH = 12
 TAIL = 16
 VMEM_BYTES = 16 << 20
 
@@ -137,9 +138,9 @@
 
 
 def pack_kernel(core_axis, tiles, record_hbm, tile_hbm, row_hbm, col_hbm, used_ref, *refs):
-    turned_tile_ref, total_ref, plain_ref, turned_ref, record_ref, tile_ref, row_ref, col_ref, record_sem, tile_sem, index_sem = refs
+    tile_ref, turned_tile_ref, total_ref, plain_ref, turned_ref, record_ref, row_ref, col_ref, record_sem, tile_sem, index_sem = refs
     core = lax.rem(lax.axis_index(core_axis), 2)
-    rows, slot_count = plain_ref.shape[0], tile_ref.shape[0]
+    rows, slot_count = plain_ref.shape[0], tile_hbm.shape[0]
     pieces = record_sem.shape[0]
     piece, groups = rows // pieces, slot_count // GROUP
 
@@ -169,7 +170,7 @@
         put_chunk(packed.astype(BF16), plain_ref, turned_ref, span, -1.0)
     for copy in index_copies:
         copy.wait()
-    step = turn_step(tiles, tile_ref, turned_tile_ref, total_ref, plain_ref, turned_ref)
+    step = turn_step(tiles, tile_ref, turned_tile_ref, 0, total_ref, plain_ref, turned_ref)
     for k in range(groups):
         tile_copy(k).wait()
 
@@ -178,29 +179,33 @@
             group_of((row_ref.at[0], col_ref.at[0], used_ref.at[0]), k, step)
 
 
-def turn_step(tiles, tile_ref, turned_tile_ref, total_ref, plain_ref, turned_ref):
+def turn_step(tiles, tile_ref, turned_tile_ref, begin, total_ref, plain_ref, turned_ref):
     def step(slot, valid, row, col):
         weights = jnp.concatenate([tile_ref[slot, 0].T, tile_ref[slot, 1].T], axis=1)
-        turned_tile_ref[slot] = weights
+        turned_tile_ref[begin + slot] = weights
         add_tile(total_ref, weights, plain_ref, turned_ref, row, jnp.where(valid, col, tiles))
 
     return step
 
 
-def first_adjoint_kernel(hyd_axis, order, tiles, tile_ref, row_vmem, col_vmem, used_vmem, own_total_ref, plain_ref, turned_ref, *refs):
-    turned_tile_ref, own_ref, sends = refs[0], refs[1], refs[2:-5]
-    total_ref, *index, index_sem = refs[-5:]
+def first_adjoint_kernel(hyd_axis, order, tiles, tile_ref, row_vmem, col_vmem, used_vmem, _, __, own_total_ref, plain_ref, turned_ref, *refs):
+    tiles_ref, turned_tile_ref, own_ref, sends = refs[0], refs[1], refs[2], refs[3:-6]
+    total_ref, *index, index_sem, tile_sem = refs[-6:]
     copies = [
         pltpu.make_async_copy(source, target, index_sem.at[k])
         for k, (source, target) in enumerate(zip((row_vmem, col_vmem, used_vmem), index))
     ]
     for copy in copies:
         copy.start()
+    count = tile_ref.shape[0]
+    join = pltpu.make_async_copy(tile_ref, tiles_ref.at[pl.ds(count, count)], tile_sem.at[0])
+    join.start()
     total_ref[...] = jnp.zeros_like(total_ref)
     for copy in copies:
         copy.wait()
-    slots([ref.at[0] for ref in index], turn_step(tiles, tile_ref, turned_tile_ref, total_ref, plain_ref, turned_ref))
+    slots([ref.at[0] for ref in index], turn_step(tiles, tile_ref, turned_tile_ref, count, total_ref, plain_ref, turned_ref))
     give_columns(hyd_axis, order, own_total_ref, total_ref, own_ref, sends)
+    join.wait()
 
 
 def give_columns(hyd_axis, order, first_ref, second_ref, own_ref, sends):
@@ -219,37 +224,45 @@
     slot_count = refs[0].shape[1]
     square = (slot_count, slot_count)
     down, along = (lax.broadcasted_iota(jnp.int32, square, k) for k in (0, 1))
-    down_f, along_f, here = down.astype(F32), along.astype(F32), down == along
+    here = down == along
+
+    def stand(row):
+        return jnp.sum(jnp.where(here, jnp.broadcast_to(row, square), 0.0), axis=1, keepdims=True)
+
+    def count(condition):
+        return jnp.sum(jnp.where(condition, 1.0, 0.0), axis=1, keepdims=True)
+
     for list_ref, (way, groups) in zip(lists, plans):
         wide = lax.broadcasted_iota(jnp.int32, (slot_count, list_ref.shape[1]), 1).astype(F32)
-        slot_f = lax.broadcasted_iota(jnp.int32, wide.shape, 0).astype(F32)
         place = way.source_place()
-        for k, index in enumerate(indices):
+        keys = []
+        for index in indices:
             offset = (index[way.source][...] * way.size // way.part) ^ place
             bucket = jnp.zeros(offset.shape, F32)
             for at, group in enumerate(groups):
                 for member in group:
                     bucket = jnp.where(offset == member, float(at), bucket)
-            bucket = jnp.where(along[:1, :] < jnp.broadcast_to(index[2][...], (1, slot_count)), bucket, float(len(groups)))
-            key = jnp.broadcast_to(bucket, square)
-            order_along = key * slot_count + along_f
-            key_down = jnp.sum(jnp.where(here, key, 0.0), axis=1, keepdims=True)
-            order_down = key_down * slot_count + down_f[:, :1]
-            rank = jnp.sum(jnp.where(order_along < order_down, 1.0, 0.0), axis=1, keepdims=True)
-            order = jnp.sum(jnp.where(rank == wide, slot_f, 0.0), axis=0, keepdims=True)
-            begin = jnp.sum(jnp.where(key_down < wide, 1.0, 0.0), axis=0, keepdims=True)
-            ordered = rank == wide
-            rows = [order, begin]
-            for which in (way.source, 1 - way.source):
-                value = jnp.broadcast_to(index[which][...].astype(F32), square)
-                value_down = jnp.sum(jnp.where(here, value, 0.0), axis=1, keepdims=True)
-                rows.append(jnp.sum(jnp.where(ordered, value_down, 0.0), axis=0, keepdims=True))
-            for at, row in enumerate(rows):
-                list_ref[2 * at + k : 2 * at + k + 1, :] = row.astype(jnp.int32)
+            used = along[:1, :] < jnp.broadcast_to(index[2][...], (1, slot_count))
+            bucket = jnp.where(used, bucket, float(len(groups)))
+            keys.append((jnp.broadcast_to(bucket, square), stand(bucket)))
+        rows = [jnp.zeros((1, list_ref.shape[1]), F32) for _ in range(4)]
+        for k, index in enumerate(indices):
+            (key, key_down), (other, _) = keys[k], keys[1 - k]
+            place_down = count((key < key_down) | ((key == key_down) & (along < down)))
+            place_down += count(other <= key_down) if k else count(other < key_down)
+            source = index[way.source][...].astype(F32) + float(k * (way.halves - 1) * (way.length // way.size))
+            target = index[1 - way.source][...].astype(F32) + float(k * way.target_shift)
+            slot = (down[:, :1] + k * slot_count).astype(F32)
+            found = place_down == wide
+            for at, value in ((0, slot), (2, stand(source)), (3, stand(target))):
+                rows[at] = rows[at] + jnp.sum(jnp.where(found, value, 0.0), axis=0, keepdims=True)
+            rows[1] = rows[1] + jnp.sum(jnp.where(key_down < wide, 1.0, 0.0), axis=0, keepdims=True)
+        for at, row in enumerate(rows):
+            list_ref[at : at + 1, :] = row.astype(jnp.int32)
 
 
 def step_kernel(way, pick, at_group, last, *refs):
-    (tile_a, tile_b, list_ref), refs = refs[:3], refs[3:]
+    (tile_ref, list_ref), refs = refs[:2], refs[2:]
     chunks, refs = refs[: len(pick)], refs[len(pick) :]
     if at_group:
         folded, refs = refs[1][...], refs[2:]
@@ -263,23 +276,21 @@
         for half in range(way.halves):
             at = pl.ds(pl.multiple_of((here ^ offset) * way.part + half * way.length, way.part), way.part)
             folded += put_chunk(chunk[half * way.part : (half + 1) * way.part, :], plain_ref, turned_ref, at, way.sign)
-    for k, tile_ref in enumerate((tile_a, tile_b)):
-        low, high = list_ref[k + 2, at_group], list_ref[k + 2, at_group + 1]
-
-        def turn_of(group, carry):
-            for lane in range(WIDTH):
-                at = low + group * WIDTH + lane
-                slot = list_ref[k, at]
-                source = list_ref[k + 4, at]
-                target = jnp.where(at < high, list_ref[k + 6, at] + k * way.target_shift, way.spare)
-                span = pl.ds(pl.multiple_of(source * way.size + k * (way.halves - 1) * way.length, way.size), way.size)
-                right = jnp.concatenate([plain_ref[span, :], turned_ref[span, :]], axis=0)
-                goal = spans(way.size, target)
-                product = jnp.dot(way.weights(tile_ref, slot), right, preferred_element_type=F32)
-                total_ref[goal, :] = total_ref[goal, :] + product
-            return carry
-
-        lax.fori_loop(0, (high - low + WIDTH - 1) // WIDTH, turn_of, 0)
+    low, high = list_ref[1, at_group], list_ref[1, at_group + 1]
+    width = LAST_WIDTH if last else WIDTH
+
+    def turn_of(group, carry):
+        for lane in range(width):
+            at = low + group * width + lane
+            target = jnp.where(at < high, list_ref[3, at], way.spare)
+            span = spans(way.size, list_ref[2, at])
+            right = jnp.concatenate([plain_ref[span, :], turned_ref[span, :]], axis=0)
+            goal = spans(way.size, target)
+            product = jnp.dot(way.weights(tile_ref, list_ref[0, at]), right, preferred_element_type=F32)
+            total_ref[goal, :] = total_ref[goal, :] + product
+        return carry
+
+    lax.fori_loop(0, (high - low + width - 1) // width, turn_of, 0)
     if not last:
         refs[0][...] = folded
         return
@@ -443,19 +454,19 @@
         pair_index = tuple(swap(v, "src", srcs, 1) for v in index)
         pieces, groups = 4, slot_count // GROUP
         table = [(v.shape, jnp.int32) for v in index]
-        turned_shape = ((slot_count, size, 2 * size), BF16)
-        turned_own, total, plain, turned = call(
+        joined = [((2 * slot_count, 2, size, size), BF16), ((2 * slot_count, size, 2 * size), BF16)]
+        both_tiles, both_turned, total, plain, turned = call(
             functools.partial(pack_kernel, "src", col_tiles), "pack",
-            [turned_shape, col_total, vector(rows, BF16), vector(rows, BF16)],
-            [(record.shape, F32), (own_tiles.shape, BF16)] + table[:2]
-            + [(n, pltpu.SemaphoreType.DMA) for n in (pieces, groups, 2)],
+            [*joined, col_total, vector(rows, BF16), vector(rows, BF16)],
+            [(record.shape, F32)] + table[:2] + [(n, pltpu.SemaphoreType.DMA) for n in (pieces, groups, 2)],
             record, own_tiles, *index, away=4,
         )
-        turned_pair, own, *sends = call(
+        both_tiles, both_turned, own, *sends = call(
             functools.partial(first_adjoint_kernel, "hyd", hyd_order, col_tiles), "first_adjoint",
-            [turned_shape, vector(2 * col_part, F32)] + [vector(2 * col_part, BF16)] * (hyds - 1),
-            [col_total] + table + [(len(table), pltpu.SemaphoreType.DMA)],
-            pair_tiles, *(pltpu.with_memory_space_constraint(v, pltpu.VMEM) for v in pair_index), total, plain, turned, vector=True,
+            [*joined, vector(2 * col_part, F32)] + [vector(2 * col_part, BF16)] * (hyds - 1),
+            [col_total] + table + [(len(table), pltpu.SemaphoreType.DMA), (1, pltpu.SemaphoreType.DMA)],
+            pair_tiles, *(pltpu.with_memory_space_constraint(v, pltpu.VMEM) for v in pair_index),
+            both_tiles, both_turned, total, plain, turned, vector=True, alias={4: 0, 5: 1},
         )
         gradient, narrow = call(
             functools.partial(start_kernel, hyds - 1), "start",
@@ -486,8 +497,8 @@
                 carry = call(
                     functools.partial(step_kernel, way, group, k, last), name,
                     [total] + (outs if last else [norm]), [vector(way.halves * way.length, BF16)] * 2,
-                    *tiles, slot_list, *chunks[at : at + len(group)], *carry,
-                    alias={3 + len(group): 0} if k else None,
+                    tiles, slot_list, *chunks[at : at + len(group)], *carry,
+                    alias={2 + len(group): 0} if k else None,
                 )
                 at += len(group)
             return carry[1:]
@@ -499,7 +510,7 @@
             chunks = [narrow, *over_hyd([narrow] * (hyds - 1), g_order[1:])]
             g_chunks += chunks
             own, own_norm, *sends = apply(
-                forward, "forward", (own_tiles, pair_tiles), lists[0], chunks, g_groups, [vector(row_part, F32), norm] + row_sends
+                forward, "forward", both_tiles, lists[0], chunks, g_groups, [vector(row_part, F32), norm] + row_sends
             )
             narrow, gamma, *more = call(
                 functools.partial(image_kernel, zs - 1, step > 0, last), "image",
@@ -513,7 +524,7 @@
             if last:
                 break
             own, own_norm, *sends = apply(
-                adjoint, "adjoint", (turned_own, turned_pair), lists[1], chunks, image_groups, [vector(2 * col_part, F32), norm] + col_sends
+                adjoint, "adjoint", both_turned, lists[1], chunks, image_groups, [vector(2 * col_part, F32), norm] + col_sends
             )
             more_steps = step + 2 < ITERS
             narrow, alpha, *wide = call(

time: 130 us -> 131 us (level)
  waiting for transfers between devices: 43.3 us -> 49.1 us
  Pallas kernels: 30.3 us -> 27.4 us
    ppermute x45, waiting for transfers between devices: 43.3 us -> 49.1 us  [swap(): return lax.ppermute(value, axis, [(i, i ^ offset) for i in range(size)])]
    pallas_call x27, Pallas kernels: 30.3 us -> 27.4 us  [call(): pl.pallas_call(kernel, name=name, out_shape=[jax.ShapeDtypeStruct(s, d) f...]
    ppermute x45, starting transfers between devices: 55.1 us -> 53.8 us  [swap(): return lax.ppermute(value, axis, [(i, i ^ offset) for i in range(size)])]
  transfers between devices with their start and end apart: 45 -> 45, of which waited for: 28 -> 37; matrix products, arithmetic and copies ran while one was open for 0% -> 0% of each run, Pallas kernels for 13% -> 11%
where the time goes in v9:
time: 131 us; the launch traced here: 132 us
  starting transfers between devices  53.8 us (41%)
  waiting for transfers between devices  49.1 us (37%)
  Pallas kernels  27.4 us (21%)
  between operations  1.53 us (1%)
    ppermute x45, starting transfers between devices, swap(): return lax.ppermute(value, axis, [(i, i ^ offset) for i in range(size)])  53.8 us
    ppermute x45, waiting for transfers between devices, swap(): return lax.ppermute(value, axis, [(i, i ^ offset) for i in range(size)])  49.1 us
    pallas_call x27, Pallas kernels, call(): pl.pallas_call(kernel, name=name, out_shape=[jax.ShapeDtypeStruct(s, d) f...  27.4 us
  transfers between devices with their start and end apart: 45, of which 37 were waited for; matrix products, arithmetic and copies ran while one was open for 0% of the time, Pallas kernels for 11%

profile of v9, /device:TPU:0, one launch (start us, length us, event | category | flops | bytes accessed | tf_op | source)
XLA Modules:
  0.0 131.8 jit_solution(18207498529984843369)
XLA Ops:
  2.5 3.2 %pack.1 = (bf16[48,2,128,128]{3,2,1,0:T(8,128)(2,1)S(1)}, bf16[48,128,256]{2,1,0:T(8,128)(2,1)S(1)}, f32[1152,128]{1,0:T(8,128)S(1)}, bf16[1024,128]{1,0:T(8,128)(2,1)S(1)}, bf16[1024,128]{1,0:T(8,128)(2,1)S(1)}) custom-call(f32[2,1024,128]{2,1,0:T(8,128)} %record_ref.1, bf16[24,2,128,128]{3,2,1,0:T(8,128)(2,1)} %bitcast.12, s32[1,24]{1,0:T(1,128)} %bitcast.6, ...), custom_call_target="tpu_custom_call" | custom-call | tf_op jit(solution)/shard_map/pack/pallas_call | solution.py:52
  5.8 1.7 %first_adjoint.1 = (bf16[48,2,128,128]{3,2,1,0:T(8,128)(2,1)S(1)}, bf16[48,128,256]{2,1,0:T(8,128)(2,1)S(1)}, f32[512,128]{1,0:T(8,128)S(1)}, bf16[512,128]{1,0:...) custom-call(bf16[24,2,128,128]{3,2,1,0:T(8,128)(2,1)S(1)} %collectiv, ...), custom_call_target="tpu_custom_call", output_to_operand_aliasing={{0}: (4, {}), {1}: (5, {})} | custom-call | tf_op jit(solution)/shard_map/first_adjoint/pallas_call | solution.py:52
  7.5 2.3 %collective-permute-start.4 = (bf16[512,128]{1,0:T(8,128)(2,1)S(1)}, bf16[512,128]{1,0:T(8,128)(2,1)S(1)}, u32[]{:S(2)}, u32[]{:S(2)}) collective-permute-start(bf16[512,128]{1,0:T(8,128)(2,1)S(1)} %get-tuple-element.91), channel_id=1, source_target_pairs={{0,8},{8,0},{16,24},{24,16},{1,9},{9,1},{17,25},{25,17},{2,10},{10... | collective-permute-start | bytes 393224 | tf_op jit(solution)/shard_map/ppermute | solution.py:424
  9.8 1.9 %collective-permute-start.5 = (bf16[512,128]{1,0:T(8,128)(2,1)S(1)}, bf16[512,128]{1,0:T(8,128)(2,1)S(1)}, u32[]{:S(2)}, u32[]{:S(2)}) collective-permute-start(bf16[512,128]{1,0:T(8,128)(2,1)S(1)} %get-tuple-element.92), channel_id=1, source_target_pairs={{0,16},{8,24},{16,0},{24,8},{1,17},{9,25},{17,1},{25,9},{2,18},{10... | collective-permute-start | bytes 393224 | tf_op jit(solution)/shard_map/ppermute | solution.py:424
  11.6 2.0 %collective-permute-done.4.refs_0_ = bf16[512,128]{1,0:T(8,128)(2,1)S(1)} collective-permute-done((bf16[512,128]{1,0:T(8,128)(2,1)S(1)}, bf16[512,128]{1,0:T(8,128)(2,1)S(1)}, u32[]{:S(2)}, u32[]{:S(2)}) %collective-permute-start.4) | collective-permute-done | bytes 131104 | tf_op jit(solution)/shard_map/ppermute | solution.py:424
  13.6 3.5 %collective-permute-done.5.refs_1_ = bf16[512,128]{1,0:T(8,128)(2,1)S(1)} collective-permute-done((bf16[512,128]{1,0:T(8,128)(2,1)S(1)}, bf16[512,128]{1,0:T(8,128)(2,1)S(1)}, u32[]{:S(2)}, u32[]{:S(2)}) %collective-permute-start.5) | collective-permute-done | bytes 131104 | tf_op jit(solution)/shard_map/ppermute | solution.py:424
  19.5 1.8 %collective-permute-start.7 = (bf16[512,128]{1,0:T(8,128)(2,1)S(1)}, bf16[512,128]{1,0:T(8,128)(2,1)S(1)}, u32[]{:S(2)}, u32[]{:S(2)}) collective-permute-start(bf16[512,128]{1,0:T(8,128)(2,1)S(1)} %get-tuple-element.94.refs_2_.refs_8_), channel_id=1, source_target_pairs={{0,24},{8,16},{16,8},{24,0},{1,25},{9,17},{17,9},{25,1},{2,26},{10... | collective-permute-start | bytes 393224 | tf_op jit(solution)/shard_map/ppermute | solution.py:424
  24.9 1.7 %collective-permute-done.7.refs_2_.refs_10_ = bf16[512,128]{1,0:T(8,128)(2,1)S(1)} collective-permute-done((bf16[512,128]{1,0:T(8,128)(2,1)S(1)}, bf16[512,128]{1,0:T(8,128)(2,1)S(1)}, u32[]{:S(2)}, u32[]{:S(2)}) %collective-permute-start.7) | collective-permute-done | bytes 131104 | tf_op jit(solution)/shard_map/ppermute | solution.py:424
  29.5 3.5 %collective-permute-start.10 = (bf16[272,128]{1,0:T(8,128)(2,1)S(1)}, bf16[272,128]{1,0:T(8,128)(2,1)S(1)}, u32[]{:S(2)}, u32[]{:S(2)}) collective-permute-start(bf16[272,128]{1,0:T(8,128)(2,1)S(1)} %get-tuple-element.101), channel_id=1, source_target_pairs={{0,6},{1,7},{2,4},{3,5},{4,2},{5,3},{6,0},{7,1},{8,14},{9,15},{10,... | collective-permute-start | bytes 208904 | tf_op jit(solution)/shard_map/ppermute | solution.py:424
  33.9 1.8 %collective-permute-done.10.refs_0_ = bf16[272,128]{1,0:T(8,128)(2,1)S(1)} collective-permute-done((bf16[272,128]{1,0:T(8,128)(2,1)S(1)}, bf16[272,128]{1,0:T(8,128)(2,1)S(1)}, u32[]{:S(2)}, u32[]{:S(2)}) %collective-permute-start.10) | collective-permute-done | bytes 69664 | tf_op jit(solution)/shard_map/ppermute | solution.py:424
  38.3 1.9 %collective-permute-start.15 = (bf16[256,128]{1,0:T(8,128)(2,1)S(1)}, bf16[256,128]{1,0:T(8,128)(2,1)S(1)}, u32[]{:S(2)}, u32[]{:S(2)}) collective-permute-start(bf16[256,128]{1,0:T(8,128)(2,1)S(1)} %get-tuple-element.104.refs_2_.refs_20_), channel_id=1, source_target_pairs={{0,6},{1,7},{2,4},{3,5},{4,2},{5,3},{6,0},{7,1},{8,14},{9,15},{10,... | collective-permute-start | bytes 196616 | tf_op jit(solution)/shard_map/ppermute | solution.py:424
  40.1 1.7 %collective-permute-start.13 = (bf16[256,128]{1,0:T(8,128)(2,1)S(1)}, bf16[256,128]{1,0:T(8,128)(2,1)S(1)}, u32[]{:S(2)}, u32[]{:S(2)}) collective-permute-start(bf16[256,128]{1,0:T(8,128)(2,1)S(1)} %get-tuple-element.104.refs_2_.refs_20_), channel_id=1, source_target_pairs={{0,4},{1,5},{2,6},{3,7},{4,0},{5,1},{6,2},{7,3},{8,12},{9,13},{10,... | collective-permute-start | bytes 196616 | tf_op jit(solution)/shard_map/ppermute | solution.py:424
  51.9 2.8 %collective-permute-done.16.refs_0_ = bf16[528,128]{1,0:T(8,128)(2,1)S(1)} collective-permute-done((bf16[528,128]{1,0:T(8,128)(2,1)S(1)}, bf16[528,128]{1,0:T(8,128)(2,1)S(1)}, u32[]{:S(2)}, u32[]{:S(2)}) %collective-permute-start.16) | collective-permute-done | bytes 135200 | tf_op jit(solution)/shard_map/ppermute | solution.py:424
  54.7 2.0 %collective-permute-done.17.refs_1_ = bf16[528,128]{1,0:T(8,128)(2,1)S(1)} collective-permute-done((bf16[528,128]{1,0:T(8,128)(2,1)S(1)}, bf16[528,128]{1,0:T(8,128)(2,1)S(1)}, u32[]{:S(2)}, u32[]{:S(2)}) %collective-permute-start.17) | collective-permute-done | bytes 135200 | tf_op jit(solution)/shard_map/ppermute | solution.py:424
  57.2 2.5 %collective-permute-start.19 = (bf16[512,128]{1,0:T(8,128)(2,1)S(1)}, bf16[512,128]{1,0:T(8,128)(2,1)S(1)}, u32[]{:S(2)}, u32[]{:S(2)}) collective-permute-start(bf16[512,128]{1,0:T(8,128)(2,1)S(1)} %get-tuple-element.116.refs_2_.refs_12_), channel_id=1, source_target_pairs={{0,24},{8,16},{16,8},{24,0},{1,25},{9,17},{17,9},{25,1},{2,26},{10... | collective-permute-start | bytes 393224 | tf_op jit(solution)/shard_map/ppermute | solution.py:424
  68.7 3.1 %collective-permute-start.24 = (bf16[272,128]{1,0:T(8,128)(2,1)S(1)}, bf16[272,128]{1,0:T(8,128)(2,1)S(1)}, u32[]{:S(2)}, u32[]{:S(2)}) collective-permute-start(bf16[272,128]{1,0:T(8,128)(2,1)S(1)} %get-tuple-element.125), channel_id=1, source_target_pairs={{0,4},{1,5},{2,6},{3,7},{4,0},{5,1},{6,2},{7,3},{8,12},{9,13},{10,... | collective-permute-start | bytes 208904 | tf_op jit(solution)/shard_map/ppermute | solution.py:424
  71.8 1.8 %collective-permute-done.22.refs_0_ = bf16[272,128]{1,0:T(8,128)(2,1)S(1)} collective-permute-done((bf16[272,128]{1,0:T(8,128)(2,1)S(1)}, bf16[272,128]{1,0:T(8,128)(2,1)S(1)}, u32[]{:S(2)}, u32[]{:S(2)}) %collective-permute-start.22) | collective-permute-done | bytes 69664 | tf_op jit(solution)/shard_map/ppermute | solution.py:424
  74.1 3.0 %collective-permute-done.24.refs_2_ = bf16[272,128]{1,0:T(8,128)(2,1)S(1)} collective-permute-done((bf16[272,128]{1,0:T(8,128)(2,1)S(1)}, bf16[272,128]{1,0:T(8,128)(2,1)S(1)}, u32[]{:S(2)}, u32[]{:S(2)}) %collective-permute-start.24) | collective-permute-done | bytes 69664 | tf_op jit(solution)/shard_map/ppermute | solution.py:424
  77.1 2.1 %collective-permute-start.27 = (bf16[256,128]{1,0:T(8,128)(2,1)S(1)}, bf16[256,128]{1,0:T(8,128)(2,1)S(1)}, u32[]{:S(2)}, u32[]{:S(2)}) collective-permute-start(bf16[256,128]{1,0:T(8,128)(2,1)S(1)} %get-tuple-element.127.refs_2_.refs_24_), channel_id=1, source_target_pairs={{0,6},{1,7},{2,4},{3,5},{4,2},{5,3},{6,0},{7,1},{8,14},{9,15},{10,... | collective-permute-start | bytes 196616 | tf_op jit(solution)/shard_map/ppermute | solution.py:424
  79.1 2.4 %collective-permute-start.26 = (bf16[256,128]{1,0:T(8,128)(2,1)S(1)}, bf16[256,128]{1,0:T(8,128)(2,1)S(1)}, u32[]{:S(2)}, u32[]{:S(2)}) collective-permute-start(bf16[256,128]{1,0:T(8,128)(2,1)S(1)} %get-tuple-element.127.refs_2_.refs_24_), channel_id=1, source_target_pairs={{0,2},{1,3},{2,0},{3,1},{4,6},{5,7},{6,4},{7,5},{8,10},{9,11},{10,... | collective-permute-start | bytes 196616 | tf_op jit(solution)/shard_map/ppermute | solution.py:424
  86.3 3.4 %collective-permute-start.30 = (bf16[528,128]{1,0:T(8,128)(2,1)S(1)}, bf16[528,128]{1,0:T(8,128)(2,1)S(1)}, u32[]{:S(2)}, u32[]{:S(2)}) collective-permute-start(bf16[528,128]{1,0:T(8,128)(2,1)S(1)} %get-tuple-element.136), channel_id=1, source_target_pairs={{0,24},{8,16},{16,8},{24,0},{1,25},{9,17},{17,9},{25,1},{2,26},{10... | collective-permute-start | bytes 405512 | tf_op jit(solution)/shard_map/ppermute | solution.py:424
  89.7 2.5 %collective-permute-done.28.refs_0_ = bf16[528,128]{1,0:T(8,128)(2,1)S(1)} collective-permute-done((bf16[528,128]{1,0:T(8,128)(2,1)S(1)}, bf16[528,128]{1,0:T(8,128)(2,1)S(1)}, u32[]{:S(2)}, u32[]{:S(2)}) %collective-permute-start.28) | collective-permute-done | bytes 135200 | tf_op jit(solution)/shard_map/ppermute | solution.py:424
  92.3 3.1 %collective-permute-done.29.refs_1_ = bf16[528,128]{1,0:T(8,128)(2,1)S(1)} collective-permute-done((bf16[528,128]{1,0:T(8,128)(2,1)S(1)}, bf16[528,128]{1,0:T(8,128)(2,1)S(1)}, u32[]{:S(2)}, u32[]{:S(2)}) %collective-permute-start.29) | collective-permute-done | bytes 135200 | tf_op jit(solution)/shard_map/ppermute | solution.py:424
  97.1 2.0 %collective-permute-start.32 = (bf16[512,128]{1,0:T(8,128)(2,1)S(1)}, bf16[512,128]{1,0:T(8,128)(2,1)S(1)}, u32[]{:S(2)}, u32[]{:S(2)}) collective-permute-start(bf16[512,128]{1,0:T(8,128)(2,1)S(1)} %get-tuple-element.139.refs_2_.refs_16_), channel_id=1, source_target_pairs={{0,16},{8,24},{16,0},{24,8},{1,17},{9,25},{17,1},{25,9},{2,18},{10... | collective-permute-start | bytes 393224 | tf_op jit(solution)/shard_map/ppermute | solution.py:424
  103.5 1.6 %forward.17 = (f32[1152,128]{1,0:T(8,128)S(1)}, f32[256,128]{1,0:T(8,128)S(1)}, f32[8,128]{1,0:T(8,128)S(1)}, bf16[272,128]{1,0:T(8,128)(2,1)S(1)}, bf16[272,128...) custom-call(bf16[48,2,128,128]{3,2,1,0:T(8,128)(2,1)S(1)} %get-tuple-element.86.refs_0_, ...), custom_call_target="tpu_custom_call", output_to_operand_aliasing={{0}: (4, {})} | custom-call | tf_op jit(solution)/shard_map/forward/pallas_call | solution.py:52
  105.1 1.8 %collective-permute-start.34 = (bf16[272,128]{1,0:T(8,128)(2,1)S(1)}, bf16[272,128]{1,0:T(8,128)(2,1)S(1)}, u32[]{:S(2)}, u32[]{:S(2)}) collective-permute-start(bf16[272,128]{1,0:T(8,128)(2,1)S(1)} %get-tuple-element.146), channel_id=1, source_target_pairs={{0,6},{1,7},{2,4},{3,5},{4,2},{5,3},{6,0},{7,1},{8,14},{9,15},{10,... | collective-permute-start | bytes 208904 | tf_op jit(solution)/shard_map/ppermute | solution.py:424
  106.9 2.6 %collective-permute-start.36 = (bf16[272,128]{1,0:T(8,128)(2,1)S(1)}, bf16[272,128]{1,0:T(8,128)(2,1)S(1)}, u32[]{:S(2)}, u32[]{:S(2)}) collective-permute-start(bf16[272,128]{1,0:T(8,128)(2,1)S(1)} %get-tuple-element.148), channel_id=1, source_target_pairs={{0,4},{1,5},{2,6},{3,7},{4,0},{5,1},{6,2},{7,3},{8,12},{9,13},{10,... | collective-permute-start | bytes 208904 | tf_op jit(solution)/shard_map/ppermute | solution.py:424
  109.5 2.1 %collective-permute-done.34.refs_0_ = bf16[272,128]{1,0:T(8,128)(2,1)S(1)} collective-permute-done((bf16[272,128]{1,0:T(8,128)(2,1)S(1)}, bf16[272,128]{1,0:T(8,128)(2,1)S(1)}, u32[]{:S(2)}, u32[]{:S(2)}) %collective-permute-start.34) | collective-permute-done | bytes 69664 | tf_op jit(solution)/shard_map/ppermute | solution.py:424
  113.0 1.8 %collective-permute-start.37 = (bf16[256,128]{1,0:T(8,128)(2,1)S(1)}, bf16[256,128]{1,0:T(8,128)(2,1)S(1)}, u32[]{:S(2)}, u32[]{:S(2)}) collective-permute-start(bf16[256,128]{1,0:T(8,128)(2,1)S(1)} %get-tuple-element.151.refs_0_.refs_28_), channel_id=1, source_target_pairs={{0,4},{1,5},{2,6},{3,7},{4,0},{5,1},{6,2},{7,3},{8,12},{9,13},{10,... | collective-permute-start | bytes 196616 | tf_op jit(solution)/shard_map/ppermute | solution.py:424
  115.5 1.9 %collective-permute-start.39 = (bf16[256,128]{1,0:T(8,128)(2,1)S(1)}, bf16[256,128]{1,0:T(8,128)(2,1)S(1)}, u32[]{:S(2)}, u32[]{:S(2)}) collective-permute-start(bf16[256,128]{1,0:T(8,128)(2,1)S(1)} %get-tuple-element.151.refs_0_.refs_28_), channel_id=1, source_target_pairs={{0,6},{1,7},{2,4},{3,5},{4,2},{5,3},{6,0},{7,1},{8,14},{9,15},{10,... | collective-permute-start | bytes 196616 | tf_op jit(solution)/shard_map/ppermute | solution.py:424
  119.1 2.5 %collective-permute-done.39.refs_3_.refs_29_ = bf16[256,128]{1,0:T(8,128)(2,1)S(1)} collective-permute-done((bf16[256,128]{1,0:T(8,128)(2,1)S(1)}, bf16[256,128]{1,0:T(8,128)(2,1)S(1)}, u32[]{:S(2)}, u32[]{:S(2)}) %collective-permute-start.39) | collective-permute-done | bytes 65568 | tf_op jit(solution)/shard_map/ppermute | solution.py:424
  121.7 1.9 %collective-permute-start.40 = (f32[8,128]{1,0:T(8,128)S(1)}, f32[8,128]{1,0:T(8,128)S(1)}, u32[]{:S(2)}, u32[]{:S(2)}) collective-permute-start(f32[8,128]{1,0:T(8,128)S(1)} %norm.1.refs_0_), channel_id=1, source_target_pairs={{0,24},{8,16},{16,8},{24,0},{1,25},{9,17},{17,9},{25,1},{2,26},{10... | collective-permute-start | bytes 12296 | tf_op jit(solution)/shard_map/ppermute | solution.py:424
  (92 shorter events, 56.5 us)
Async XLA Ops:
  0.6 5.1 %collective-permute-start = (bf16[24,2,128,128]{3,2,1,0:T(8,128)(2,1)}, bf16[24,2,128,128]{3,2,1,0:T(8,128)(2,1)S(1)}, u32[]{:S(2)}, u32[]{:S(2)}) collective-permute-start(bf16[24,2,128,128]{3,2,1,0:T(8,128)(2,1)} %bitcast.11), channel_id=1, source_target_pairs={{0,1},{1,0},{2,3},{3,2},{4,5},{5,4},{6,7},{7,6},{8,9},{9,8},{10,11... | collective-permute-start | bytes 4718600 | tf_op jit(solution)/shard_map/ppermute | solution.py:424
  7.5 6.2 %collective-permute-start.4 = (bf16[512,128]{1,0:T(8,128)(2,1)S(1)}, bf16[512,128]{1,0:T(8,128)(2,1)S(1)}, u32[]{:S(2)}, u32[]{:S(2)}) collective-permute-start(bf16[512,128]{1,0:T(8,128)(2,1)S(1)} %get-tuple-element.91), channel_id=1, source_target_pairs={{0,8},{8,0},{16,24},{24,16},{1,9},{9,1},{17,25},{25,17},{2,10},{10... | collective-permute-start | bytes 393224 | tf_op jit(solution)/shard_map/ppermute | solution.py:424
  9.8 7.4 %collective-permute-start.5 = (bf16[512,128]{1,0:T(8,128)(2,1)S(1)}, bf16[512,128]{1,0:T(8,128)(2,1)S(1)}, u32[]{:S(2)}, u32[]{:S(2)}) collective-permute-start(bf16[512,128]{1,0:T(8,128)(2,1)S(1)} %get-tuple-element.92), channel_id=1, source_target_pairs={{0,16},{8,24},{16,0},{24,8},{1,17},{9,25},{17,1},{25,9},{2,18},{10... | collective-permute-start | bytes 393224 | tf_op jit(solution)/shard_map/ppermute | solution.py:424
  11.6 6.3 %collective-permute-start.6 = (bf16[512,128]{1,0:T(8,128)(2,1)S(1)}, bf16[512,128]{1,0:T(8,128)(2,1)S(1)}, u32[]{:S(2)}, u32[]{:S(2)}) collective-permute-start(bf16[512,128]{1,0:T(8,128)(2,1)S(1)} %get-tuple-element.93), channel_id=1, source_target_pairs={{0,24},{8,16},{16,8},{24,0},{1,25},{9,17},{17,9},{25,1},{2,26},{10... | collective-permute-start | bytes 393224 | tf_op jit(solution)/shard_map/ppermute | solution.py:424
  18.0 5.9 %collective-permute-start.9 = (bf16[512,128]{1,0:T(8,128)(2,1)S(1)}, bf16[512,128]{1,0:T(8,128)(2,1)S(1)}, u32[]{:S(2)}, u32[]{:S(2)}) collective-permute-start(bf16[512,128]{1,0:T(8,128)(2,1)S(1)} %get-tuple-element.94.refs_2_.refs_8_), channel_id=1, source_target_pairs={{0,8},{8,0},{16,24},{24,16},{1,9},{9,1},{17,25},{25,17},{2,10},{10... | collective-permute-start | bytes 393224 | tf_op jit(solution)/shard_map/ppermute | solution.py:424
  19.5 7.1 %collective-permute-start.7 = (bf16[512,128]{1,0:T(8,128)(2,1)S(1)}, bf16[512,128]{1,0:T(8,128)(2,1)S(1)}, u32[]{:S(2)}, u32[]{:S(2)}) collective-permute-start(bf16[512,128]{1,0:T(8,128)(2,1)S(1)} %get-tuple-element.94.refs_2_.refs_8_), channel_id=1, source_target_pairs={{0,24},{8,16},{16,8},{24,0},{1,25},{9,17},{17,9},{25,1},{2,26},{10... | collective-permute-start | bytes 393224 | tf_op jit(solution)/shard_map/ppermute | solution.py:424
  21.2 6.7 %collective-permute-start.8 = (bf16[512,128]{1,0:T(8,128)(2,1)S(1)}, bf16[512,128]{1,0:T(8,128)(2,1)S(1)}, u32[]{:S(2)}, u32[]{:S(2)}) collective-permute-start(bf16[512,128]{1,0:T(8,128)(2,1)S(1)} %get-tuple-element.94.refs_2_.refs_8_), channel_id=1, source_target_pairs={{0,16},{8,24},{16,0},{24,8},{1,17},{9,25},{17,1},{25,9},{2,18},{10... | collective-permute-start | bytes 393224 | tf_op jit(solution)/shard_map/ppermute | solution.py:424
  29.5 6.2 %collective-permute-start.10 = (bf16[272,128]{1,0:T(8,128)(2,1)S(1)}, bf16[272,128]{1,0:T(8,128)(2,1)S(1)}, u32[]{:S(2)}, u32[]{:S(2)}) collective-permute-start(bf16[272,128]{1,0:T(8,128)(2,1)S(1)} %get-tuple-element.101), channel_id=1, source_target_pairs={{0,6},{1,7},{2,4},{3,5},{4,2},{5,3},{6,0},{7,1},{8,14},{9,15},{10,... | collective-permute-start | bytes 208904 | tf_op jit(solution)/shard_map/ppermute | solution.py:424
  33.0 5.2 %collective-permute-start.12 = (bf16[272,128]{1,0:T(8,128)(2,1)S(1)}, bf16[272,128]{1,0:T(8,128)(2,1)S(1)}, u32[]{:S(2)}, u32[]{:S(2)}) collective-permute-start(bf16[272,128]{1,0:T(8,128)(2,1)S(1)} %get-tuple-element.103), channel_id=1, source_target_pairs={{0,4},{1,5},{2,6},{3,7},{4,0},{5,1},{6,2},{7,3},{8,12},{9,13},{10,... | collective-permute-start | bytes 208904 | tf_op jit(solution)/shard_map/ppermute | solution.py:424
  38.3 6.2 %collective-permute-start.15 = (bf16[256,128]{1,0:T(8,128)(2,1)S(1)}, bf16[256,128]{1,0:T(8,128)(2,1)S(1)}, u32[]{:S(2)}, u32[]{:S(2)}) collective-permute-start(bf16[256,128]{1,0:T(8,128)(2,1)S(1)} %get-tuple-element.104.refs_2_.refs_20_), channel_id=1, source_target_pairs={{0,6},{1,7},{2,4},{3,5},{4,2},{5,3},{6,0},{7,1},{8,14},{9,15},{10,... | collective-permute-start | bytes 196616 | tf_op jit(solution)/shard_map/ppermute | solution.py:424
  40.1 6.1 %collective-permute-start.13 = (bf16[256,128]{1,0:T(8,128)(2,1)S(1)}, bf16[256,128]{1,0:T(8,128)(2,1)S(1)}, u32[]{:S(2)}, u32[]{:S(2)}) collective-permute-start(bf16[256,128]{1,0:T(8,128)(2,1)S(1)} %get-tuple-element.104.refs_2_.refs_20_), channel_id=1, source_target_pairs={{0,4},{1,5},{2,6},{3,7},{4,0},{5,1},{6,2},{7,3},{8,12},{9,13},{10,... | collective-permute-start | bytes 196616 | tf_op jit(solution)/shard_map/ppermute | solution.py:424
  48.3 6.4 %collective-permute-start.16 = (bf16[528,128]{1,0:T(8,128)(2,1)S(1)}, bf16[528,128]{1,0:T(8,128)(2,1)S(1)}, u32[]{:S(2)}, u32[]{:S(2)}) collective-permute-start(bf16[528,128]{1,0:T(8,128)(2,1)S(1)} %get-tuple-element.111), channel_id=1, source_target_pairs={{0,8},{8,0},{16,24},{24,16},{1,9},{9,1},{17,25},{25,17},{2,10},{10... | collective-permute-start | bytes 405512 | tf_op jit(solution)/shard_map/ppermute | solution.py:424
  49.3 7.4 %collective-permute-start.17 = (bf16[528,128]{1,0:T(8,128)(2,1)S(1)}, bf16[528,128]{1,0:T(8,128)(2,1)S(1)}, u32[]{:S(2)}, u32[]{:S(2)}) collective-permute-start(bf16[528,128]{1,0:T(8,128)(2,1)S(1)} %get-tuple-element.112), channel_id=1, source_target_pairs={{0,16},{8,24},{16,0},{24,8},{1,17},{9,25},{17,1},{25,9},{2,18},{10... | collective-permute-start | bytes 405512 | tf_op jit(solution)/shard_map/ppermute | solution.py:424
  50.4 6.3 %collective-permute-start.18 = (bf16[528,128]{1,0:T(8,128)(2,1)S(1)}, bf16[528,128]{1,0:T(8,128)(2,1)S(1)}, u32[]{:S(2)}, u32[]{:S(2)}) collective-permute-start(bf16[528,128]{1,0:T(8,128)(2,1)S(1)} %get-tuple-element.113), channel_id=1, source_target_pairs={{0,24},{8,16},{16,8},{24,0},{1,25},{9,17},{17,9},{25,1},{2,26},{10... | collective-permute-start | bytes 405512 | tf_op jit(solution)/shard_map/ppermute | solution.py:424
  57.2 7.2 %collective-permute-start.19 = (bf16[512,128]{1,0:T(8,128)(2,1)S(1)}, bf16[512,128]{1,0:T(8,128)(2,1)S(1)}, u32[]{:S(2)}, u32[]{:S(2)}) collective-permute-start(bf16[512,128]{1,0:T(8,128)(2,1)S(1)} %get-tuple-element.116.refs_2_.refs_12_), channel_id=1, source_target_pairs={{0,24},{8,16},{16,8},{24,0},{1,25},{9,17},{17,9},{25,1},{2,26},{10... | collective-permute-start | bytes 393224 | tf_op jit(solution)/shard_map/ppermute | solution.py:424
  59.7 6.0 %collective-permute-start.20 = (bf16[512,128]{1,0:T(8,128)(2,1)S(1)}, bf16[512,128]{1,0:T(8,128)(2,1)S(1)}, u32[]{:S(2)}, u32[]{:S(2)}) collective-permute-start(bf16[512,128]{1,0:T(8,128)(2,1)S(1)} %get-tuple-element.116.refs_2_.refs_12_), channel_id=1, source_target_pairs={{0,16},{8,24},{16,0},{24,8},{1,17},{9,25},{17,1},{25,9},{2,18},{10... | collective-permute-start | bytes 393224 | tf_op jit(solution)/shard_map/ppermute | solution.py:424
  67.4 6.3 %collective-permute-start.22 = (bf16[272,128]{1,0:T(8,128)(2,1)S(1)}, bf16[272,128]{1,0:T(8,128)(2,1)S(1)}, u32[]{:S(2)}, u32[]{:S(2)}) collective-permute-start(bf16[272,128]{1,0:T(8,128)(2,1)S(1)} %get-tuple-element.123), channel_id=1, source_target_pairs={{0,6},{1,7},{2,4},{3,5},{4,2},{5,3},{6,0},{7,1},{8,14},{9,15},{10,... | collective-permute-start | bytes 208904 | tf_op jit(solution)/shard_map/ppermute | solution.py:424
  68.7 5.4 %collective-permute-start.23 = (bf16[272,128]{1,0:T(8,128)(2,1)S(1)}, bf16[272,128]{1,0:T(8,128)(2,1)S(1)}, u32[]{:S(2)}, u32[]{:S(2)}) collective-permute-start(bf16[272,128]{1,0:T(8,128)(2,1)S(1)} %get-tuple-element.124), channel_id=1, source_target_pairs={{0,2},{1,3},{2,0},{3,1},{4,6},{5,7},{6,4},{7,5},{8,10},{9,11},{10,... | collective-permute-start | bytes 208904 | tf_op jit(solution)/shard_map/ppermute | solution.py:424
  68.7 8.3 %collective-permute-start.24 = (bf16[272,128]{1,0:T(8,128)(2,1)S(1)}, bf16[272,128]{1,0:T(8,128)(2,1)S(1)}, u32[]{:S(2)}, u32[]{:S(2)}) collective-permute-start(bf16[272,128]{1,0:T(8,128)(2,1)S(1)} %get-tuple-element.125), channel_id=1, source_target_pairs={{0,4},{1,5},{2,6},{3,7},{4,0},{5,1},{6,2},{7,3},{8,12},{9,13},{10,... | collective-permute-start | bytes 208904 | tf_op jit(solution)/shard_map/ppermute | solution.py:424
  77.1 6.1 %collective-permute-start.27 = (bf16[256,128]{1,0:T(8,128)(2,1)S(1)}, bf16[256,128]{1,0:T(8,128)(2,1)S(1)}, u32[]{:S(2)}, u32[]{:S(2)}) collective-permute-start(bf16[256,128]{1,0:T(8,128)(2,1)S(1)} %get-tuple-element.127.refs_2_.refs_24_), channel_id=1, source_target_pairs={{0,6},{1,7},{2,4},{3,5},{4,2},{5,3},{6,0},{7,1},{8,14},{9,15},{10,... | collective-permute-start | bytes 196616 | tf_op jit(solution)/shard_map/ppermute | solution.py:424
  79.1 5.5 %collective-permute-start.25 = (bf16[256,128]{1,0:T(8,128)(2,1)S(1)}, bf16[256,128]{1,0:T(8,128)(2,1)S(1)}, u32[]{:S(2)}, u32[]{:S(2)}) collective-permute-start(bf16[256,128]{1,0:T(8,128)(2,1)S(1)} %get-tuple-element.127.refs_2_.refs_24_), channel_id=1, source_target_pairs={{0,4},{1,5},{2,6},{3,7},{4,0},{5,1},{6,2},{7,3},{8,12},{9,13},{10,... | collective-permute-start | bytes 196616 | tf_op jit(solution)/shard_map/ppermute | solution.py:424
  79.1 5.5 %collective-permute-start.26 = (bf16[256,128]{1,0:T(8,128)(2,1)S(1)}, bf16[256,128]{1,0:T(8,128)(2,1)S(1)}, u32[]{:S(2)}, u32[]{:S(2)}) collective-permute-start(bf16[256,128]{1,0:T(8,128)(2,1)S(1)} %get-tuple-element.127.refs_2_.refs_24_), channel_id=1, source_target_pairs={{0,2},{1,3},{2,0},{3,1},{4,6},{5,7},{6,4},{7,5},{8,10},{9,11},{10,... | collective-permute-start | bytes 196616 | tf_op jit(solution)/shard_map/ppermute | solution.py:424
  86.2 6.1 %collective-permute-start.28 = (bf16[528,128]{1,0:T(8,128)(2,1)S(1)}, bf16[528,128]{1,0:T(8,128)(2,1)S(1)}, u32[]{:S(2)}, u32[]{:S(2)}) collective-permute-start(bf16[528,128]{1,0:T(8,128)(2,1)S(1)} %get-tuple-element.134), channel_id=1, source_target_pairs={{0,8},{8,0},{16,24},{24,16},{1,9},{9,1},{17,25},{25,17},{2,10},{10... | collective-permute-start | bytes 405512 | tf_op jit(solution)/shard_map/ppermute | solution.py:424
  86.3 9.1 %collective-permute-start.29 = (bf16[528,128]{1,0:T(8,128)(2,1)S(1)}, bf16[528,128]{1,0:T(8,128)(2,1)S(1)}, u32[]{:S(2)}, u32[]{:S(2)}) collective-permute-start(bf16[528,128]{1,0:T(8,128)(2,1)S(1)} %get-tuple-element.135), channel_id=1, source_target_pairs={{0,16},{8,24},{16,0},{24,8},{1,17},{9,25},{17,1},{25,9},{2,18},{10... | collective-permute-start | bytes 405512 | tf_op jit(solution)/shard_map/ppermute | solution.py:424
  86.3 9.1 %collective-permute-start.30 = (bf16[528,128]{1,0:T(8,128)(2,1)S(1)}, bf16[528,128]{1,0:T(8,128)(2,1)S(1)}, u32[]{:S(2)}, u32[]{:S(2)}) collective-permute-start(bf16[528,128]{1,0:T(8,128)(2,1)S(1)} %get-tuple-element.136), channel_id=1, source_target_pairs={{0,24},{8,16},{16,8},{24,0},{1,25},{9,17},{17,9},{25,1},{2,26},{10... | collective-permute-start | bytes 405512 | tf_op jit(solution)/shard_map/ppermute | solution.py:424
  97.0 6.0 %collective-permute-start.31 = (bf16[512,128]{1,0:T(8,128)(2,1)S(1)}, bf16[512,128]{1,0:T(8,128)(2,1)S(1)}, u32[]{:S(2)}, u32[]{:S(2)}) collective-permute-start(bf16[512,128]{1,0:T(8,128)(2,1)S(1)} %get-tuple-element.139.refs_2_.refs_16_), channel_id=1, source_target_pairs={{0,24},{8,16},{16,8},{24,0},{1,25},{9,17},{17,9},{25,1},{2,26},{10... | collective-permute-start | bytes 393224 | tf_op jit(solution)/shard_map/ppermute | solution.py:424
  97.1 6.4 %collective-permute-start.32 = (bf16[512,128]{1,0:T(8,128)(2,1)S(1)}, bf16[512,128]{1,0:T(8,128)(2,1)S(1)}, u32[]{:S(2)}, u32[]{:S(2)}) collective-permute-start(bf16[512,128]{1,0:T(8,128)(2,1)S(1)} %get-tuple-element.139.refs_2_.refs_16_), channel_id=1, source_target_pairs={{0,16},{8,24},{16,0},{24,8},{1,17},{9,25},{17,1},{25,9},{2,18},{10... | collective-permute-start | bytes 393224 | tf_op jit(solution)/shard_map/ppermute | solution.py:424
  105.1 6.5 %collective-permute-start.34 = (bf16[272,128]{1,0:T(8,128)(2,1)S(1)}, bf16[272,128]{1,0:T(8,128)(2,1)S(1)}, u32[]{:S(2)}, u32[]{:S(2)}) collective-permute-start(bf16[272,128]{1,0:T(8,128)(2,1)S(1)} %get-tuple-element.146), channel_id=1, source_target_pairs={{0,6},{1,7},{2,4},{3,5},{4,2},{5,3},{6,0},{7,1},{8,14},{9,15},{10,... | collective-permute-start | bytes 208904 | tf_op jit(solution)/shard_map/ppermute | solution.py:424
  106.9 6.1 %collective-permute-start.35 = (bf16[272,128]{1,0:T(8,128)(2,1)S(1)}, bf16[272,128]{1,0:T(8,128)(2,1)S(1)}, u32[]{:S(2)}, u32[]{:S(2)}) collective-permute-start(bf16[272,128]{1,0:T(8,128)(2,1)S(1)} %get-tuple-element.147), channel_id=1, source_target_pairs={{0,2},{1,3},{2,0},{3,1},{4,6},{5,7},{6,4},{7,5},{8,10},{9,11},{10,... | collective-permute-start | bytes 208904 | tf_op jit(solution)/shard_map/ppermute | solution.py:424
  106.9 6.1 %collective-permute-start.36 = (bf16[272,128]{1,0:T(8,128)(2,1)S(1)}, bf16[272,128]{1,0:T(8,128)(2,1)S(1)}, u32[]{:S(2)}, u32[]{:S(2)}) collective-permute-start(bf16[272,128]{1,0:T(8,128)(2,1)S(1)} %get-tuple-element.148), channel_id=1, source_target_pairs={{0,4},{1,5},{2,6},{3,7},{4,0},{5,1},{6,2},{7,3},{8,12},{9,13},{10,... | collective-permute-start | bytes 208904 | tf_op jit(solution)/shard_map/ppermute | solution.py:424
  113.0 6.0 %collective-permute-start.37 = (bf16[256,128]{1,0:T(8,128)(2,1)S(1)}, bf16[256,128]{1,0:T(8,128)(2,1)S(1)}, u32[]{:S(2)}, u32[]{:S(2)}) collective-permute-start(bf16[256,128]{1,0:T(8,128)(2,1)S(1)} %get-tuple-element.151.refs_0_.refs_28_), channel_id=1, source_target_pairs={{0,4},{1,5},{2,6},{3,7},{4,0},{5,1},{6,2},{7,3},{8,12},{9,13},{10,... | collective-permute-start | bytes 196616 | tf_op jit(solution)/shard_map/ppermute | solution.py:424
  115.5 6.1 %collective-permute-start.39 = (bf16[256,128]{1,0:T(8,128)(2,1)S(1)}, bf16[256,128]{1,0:T(8,128)(2,1)S(1)}, u32[]{:S(2)}, u32[]{:S(2)}) collective-permute-start(bf16[256,128]{1,0:T(8,128)(2,1)S(1)} %get-tuple-element.151.refs_0_.refs_28_), channel_id=1, source_target_pairs={{0,6},{1,7},{2,4},{3,5},{4,2},{5,3},{6,0},{7,1},{8,14},{9,15},{10,... | collective-permute-start | bytes 196616 | tf_op jit(solution)/shard_map/ppermute | solution.py:424
  (16 other events, 105.6 us)

commit v10 on v9

--- a/solution.py
+++ b/solution.py
@@ -482,7 +482,7 @@
             0, -1.0, size, row_part, 1, rows, col_part, (0, cols), col_tiles, 2 * col_tiles, hyd_order,
             z_place, hyd_place, lambda tile_ref, slot: tile_ref[slot],
         )
-        g_order, image_order = ((0, *o[: len(o) // 2], *o[len(o) // 2 :][::-1]) for o in (hyd_order, z_order))
+        g_order, image_order = (0, *hyd_order), (0, *z_order)
         g_groups, image_groups = (groups_of(order, w) for order, w in ((g_order, forward), (image_order, adjoint)))
         lists = call(
             functools.partial(list_kernel, ((forward, g_groups), (adjoint, image_groups))),
@@ -535,9 +535,8 @@
             gradient = wide[0] if more_steps else None
             alphas.append(alpha)
 
-        chunks = [chunks[image_order.index(o)] for o in (0, *z_order[::-1])]
         (own_norm,) = call(norm_kernel, "norm", [norm], [], *chunks)
-        norms = [own_norm] + over_hyd([own_norm] * (hyds - 1), hyd_order[::-1])
+        norms = [own_norm] + over_hyd([own_norm] * (hyds - 1), hyd_order)
         own_x, pair_x, wide_r, narrow_r = call(
             functools.partial(answer_kernel, "hyd", "src", g_order, image_order), "answer",
             [vector(cols, F32), vector(cols, BF16), vector(rows, F32), vector(rows, BF16)], [],

time: 131 us -> 128 us (0.977); the launches traced: 132 us -> 127 us
  waiting for transfers between devices: 49.1 us -> 45.8 us
  Pallas kernels: 27.4 us -> 25.3 us
    ppermute x45, waiting for transfers between devices: 49.1 us -> 45.8 us  [swap(): return lax.ppermute(value, axis, [(i, i ^ offset) for i in range(size)])]
    pallas_call x27, Pallas kernels: 27.4 us -> 25.3 us  [call(): pl.pallas_call(kernel, name=name, out_shape=[jax.ShapeDtypeStruct(s, d) f...]
  transfers between devices with their start and end apart: 45 -> 45, of which waited for: 37 -> 35; matrix products, arithmetic and copies ran while one was open for 0% -> 0% of each run, Pallas kernels for 11% -> 11%
where the time goes in v10:
time: 128 us; the launch traced here: 127 us
  starting transfers between devices  54.8 us (43%)
  waiting for transfers between devices  45.8 us (36%)
  Pallas kernels  25.3 us (20%)
  between operations  1.54 us (1%)
    ppermute x45, starting transfers between devices, swap(): return lax.ppermute(value, axis, [(i, i ^ offset) for i in range(size)])  54.8 us
    ppermute x45, waiting for transfers between devices, swap(): return lax.ppermute(value, axis, [(i, i ^ offset) for i in range(size)])  45.8 us
    pallas_call x27, Pallas kernels, call(): pl.pallas_call(kernel, name=name, out_shape=[jax.ShapeDtypeStruct(s, d) f...  25.3 us
  transfers between devices with their start and end apart: 45, of which 35 were waited for; matrix products, arithmetic and copies ran while one was open for 0% of the time, Pallas kernels for 11%

profile of v10, /device:TPU:0, one launch (start us, length us, event | category | flops | bytes accessed | tf_op | source)
XLA Modules:
  0.0 127.5 jit_solution(6982341361114074402)
XLA Ops:
  2.5 3.2 %pack.1 = (bf16[48,2,128,128]{3,2,1,0:T(8,128)(2,1)S(1)}, bf16[48,128,256]{2,1,0:T(8,128)(2,1)S(1)}, f32[1152,128]{1,0:T(8,128)S(1)}, bf16[1024,128]{1,0:T(8,128)(2,1)S(1)}, bf16[1024,128]{1,0:T(8,128)(2,1)S(1)}) custom-call(f32[2,1024,128]{2,1,0:T(8,128)} %record_ref.1, bf16[24,2,128,128]{3,2,1,0:T(8,128)(2,1)} %bitcast.12, s32[1,24]{1,0:T(1,128)} %bitcast.6, ...), custom_call_target="tpu_custom_call" | custom-call | tf_op jit(solution)/shard_map/pack/pallas_call | solution.py:52
  7.1 3.7 %collective-permute-start.4 = (bf16[512,128]{1,0:T(8,128)(2,1)S(1)}, bf16[512,128]{1,0:T(8,128)(2,1)S(1)}, u32[]{:S(2)}, u32[]{:S(2)}) collective-permute-start(bf16[512,128]{1,0:T(8,128)(2,1)S(1)} %get-tuple-element.91), channel_id=1, source_target_pairs={{0,8},{8,0},{16,24},{24,16},{1,9},{9,1},{17,25},{25,17},{2,10},{10... | collective-permute-start | bytes 393224 | tf_op jit(solution)/shard_map/ppermute | solution.py:424
  12.3 2.4 %collective-permute-done.4.refs_0_ = bf16[512,128]{1,0:T(8,128)(2,1)S(1)} collective-permute-done((bf16[512,128]{1,0:T(8,128)(2,1)S(1)}, bf16[512,128]{1,0:T(8,128)(2,1)S(1)}, u32[]{:S(2)}, u32[]{:S(2)}) %collective-permute-start.4) | collective-permute-done | bytes 131104 | tf_op jit(solution)/shard_map/ppermute | solution.py:424
  14.7 4.1 %collective-permute-done.5.refs_1_ = bf16[512,128]{1,0:T(8,128)(2,1)S(1)} collective-permute-done((bf16[512,128]{1,0:T(8,128)(2,1)S(1)}, bf16[512,128]{1,0:T(8,128)(2,1)S(1)}, u32[]{:S(2)}, u32[]{:S(2)}) %collective-permute-start.5) | collective-permute-done | bytes 131104 | tf_op jit(solution)/shard_map/ppermute | solution.py:424
  20.7 1.8 %collective-permute-start.8 = (bf16[512,128]{1,0:T(8,128)(2,1)S(1)}, bf16[512,128]{1,0:T(8,128)(2,1)S(1)}, u32[]{:S(2)}, u32[]{:S(2)}) collective-permute-start(bf16[512,128]{1,0:T(8,128)(2,1)S(1)} %get-tuple-element.94.refs_2_.refs_8_), channel_id=1, source_target_pairs={{0,24},{8,16},{16,8},{24,0},{1,25},{9,17},{17,9},{25,1},{2,26},{10... | collective-permute-start | bytes 393224 | tf_op jit(solution)/shard_map/ppermute | solution.py:424
  28.7 3.4 %collective-permute-start.10 = (bf16[272,128]{1,0:T(8,128)(2,1)S(1)}, bf16[272,128]{1,0:T(8,128)(2,1)S(1)}, u32[]{:S(2)}, u32[]{:S(2)}) collective-permute-start(bf16[272,128]{1,0:T(8,128)(2,1)S(1)} %get-tuple-element.101), channel_id=1, source_target_pairs={{0,6},{1,7},{2,4},{3,5},{4,2},{5,3},{6,0},{7,1},{8,14},{9,15},{10,... | collective-permute-start | bytes 208904 | tf_op jit(solution)/shard_map/ppermute | solution.py:424
  33.1 1.8 %collective-permute-done.10.refs_0_ = bf16[272,128]{1,0:T(8,128)(2,1)S(1)} collective-permute-done((bf16[272,128]{1,0:T(8,128)(2,1)S(1)}, bf16[272,128]{1,0:T(8,128)(2,1)S(1)}, u32[]{:S(2)}, u32[]{:S(2)}) %collective-permute-start.10) | collective-permute-done | bytes 69664 | tf_op jit(solution)/shard_map/ppermute | solution.py:424
  37.3 3.3 %collective-permute-start.15 = (bf16[256,128]{1,0:T(8,128)(2,1)S(1)}, bf16[256,128]{1,0:T(8,128)(2,1)S(1)}, u32[]{:S(2)}, u32[]{:S(2)}) collective-permute-start(bf16[256,128]{1,0:T(8,128)(2,1)S(1)} %get-tuple-element.104.refs_2_.refs_20_), channel_id=1, source_target_pairs={{0,6},{1,7},{2,4},{3,5},{4,2},{5,3},{6,0},{7,1},{8,14},{9,15},{10,... | collective-permute-start | bytes 196616 | tf_op jit(solution)/shard_map/ppermute | solution.py:424
  48.0 2.5 %collective-permute-start.18 = (bf16[528,128]{1,0:T(8,128)(2,1)S(1)}, bf16[528,128]{1,0:T(8,128)(2,1)S(1)}, u32[]{:S(2)}, u32[]{:S(2)}) collective-permute-start(bf16[528,128]{1,0:T(8,128)(2,1)S(1)} %get-tuple-element.113), channel_id=1, source_target_pairs={{0,24},{8,16},{16,8},{24,0},{1,25},{9,17},{17,9},{25,1},{2,26},{10... | collective-permute-start | bytes 405512 | tf_op jit(solution)/shard_map/ppermute | solution.py:424
  52.3 2.4 %collective-permute-done.18.refs_2_ = bf16[528,128]{1,0:T(8,128)(2,1)S(1)} collective-permute-done((bf16[528,128]{1,0:T(8,128)(2,1)S(1)}, bf16[528,128]{1,0:T(8,128)(2,1)S(1)}, u32[]{:S(2)}, u32[]{:S(2)}) %collective-permute-start.18) | collective-permute-done | bytes 135200 | tf_op jit(solution)/shard_map/ppermute | solution.py:424
  56.1 2.2 %collective-permute-start.19 = (bf16[512,128]{1,0:T(8,128)(2,1)S(1)}, bf16[512,128]{1,0:T(8,128)(2,1)S(1)}, u32[]{:S(2)}, u32[]{:S(2)}) collective-permute-start(bf16[512,128]{1,0:T(8,128)(2,1)S(1)} %get-tuple-element.116.refs_2_.refs_12_), channel_id=1, source_target_pairs={{0,16},{8,24},{16,0},{24,8},{1,17},{9,25},{17,1},{25,9},{2,18},{10... | collective-permute-start | bytes 393224 | tf_op jit(solution)/shard_map/ppermute | solution.py:424
  62.3 1.9 %collective-permute-done.20.refs_3_.refs_15_ = bf16[512,128]{1,0:T(8,128)(2,1)S(1)} collective-permute-done((bf16[512,128]{1,0:T(8,128)(2,1)S(1)}, bf16[512,128]{1,0:T(8,128)(2,1)S(1)}, u32[]{:S(2)}, u32[]{:S(2)}) %collective-permute-start.20) | collective-permute-done | bytes 131104 | tf_op jit(solution)/shard_map/ppermute | solution.py:424
  64.2 1.6 %forward.14 = (f32[1152,128]{1,0:T(8,128)S(1)}, f32[256,128]{1,0:T(8,128)S(1)}, f32[8,128]{1,0:T(8,128)S(1)}, bf16[272,128]{1,0:T(8,128)(2,1)S(1)}, bf16[272,128...) custom-call(bf16[48,2,128,128]{3,2,1,0:T(8,128)(2,1)S(1)} %get-tuple-element.86.refs_0_, ...), custom_call_target="tpu_custom_call", output_to_operand_aliasing={{0}: (4, {})} | custom-call | tf_op jit(solution)/shard_map/forward/pallas_call | solution.py:52
  65.9 2.4 %collective-permute-start.22 = (bf16[272,128]{1,0:T(8,128)(2,1)S(1)}, bf16[272,128]{1,0:T(8,128)(2,1)S(1)}, u32[]{:S(2)}, u32[]{:S(2)}) collective-permute-start(bf16[272,128]{1,0:T(8,128)(2,1)S(1)} %get-tuple-element.123), channel_id=1, source_target_pairs={{0,6},{1,7},{2,4},{3,5},{4,2},{5,3},{6,0},{7,1},{8,14},{9,15},{10,... | collective-permute-start | bytes 208904 | tf_op jit(solution)/shard_map/ppermute | solution.py:424
  68.3 2.0 %collective-permute-start.24 = (bf16[272,128]{1,0:T(8,128)(2,1)S(1)}, bf16[272,128]{1,0:T(8,128)(2,1)S(1)}, u32[]{:S(2)}, u32[]{:S(2)}) collective-permute-start(bf16[272,128]{1,0:T(8,128)(2,1)S(1)} %get-tuple-element.125), channel_id=1, source_target_pairs={{0,4},{1,5},{2,6},{3,7},{4,0},{5,1},{6,2},{7,3},{8,12},{9,13},{10,... | collective-permute-start | bytes 208904 | tf_op jit(solution)/shard_map/ppermute | solution.py:424
  70.3 2.5 %collective-permute-done.22.refs_0_ = bf16[272,128]{1,0:T(8,128)(2,1)S(1)} collective-permute-done((bf16[272,128]{1,0:T(8,128)(2,1)S(1)}, bf16[272,128]{1,0:T(8,128)(2,1)S(1)}, u32[]{:S(2)}, u32[]{:S(2)}) %collective-permute-start.22) | collective-permute-done | bytes 69664 | tf_op jit(solution)/shard_map/ppermute | solution.py:424
  73.8 1.9 %collective-permute-done.24.refs_2_ = bf16[272,128]{1,0:T(8,128)(2,1)S(1)} collective-permute-done((bf16[272,128]{1,0:T(8,128)(2,1)S(1)}, bf16[272,128]{1,0:T(8,128)(2,1)S(1)}, u32[]{:S(2)}, u32[]{:S(2)}) %collective-permute-start.24) | collective-permute-done | bytes 69664 | tf_op jit(solution)/shard_map/ppermute | solution.py:424
  75.7 1.7 %collective-permute-start.27 = (bf16[256,128]{1,0:T(8,128)(2,1)S(1)}, bf16[256,128]{1,0:T(8,128)(2,1)S(1)}, u32[]{:S(2)}, u32[]{:S(2)}) collective-permute-start(bf16[256,128]{1,0:T(8,128)(2,1)S(1)} %get-tuple-element.127.refs_2_.refs_24_), channel_id=1, source_target_pairs={{0,6},{1,7},{2,4},{3,5},{4,2},{5,3},{6,0},{7,1},{8,14},{9,15},{10,... | collective-permute-start | bytes 196616 | tf_op jit(solution)/shard_map/ppermute | solution.py:424
  77.4 2.8 %collective-permute-start.26 = (bf16[256,128]{1,0:T(8,128)(2,1)S(1)}, bf16[256,128]{1,0:T(8,128)(2,1)S(1)}, u32[]{:S(2)}, u32[]{:S(2)}) collective-permute-start(bf16[256,128]{1,0:T(8,128)(2,1)S(1)} %get-tuple-element.127.refs_2_.refs_24_), channel_id=1, source_target_pairs={{0,4},{1,5},{2,6},{3,7},{4,0},{5,1},{6,2},{7,3},{8,12},{9,13},{10,... | collective-permute-start | bytes 196616 | tf_op jit(solution)/shard_map/ppermute | solution.py:424
  85.6 2.4 %collective-permute-start.30 = (bf16[528,128]{1,0:T(8,128)(2,1)S(1)}, bf16[528,128]{1,0:T(8,128)(2,1)S(1)}, u32[]{:S(2)}, u32[]{:S(2)}) collective-permute-start(bf16[528,128]{1,0:T(8,128)(2,1)S(1)} %get-tuple-element.136), channel_id=1, source_target_pairs={{0,24},{8,16},{16,8},{24,0},{1,25},{9,17},{17,9},{25,1},{2,26},{10... | collective-permute-start | bytes 405512 | tf_op jit(solution)/shard_map/ppermute | solution.py:424
  89.7 1.8 %collective-permute-done.30.refs_2_ = bf16[528,128]{1,0:T(8,128)(2,1)S(1)} collective-permute-done((bf16[528,128]{1,0:T(8,128)(2,1)S(1)}, bf16[528,128]{1,0:T(8,128)(2,1)S(1)}, u32[]{:S(2)}, u32[]{:S(2)}) %collective-permute-start.30) | collective-permute-done | bytes 135200 | tf_op jit(solution)/shard_map/ppermute | solution.py:424
  91.6 2.0 %collective-permute-start.33 = (bf16[512,128]{1,0:T(8,128)(2,1)S(1)}, bf16[512,128]{1,0:T(8,128)(2,1)S(1)}, u32[]{:S(2)}, u32[]{:S(2)}) collective-permute-start(bf16[512,128]{1,0:T(8,128)(2,1)S(1)} %get-tuple-element.139.refs_2_.refs_16_), channel_id=1, source_target_pairs={{0,8},{8,0},{16,24},{24,16},{1,9},{9,1},{17,25},{25,17},{2,10},{10... | collective-permute-start | bytes 393224 | tf_op jit(solution)/shard_map/ppermute | solution.py:424
  98.6 1.9 %collective-permute-done.32.refs_3_.refs_19_ = bf16[512,128]{1,0:T(8,128)(2,1)S(1)} collective-permute-done((bf16[512,128]{1,0:T(8,128)(2,1)S(1)}, bf16[512,128]{1,0:T(8,128)(2,1)S(1)}, u32[]{:S(2)}, u32[]{:S(2)}) %collective-permute-start.32) | collective-permute-done | bytes 131104 | tf_op jit(solution)/shard_map/ppermute | solution.py:424
  100.5 1.6 %forward.17 = (f32[1152,128]{1,0:T(8,128)S(1)}, f32[256,128]{1,0:T(8,128)S(1)}, f32[8,128]{1,0:T(8,128)S(1)}, bf16[272,128]{1,0:T(8,128)(2,1)S(1)}, bf16[272,128...) custom-call(bf16[48,2,128,128]{3,2,1,0:T(8,128)(2,1)S(1)} %get-tuple-element.86.refs_0_, ...), custom_call_target="tpu_custom_call", output_to_operand_aliasing={{0}: (4, {})} | custom-call | tf_op jit(solution)/shard_map/forward/pallas_call | solution.py:52
  102.1 1.6 %collective-permute-start.34 = (bf16[272,128]{1,0:T(8,128)(2,1)S(1)}, bf16[272,128]{1,0:T(8,128)(2,1)S(1)}, u32[]{:S(2)}, u32[]{:S(2)}) collective-permute-start(bf16[272,128]{1,0:T(8,128)(2,1)S(1)} %get-tuple-element.146), channel_id=1, source_target_pairs={{0,6},{1,7},{2,4},{3,5},{4,2},{5,3},{6,0},{7,1},{8,14},{9,15},{10,... | collective-permute-start | bytes 208904 | tf_op jit(solution)/shard_map/ppermute | solution.py:424
  104.8 1.8 %collective-permute-start.36 = (bf16[272,128]{1,0:T(8,128)(2,1)S(1)}, bf16[272,128]{1,0:T(8,128)(2,1)S(1)}, u32[]{:S(2)}, u32[]{:S(2)}) collective-permute-start(bf16[272,128]{1,0:T(8,128)(2,1)S(1)} %get-tuple-element.148), channel_id=1, source_target_pairs={{0,4},{1,5},{2,6},{3,7},{4,0},{5,1},{6,2},{7,3},{8,12},{9,13},{10,... | collective-permute-start | bytes 208904 | tf_op jit(solution)/shard_map/ppermute | solution.py:424
  106.5 1.8 %collective-permute-done.34.refs_0_ = bf16[272,128]{1,0:T(8,128)(2,1)S(1)} collective-permute-done((bf16[272,128]{1,0:T(8,128)(2,1)S(1)}, bf16[272,128]{1,0:T(8,128)(2,1)S(1)}, u32[]{:S(2)}, u32[]{:S(2)}) %collective-permute-start.34) | collective-permute-done | bytes 69664 | tf_op jit(solution)/shard_map/ppermute | solution.py:424
  108.8 1.9 %collective-permute-done.36.refs_2_ = bf16[272,128]{1,0:T(8,128)(2,1)S(1)} collective-permute-done((bf16[272,128]{1,0:T(8,128)(2,1)S(1)}, bf16[272,128]{1,0:T(8,128)(2,1)S(1)}, u32[]{:S(2)}, u32[]{:S(2)}) %collective-permute-start.36) | collective-permute-done | bytes 69664 | tf_op jit(solution)/shard_map/ppermute | solution.py:424
  112.4 2.8 %collective-permute-start.39 = (bf16[256,128]{1,0:T(8,128)(2,1)S(1)}, bf16[256,128]{1,0:T(8,128)(2,1)S(1)}, u32[]{:S(2)}, u32[]{:S(2)}) collective-permute-start(bf16[256,128]{1,0:T(8,128)(2,1)S(1)} %get-tuple-element.151.refs_0_.refs_28_), channel_id=1, source_target_pairs={{0,4},{1,5},{2,6},{3,7},{4,0},{5,1},{6,2},{7,3},{8,12},{9,13},{10,... | collective-permute-start | bytes 196616 | tf_op jit(solution)/shard_map/ppermute | solution.py:424
  115.2 1.7 %collective-permute-done.37.refs_1_.refs_29_ = bf16[256,128]{1,0:T(8,128)(2,1)S(1)} collective-permute-done((bf16[256,128]{1,0:T(8,128)(2,1)S(1)}, bf16[256,128]{1,0:T(8,128)(2,1)S(1)}, u32[]{:S(2)}, u32[]{:S(2)}) %collective-permute-start.37) | collective-permute-done | bytes 65568 | tf_op jit(solution)/shard_map/ppermute | solution.py:424
  118.9 2.3 %collective-permute-start.42 = (f32[8,128]{1,0:T(8,128)S(1)}, f32[8,128]{1,0:T(8,128)S(1)}, u32[]{:S(2)}, u32[]{:S(2)}) collective-permute-start(f32[8,128]{1,0:T(8,128)S(1)} %norm.1.refs_0_), channel_id=1, source_target_pairs={{0,24},{8,16},{16,8},{24,0},{1,25},{9,17},{17,9},{25,1},{2,26},{10... | collective-permute-start | bytes 12296 | tf_op jit(solution)/shard_map/ppermute | solution.py:424
  121.4 2.0 %collective-permute-done.42.refs_3_ = f32[8,128]{1,0:T(8,128)S(1)} collective-permute-done((f32[8,128]{1,0:T(8,128)S(1)}, f32[8,128]{1,0:T(8,128)S(1)}, u32[]{:S(2)}, u32[]{:S(2)}) %collective-permute-start.42) | collective-permute-done | bytes 4128 | tf_op jit(solution)/shard_map/ppermute | solution.py:424
  (92 shorter events, 52.9 us)
Async XLA Ops:
  0.6 5.1 %collective-permute-start = (bf16[24,2,128,128]{3,2,1,0:T(8,128)(2,1)}, bf16[24,2,128,128]{3,2,1,0:T(8,128)(2,1)S(1)}, u32[]{:S(2)}, u32[]{:S(2)}) collective-permute-start(bf16[24,2,128,128]{3,2,1,0:T(8,128)(2,1)} %bitcast.11), channel_id=1, source_target_pairs={{0,1},{1,0},{2,3},{3,2},{4,5},{5,4},{6,7},{7,6},{8,9},{9,8},{10,11... | collective-permute-start | bytes 4718600 | tf_op jit(solution)/shard_map/ppermute | solution.py:424
  7.1 7.6 %collective-permute-start.4 = (bf16[512,128]{1,0:T(8,128)(2,1)S(1)}, bf16[512,128]{1,0:T(8,128)(2,1)S(1)}, u32[]{:S(2)}, u32[]{:S(2)}) collective-permute-start(bf16[512,128]{1,0:T(8,128)(2,1)S(1)} %get-tuple-element.91), channel_id=1, source_target_pairs={{0,8},{8,0},{16,24},{24,16},{1,9},{9,1},{17,25},{25,17},{2,10},{10... | collective-permute-start | bytes 393224 | tf_op jit(solution)/shard_map/ppermute | solution.py:424
  10.8 8.0 %collective-permute-start.5 = (bf16[512,128]{1,0:T(8,128)(2,1)S(1)}, bf16[512,128]{1,0:T(8,128)(2,1)S(1)}, u32[]{:S(2)}, u32[]{:S(2)}) collective-permute-start(bf16[512,128]{1,0:T(8,128)(2,1)S(1)} %get-tuple-element.92), channel_id=1, source_target_pairs={{0,16},{8,24},{16,0},{24,8},{1,17},{9,25},{17,1},{25,9},{2,18},{10... | collective-permute-start | bytes 393224 | tf_op jit(solution)/shard_map/ppermute | solution.py:424
  11.3 7.5 %collective-permute-start.6 = (bf16[512,128]{1,0:T(8,128)(2,1)S(1)}, bf16[512,128]{1,0:T(8,128)(2,1)S(1)}, u32[]{:S(2)}, u32[]{:S(2)}) collective-permute-start(bf16[512,128]{1,0:T(8,128)(2,1)S(1)} %get-tuple-element.93), channel_id=1, source_target_pairs={{0,24},{8,16},{16,8},{24,0},{1,25},{9,17},{17,9},{25,1},{2,26},{10... | collective-permute-start | bytes 393224 | tf_op jit(solution)/shard_map/ppermute | solution.py:424
  18.9 6.0 %collective-permute-start.9 = (bf16[512,128]{1,0:T(8,128)(2,1)S(1)}, bf16[512,128]{1,0:T(8,128)(2,1)S(1)}, u32[]{:S(2)}, u32[]{:S(2)}) collective-permute-start(bf16[512,128]{1,0:T(8,128)(2,1)S(1)} %get-tuple-element.94.refs_2_.refs_8_), channel_id=1, source_target_pairs={{0,8},{8,0},{16,24},{24,16},{1,9},{9,1},{17,25},{25,17},{2,10},{10... | collective-permute-start | bytes 393224 | tf_op jit(solution)/shard_map/ppermute | solution.py:424
  19.3 7.8 %collective-permute-start.7 = (bf16[512,128]{1,0:T(8,128)(2,1)S(1)}, bf16[512,128]{1,0:T(8,128)(2,1)S(1)}, u32[]{:S(2)}, u32[]{:S(2)}) collective-permute-start(bf16[512,128]{1,0:T(8,128)(2,1)S(1)} %get-tuple-element.94.refs_2_.refs_8_), channel_id=1, source_target_pairs={{0,16},{8,24},{16,0},{24,8},{1,17},{9,25},{17,1},{25,9},{2,18},{10... | collective-permute-start | bytes 393224 | tf_op jit(solution)/shard_map/ppermute | solution.py:424
  20.7 6.4 %collective-permute-start.8 = (bf16[512,128]{1,0:T(8,128)(2,1)S(1)}, bf16[512,128]{1,0:T(8,128)(2,1)S(1)}, u32[]{:S(2)}, u32[]{:S(2)}) collective-permute-start(bf16[512,128]{1,0:T(8,128)(2,1)S(1)} %get-tuple-element.94.refs_2_.refs_8_), channel_id=1, source_target_pairs={{0,24},{8,16},{16,8},{24,0},{1,25},{9,17},{17,9},{25,1},{2,26},{10... | collective-permute-start | bytes 393224 | tf_op jit(solution)/shard_map/ppermute | solution.py:424
  28.7 6.2 %collective-permute-start.10 = (bf16[272,128]{1,0:T(8,128)(2,1)S(1)}, bf16[272,128]{1,0:T(8,128)(2,1)S(1)}, u32[]{:S(2)}, u32[]{:S(2)}) collective-permute-start(bf16[272,128]{1,0:T(8,128)(2,1)S(1)} %get-tuple-element.101), channel_id=1, source_target_pairs={{0,6},{1,7},{2,4},{3,5},{4,2},{5,3},{6,0},{7,1},{8,14},{9,15},{10,... | collective-permute-start | bytes 208904 | tf_op jit(solution)/shard_map/ppermute | solution.py:424
  32.1 5.2 %collective-permute-start.12 = (bf16[272,128]{1,0:T(8,128)(2,1)S(1)}, bf16[272,128]{1,0:T(8,128)(2,1)S(1)}, u32[]{:S(2)}, u32[]{:S(2)}) collective-permute-start(bf16[272,128]{1,0:T(8,128)(2,1)S(1)} %get-tuple-element.103), channel_id=1, source_target_pairs={{0,4},{1,5},{2,6},{3,7},{4,0},{5,1},{6,2},{7,3},{8,12},{9,13},{10,... | collective-permute-start | bytes 208904 | tf_op jit(solution)/shard_map/ppermute | solution.py:424
  37.3 6.6 %collective-permute-start.15 = (bf16[256,128]{1,0:T(8,128)(2,1)S(1)}, bf16[256,128]{1,0:T(8,128)(2,1)S(1)}, u32[]{:S(2)}, u32[]{:S(2)}) collective-permute-start(bf16[256,128]{1,0:T(8,128)(2,1)S(1)} %get-tuple-element.104.refs_2_.refs_20_), channel_id=1, source_target_pairs={{0,6},{1,7},{2,4},{3,5},{4,2},{5,3},{6,0},{7,1},{8,14},{9,15},{10,... | collective-permute-start | bytes 196616 | tf_op jit(solution)/shard_map/ppermute | solution.py:424
  40.6 5.2 %collective-permute-start.14 = (bf16[256,128]{1,0:T(8,128)(2,1)S(1)}, bf16[256,128]{1,0:T(8,128)(2,1)S(1)}, u32[]{:S(2)}, u32[]{:S(2)}) collective-permute-start(bf16[256,128]{1,0:T(8,128)(2,1)S(1)} %get-tuple-element.104.refs_2_.refs_20_), channel_id=1, source_target_pairs={{0,4},{1,5},{2,6},{3,7},{4,0},{5,1},{6,2},{7,3},{8,12},{9,13},{10,... | collective-permute-start | bytes 196616 | tf_op jit(solution)/shard_map/ppermute | solution.py:424
  47.0 5.1 %collective-permute-start.16 = (bf16[528,128]{1,0:T(8,128)(2,1)S(1)}, bf16[528,128]{1,0:T(8,128)(2,1)S(1)}, u32[]{:S(2)}, u32[]{:S(2)}) collective-permute-start(bf16[528,128]{1,0:T(8,128)(2,1)S(1)} %get-tuple-element.111), channel_id=1, source_target_pairs={{0,8},{8,0},{16,24},{24,16},{1,9},{9,1},{17,25},{25,17},{2,10},{10... | collective-permute-start | bytes 405512 | tf_op jit(solution)/shard_map/ppermute | solution.py:424
  48.0 6.7 %collective-permute-start.18 = (bf16[528,128]{1,0:T(8,128)(2,1)S(1)}, bf16[528,128]{1,0:T(8,128)(2,1)S(1)}, u32[]{:S(2)}, u32[]{:S(2)}) collective-permute-start(bf16[528,128]{1,0:T(8,128)(2,1)S(1)} %get-tuple-element.113), channel_id=1, source_target_pairs={{0,24},{8,16},{16,8},{24,0},{1,25},{9,17},{17,9},{25,1},{2,26},{10... | collective-permute-start | bytes 405512 | tf_op jit(solution)/shard_map/ppermute | solution.py:424
  54.8 5.0 %collective-permute-start.21 = (bf16[512,128]{1,0:T(8,128)(2,1)S(1)}, bf16[512,128]{1,0:T(8,128)(2,1)S(1)}, u32[]{:S(2)}, u32[]{:S(2)}) collective-permute-start(bf16[512,128]{1,0:T(8,128)(2,1)S(1)} %get-tuple-element.116.refs_2_.refs_12_), channel_id=1, source_target_pairs={{0,8},{8,0},{16,24},{24,16},{1,9},{9,1},{17,25},{25,17},{2,10},{10... | collective-permute-start | bytes 393224 | tf_op jit(solution)/shard_map/ppermute | solution.py:424
  56.1 6.2 %collective-permute-start.19 = (bf16[512,128]{1,0:T(8,128)(2,1)S(1)}, bf16[512,128]{1,0:T(8,128)(2,1)S(1)}, u32[]{:S(2)}, u32[]{:S(2)}) collective-permute-start(bf16[512,128]{1,0:T(8,128)(2,1)S(1)} %get-tuple-element.116.refs_2_.refs_12_), channel_id=1, source_target_pairs={{0,16},{8,24},{16,0},{24,8},{1,17},{9,25},{17,1},{25,9},{2,18},{10... | collective-permute-start | bytes 393224 | tf_op jit(solution)/shard_map/ppermute | solution.py:424
  58.4 5.9 %collective-permute-start.20 = (bf16[512,128]{1,0:T(8,128)(2,1)S(1)}, bf16[512,128]{1,0:T(8,128)(2,1)S(1)}, u32[]{:S(2)}, u32[]{:S(2)}) collective-permute-start(bf16[512,128]{1,0:T(8,128)(2,1)S(1)} %get-tuple-element.116.refs_2_.refs_12_), channel_id=1, source_target_pairs={{0,24},{8,16},{16,8},{24,0},{1,25},{9,17},{17,9},{25,1},{2,26},{10... | collective-permute-start | bytes 393224 | tf_op jit(solution)/shard_map/ppermute | solution.py:424
  65.9 6.9 %collective-permute-start.22 = (bf16[272,128]{1,0:T(8,128)(2,1)S(1)}, bf16[272,128]{1,0:T(8,128)(2,1)S(1)}, u32[]{:S(2)}, u32[]{:S(2)}) collective-permute-start(bf16[272,128]{1,0:T(8,128)(2,1)S(1)} %get-tuple-element.123), channel_id=1, source_target_pairs={{0,6},{1,7},{2,4},{3,5},{4,2},{5,3},{6,0},{7,1},{8,14},{9,15},{10,... | collective-permute-start | bytes 208904 | tf_op jit(solution)/shard_map/ppermute | solution.py:424
  68.2 5.5 %collective-permute-start.23 = (bf16[272,128]{1,0:T(8,128)(2,1)S(1)}, bf16[272,128]{1,0:T(8,128)(2,1)S(1)}, u32[]{:S(2)}, u32[]{:S(2)}) collective-permute-start(bf16[272,128]{1,0:T(8,128)(2,1)S(1)} %get-tuple-element.124), channel_id=1, source_target_pairs={{0,2},{1,3},{2,0},{3,1},{4,6},{5,7},{6,4},{7,5},{8,10},{9,11},{10,... | collective-permute-start | bytes 208904 | tf_op jit(solution)/shard_map/ppermute | solution.py:424
  68.3 7.4 %collective-permute-start.24 = (bf16[272,128]{1,0:T(8,128)(2,1)S(1)}, bf16[272,128]{1,0:T(8,128)(2,1)S(1)}, u32[]{:S(2)}, u32[]{:S(2)}) collective-permute-start(bf16[272,128]{1,0:T(8,128)(2,1)S(1)} %get-tuple-element.125), channel_id=1, source_target_pairs={{0,4},{1,5},{2,6},{3,7},{4,0},{5,1},{6,2},{7,3},{8,12},{9,13},{10,... | collective-permute-start | bytes 208904 | tf_op jit(solution)/shard_map/ppermute | solution.py:424
  75.7 6.2 %collective-permute-start.27 = (bf16[256,128]{1,0:T(8,128)(2,1)S(1)}, bf16[256,128]{1,0:T(8,128)(2,1)S(1)}, u32[]{:S(2)}, u32[]{:S(2)}) collective-permute-start(bf16[256,128]{1,0:T(8,128)(2,1)S(1)} %get-tuple-element.127.refs_2_.refs_24_), channel_id=1, source_target_pairs={{0,6},{1,7},{2,4},{3,5},{4,2},{5,3},{6,0},{7,1},{8,14},{9,15},{10,... | collective-permute-start | bytes 196616 | tf_op jit(solution)/shard_map/ppermute | solution.py:424
  77.4 5.8 %collective-permute-start.25 = (bf16[256,128]{1,0:T(8,128)(2,1)S(1)}, bf16[256,128]{1,0:T(8,128)(2,1)S(1)}, u32[]{:S(2)}, u32[]{:S(2)}) collective-permute-start(bf16[256,128]{1,0:T(8,128)(2,1)S(1)} %get-tuple-element.127.refs_2_.refs_24_), channel_id=1, source_target_pairs={{0,2},{1,3},{2,0},{3,1},{4,6},{5,7},{6,4},{7,5},{8,10},{9,11},{10,... | collective-permute-start | bytes 196616 | tf_op jit(solution)/shard_map/ppermute | solution.py:424
  77.4 5.9 %collective-permute-start.26 = (bf16[256,128]{1,0:T(8,128)(2,1)S(1)}, bf16[256,128]{1,0:T(8,128)(2,1)S(1)}, u32[]{:S(2)}, u32[]{:S(2)}) collective-permute-start(bf16[256,128]{1,0:T(8,128)(2,1)S(1)} %get-tuple-element.127.refs_2_.refs_24_), channel_id=1, source_target_pairs={{0,4},{1,5},{2,6},{3,7},{4,0},{5,1},{6,2},{7,3},{8,12},{9,13},{10,... | collective-permute-start | bytes 196616 | tf_op jit(solution)/shard_map/ppermute | solution.py:424
  84.5 5.1 %collective-permute-start.28 = (bf16[528,128]{1,0:T(8,128)(2,1)S(1)}, bf16[528,128]{1,0:T(8,128)(2,1)S(1)}, u32[]{:S(2)}, u32[]{:S(2)}) collective-permute-start(bf16[528,128]{1,0:T(8,128)(2,1)S(1)} %get-tuple-element.134), channel_id=1, source_target_pairs={{0,8},{8,0},{16,24},{24,16},{1,9},{9,1},{17,25},{25,17},{2,10},{10... | collective-permute-start | bytes 405512 | tf_op jit(solution)/shard_map/ppermute | solution.py:424
  84.5 5.2 %collective-permute-start.29 = (bf16[528,128]{1,0:T(8,128)(2,1)S(1)}, bf16[528,128]{1,0:T(8,128)(2,1)S(1)}, u32[]{:S(2)}, u32[]{:S(2)}) collective-permute-start(bf16[528,128]{1,0:T(8,128)(2,1)S(1)} %get-tuple-element.135), channel_id=1, source_target_pairs={{0,16},{8,24},{16,0},{24,8},{1,17},{9,25},{17,1},{25,9},{2,18},{10... | collective-permute-start | bytes 405512 | tf_op jit(solution)/shard_map/ppermute | solution.py:424
  85.6 5.9 %collective-permute-start.30 = (bf16[528,128]{1,0:T(8,128)(2,1)S(1)}, bf16[528,128]{1,0:T(8,128)(2,1)S(1)}, u32[]{:S(2)}, u32[]{:S(2)}) collective-permute-start(bf16[528,128]{1,0:T(8,128)(2,1)S(1)} %get-tuple-element.136), channel_id=1, source_target_pairs={{0,24},{8,16},{16,8},{24,0},{1,25},{9,17},{17,9},{25,1},{2,26},{10... | collective-permute-start | bytes 405512 | tf_op jit(solution)/shard_map/ppermute | solution.py:424
  94.6 5.9 %collective-permute-start.32 = (bf16[512,128]{1,0:T(8,128)(2,1)S(1)}, bf16[512,128]{1,0:T(8,128)(2,1)S(1)}, u32[]{:S(2)}, u32[]{:S(2)}) collective-permute-start(bf16[512,128]{1,0:T(8,128)(2,1)S(1)} %get-tuple-element.139.refs_2_.refs_16_), channel_id=1, source_target_pairs={{0,24},{8,16},{16,8},{24,0},{1,25},{9,17},{17,9},{25,1},{2,26},{10... | collective-permute-start | bytes 393224 | tf_op jit(solution)/shard_map/ppermute | solution.py:424
  102.1 6.2 %collective-permute-start.34 = (bf16[272,128]{1,0:T(8,128)(2,1)S(1)}, bf16[272,128]{1,0:T(8,128)(2,1)S(1)}, u32[]{:S(2)}, u32[]{:S(2)}) collective-permute-start(bf16[272,128]{1,0:T(8,128)(2,1)S(1)} %get-tuple-element.146), channel_id=1, source_target_pairs={{0,6},{1,7},{2,4},{3,5},{4,2},{5,3},{6,0},{7,1},{8,14},{9,15},{10,... | collective-permute-start | bytes 208904 | tf_op jit(solution)/shard_map/ppermute | solution.py:424
  103.8 5.1 %collective-permute-start.35 = (bf16[272,128]{1,0:T(8,128)(2,1)S(1)}, bf16[272,128]{1,0:T(8,128)(2,1)S(1)}, u32[]{:S(2)}, u32[]{:S(2)}) collective-permute-start(bf16[272,128]{1,0:T(8,128)(2,1)S(1)} %get-tuple-element.147), channel_id=1, source_target_pairs={{0,2},{1,3},{2,0},{3,1},{4,6},{5,7},{6,4},{7,5},{8,10},{9,11},{10,... | collective-permute-start | bytes 208904 | tf_op jit(solution)/shard_map/ppermute | solution.py:424
  104.8 6.0 %collective-permute-start.36 = (bf16[272,128]{1,0:T(8,128)(2,1)S(1)}, bf16[272,128]{1,0:T(8,128)(2,1)S(1)}, u32[]{:S(2)}, u32[]{:S(2)}) collective-permute-start(bf16[272,128]{1,0:T(8,128)(2,1)S(1)} %get-tuple-element.148), channel_id=1, source_target_pairs={{0,4},{1,5},{2,6},{3,7},{4,0},{5,1},{6,2},{7,3},{8,12},{9,13},{10,... | collective-permute-start | bytes 208904 | tf_op jit(solution)/shard_map/ppermute | solution.py:424
  110.8 6.1 %collective-permute-start.37 = (bf16[256,128]{1,0:T(8,128)(2,1)S(1)}, bf16[256,128]{1,0:T(8,128)(2,1)S(1)}, u32[]{:S(2)}, u32[]{:S(2)}) collective-permute-start(bf16[256,128]{1,0:T(8,128)(2,1)S(1)} %get-tuple-element.151.refs_0_.refs_28_), channel_id=1, source_target_pairs={{0,6},{1,7},{2,4},{3,5},{4,2},{5,3},{6,0},{7,1},{8,14},{9,15},{10,... | collective-permute-start | bytes 196616 | tf_op jit(solution)/shard_map/ppermute | solution.py:424
  111.6 5.3 %collective-permute-start.38 = (bf16[256,128]{1,0:T(8,128)(2,1)S(1)}, bf16[256,128]{1,0:T(8,128)(2,1)S(1)}, u32[]{:S(2)}, u32[]{:S(2)}) collective-permute-start(bf16[256,128]{1,0:T(8,128)(2,1)S(1)} %get-tuple-element.151.refs_0_.refs_28_), channel_id=1, source_target_pairs={{0,2},{1,3},{2,0},{3,1},{4,6},{5,7},{6,4},{7,5},{8,10},{9,11},{10,... | collective-permute-start | bytes 196616 | tf_op jit(solution)/shard_map/ppermute | solution.py:424
  112.4 5.2 %collective-permute-start.39 = (bf16[256,128]{1,0:T(8,128)(2,1)S(1)}, bf16[256,128]{1,0:T(8,128)(2,1)S(1)}, u32[]{:S(2)}, u32[]{:S(2)}) collective-permute-start(bf16[256,128]{1,0:T(8,128)(2,1)S(1)} %get-tuple-element.151.refs_0_.refs_28_), channel_id=1, source_target_pairs={{0,4},{1,5},{2,6},{3,7},{4,0},{5,1},{6,2},{7,3},{8,12},{9,13},{10,... | collective-permute-start | bytes 196616 | tf_op jit(solution)/shard_map/ppermute | solution.py:424
  (16 other events, 106.3 us)

commit v11 on v10

--- a/solution.py
+++ b/solution.py
@@ -277,7 +277,7 @@
             at = pl.ds(pl.multiple_of((here ^ offset) * way.part + half * way.length, way.part), way.part)
             folded += put_chunk(chunk[half * way.part : (half + 1) * way.part, :], plain_ref, turned_ref, at, way.sign)
     low, high = list_ref[1, at_group], list_ref[1, at_group + 1]
-    width = LAST_WIDTH if last else WIDTH
+    width = min(LAST_WIDTH * len(pick), 2 * LAST_WIDTH) if last else WIDTH
 
     def turn_of(group, carry):
         for lane in range(width):
@@ -434,7 +434,9 @@
 
     def groups_of(order, way):
         half = len(order) // 2
-        return (order[:1], order[1:half], order[half:]) if way.part % way.size == 0 else (order,)
+        if way.part % way.size:
+            return (order,)
+        return (order[:1], order[1:half], order[half:-1], order[-1:]) if way.halves == 2 else (order[:1], order[1:half], order[half:])
 
     def body(record, tile_data, tile_rows, tile_cols, tile_counts):
         own_tiles = tile_data[0, 0]

time: 128 us -> 130 us (1.016); the launches traced: 127 us -> 131 us
  waiting for transfers between devices: 45.8 us -> 48 us
  Pallas kernels: 25.3 us -> 26.7 us
    ppermute x45, waiting for transfers between devices: 45.8 us -> 48 us  [swap(): return lax.ppermute(value, axis, [(i, i ^ offset) for i in range(size)])]
    pallas_call x27 -> x30, Pallas kernels: 25.3 us -> 26.7 us  [call(): pl.pallas_call(kernel, name=name, out_shape=[jax.ShapeDtypeStruct(s, d) f...]
  transfers between devices with their start and end apart: 45 -> 45, of which waited for: 35 -> 37; matrix products, arithmetic and copies ran while one was open for 0% -> 0% of each run, Pallas kernels for 11% -> 13%
where the time goes in v11:
time: 130 us; the launch traced here: 131 us
  starting transfers between devices  54.5 us (42%)
  waiting for transfers between devices  48 us (37%)
  Pallas kernels  26.7 us (21%)
  between operations  1.72 us (1%)
    ppermute x45, starting transfers between devices, swap(): return lax.ppermute(value, axis, [(i, i ^ offset) for i in range(size)])  54.5 us
    ppermute x45, waiting for transfers between devices, swap(): return lax.ppermute(value, axis, [(i, i ^ offset) for i in range(size)])  48 us
    pallas_call x30, Pallas kernels, call(): pl.pallas_call(kernel, name=name, out_shape=[jax.ShapeDtypeStruct(s, d) f...  26.7 us
  transfers between devices with their start and end apart: 45, of which 37 were waited for; matrix products, arithmetic and copies ran while one was open for 0% of the time, Pallas kernels for 13%

profile of v11, /device:TPU:0, one launch (start us, length us, event | category | flops | bytes accessed | tf_op | source)
XLA Modules:
  0.0 130.9 jit_solution(8807307429881190799)
XLA Ops:
  2.5 2.8 %pack.1 = (bf16[48,2,128,128]{3,2,1,0:T(8,128)(2,1)S(1)}, bf16[48,128,256]{2,1,0:T(8,128)(2,1)S(1)}, f32[1152,128]{1,0:T(8,128)S(1)}, bf16[1024,128]{1,0:T(8,128)(2,1)S(1)}, bf16[1024,128]{1,0:T(8,128)(2,1)S(1)}) custom-call(f32[2,1024,128]{2,1,0:T(8,128)} %record_ref.1, bf16[24,2,128,128]{3,2,1,0:T(8,128)(2,1)} %bitcast.12, s32[1,24]{1,0:T(1,128)} %bitcast.6, ...), custom_call_target="tpu_custom_call" | custom-call | tf_op jit(solution)/shard_map/pack/pallas_call | solution.py:52
  6.8 3.0 %collective-permute-start.4 = (bf16[512,128]{1,0:T(8,128)(2,1)S(1)}, bf16[512,128]{1,0:T(8,128)(2,1)S(1)}, u32[]{:S(2)}, u32[]{:S(2)}) collective-permute-start(bf16[512,128]{1,0:T(8,128)(2,1)S(1)} %get-tuple-element.97), channel_id=1, source_target_pairs={{0,8},{8,0},{16,24},{24,16},{1,9},{9,1},{17,25},{25,17},{2,10},{10... | collective-permute-start | bytes 393224 | tf_op jit(solution)/shard_map/ppermute | solution.py:424
  9.8 1.9 %collective-permute-start.5 = (bf16[512,128]{1,0:T(8,128)(2,1)S(1)}, bf16[512,128]{1,0:T(8,128)(2,1)S(1)}, u32[]{:S(2)}, u32[]{:S(2)}) collective-permute-start(bf16[512,128]{1,0:T(8,128)(2,1)S(1)} %get-tuple-element.98), channel_id=1, source_target_pairs={{0,16},{8,24},{16,0},{24,8},{1,17},{9,25},{17,1},{25,9},{2,18},{10... | collective-permute-start | bytes 393224 | tf_op jit(solution)/shard_map/ppermute | solution.py:424
  11.6 2.0 %collective-permute-done.4.refs_0_ = bf16[512,128]{1,0:T(8,128)(2,1)S(1)} collective-permute-done((bf16[512,128]{1,0:T(8,128)(2,1)S(1)}, bf16[512,128]{1,0:T(8,128)(2,1)S(1)}, u32[]{:S(2)}, u32[]{:S(2)}) %collective-permute-start.4) | collective-permute-done | bytes 131104 | tf_op jit(solution)/shard_map/ppermute | solution.py:424
  13.6 3.5 %collective-permute-done.5.refs_1_ = bf16[512,128]{1,0:T(8,128)(2,1)S(1)} collective-permute-done((bf16[512,128]{1,0:T(8,128)(2,1)S(1)}, bf16[512,128]{1,0:T(8,128)(2,1)S(1)}, u32[]{:S(2)}, u32[]{:S(2)}) %collective-permute-start.5) | collective-permute-done | bytes 131104 | tf_op jit(solution)/shard_map/ppermute | solution.py:424
  24.8 1.8 %collective-permute-done.8.refs_2_.refs_10_ = bf16[512,128]{1,0:T(8,128)(2,1)S(1)} collective-permute-done((bf16[512,128]{1,0:T(8,128)(2,1)S(1)}, bf16[512,128]{1,0:T(8,128)(2,1)S(1)}, u32[]{:S(2)}, u32[]{:S(2)}) %collective-permute-start.8) | collective-permute-done | bytes 131104 | tf_op jit(solution)/shard_map/ppermute | solution.py:424
  28.8 3.6 %collective-permute-start.10 = (bf16[272,128]{1,0:T(8,128)(2,1)S(1)}, bf16[272,128]{1,0:T(8,128)(2,1)S(1)}, u32[]{:S(2)}, u32[]{:S(2)}) collective-permute-start(bf16[272,128]{1,0:T(8,128)(2,1)S(1)} %get-tuple-element.109), channel_id=1, source_target_pairs={{0,6},{1,7},{2,4},{3,5},{4,2},{5,3},{6,0},{7,1},{8,14},{9,15},{10,... | collective-permute-start | bytes 208904 | tf_op jit(solution)/shard_map/ppermute | solution.py:424
  33.3 2.1 %collective-permute-done.10.refs_0_ = bf16[272,128]{1,0:T(8,128)(2,1)S(1)} collective-permute-done((bf16[272,128]{1,0:T(8,128)(2,1)S(1)}, bf16[272,128]{1,0:T(8,128)(2,1)S(1)}, u32[]{:S(2)}, u32[]{:S(2)}) %collective-permute-start.10) | collective-permute-done | bytes 69664 | tf_op jit(solution)/shard_map/ppermute | solution.py:424
  36.8 2.4 %collective-permute-done.12.refs_2_ = bf16[272,128]{1,0:T(8,128)(2,1)S(1)} collective-permute-done((bf16[272,128]{1,0:T(8,128)(2,1)S(1)}, bf16[272,128]{1,0:T(8,128)(2,1)S(1)}, u32[]{:S(2)}, u32[]{:S(2)}) %collective-permute-start.12) | collective-permute-done | bytes 69664 | tf_op jit(solution)/shard_map/ppermute | solution.py:424
  39.2 2.4 %collective-permute-start.15 = (bf16[256,128]{1,0:T(8,128)(2,1)S(1)}, bf16[256,128]{1,0:T(8,128)(2,1)S(1)}, u32[]{:S(2)}, u32[]{:S(2)}) collective-permute-start(bf16[256,128]{1,0:T(8,128)(2,1)S(1)} %get-tuple-element.112.refs_2_.refs_20_), channel_id=1, source_target_pairs={{0,6},{1,7},{2,4},{3,5},{4,2},{5,3},{6,0},{7,1},{8,14},{9,15},{10,... | collective-permute-start | bytes 196616 | tf_op jit(solution)/shard_map/ppermute | solution.py:424
  41.6 2.0 %collective-permute-start.14 = (bf16[256,128]{1,0:T(8,128)(2,1)S(1)}, bf16[256,128]{1,0:T(8,128)(2,1)S(1)}, u32[]{:S(2)}, u32[]{:S(2)}) collective-permute-start(bf16[256,128]{1,0:T(8,128)(2,1)S(1)} %get-tuple-element.112.refs_2_.refs_20_), channel_id=1, source_target_pairs={{0,4},{1,5},{2,6},{3,7},{4,0},{5,1},{6,2},{7,3},{8,12},{9,13},{10,... | collective-permute-start | bytes 196616 | tf_op jit(solution)/shard_map/ppermute | solution.py:424
  49.2 2.2 %collective-permute-start.17 = (bf16[528,128]{1,0:T(8,128)(2,1)S(1)}, bf16[528,128]{1,0:T(8,128)(2,1)S(1)}, u32[]{:S(2)}, u32[]{:S(2)}) collective-permute-start(bf16[528,128]{1,0:T(8,128)(2,1)S(1)} %get-tuple-element.120), channel_id=1, source_target_pairs={{0,16},{8,24},{16,0},{24,8},{1,17},{9,25},{17,1},{25,9},{2,18},{10... | collective-permute-start | bytes 405512 | tf_op jit(solution)/shard_map/ppermute | solution.py:424
  51.7 2.3 %collective-permute-done.16.refs_0_ = bf16[528,128]{1,0:T(8,128)(2,1)S(1)} collective-permute-done((bf16[528,128]{1,0:T(8,128)(2,1)S(1)}, bf16[528,128]{1,0:T(8,128)(2,1)S(1)}, u32[]{:S(2)}, u32[]{:S(2)}) %collective-permute-start.16) | collective-permute-done | bytes 135200 | tf_op jit(solution)/shard_map/ppermute | solution.py:424
  54.0 3.8 %collective-permute-done.17.refs_1_ = bf16[528,128]{1,0:T(8,128)(2,1)S(1)} collective-permute-done((bf16[528,128]{1,0:T(8,128)(2,1)S(1)}, bf16[528,128]{1,0:T(8,128)(2,1)S(1)}, u32[]{:S(2)}, u32[]{:S(2)}) %collective-permute-start.17) | collective-permute-done | bytes 135200 | tf_op jit(solution)/shard_map/ppermute | solution.py:424
  58.3 1.8 %collective-permute-start.21 = (bf16[512,128]{1,0:T(8,128)(2,1)S(1)}, bf16[512,128]{1,0:T(8,128)(2,1)S(1)}, u32[]{:S(2)}, u32[]{:S(2)}) collective-permute-start(bf16[512,128]{1,0:T(8,128)(2,1)S(1)} %get-tuple-element.124.refs_2_.refs_12_), channel_id=1, source_target_pairs={{0,8},{8,0},{16,24},{24,16},{1,9},{9,1},{17,25},{25,17},{2,10},{10... | collective-permute-start | bytes 393224 | tf_op jit(solution)/shard_map/ppermute | solution.py:424
  67.8 1.9 %collective-permute-start.22 = (bf16[272,128]{1,0:T(8,128)(2,1)S(1)}, bf16[272,128]{1,0:T(8,128)(2,1)S(1)}, u32[]{:S(2)}, u32[]{:S(2)}) collective-permute-start(bf16[272,128]{1,0:T(8,128)(2,1)S(1)} %get-tuple-element.133), channel_id=1, source_target_pairs={{0,6},{1,7},{2,4},{3,5},{4,2},{5,3},{6,0},{7,1},{8,14},{9,15},{10,... | collective-permute-start | bytes 208904 | tf_op jit(solution)/shard_map/ppermute | solution.py:424
  70.1 2.2 %collective-permute-start.24 = (bf16[272,128]{1,0:T(8,128)(2,1)S(1)}, bf16[272,128]{1,0:T(8,128)(2,1)S(1)}, u32[]{:S(2)}, u32[]{:S(2)}) collective-permute-start(bf16[272,128]{1,0:T(8,128)(2,1)S(1)} %get-tuple-element.135), channel_id=1, source_target_pairs={{0,4},{1,5},{2,6},{3,7},{4,0},{5,1},{6,2},{7,3},{8,12},{9,13},{10,... | collective-permute-start | bytes 208904 | tf_op jit(solution)/shard_map/ppermute | solution.py:424
  72.2 2.5 %collective-permute-done.22.refs_0_ = bf16[272,128]{1,0:T(8,128)(2,1)S(1)} collective-permute-done((bf16[272,128]{1,0:T(8,128)(2,1)S(1)}, bf16[272,128]{1,0:T(8,128)(2,1)S(1)}, u32[]{:S(2)}, u32[]{:S(2)}) %collective-permute-start.22) | collective-permute-done | bytes 69664 | tf_op jit(solution)/shard_map/ppermute | solution.py:424
  74.7 1.6 %collective-permute-done.23.refs_1_ = bf16[272,128]{1,0:T(8,128)(2,1)S(1)} collective-permute-done((bf16[272,128]{1,0:T(8,128)(2,1)S(1)}, bf16[272,128]{1,0:T(8,128)(2,1)S(1)}, u32[]{:S(2)}, u32[]{:S(2)}) %collective-permute-start.23) | collective-permute-done | bytes 69664 | tf_op jit(solution)/shard_map/ppermute | solution.py:424
  77.1 2.0 %collective-permute-start.27 = (bf16[256,128]{1,0:T(8,128)(2,1)S(1)}, bf16[256,128]{1,0:T(8,128)(2,1)S(1)}, u32[]{:S(2)}, u32[]{:S(2)}) collective-permute-start(bf16[256,128]{1,0:T(8,128)(2,1)S(1)} %get-tuple-element.137.refs_2_.refs_24_), channel_id=1, source_target_pairs={{0,6},{1,7},{2,4},{3,5},{4,2},{5,3},{6,0},{7,1},{8,14},{9,15},{10,... | collective-permute-start | bytes 196616 | tf_op jit(solution)/shard_map/ppermute | solution.py:424
  79.2 2.4 %collective-permute-start.26 = (bf16[256,128]{1,0:T(8,128)(2,1)S(1)}, bf16[256,128]{1,0:T(8,128)(2,1)S(1)}, u32[]{:S(2)}, u32[]{:S(2)}) collective-permute-start(bf16[256,128]{1,0:T(8,128)(2,1)S(1)} %get-tuple-element.137.refs_2_.refs_24_), channel_id=1, source_target_pairs={{0,4},{1,5},{2,6},{3,7},{4,0},{5,1},{6,2},{7,3},{8,12},{9,13},{10,... | collective-permute-start | bytes 196616 | tf_op jit(solution)/shard_map/ppermute | solution.py:424
  87.1 1.5 %collective-permute-start.29 = (bf16[528,128]{1,0:T(8,128)(2,1)S(1)}, bf16[528,128]{1,0:T(8,128)(2,1)S(1)}, u32[]{:S(2)}, u32[]{:S(2)}) collective-permute-start(bf16[528,128]{1,0:T(8,128)(2,1)S(1)} %get-tuple-element.145), channel_id=1, source_target_pairs={{0,16},{8,24},{16,0},{24,8},{1,17},{9,25},{17,1},{25,9},{2,18},{10... | collective-permute-start | bytes 405512 | tf_op jit(solution)/shard_map/ppermute | solution.py:424
  92.1 2.4 %collective-permute-done.30.refs_2_ = bf16[528,128]{1,0:T(8,128)(2,1)S(1)} collective-permute-done((bf16[528,128]{1,0:T(8,128)(2,1)S(1)}, bf16[528,128]{1,0:T(8,128)(2,1)S(1)}, u32[]{:S(2)}, u32[]{:S(2)}) %collective-permute-start.30) | collective-permute-done | bytes 135200 | tf_op jit(solution)/shard_map/ppermute | solution.py:424
  96.2 2.0 %collective-permute-start.31 = (bf16[512,128]{1,0:T(8,128)(2,1)S(1)}, bf16[512,128]{1,0:T(8,128)(2,1)S(1)}, u32[]{:S(2)}, u32[]{:S(2)}) collective-permute-start(bf16[512,128]{1,0:T(8,128)(2,1)S(1)} %get-tuple-element.149.refs_2_.refs_16_), channel_id=1, source_target_pairs={{0,24},{8,16},{16,8},{24,0},{1,25},{9,17},{17,9},{25,1},{2,26},{10... | collective-permute-start | bytes 393224 | tf_op jit(solution)/shard_map/ppermute | solution.py:424
  103.3 2.0 %collective-permute-start.34 = (bf16[272,128]{1,0:T(8,128)(2,1)S(1)}, bf16[272,128]{1,0:T(8,128)(2,1)S(1)}, u32[]{:S(2)}, u32[]{:S(2)}) collective-permute-start(bf16[272,128]{1,0:T(8,128)(2,1)S(1)} %get-tuple-element.158), channel_id=1, source_target_pairs={{0,6},{1,7},{2,4},{3,5},{4,2},{5,3},{6,0},{7,1},{8,14},{9,15},{10,... | collective-permute-start | bytes 208904 | tf_op jit(solution)/shard_map/ppermute | solution.py:424
  106.0 1.7 %collective-permute-start.36 = (bf16[272,128]{1,0:T(8,128)(2,1)S(1)}, bf16[272,128]{1,0:T(8,128)(2,1)S(1)}, u32[]{:S(2)}, u32[]{:S(2)}) collective-permute-start(bf16[272,128]{1,0:T(8,128)(2,1)S(1)} %get-tuple-element.160), channel_id=1, source_target_pairs={{0,4},{1,5},{2,6},{3,7},{4,0},{5,1},{6,2},{7,3},{8,12},{9,13},{10,... | collective-permute-start | bytes 208904 | tf_op jit(solution)/shard_map/ppermute | solution.py:424
  107.7 1.9 %collective-permute-done.34.refs_0_ = bf16[272,128]{1,0:T(8,128)(2,1)S(1)} collective-permute-done((bf16[272,128]{1,0:T(8,128)(2,1)S(1)}, bf16[272,128]{1,0:T(8,128)(2,1)S(1)}, u32[]{:S(2)}, u32[]{:S(2)}) %collective-permute-start.34) | collective-permute-done | bytes 69664 | tf_op jit(solution)/shard_map/ppermute | solution.py:424
  111.2 2.1 %collective-permute-start.37 = (bf16[256,128]{1,0:T(8,128)(2,1)S(1)}, bf16[256,128]{1,0:T(8,128)(2,1)S(1)}, u32[]{:S(2)}, u32[]{:S(2)}) collective-permute-start(bf16[256,128]{1,0:T(8,128)(2,1)S(1)} %get-tuple-element.163.refs_0_.refs_28_), channel_id=1, source_target_pairs={{0,6},{1,7},{2,4},{3,5},{4,2},{5,3},{6,0},{7,1},{8,14},{9,15},{10,... | collective-permute-start | bytes 196616 | tf_op jit(solution)/shard_map/ppermute | solution.py:424
  113.7 2.0 %collective-permute-start.39 = (bf16[256,128]{1,0:T(8,128)(2,1)S(1)}, bf16[256,128]{1,0:T(8,128)(2,1)S(1)}, u32[]{:S(2)}, u32[]{:S(2)}) collective-permute-start(bf16[256,128]{1,0:T(8,128)(2,1)S(1)} %get-tuple-element.163.refs_0_.refs_28_), channel_id=1, source_target_pairs={{0,4},{1,5},{2,6},{3,7},{4,0},{5,1},{6,2},{7,3},{8,12},{9,13},{10,... | collective-permute-start | bytes 196616 | tf_op jit(solution)/shard_map/ppermute | solution.py:424
  115.7 1.7 %collective-permute-done.37.refs_1_.refs_29_ = bf16[256,128]{1,0:T(8,128)(2,1)S(1)} collective-permute-done((bf16[256,128]{1,0:T(8,128)(2,1)S(1)}, bf16[256,128]{1,0:T(8,128)(2,1)S(1)}, u32[]{:S(2)}, u32[]{:S(2)}) %collective-permute-start.37) | collective-permute-done | bytes 65568 | tf_op jit(solution)/shard_map/ppermute | solution.py:424
  120.0 2.2 %collective-permute-start.41 = (f32[8,128]{1,0:T(8,128)S(1)}, f32[8,128]{1,0:T(8,128)S(1)}, u32[]{:S(2)}, u32[]{:S(2)}) collective-permute-start(f32[8,128]{1,0:T(8,128)S(1)} %norm.1.refs_0_), channel_id=1, source_target_pairs={{0,16},{8,24},{16,0},{24,8},{1,17},{9,25},{17,1},{25,9},{2,18},{10... | collective-permute-start | bytes 12296 | tf_op jit(solution)/shard_map/ppermute | solution.py:424
  123.7 2.9 %collective-permute-done.42.refs_3_ = f32[8,128]{1,0:T(8,128)S(1)} collective-permute-done((f32[8,128]{1,0:T(8,128)S(1)}, f32[8,128]{1,0:T(8,128)S(1)}, u32[]{:S(2)}, u32[]{:S(2)}) %collective-permute-start.42) | collective-permute-done | bytes 4128 | tf_op jit(solution)/shard_map/ppermute | solution.py:424
  (95 shorter events, 56.5 us)
Async XLA Ops:
  6.8 6.9 %collective-permute-start.4 = (bf16[512,128]{1,0:T(8,128)(2,1)S(1)}, bf16[512,128]{1,0:T(8,128)(2,1)S(1)}, u32[]{:S(2)}, u32[]{:S(2)}) collective-permute-start(bf16[512,128]{1,0:T(8,128)(2,1)S(1)} %get-tuple-element.97), channel_id=1, source_target_pairs={{0,8},{8,0},{16,24},{24,16},{1,9},{9,1},{17,25},{25,17},{2,10},{10... | collective-permute-start | bytes 393224 | tf_op jit(solution)/shard_map/ppermute | solution.py:424
  9.8 7.4 %collective-permute-start.5 = (bf16[512,128]{1,0:T(8,128)(2,1)S(1)}, bf16[512,128]{1,0:T(8,128)(2,1)S(1)}, u32[]{:S(2)}, u32[]{:S(2)}) collective-permute-start(bf16[512,128]{1,0:T(8,128)(2,1)S(1)} %get-tuple-element.98), channel_id=1, source_target_pairs={{0,16},{8,24},{16,0},{24,8},{1,17},{9,25},{17,1},{25,9},{2,18},{10... | collective-permute-start | bytes 393224 | tf_op jit(solution)/shard_map/ppermute | solution.py:424
  11.6 6.3 %collective-permute-start.6 = (bf16[512,128]{1,0:T(8,128)(2,1)S(1)}, bf16[512,128]{1,0:T(8,128)(2,1)S(1)}, u32[]{:S(2)}, u32[]{:S(2)}) collective-permute-start(bf16[512,128]{1,0:T(8,128)(2,1)S(1)} %get-tuple-element.99), channel_id=1, source_target_pairs={{0,24},{8,16},{16,8},{24,0},{1,25},{9,17},{17,9},{25,1},{2,26},{10... | collective-permute-start | bytes 393224 | tf_op jit(solution)/shard_map/ppermute | solution.py:424
  18.0 5.8 %collective-permute-start.9 = (bf16[512,128]{1,0:T(8,128)(2,1)S(1)}, bf16[512,128]{1,0:T(8,128)(2,1)S(1)}, u32[]{:S(2)}, u32[]{:S(2)}) collective-permute-start(bf16[512,128]{1,0:T(8,128)(2,1)S(1)} %get-tuple-element.100.refs_2_.refs_8_), channel_id=1, source_target_pairs={{0,8},{8,0},{16,24},{24,16},{1,9},{9,1},{17,25},{25,17},{2,10},{10... | collective-permute-start | bytes 393224 | tf_op jit(solution)/shard_map/ppermute | solution.py:424
  19.5 7.2 %collective-permute-start.8 = (bf16[512,128]{1,0:T(8,128)(2,1)S(1)}, bf16[512,128]{1,0:T(8,128)(2,1)S(1)}, u32[]{:S(2)}, u32[]{:S(2)}) collective-permute-start(bf16[512,128]{1,0:T(8,128)(2,1)S(1)} %get-tuple-element.100.refs_2_.refs_8_), channel_id=1, source_target_pairs={{0,16},{8,24},{16,0},{24,8},{1,17},{9,25},{17,1},{25,9},{2,18},{10... | collective-permute-start | bytes 393224 | tf_op jit(solution)/shard_map/ppermute | solution.py:424
  20.3 7.4 %collective-permute-start.7 = (bf16[512,128]{1,0:T(8,128)(2,1)S(1)}, bf16[512,128]{1,0:T(8,128)(2,1)S(1)}, u32[]{:S(2)}, u32[]{:S(2)}) collective-permute-start(bf16[512,128]{1,0:T(8,128)(2,1)S(1)} %get-tuple-element.100.refs_2_.refs_8_), channel_id=1, source_target_pairs={{0,24},{8,16},{16,8},{24,0},{1,25},{9,17},{17,9},{25,1},{2,26},{10... | collective-permute-start | bytes 393224 | tf_op jit(solution)/shard_map/ppermute | solution.py:424
  28.8 6.5 %collective-permute-start.10 = (bf16[272,128]{1,0:T(8,128)(2,1)S(1)}, bf16[272,128]{1,0:T(8,128)(2,1)S(1)}, u32[]{:S(2)}, u32[]{:S(2)}) collective-permute-start(bf16[272,128]{1,0:T(8,128)(2,1)S(1)} %get-tuple-element.109), channel_id=1, source_target_pairs={{0,6},{1,7},{2,4},{3,5},{4,2},{5,3},{6,0},{7,1},{8,14},{9,15},{10,... | collective-permute-start | bytes 208904 | tf_op jit(solution)/shard_map/ppermute | solution.py:424
  32.5 6.7 %collective-permute-start.12 = (bf16[272,128]{1,0:T(8,128)(2,1)S(1)}, bf16[272,128]{1,0:T(8,128)(2,1)S(1)}, u32[]{:S(2)}, u32[]{:S(2)}) collective-permute-start(bf16[272,128]{1,0:T(8,128)(2,1)S(1)} %get-tuple-element.111), channel_id=1, source_target_pairs={{0,4},{1,5},{2,6},{3,7},{4,0},{5,1},{6,2},{7,3},{8,12},{9,13},{10,... | collective-permute-start | bytes 208904 | tf_op jit(solution)/shard_map/ppermute | solution.py:424
  39.2 6.1 %collective-permute-start.15 = (bf16[256,128]{1,0:T(8,128)(2,1)S(1)}, bf16[256,128]{1,0:T(8,128)(2,1)S(1)}, u32[]{:S(2)}, u32[]{:S(2)}) collective-permute-start(bf16[256,128]{1,0:T(8,128)(2,1)S(1)} %get-tuple-element.112.refs_2_.refs_20_), channel_id=1, source_target_pairs={{0,6},{1,7},{2,4},{3,5},{4,2},{5,3},{6,0},{7,1},{8,14},{9,15},{10,... | collective-permute-start | bytes 196616 | tf_op jit(solution)/shard_map/ppermute | solution.py:424
  41.6 5.2 %collective-permute-start.14 = (bf16[256,128]{1,0:T(8,128)(2,1)S(1)}, bf16[256,128]{1,0:T(8,128)(2,1)S(1)}, u32[]{:S(2)}, u32[]{:S(2)}) collective-permute-start(bf16[256,128]{1,0:T(8,128)(2,1)S(1)} %get-tuple-element.112.refs_2_.refs_20_), channel_id=1, source_target_pairs={{0,4},{1,5},{2,6},{3,7},{4,0},{5,1},{6,2},{7,3},{8,12},{9,13},{10,... | collective-permute-start | bytes 196616 | tf_op jit(solution)/shard_map/ppermute | solution.py:424
  48.2 5.8 %collective-permute-start.16 = (bf16[528,128]{1,0:T(8,128)(2,1)S(1)}, bf16[528,128]{1,0:T(8,128)(2,1)S(1)}, u32[]{:S(2)}, u32[]{:S(2)}) collective-permute-start(bf16[528,128]{1,0:T(8,128)(2,1)S(1)} %get-tuple-element.119), channel_id=1, source_target_pairs={{0,8},{8,0},{16,24},{24,16},{1,9},{9,1},{17,25},{25,17},{2,10},{10... | collective-permute-start | bytes 405512 | tf_op jit(solution)/shard_map/ppermute | solution.py:424
  49.2 8.6 %collective-permute-start.17 = (bf16[528,128]{1,0:T(8,128)(2,1)S(1)}, bf16[528,128]{1,0:T(8,128)(2,1)S(1)}, u32[]{:S(2)}, u32[]{:S(2)}) collective-permute-start(bf16[528,128]{1,0:T(8,128)(2,1)S(1)} %get-tuple-element.120), channel_id=1, source_target_pairs={{0,16},{8,24},{16,0},{24,8},{1,17},{9,25},{17,1},{25,9},{2,18},{10... | collective-permute-start | bytes 405512 | tf_op jit(solution)/shard_map/ppermute | solution.py:424
  51.4 6.8 %collective-permute-start.18 = (bf16[528,128]{1,0:T(8,128)(2,1)S(1)}, bf16[528,128]{1,0:T(8,128)(2,1)S(1)}, u32[]{:S(2)}, u32[]{:S(2)}) collective-permute-start(bf16[528,128]{1,0:T(8,128)(2,1)S(1)} %get-tuple-element.121), channel_id=1, source_target_pairs={{0,24},{8,16},{16,8},{24,0},{1,25},{9,17},{17,9},{25,1},{2,26},{10... | collective-permute-start | bytes 405512 | tf_op jit(solution)/shard_map/ppermute | solution.py:424
  58.3 5.0 %collective-permute-start.21 = (bf16[512,128]{1,0:T(8,128)(2,1)S(1)}, bf16[512,128]{1,0:T(8,128)(2,1)S(1)}, u32[]{:S(2)}, u32[]{:S(2)}) collective-permute-start(bf16[512,128]{1,0:T(8,128)(2,1)S(1)} %get-tuple-element.124.refs_2_.refs_12_), channel_id=1, source_target_pairs={{0,8},{8,0},{16,24},{24,16},{1,9},{9,1},{17,25},{25,17},{2,10},{10... | collective-permute-start | bytes 393224 | tf_op jit(solution)/shard_map/ppermute | solution.py:424
  60.1 5.0 %collective-permute-start.20 = (bf16[512,128]{1,0:T(8,128)(2,1)S(1)}, bf16[512,128]{1,0:T(8,128)(2,1)S(1)}, u32[]{:S(2)}, u32[]{:S(2)}) collective-permute-start(bf16[512,128]{1,0:T(8,128)(2,1)S(1)} %get-tuple-element.124.refs_2_.refs_12_), channel_id=1, source_target_pairs={{0,16},{8,24},{16,0},{24,8},{1,17},{9,25},{17,1},{25,9},{2,18},{10... | collective-permute-start | bytes 393224 | tf_op jit(solution)/shard_map/ppermute | solution.py:424
  60.8 5.9 %collective-permute-start.19 = (bf16[512,128]{1,0:T(8,128)(2,1)S(1)}, bf16[512,128]{1,0:T(8,128)(2,1)S(1)}, u32[]{:S(2)}, u32[]{:S(2)}) collective-permute-start(bf16[512,128]{1,0:T(8,128)(2,1)S(1)} %get-tuple-element.124.refs_2_.refs_12_), channel_id=1, source_target_pairs={{0,24},{8,16},{16,8},{24,0},{1,25},{9,17},{17,9},{25,1},{2,26},{10... | collective-permute-start | bytes 393224 | tf_op jit(solution)/shard_map/ppermute | solution.py:424
  67.8 6.9 %collective-permute-start.22 = (bf16[272,128]{1,0:T(8,128)(2,1)S(1)}, bf16[272,128]{1,0:T(8,128)(2,1)S(1)}, u32[]{:S(2)}, u32[]{:S(2)}) collective-permute-start(bf16[272,128]{1,0:T(8,128)(2,1)S(1)} %get-tuple-element.133), channel_id=1, source_target_pairs={{0,6},{1,7},{2,4},{3,5},{4,2},{5,3},{6,0},{7,1},{8,14},{9,15},{10,... | collective-permute-start | bytes 208904 | tf_op jit(solution)/shard_map/ppermute | solution.py:424
  69.7 6.7 %collective-permute-start.23 = (bf16[272,128]{1,0:T(8,128)(2,1)S(1)}, bf16[272,128]{1,0:T(8,128)(2,1)S(1)}, u32[]{:S(2)}, u32[]{:S(2)}) collective-permute-start(bf16[272,128]{1,0:T(8,128)(2,1)S(1)} %get-tuple-element.134), channel_id=1, source_target_pairs={{0,2},{1,3},{2,0},{3,1},{4,6},{5,7},{6,4},{7,5},{8,10},{9,11},{10,... | collective-permute-start | bytes 208904 | tf_op jit(solution)/shard_map/ppermute | solution.py:424
  70.1 7.0 %collective-permute-start.24 = (bf16[272,128]{1,0:T(8,128)(2,1)S(1)}, bf16[272,128]{1,0:T(8,128)(2,1)S(1)}, u32[]{:S(2)}, u32[]{:S(2)}) collective-permute-start(bf16[272,128]{1,0:T(8,128)(2,1)S(1)} %get-tuple-element.135), channel_id=1, source_target_pairs={{0,4},{1,5},{2,6},{3,7},{4,0},{5,1},{6,2},{7,3},{8,12},{9,13},{10,... | collective-permute-start | bytes 208904 | tf_op jit(solution)/shard_map/ppermute | solution.py:424
  77.1 6.2 %collective-permute-start.27 = (bf16[256,128]{1,0:T(8,128)(2,1)S(1)}, bf16[256,128]{1,0:T(8,128)(2,1)S(1)}, u32[]{:S(2)}, u32[]{:S(2)}) collective-permute-start(bf16[256,128]{1,0:T(8,128)(2,1)S(1)} %get-tuple-element.137.refs_2_.refs_24_), channel_id=1, source_target_pairs={{0,6},{1,7},{2,4},{3,5},{4,2},{5,3},{6,0},{7,1},{8,14},{9,15},{10,... | collective-permute-start | bytes 196616 | tf_op jit(solution)/shard_map/ppermute | solution.py:424
  79.2 5.5 %collective-permute-start.25 = (bf16[256,128]{1,0:T(8,128)(2,1)S(1)}, bf16[256,128]{1,0:T(8,128)(2,1)S(1)}, u32[]{:S(2)}, u32[]{:S(2)}) collective-permute-start(bf16[256,128]{1,0:T(8,128)(2,1)S(1)} %get-tuple-element.137.refs_2_.refs_24_), channel_id=1, source_target_pairs={{0,2},{1,3},{2,0},{3,1},{4,6},{5,7},{6,4},{7,5},{8,10},{9,11},{10,... | collective-permute-start | bytes 196616 | tf_op jit(solution)/shard_map/ppermute | solution.py:424
  79.2 5.5 %collective-permute-start.26 = (bf16[256,128]{1,0:T(8,128)(2,1)S(1)}, bf16[256,128]{1,0:T(8,128)(2,1)S(1)}, u32[]{:S(2)}, u32[]{:S(2)}) collective-permute-start(bf16[256,128]{1,0:T(8,128)(2,1)S(1)} %get-tuple-element.137.refs_2_.refs_24_), channel_id=1, source_target_pairs={{0,4},{1,5},{2,6},{3,7},{4,0},{5,1},{6,2},{7,3},{8,12},{9,13},{10,... | collective-permute-start | bytes 196616 | tf_op jit(solution)/shard_map/ppermute | solution.py:424
  86.1 5.1 %collective-permute-start.28 = (bf16[528,128]{1,0:T(8,128)(2,1)S(1)}, bf16[528,128]{1,0:T(8,128)(2,1)S(1)}, u32[]{:S(2)}, u32[]{:S(2)}) collective-permute-start(bf16[528,128]{1,0:T(8,128)(2,1)S(1)} %get-tuple-element.144), channel_id=1, source_target_pairs={{0,8},{8,0},{16,24},{24,16},{1,9},{9,1},{17,25},{25,17},{2,10},{10... | collective-permute-start | bytes 405512 | tf_op jit(solution)/shard_map/ppermute | solution.py:424
  87.1 5.0 %collective-permute-start.29 = (bf16[528,128]{1,0:T(8,128)(2,1)S(1)}, bf16[528,128]{1,0:T(8,128)(2,1)S(1)}, u32[]{:S(2)}, u32[]{:S(2)}) collective-permute-start(bf16[528,128]{1,0:T(8,128)(2,1)S(1)} %get-tuple-element.145), channel_id=1, source_target_pairs={{0,16},{8,24},{16,0},{24,8},{1,17},{9,25},{17,1},{25,9},{2,18},{10... | collective-permute-start | bytes 405512 | tf_op jit(solution)/shard_map/ppermute | solution.py:424
  88.7 5.9 %collective-permute-start.30 = (bf16[528,128]{1,0:T(8,128)(2,1)S(1)}, bf16[528,128]{1,0:T(8,128)(2,1)S(1)}, u32[]{:S(2)}, u32[]{:S(2)}) collective-permute-start(bf16[528,128]{1,0:T(8,128)(2,1)S(1)} %get-tuple-element.146), channel_id=1, source_target_pairs={{0,24},{8,16},{16,8},{24,0},{1,25},{9,17},{17,9},{25,1},{2,26},{10... | collective-permute-start | bytes 405512 | tf_op jit(solution)/shard_map/ppermute | solution.py:424
  94.7 5.0 %collective-permute-start.33 = (bf16[512,128]{1,0:T(8,128)(2,1)S(1)}, bf16[512,128]{1,0:T(8,128)(2,1)S(1)}, u32[]{:S(2)}, u32[]{:S(2)}) collective-permute-start(bf16[512,128]{1,0:T(8,128)(2,1)S(1)} %get-tuple-element.149.refs_2_.refs_16_), channel_id=1, source_target_pairs={{0,8},{8,0},{16,24},{24,16},{1,9},{9,1},{17,25},{25,17},{2,10},{10... | collective-permute-start | bytes 393224 | tf_op jit(solution)/shard_map/ppermute | solution.py:424
  94.9 5.8 %collective-permute-start.32 = (bf16[512,128]{1,0:T(8,128)(2,1)S(1)}, bf16[512,128]{1,0:T(8,128)(2,1)S(1)}, u32[]{:S(2)}, u32[]{:S(2)}) collective-permute-start(bf16[512,128]{1,0:T(8,128)(2,1)S(1)} %get-tuple-element.149.refs_2_.refs_16_), channel_id=1, source_target_pairs={{0,16},{8,24},{16,0},{24,8},{1,17},{9,25},{17,1},{25,9},{2,18},{10... | collective-permute-start | bytes 393224 | tf_op jit(solution)/shard_map/ppermute | solution.py:424
  96.2 5.9 %collective-permute-start.31 = (bf16[512,128]{1,0:T(8,128)(2,1)S(1)}, bf16[512,128]{1,0:T(8,128)(2,1)S(1)}, u32[]{:S(2)}, u32[]{:S(2)}) collective-permute-start(bf16[512,128]{1,0:T(8,128)(2,1)S(1)} %get-tuple-element.149.refs_2_.refs_16_), channel_id=1, source_target_pairs={{0,24},{8,16},{16,8},{24,0},{1,25},{9,17},{17,9},{25,1},{2,26},{10... | collective-permute-start | bytes 393224 | tf_op jit(solution)/shard_map/ppermute | solution.py:424
  103.3 6.3 %collective-permute-start.34 = (bf16[272,128]{1,0:T(8,128)(2,1)S(1)}, bf16[272,128]{1,0:T(8,128)(2,1)S(1)}, u32[]{:S(2)}, u32[]{:S(2)}) collective-permute-start(bf16[272,128]{1,0:T(8,128)(2,1)S(1)} %get-tuple-element.158), channel_id=1, source_target_pairs={{0,6},{1,7},{2,4},{3,5},{4,2},{5,3},{6,0},{7,1},{8,14},{9,15},{10,... | collective-permute-start | bytes 208904 | tf_op jit(solution)/shard_map/ppermute | solution.py:424
  106.0 5.2 %collective-permute-start.36 = (bf16[272,128]{1,0:T(8,128)(2,1)S(1)}, bf16[272,128]{1,0:T(8,128)(2,1)S(1)}, u32[]{:S(2)}, u32[]{:S(2)}) collective-permute-start(bf16[272,128]{1,0:T(8,128)(2,1)S(1)} %get-tuple-element.160), channel_id=1, source_target_pairs={{0,4},{1,5},{2,6},{3,7},{4,0},{5,1},{6,2},{7,3},{8,12},{9,13},{10,... | collective-permute-start | bytes 208904 | tf_op jit(solution)/shard_map/ppermute | solution.py:424
  111.2 6.2 %collective-permute-start.37 = (bf16[256,128]{1,0:T(8,128)(2,1)S(1)}, bf16[256,128]{1,0:T(8,128)(2,1)S(1)}, u32[]{:S(2)}, u32[]{:S(2)}) collective-permute-start(bf16[256,128]{1,0:T(8,128)(2,1)S(1)} %get-tuple-element.163.refs_0_.refs_28_), channel_id=1, source_target_pairs={{0,6},{1,7},{2,4},{3,5},{4,2},{5,3},{6,0},{7,1},{8,14},{9,15},{10,... | collective-permute-start | bytes 196616 | tf_op jit(solution)/shard_map/ppermute | solution.py:424
  113.7 5.2 %collective-permute-start.39 = (bf16[256,128]{1,0:T(8,128)(2,1)S(1)}, bf16[256,128]{1,0:T(8,128)(2,1)S(1)}, u32[]{:S(2)}, u32[]{:S(2)}) collective-permute-start(bf16[256,128]{1,0:T(8,128)(2,1)S(1)} %get-tuple-element.163.refs_0_.refs_28_), channel_id=1, source_target_pairs={{0,4},{1,5},{2,6},{3,7},{4,0},{5,1},{6,2},{7,3},{8,12},{9,13},{10,... | collective-permute-start | bytes 196616 | tf_op jit(solution)/shard_map/ppermute | solution.py:424
  (16 other events, 105.5 us)

commit v12 on v10

--- a/solution.py
+++ b/solution.py
@@ -262,7 +262,9 @@
 
 
 def step_kernel(way, pick, at_group, last, *refs):
-    (tile_ref, list_ref), refs = refs[:2], refs[2:]
+    (tile_ref, list_vmem), refs, (list_ref, list_sem) = refs[:2], refs[2:-2], refs[-2:]
+    fetch = pltpu.make_async_copy(list_vmem, list_ref, list_sem.at[0])
+    fetch.start()
     chunks, refs = refs[: len(pick)], refs[len(pick) :]
     if at_group:
         folded, refs = refs[1][...], refs[2:]
@@ -276,6 +278,7 @@
         for half in range(way.halves):
             at = pl.ds(pl.multiple_of((here ^ offset) * way.part + half * way.length, way.part), way.part)
             folded += put_chunk(chunk[half * way.part : (half + 1) * way.part, :], plain_ref, turned_ref, at, way.sign)
+    fetch.wait()
     low, high = list_ref[1, at_group], list_ref[1, at_group + 1]
     width = LAST_WIDTH if last else WIDTH
 
@@ -496,9 +499,10 @@
                 last = k + 1 == len(groups)
                 carry = call(
                     functools.partial(step_kernel, way, group, k, last), name,
-                    [total] + (outs if last else [norm]), [vector(way.halves * way.length, BF16)] * 2,
+                    [total] + (outs if last else [norm]),
+                    [vector(way.halves * way.length, BF16)] * 2 + [((8, 128), jnp.int32), (1, pltpu.SemaphoreType.DMA)],
                     tiles, slot_list, *chunks[at : at + len(group)], *carry,
-                    alias={2 + len(group): 0} if k else None,
+                    alias={2 + len(group): 0} if k else None, vector=True,
                 )
                 at += len(group)
             return carry[1:]

time: 128 us -> 127 us (level)
  transfers between devices with their start and end apart: 45 -> 45, of which waited for: 35 -> 32; matrix products, arithmetic and copies ran while one was open for 0% -> 0% of each run, Pallas kernels for 11% -> 11%
where the time goes in v12:
time: 127 us
  starting transfers between devices  53.6 us (42%)
  waiting for transfers between devices  46.3 us (36%)
  Pallas kernels  25.4 us (20%)
  between operations  1.59 us (1%)
    ppermute x45, starting transfers between devices, swap(): return lax.ppermute(value, axis, [(i, i ^ offset) for i in range(size)])  53.6 us
    ppermute x45, waiting for transfers between devices, swap(): return lax.ppermute(value, axis, [(i, i ^ offset) for i in range(size)])  46.3 us
    pallas_call x27, Pallas kernels, call(): pl.pallas_call(kernel, name=name, out_shape=[jax.ShapeDtypeStruct(s, d) f...  25.4 us
  transfers between devices with their start and end apart: 45, of which 32 were waited for; matrix products, arithmetic and copies ran while one was open for 0% of the time, Pallas kernels for 11%

profile of v12, /device:TPU:0, one launch (start us, length us, event | category | flops | bytes accessed | tf_op | source)
XLA Modules:
  0.0 126.9 jit_solution(18430955492615902119)
XLA Ops:
  2.5 3.5 %pack.1 = (bf16[48,2,128,128]{3,2,1,0:T(8,128)(2,1)S(1)}, bf16[48,128,256]{2,1,0:T(8,128)(2,1)S(1)}, f32[1152,128]{1,0:T(8,128)S(1)}, bf16[1024,128]{1,0:T(8,128)(2,1)S(1)}, bf16[1024,128]{1,0:T(8,128)(2,1)S(1)}) custom-call(f32[2,1024,128]{2,1,0:T(8,128)} %record_ref.1, bf16[24,2,128,128]{3,2,1,0:T(8,128)(2,1)} %bitcast.12, s32[1,24]{1,0:T(1,128)} %bitcast.6, ...), custom_call_target="tpu_custom_call" | custom-call | tf_op jit(solution)/shard_map/pack/pallas_call | solution.py:52
  7.5 2.3 %collective-permute-start.4 = (bf16[512,128]{1,0:T(8,128)(2,1)S(1)}, bf16[512,128]{1,0:T(8,128)(2,1)S(1)}, u32[]{:S(2)}, u32[]{:S(2)}) collective-permute-start(bf16[512,128]{1,0:T(8,128)(2,1)S(1)} %get-tuple-element.91), channel_id=1, source_target_pairs={{0,8},{8,0},{16,24},{24,16},{1,9},{9,1},{17,25},{25,17},{2,10},{10... | collective-permute-start | bytes 393224 | tf_op jit(solution)/shard_map/ppermute | solution.py:427
  9.8 1.5 %collective-permute-start.5 = (bf16[512,128]{1,0:T(8,128)(2,1)S(1)}, bf16[512,128]{1,0:T(8,128)(2,1)S(1)}, u32[]{:S(2)}, u32[]{:S(2)}) collective-permute-start(bf16[512,128]{1,0:T(8,128)(2,1)S(1)} %get-tuple-element.92), channel_id=1, source_target_pairs={{0,16},{8,24},{16,0},{24,8},{1,17},{9,25},{17,1},{25,9},{2,18},{10... | collective-permute-start | bytes 393224 | tf_op jit(solution)/shard_map/ppermute | solution.py:427
  11.3 2.4 %collective-permute-done.4.refs_0_ = bf16[512,128]{1,0:T(8,128)(2,1)S(1)} collective-permute-done((bf16[512,128]{1,0:T(8,128)(2,1)S(1)}, bf16[512,128]{1,0:T(8,128)(2,1)S(1)}, u32[]{:S(2)}, u32[]{:S(2)}) %collective-permute-start.4) | collective-permute-done | bytes 131104 | tf_op jit(solution)/shard_map/ppermute | solution.py:427
  13.7 4.1 %collective-permute-done.5.refs_1_ = bf16[512,128]{1,0:T(8,128)(2,1)S(1)} collective-permute-done((bf16[512,128]{1,0:T(8,128)(2,1)S(1)}, bf16[512,128]{1,0:T(8,128)(2,1)S(1)}, u32[]{:S(2)}, u32[]{:S(2)}) %collective-permute-start.5) | collective-permute-done | bytes 131104 | tf_op jit(solution)/shard_map/ppermute | solution.py:427
  26.3 1.5 %forward.11 = (f32[1152,128]{1,0:T(8,128)S(1)}, f32[256,128]{1,0:T(8,128)S(1)}, f32[8,128]{1,0:T(8,128)S(1)}, bf16[272,128]{1,0:T(8,128)(2,1)S(1)}, bf16[272,128...) custom-call(bf16[48,2,128,128]{3,2,1,0:T(8,128)(2,1)S(1)} %get-tuple-element.86.refs_0_, ...), custom_call_target="tpu_custom_call", output_to_operand_aliasing={{0}: (4, {})} | custom-call | tf_op jit(solution)/shard_map/forward/pallas_call | solution.py:52
  27.8 3.6 %collective-permute-start.10 = (bf16[272,128]{1,0:T(8,128)(2,1)S(1)}, bf16[272,128]{1,0:T(8,128)(2,1)S(1)}, u32[]{:S(2)}, u32[]{:S(2)}) collective-permute-start(bf16[272,128]{1,0:T(8,128)(2,1)S(1)} %get-tuple-element.101), channel_id=1, source_target_pairs={{0,6},{1,7},{2,4},{3,5},{4,2},{5,3},{6,0},{7,1},{8,14},{9,15},{10,... | collective-permute-start | bytes 208904 | tf_op jit(solution)/shard_map/ppermute | solution.py:427
  32.3 2.2 %collective-permute-done.10.refs_0_ = bf16[272,128]{1,0:T(8,128)(2,1)S(1)} collective-permute-done((bf16[272,128]{1,0:T(8,128)(2,1)S(1)}, bf16[272,128]{1,0:T(8,128)(2,1)S(1)}, u32[]{:S(2)}, u32[]{:S(2)}) %collective-permute-start.10) | collective-permute-done | bytes 69664 | tf_op jit(solution)/shard_map/ppermute | solution.py:427
  36.7 1.7 %collective-permute-start.15 = (bf16[256,128]{1,0:T(8,128)(2,1)S(1)}, bf16[256,128]{1,0:T(8,128)(2,1)S(1)}, u32[]{:S(2)}, u32[]{:S(2)}) collective-permute-start(bf16[256,128]{1,0:T(8,128)(2,1)S(1)} %get-tuple-element.104.refs_2_.refs_20_), channel_id=1, source_target_pairs={{0,6},{1,7},{2,4},{3,5},{4,2},{5,3},{6,0},{7,1},{8,14},{9,15},{10,... | collective-permute-start | bytes 196616 | tf_op jit(solution)/shard_map/ppermute | solution.py:427
  38.9 2.2 %collective-permute-start.14 = (bf16[256,128]{1,0:T(8,128)(2,1)S(1)}, bf16[256,128]{1,0:T(8,128)(2,1)S(1)}, u32[]{:S(2)}, u32[]{:S(2)}) collective-permute-start(bf16[256,128]{1,0:T(8,128)(2,1)S(1)} %get-tuple-element.104.refs_2_.refs_20_), channel_id=1, source_target_pairs={{0,4},{1,5},{2,6},{3,7},{4,0},{5,1},{6,2},{7,3},{8,12},{9,13},{10,... | collective-permute-start | bytes 196616 | tf_op jit(solution)/shard_map/ppermute | solution.py:427
  44.2 1.5 %adjoint.8 = (f32[2176,128]{1,0:T(8,128)S(1)}, f32[512,128]{1,0:T(8,128)S(1)}, f32[8,128]{1,0:T(8,128)S(1)}, bf16[528,128]{1,0:T(8,128)(2,1)S(1)}, bf16[528,128]...) custom-call(bf16[48,128,256]{2,1,0:T(8,128)(2,1)S(1)} %get-tuple-element.88.refs_0_, ...), custom_call_target="tpu_custom_call", output_to_operand_aliasing={{0}: (4, {})} | custom-call | tf_op jit(solution)/shard_map/adjoint/pallas_call | solution.py:52
  49.3 1.5 %collective-permute-done.16.refs_0_ = bf16[528,128]{1,0:T(8,128)(2,1)S(1)} collective-permute-done((bf16[528,128]{1,0:T(8,128)(2,1)S(1)}, bf16[528,128]{1,0:T(8,128)(2,1)S(1)}, u32[]{:S(2)}, u32[]{:S(2)}) %collective-permute-start.16) | collective-permute-done | bytes 135200 | tf_op jit(solution)/shard_map/ppermute | solution.py:427
  51.8 3.5 %collective-permute-done.18.refs_2_ = bf16[528,128]{1,0:T(8,128)(2,1)S(1)} collective-permute-done((bf16[528,128]{1,0:T(8,128)(2,1)S(1)}, bf16[528,128]{1,0:T(8,128)(2,1)S(1)}, u32[]{:S(2)}, u32[]{:S(2)}) %collective-permute-start.18) | collective-permute-done | bytes 135200 | tf_op jit(solution)/shard_map/ppermute | solution.py:427
  55.8 1.7 %collective-permute-start.19 = (bf16[512,128]{1,0:T(8,128)(2,1)S(1)}, bf16[512,128]{1,0:T(8,128)(2,1)S(1)}, u32[]{:S(2)}, u32[]{:S(2)}) collective-permute-start(bf16[512,128]{1,0:T(8,128)(2,1)S(1)} %get-tuple-element.116.refs_2_.refs_12_), channel_id=1, source_target_pairs={{0,16},{8,24},{16,0},{24,8},{1,17},{9,25},{17,1},{25,9},{2,18},{10... | collective-permute-start | bytes 393224 | tf_op jit(solution)/shard_map/ppermute | solution.py:427
  61.4 2.0 %collective-permute-done.20.refs_3_.refs_15_ = bf16[512,128]{1,0:T(8,128)(2,1)S(1)} collective-permute-done((bf16[512,128]{1,0:T(8,128)(2,1)S(1)}, bf16[512,128]{1,0:T(8,128)(2,1)S(1)}, u32[]{:S(2)}, u32[]{:S(2)}) %collective-permute-start.20) | collective-permute-done | bytes 131104 | tf_op jit(solution)/shard_map/ppermute | solution.py:427
  64.9 3.0 %collective-permute-start.22 = (bf16[272,128]{1,0:T(8,128)(2,1)S(1)}, bf16[272,128]{1,0:T(8,128)(2,1)S(1)}, u32[]{:S(2)}, u32[]{:S(2)}) collective-permute-start(bf16[272,128]{1,0:T(8,128)(2,1)S(1)} %get-tuple-element.123), channel_id=1, source_target_pairs={{0,6},{1,7},{2,4},{3,5},{4,2},{5,3},{6,0},{7,1},{8,14},{9,15},{10,... | collective-permute-start | bytes 208904 | tf_op jit(solution)/shard_map/ppermute | solution.py:427
  69.3 1.9 %collective-permute-done.22.refs_0_ = bf16[272,128]{1,0:T(8,128)(2,1)S(1)} collective-permute-done((bf16[272,128]{1,0:T(8,128)(2,1)S(1)}, bf16[272,128]{1,0:T(8,128)(2,1)S(1)}, u32[]{:S(2)}, u32[]{:S(2)}) %collective-permute-start.22) | collective-permute-done | bytes 69664 | tf_op jit(solution)/shard_map/ppermute | solution.py:427
  71.3 2.1 %collective-permute-done.23.refs_1_ = bf16[272,128]{1,0:T(8,128)(2,1)S(1)} collective-permute-done((bf16[272,128]{1,0:T(8,128)(2,1)S(1)}, bf16[272,128]{1,0:T(8,128)(2,1)S(1)}, u32[]{:S(2)}, u32[]{:S(2)}) %collective-permute-start.23) | collective-permute-done | bytes 69664 | tf_op jit(solution)/shard_map/ppermute | solution.py:427
  73.4 2.7 %collective-permute-start.27 = (bf16[256,128]{1,0:T(8,128)(2,1)S(1)}, bf16[256,128]{1,0:T(8,128)(2,1)S(1)}, u32[]{:S(2)}, u32[]{:S(2)}) collective-permute-start(bf16[256,128]{1,0:T(8,128)(2,1)S(1)} %get-tuple-element.127.refs_2_.refs_24_), channel_id=1, source_target_pairs={{0,6},{1,7},{2,4},{3,5},{4,2},{5,3},{6,0},{7,1},{8,14},{9,15},{10,... | collective-permute-start | bytes 196616 | tf_op jit(solution)/shard_map/ppermute | solution.py:427
  76.0 1.8 %collective-permute-start.26 = (bf16[256,128]{1,0:T(8,128)(2,1)S(1)}, bf16[256,128]{1,0:T(8,128)(2,1)S(1)}, u32[]{:S(2)}, u32[]{:S(2)}) collective-permute-start(bf16[256,128]{1,0:T(8,128)(2,1)S(1)} %get-tuple-element.127.refs_2_.refs_24_), channel_id=1, source_target_pairs={{0,4},{1,5},{2,6},{3,7},{4,0},{5,1},{6,2},{7,3},{8,12},{9,13},{10,... | collective-permute-start | bytes 196616 | tf_op jit(solution)/shard_map/ppermute | solution.py:427
  86.3 1.6 %collective-permute-done.28.refs_0_ = bf16[528,128]{1,0:T(8,128)(2,1)S(1)} collective-permute-done((bf16[528,128]{1,0:T(8,128)(2,1)S(1)}, bf16[528,128]{1,0:T(8,128)(2,1)S(1)}, u32[]{:S(2)}, u32[]{:S(2)}) %collective-permute-start.28) | collective-permute-done | bytes 135200 | tf_op jit(solution)/shard_map/ppermute | solution.py:427
  89.0 1.8 %collective-permute-done.30.refs_2_ = bf16[528,128]{1,0:T(8,128)(2,1)S(1)} collective-permute-done((bf16[528,128]{1,0:T(8,128)(2,1)S(1)}, bf16[528,128]{1,0:T(8,128)(2,1)S(1)}, u32[]{:S(2)}, u32[]{:S(2)}) %collective-permute-start.30) | collective-permute-done | bytes 135200 | tf_op jit(solution)/shard_map/ppermute | solution.py:427
  92.9 1.5 %collective-permute-start.32 = (bf16[512,128]{1,0:T(8,128)(2,1)S(1)}, bf16[512,128]{1,0:T(8,128)(2,1)S(1)}, u32[]{:S(2)}, u32[]{:S(2)}) collective-permute-start(bf16[512,128]{1,0:T(8,128)(2,1)S(1)} %get-tuple-element.139.refs_2_.refs_16_), channel_id=1, source_target_pairs={{0,24},{8,16},{16,8},{24,0},{1,25},{9,17},{17,9},{25,1},{2,26},{10... | collective-permute-start | bytes 393224 | tf_op jit(solution)/shard_map/ppermute | solution.py:427
  96.9 1.9 %collective-permute-done.32.refs_3_.refs_19_ = bf16[512,128]{1,0:T(8,128)(2,1)S(1)} collective-permute-done((bf16[512,128]{1,0:T(8,128)(2,1)S(1)}, bf16[512,128]{1,0:T(8,128)(2,1)S(1)}, u32[]{:S(2)}, u32[]{:S(2)}) %collective-permute-start.32) | collective-permute-done | bytes 131104 | tf_op jit(solution)/shard_map/ppermute | solution.py:427
  98.8 1.5 %forward.17 = (f32[1152,128]{1,0:T(8,128)S(1)}, f32[256,128]{1,0:T(8,128)S(1)}, f32[8,128]{1,0:T(8,128)S(1)}, bf16[272,128]{1,0:T(8,128)(2,1)S(1)}, bf16[272,128...) custom-call(bf16[48,2,128,128]{3,2,1,0:T(8,128)(2,1)S(1)} %get-tuple-element.86.refs_0_, ...), custom_call_target="tpu_custom_call", output_to_operand_aliasing={{0}: (4, {})} | custom-call | tf_op jit(solution)/shard_map/forward/pallas_call | solution.py:52
  100.3 2.1 %collective-permute-start.34 = (bf16[272,128]{1,0:T(8,128)(2,1)S(1)}, bf16[272,128]{1,0:T(8,128)(2,1)S(1)}, u32[]{:S(2)}, u32[]{:S(2)}) collective-permute-start(bf16[272,128]{1,0:T(8,128)(2,1)S(1)} %get-tuple-element.146), channel_id=1, source_target_pairs={{0,6},{1,7},{2,4},{3,5},{4,2},{5,3},{6,0},{7,1},{8,14},{9,15},{10,... | collective-permute-start | bytes 208904 | tf_op jit(solution)/shard_map/ppermute | solution.py:427
  102.4 2.3 %collective-permute-start.36 = (bf16[272,128]{1,0:T(8,128)(2,1)S(1)}, bf16[272,128]{1,0:T(8,128)(2,1)S(1)}, u32[]{:S(2)}, u32[]{:S(2)}) collective-permute-start(bf16[272,128]{1,0:T(8,128)(2,1)S(1)} %get-tuple-element.148), channel_id=1, source_target_pairs={{0,4},{1,5},{2,6},{3,7},{4,0},{5,1},{6,2},{7,3},{8,12},{9,13},{10,... | collective-permute-start | bytes 208904 | tf_op jit(solution)/shard_map/ppermute | solution.py:427
  104.8 1.8 %collective-permute-done.34.refs_0_ = bf16[272,128]{1,0:T(8,128)(2,1)S(1)} collective-permute-done((bf16[272,128]{1,0:T(8,128)(2,1)S(1)}, bf16[272,128]{1,0:T(8,128)(2,1)S(1)}, u32[]{:S(2)}, u32[]{:S(2)}) %collective-permute-start.34) | collective-permute-done | bytes 69664 | tf_op jit(solution)/shard_map/ppermute | solution.py:427
  108.0 2.2 %collective-permute-start.37 = (bf16[256,128]{1,0:T(8,128)(2,1)S(1)}, bf16[256,128]{1,0:T(8,128)(2,1)S(1)}, u32[]{:S(2)}, u32[]{:S(2)}) collective-permute-start(bf16[256,128]{1,0:T(8,128)(2,1)S(1)} %get-tuple-element.151.refs_0_.refs_28_), channel_id=1, source_target_pairs={{0,6},{1,7},{2,4},{3,5},{4,2},{5,3},{6,0},{7,1},{8,14},{9,15},{10,... | collective-permute-start | bytes 196616 | tf_op jit(solution)/shard_map/ppermute | solution.py:427
  110.7 1.8 %collective-permute-start.39 = (bf16[256,128]{1,0:T(8,128)(2,1)S(1)}, bf16[256,128]{1,0:T(8,128)(2,1)S(1)}, u32[]{:S(2)}, u32[]{:S(2)}) collective-permute-start(bf16[256,128]{1,0:T(8,128)(2,1)S(1)} %get-tuple-element.151.refs_0_.refs_28_), channel_id=1, source_target_pairs={{0,4},{1,5},{2,6},{3,7},{4,0},{5,1},{6,2},{7,3},{8,12},{9,13},{10,... | collective-permute-start | bytes 196616 | tf_op jit(solution)/shard_map/ppermute | solution.py:427
  112.5 1.7 %collective-permute-done.37.refs_1_.refs_29_ = bf16[256,128]{1,0:T(8,128)(2,1)S(1)} collective-permute-done((bf16[256,128]{1,0:T(8,128)(2,1)S(1)}, bf16[256,128]{1,0:T(8,128)(2,1)S(1)}, u32[]{:S(2)}, u32[]{:S(2)}) %collective-permute-start.37) | collective-permute-done | bytes 65568 | tf_op jit(solution)/shard_map/ppermute | solution.py:427
  120.7 2.1 %collective-permute-done.42.refs_3_ = f32[8,128]{1,0:T(8,128)S(1)} collective-permute-done((f32[8,128]{1,0:T(8,128)S(1)}, f32[8,128]{1,0:T(8,128)S(1)}, u32[]{:S(2)}, u32[]{:S(2)}) %collective-permute-start.42) | collective-permute-done | bytes 4128 | tf_op jit(solution)/shard_map/ppermute | solution.py:427
  (92 shorter events, 56.1 us)
Async XLA Ops:
  0.6 5.4 %collective-permute-start = (bf16[24,2,128,128]{3,2,1,0:T(8,128)(2,1)}, bf16[24,2,128,128]{3,2,1,0:T(8,128)(2,1)S(1)}, u32[]{:S(2)}, u32[]{:S(2)}) collective-permute-start(bf16[24,2,128,128]{3,2,1,0:T(8,128)(2,1)} %bitcast.11), channel_id=1, source_target_pairs={{0,1},{1,0},{2,3},{3,2},{4,5},{5,4},{6,7},{7,6},{8,9},{9,8},{10,11... | collective-permute-start | bytes 4718600 | tf_op jit(solution)/shard_map/ppermute | solution.py:427
  7.5 6.2 %collective-permute-start.4 = (bf16[512,128]{1,0:T(8,128)(2,1)S(1)}, bf16[512,128]{1,0:T(8,128)(2,1)S(1)}, u32[]{:S(2)}, u32[]{:S(2)}) collective-permute-start(bf16[512,128]{1,0:T(8,128)(2,1)S(1)} %get-tuple-element.91), channel_id=1, source_target_pairs={{0,8},{8,0},{16,24},{24,16},{1,9},{9,1},{17,25},{25,17},{2,10},{10... | collective-permute-start | bytes 393224 | tf_op jit(solution)/shard_map/ppermute | solution.py:427
  9.8 8.0 %collective-permute-start.5 = (bf16[512,128]{1,0:T(8,128)(2,1)S(1)}, bf16[512,128]{1,0:T(8,128)(2,1)S(1)}, u32[]{:S(2)}, u32[]{:S(2)}) collective-permute-start(bf16[512,128]{1,0:T(8,128)(2,1)S(1)} %get-tuple-element.92), channel_id=1, source_target_pairs={{0,16},{8,24},{16,0},{24,8},{1,17},{9,25},{17,1},{25,9},{2,18},{10... | collective-permute-start | bytes 393224 | tf_op jit(solution)/shard_map/ppermute | solution.py:427
  11.3 6.5 %collective-permute-start.6 = (bf16[512,128]{1,0:T(8,128)(2,1)S(1)}, bf16[512,128]{1,0:T(8,128)(2,1)S(1)}, u32[]{:S(2)}, u32[]{:S(2)}) collective-permute-start(bf16[512,128]{1,0:T(8,128)(2,1)S(1)} %get-tuple-element.93), channel_id=1, source_target_pairs={{0,24},{8,16},{16,8},{24,0},{1,25},{9,17},{17,9},{25,1},{2,26},{10... | collective-permute-start | bytes 393224 | tf_op jit(solution)/shard_map/ppermute | solution.py:427
  17.8 6.1 %collective-permute-start.9 = (bf16[512,128]{1,0:T(8,128)(2,1)S(1)}, bf16[512,128]{1,0:T(8,128)(2,1)S(1)}, u32[]{:S(2)}, u32[]{:S(2)}) collective-permute-start(bf16[512,128]{1,0:T(8,128)(2,1)S(1)} %get-tuple-element.94.refs_2_.refs_8_), channel_id=1, source_target_pairs={{0,8},{8,0},{16,24},{24,16},{1,9},{9,1},{17,25},{25,17},{2,10},{10... | collective-permute-start | bytes 393224 | tf_op jit(solution)/shard_map/ppermute | solution.py:427
  19.1 7.1 %collective-permute-start.7 = (bf16[512,128]{1,0:T(8,128)(2,1)S(1)}, bf16[512,128]{1,0:T(8,128)(2,1)S(1)}, u32[]{:S(2)}, u32[]{:S(2)}) collective-permute-start(bf16[512,128]{1,0:T(8,128)(2,1)S(1)} %get-tuple-element.94.refs_2_.refs_8_), channel_id=1, source_target_pairs={{0,16},{8,24},{16,0},{24,8},{1,17},{9,25},{17,1},{25,9},{2,18},{10... | collective-permute-start | bytes 393224 | tf_op jit(solution)/shard_map/ppermute | solution.py:427
  20.0 6.3 %collective-permute-start.8 = (bf16[512,128]{1,0:T(8,128)(2,1)S(1)}, bf16[512,128]{1,0:T(8,128)(2,1)S(1)}, u32[]{:S(2)}, u32[]{:S(2)}) collective-permute-start(bf16[512,128]{1,0:T(8,128)(2,1)S(1)} %get-tuple-element.94.refs_2_.refs_8_), channel_id=1, source_target_pairs={{0,24},{8,16},{16,8},{24,0},{1,25},{9,17},{17,9},{25,1},{2,26},{10... | collective-permute-start | bytes 393224 | tf_op jit(solution)/shard_map/ppermute | solution.py:427
  27.8 6.6 %collective-permute-start.10 = (bf16[272,128]{1,0:T(8,128)(2,1)S(1)}, bf16[272,128]{1,0:T(8,128)(2,1)S(1)}, u32[]{:S(2)}, u32[]{:S(2)}) collective-permute-start(bf16[272,128]{1,0:T(8,128)(2,1)S(1)} %get-tuple-element.101), channel_id=1, source_target_pairs={{0,6},{1,7},{2,4},{3,5},{4,2},{5,3},{6,0},{7,1},{8,14},{9,15},{10,... | collective-permute-start | bytes 208904 | tf_op jit(solution)/shard_map/ppermute | solution.py:427
  31.5 5.2 %collective-permute-start.12 = (bf16[272,128]{1,0:T(8,128)(2,1)S(1)}, bf16[272,128]{1,0:T(8,128)(2,1)S(1)}, u32[]{:S(2)}, u32[]{:S(2)}) collective-permute-start(bf16[272,128]{1,0:T(8,128)(2,1)S(1)} %get-tuple-element.103), channel_id=1, source_target_pairs={{0,4},{1,5},{2,6},{3,7},{4,0},{5,1},{6,2},{7,3},{8,12},{9,13},{10,... | collective-permute-start | bytes 208904 | tf_op jit(solution)/shard_map/ppermute | solution.py:427
  36.7 6.2 %collective-permute-start.15 = (bf16[256,128]{1,0:T(8,128)(2,1)S(1)}, bf16[256,128]{1,0:T(8,128)(2,1)S(1)}, u32[]{:S(2)}, u32[]{:S(2)}) collective-permute-start(bf16[256,128]{1,0:T(8,128)(2,1)S(1)} %get-tuple-element.104.refs_2_.refs_20_), channel_id=1, source_target_pairs={{0,6},{1,7},{2,4},{3,5},{4,2},{5,3},{6,0},{7,1},{8,14},{9,15},{10,... | collective-permute-start | bytes 196616 | tf_op jit(solution)/shard_map/ppermute | solution.py:427
  38.4 5.8 %collective-permute-start.13 = (bf16[256,128]{1,0:T(8,128)(2,1)S(1)}, bf16[256,128]{1,0:T(8,128)(2,1)S(1)}, u32[]{:S(2)}, u32[]{:S(2)}) collective-permute-start(bf16[256,128]{1,0:T(8,128)(2,1)S(1)} %get-tuple-element.104.refs_2_.refs_20_), channel_id=1, source_target_pairs={{0,2},{1,3},{2,0},{3,1},{4,6},{5,7},{6,4},{7,5},{8,10},{9,11},{10,... | collective-permute-start | bytes 196616 | tf_op jit(solution)/shard_map/ppermute | solution.py:427
  38.9 5.3 %collective-permute-start.14 = (bf16[256,128]{1,0:T(8,128)(2,1)S(1)}, bf16[256,128]{1,0:T(8,128)(2,1)S(1)}, u32[]{:S(2)}, u32[]{:S(2)}) collective-permute-start(bf16[256,128]{1,0:T(8,128)(2,1)S(1)} %get-tuple-element.104.refs_2_.refs_20_), channel_id=1, source_target_pairs={{0,4},{1,5},{2,6},{3,7},{4,0},{5,1},{6,2},{7,3},{8,12},{9,13},{10,... | collective-permute-start | bytes 196616 | tf_op jit(solution)/shard_map/ppermute | solution.py:427
  45.7 5.1 %collective-permute-start.16 = (bf16[528,128]{1,0:T(8,128)(2,1)S(1)}, bf16[528,128]{1,0:T(8,128)(2,1)S(1)}, u32[]{:S(2)}, u32[]{:S(2)}) collective-permute-start(bf16[528,128]{1,0:T(8,128)(2,1)S(1)} %get-tuple-element.111), channel_id=1, source_target_pairs={{0,8},{8,0},{16,24},{24,16},{1,9},{9,1},{17,25},{25,17},{2,10},{10... | collective-permute-start | bytes 405512 | tf_op jit(solution)/shard_map/ppermute | solution.py:427
  47.8 7.5 %collective-permute-start.18 = (bf16[528,128]{1,0:T(8,128)(2,1)S(1)}, bf16[528,128]{1,0:T(8,128)(2,1)S(1)}, u32[]{:S(2)}, u32[]{:S(2)}) collective-permute-start(bf16[528,128]{1,0:T(8,128)(2,1)S(1)} %get-tuple-element.113), channel_id=1, source_target_pairs={{0,24},{8,16},{16,8},{24,0},{1,25},{9,17},{17,9},{25,1},{2,26},{10... | collective-permute-start | bytes 405512 | tf_op jit(solution)/shard_map/ppermute | solution.py:427
  55.4 5.0 %collective-permute-start.21 = (bf16[512,128]{1,0:T(8,128)(2,1)S(1)}, bf16[512,128]{1,0:T(8,128)(2,1)S(1)}, u32[]{:S(2)}, u32[]{:S(2)}) collective-permute-start(bf16[512,128]{1,0:T(8,128)(2,1)S(1)} %get-tuple-element.116.refs_2_.refs_12_), channel_id=1, source_target_pairs={{0,8},{8,0},{16,24},{24,16},{1,9},{9,1},{17,25},{25,17},{2,10},{10... | collective-permute-start | bytes 393224 | tf_op jit(solution)/shard_map/ppermute | solution.py:427
  55.8 5.6 %collective-permute-start.19 = (bf16[512,128]{1,0:T(8,128)(2,1)S(1)}, bf16[512,128]{1,0:T(8,128)(2,1)S(1)}, u32[]{:S(2)}, u32[]{:S(2)}) collective-permute-start(bf16[512,128]{1,0:T(8,128)(2,1)S(1)} %get-tuple-element.116.refs_2_.refs_12_), channel_id=1, source_target_pairs={{0,16},{8,24},{16,0},{24,8},{1,17},{9,25},{17,1},{25,9},{2,18},{10... | collective-permute-start | bytes 393224 | tf_op jit(solution)/shard_map/ppermute | solution.py:427
  57.5 5.9 %collective-permute-start.20 = (bf16[512,128]{1,0:T(8,128)(2,1)S(1)}, bf16[512,128]{1,0:T(8,128)(2,1)S(1)}, u32[]{:S(2)}, u32[]{:S(2)}) collective-permute-start(bf16[512,128]{1,0:T(8,128)(2,1)S(1)} %get-tuple-element.116.refs_2_.refs_12_), channel_id=1, source_target_pairs={{0,24},{8,16},{16,8},{24,0},{1,25},{9,17},{17,9},{25,1},{2,26},{10... | collective-permute-start | bytes 393224 | tf_op jit(solution)/shard_map/ppermute | solution.py:427
  64.9 6.4 %collective-permute-start.22 = (bf16[272,128]{1,0:T(8,128)(2,1)S(1)}, bf16[272,128]{1,0:T(8,128)(2,1)S(1)}, u32[]{:S(2)}, u32[]{:S(2)}) collective-permute-start(bf16[272,128]{1,0:T(8,128)(2,1)S(1)} %get-tuple-element.123), channel_id=1, source_target_pairs={{0,6},{1,7},{2,4},{3,5},{4,2},{5,3},{6,0},{7,1},{8,14},{9,15},{10,... | collective-permute-start | bytes 208904 | tf_op jit(solution)/shard_map/ppermute | solution.py:427
  67.9 5.5 %collective-permute-start.23 = (bf16[272,128]{1,0:T(8,128)(2,1)S(1)}, bf16[272,128]{1,0:T(8,128)(2,1)S(1)}, u32[]{:S(2)}, u32[]{:S(2)}) collective-permute-start(bf16[272,128]{1,0:T(8,128)(2,1)S(1)} %get-tuple-element.124), channel_id=1, source_target_pairs={{0,2},{1,3},{2,0},{3,1},{4,6},{5,7},{6,4},{7,5},{8,10},{9,11},{10,... | collective-permute-start | bytes 208904 | tf_op jit(solution)/shard_map/ppermute | solution.py:427
  67.9 5.5 %collective-permute-start.24 = (bf16[272,128]{1,0:T(8,128)(2,1)S(1)}, bf16[272,128]{1,0:T(8,128)(2,1)S(1)}, u32[]{:S(2)}, u32[]{:S(2)}) collective-permute-start(bf16[272,128]{1,0:T(8,128)(2,1)S(1)} %get-tuple-element.125), channel_id=1, source_target_pairs={{0,4},{1,5},{2,6},{3,7},{4,0},{5,1},{6,2},{7,3},{8,12},{9,13},{10,... | collective-permute-start | bytes 208904 | tf_op jit(solution)/shard_map/ppermute | solution.py:427
  73.4 6.2 %collective-permute-start.27 = (bf16[256,128]{1,0:T(8,128)(2,1)S(1)}, bf16[256,128]{1,0:T(8,128)(2,1)S(1)}, u32[]{:S(2)}, u32[]{:S(2)}) collective-permute-start(bf16[256,128]{1,0:T(8,128)(2,1)S(1)} %get-tuple-element.127.refs_2_.refs_24_), channel_id=1, source_target_pairs={{0,6},{1,7},{2,4},{3,5},{4,2},{5,3},{6,0},{7,1},{8,14},{9,15},{10,... | collective-permute-start | bytes 196616 | tf_op jit(solution)/shard_map/ppermute | solution.py:427
  76.0 5.2 %collective-permute-start.26 = (bf16[256,128]{1,0:T(8,128)(2,1)S(1)}, bf16[256,128]{1,0:T(8,128)(2,1)S(1)}, u32[]{:S(2)}, u32[]{:S(2)}) collective-permute-start(bf16[256,128]{1,0:T(8,128)(2,1)S(1)} %get-tuple-element.127.refs_2_.refs_24_), channel_id=1, source_target_pairs={{0,4},{1,5},{2,6},{3,7},{4,0},{5,1},{6,2},{7,3},{8,12},{9,13},{10,... | collective-permute-start | bytes 196616 | tf_op jit(solution)/shard_map/ppermute | solution.py:427
  82.7 5.2 %collective-permute-start.28 = (bf16[528,128]{1,0:T(8,128)(2,1)S(1)}, bf16[528,128]{1,0:T(8,128)(2,1)S(1)}, u32[]{:S(2)}, u32[]{:S(2)}) collective-permute-start(bf16[528,128]{1,0:T(8,128)(2,1)S(1)} %get-tuple-element.134), channel_id=1, source_target_pairs={{0,8},{8,0},{16,24},{24,16},{1,9},{9,1},{17,25},{25,17},{2,10},{10... | collective-permute-start | bytes 405512 | tf_op jit(solution)/shard_map/ppermute | solution.py:427
  83.5 5.5 %collective-permute-start.29 = (bf16[528,128]{1,0:T(8,128)(2,1)S(1)}, bf16[528,128]{1,0:T(8,128)(2,1)S(1)}, u32[]{:S(2)}, u32[]{:S(2)}) collective-permute-start(bf16[528,128]{1,0:T(8,128)(2,1)S(1)} %get-tuple-element.135), channel_id=1, source_target_pairs={{0,16},{8,24},{16,0},{24,8},{1,17},{9,25},{17,1},{25,9},{2,18},{10... | collective-permute-start | bytes 405512 | tf_op jit(solution)/shard_map/ppermute | solution.py:427
  84.9 5.9 %collective-permute-start.30 = (bf16[528,128]{1,0:T(8,128)(2,1)S(1)}, bf16[528,128]{1,0:T(8,128)(2,1)S(1)}, u32[]{:S(2)}, u32[]{:S(2)}) collective-permute-start(bf16[528,128]{1,0:T(8,128)(2,1)S(1)} %get-tuple-element.136), channel_id=1, source_target_pairs={{0,24},{8,16},{16,8},{24,0},{1,25},{9,17},{17,9},{25,1},{2,26},{10... | collective-permute-start | bytes 405512 | tf_op jit(solution)/shard_map/ppermute | solution.py:427
  91.4 5.5 %collective-permute-start.31 = (bf16[512,128]{1,0:T(8,128)(2,1)S(1)}, bf16[512,128]{1,0:T(8,128)(2,1)S(1)}, u32[]{:S(2)}, u32[]{:S(2)}) collective-permute-start(bf16[512,128]{1,0:T(8,128)(2,1)S(1)} %get-tuple-element.139.refs_2_.refs_16_), channel_id=1, source_target_pairs={{0,16},{8,24},{16,0},{24,8},{1,17},{9,25},{17,1},{25,9},{2,18},{10... | collective-permute-start | bytes 393224 | tf_op jit(solution)/shard_map/ppermute | solution.py:427
  92.9 5.9 %collective-permute-start.32 = (bf16[512,128]{1,0:T(8,128)(2,1)S(1)}, bf16[512,128]{1,0:T(8,128)(2,1)S(1)}, u32[]{:S(2)}, u32[]{:S(2)}) collective-permute-start(bf16[512,128]{1,0:T(8,128)(2,1)S(1)} %get-tuple-element.139.refs_2_.refs_16_), channel_id=1, source_target_pairs={{0,24},{8,16},{16,8},{24,0},{1,25},{9,17},{17,9},{25,1},{2,26},{10... | collective-permute-start | bytes 393224 | tf_op jit(solution)/shard_map/ppermute | solution.py:427
  100.3 6.2 %collective-permute-start.34 = (bf16[272,128]{1,0:T(8,128)(2,1)S(1)}, bf16[272,128]{1,0:T(8,128)(2,1)S(1)}, u32[]{:S(2)}, u32[]{:S(2)}) collective-permute-start(bf16[272,128]{1,0:T(8,128)(2,1)S(1)} %get-tuple-element.146), channel_id=1, source_target_pairs={{0,6},{1,7},{2,4},{3,5},{4,2},{5,3},{6,0},{7,1},{8,14},{9,15},{10,... | collective-permute-start | bytes 208904 | tf_op jit(solution)/shard_map/ppermute | solution.py:427
  102.4 5.6 %collective-permute-start.35 = (bf16[272,128]{1,0:T(8,128)(2,1)S(1)}, bf16[272,128]{1,0:T(8,128)(2,1)S(1)}, u32[]{:S(2)}, u32[]{:S(2)}) collective-permute-start(bf16[272,128]{1,0:T(8,128)(2,1)S(1)} %get-tuple-element.147), channel_id=1, source_target_pairs={{0,2},{1,3},{2,0},{3,1},{4,6},{5,7},{6,4},{7,5},{8,10},{9,11},{10,... | collective-permute-start | bytes 208904 | tf_op jit(solution)/shard_map/ppermute | solution.py:427
  102.4 5.6 %collective-permute-start.36 = (bf16[272,128]{1,0:T(8,128)(2,1)S(1)}, bf16[272,128]{1,0:T(8,128)(2,1)S(1)}, u32[]{:S(2)}, u32[]{:S(2)}) collective-permute-start(bf16[272,128]{1,0:T(8,128)(2,1)S(1)} %get-tuple-element.148), channel_id=1, source_target_pairs={{0,4},{1,5},{2,6},{3,7},{4,0},{5,1},{6,2},{7,3},{8,12},{9,13},{10,... | collective-permute-start | bytes 208904 | tf_op jit(solution)/shard_map/ppermute | solution.py:427
  108.0 6.2 %collective-permute-start.37 = (bf16[256,128]{1,0:T(8,128)(2,1)S(1)}, bf16[256,128]{1,0:T(8,128)(2,1)S(1)}, u32[]{:S(2)}, u32[]{:S(2)}) collective-permute-start(bf16[256,128]{1,0:T(8,128)(2,1)S(1)} %get-tuple-element.151.refs_0_.refs_28_), channel_id=1, source_target_pairs={{0,6},{1,7},{2,4},{3,5},{4,2},{5,3},{6,0},{7,1},{8,14},{9,15},{10,... | collective-permute-start | bytes 196616 | tf_op jit(solution)/shard_map/ppermute | solution.py:427
  110.7 5.2 %collective-permute-start.39 = (bf16[256,128]{1,0:T(8,128)(2,1)S(1)}, bf16[256,128]{1,0:T(8,128)(2,1)S(1)}, u32[]{:S(2)}, u32[]{:S(2)}) collective-permute-start(bf16[256,128]{1,0:T(8,128)(2,1)S(1)} %get-tuple-element.151.refs_0_.refs_28_), channel_id=1, source_target_pairs={{0,4},{1,5},{2,6},{3,7},{4,0},{5,1},{6,2},{7,3},{8,12},{9,13},{10,... | collective-permute-start | bytes 196616 | tf_op jit(solution)/shard_map/ppermute | solution.py:427
  (16 other events, 105.7 us)

commit v13 on v10

--- a/solution.py
+++ b/solution.py
@@ -13,7 +13,7 @@
 EPSILON = 1e-06
 GROUP = 8
 WIDTH = 8
-LAST_WIDTH = 12
+LAST_WIDTH = 24
 TAIL = 16
 VMEM_BYTES = 16 << 20
 

time: 128 us -> 129 us (level)
  transfers between devices with their start and end apart: 45 -> 45, of which waited for: 35 -> 33; matrix products, arithmetic and copies ran while one was open for 0% -> 0% of each run, Pallas kernels for 11% -> 11%
where the time goes in v13:
time: 129 us; the launch traced here: 128 us
  starting transfers between devices  54.9 us (43%)
  waiting for transfers between devices  45.5 us (35%)
  Pallas kernels  25.5 us (20%)
  between operations  1.7 us (1%)
    ppermute x45, starting transfers between devices, swap(): return lax.ppermute(value, axis, [(i, i ^ offset) for i in range(size)])  54.9 us
    ppermute x45, waiting for transfers between devices, swap(): return lax.ppermute(value, axis, [(i, i ^ offset) for i in range(size)])  45.5 us
    pallas_call x27, Pallas kernels, call(): pl.pallas_call(kernel, name=name, out_shape=[jax.ShapeDtypeStruct(s, d) f...  25.5 us
  transfers between devices with their start and end apart: 45, of which 33 were waited for; matrix products, arithmetic and copies ran while one was open for 0% of the time, Pallas kernels for 11%

profile of v13, /device:TPU:0, one launch (start us, length us, event | category | flops | bytes accessed | tf_op | source)
XLA Modules:
  0.0 127.6 jit_solution(1848277326793137810)
XLA Ops:
  2.5 3.2 %pack.1 = (bf16[48,2,128,128]{3,2,1,0:T(8,128)(2,1)S(1)}, bf16[48,128,256]{2,1,0:T(8,128)(2,1)S(1)}, f32[1152,128]{1,0:T(8,128)S(1)}, bf16[1024,128]{1,0:T(8,128)(2,1)S(1)}, bf16[1024,128]{1,0:T(8,128)(2,1)S(1)}) custom-call(f32[2,1024,128]{2,1,0:T(8,128)} %record_ref.1, bf16[24,2,128,128]{3,2,1,0:T(8,128)(2,1)} %bitcast.12, s32[1,24]{1,0:T(1,128)} %bitcast.6, ...), custom_call_target="tpu_custom_call" | custom-call | tf_op jit(solution)/shard_map/pack/pallas_call | solution.py:52
  7.1 2.6 %collective-permute-start.4 = (bf16[512,128]{1,0:T(8,128)(2,1)S(1)}, bf16[512,128]{1,0:T(8,128)(2,1)S(1)}, u32[]{:S(2)}, u32[]{:S(2)}) collective-permute-start(bf16[512,128]{1,0:T(8,128)(2,1)S(1)} %get-tuple-element.91), channel_id=1, source_target_pairs={{0,8},{8,0},{16,24},{24,16},{1,9},{9,1},{17,25},{25,17},{2,10},{10... | collective-permute-start | bytes 393224 | tf_op jit(solution)/shard_map/ppermute | solution.py:424
  9.8 2.2 %collective-permute-start.5 = (bf16[512,128]{1,0:T(8,128)(2,1)S(1)}, bf16[512,128]{1,0:T(8,128)(2,1)S(1)}, u32[]{:S(2)}, u32[]{:S(2)}) collective-permute-start(bf16[512,128]{1,0:T(8,128)(2,1)S(1)} %get-tuple-element.92), channel_id=1, source_target_pairs={{0,16},{8,24},{16,0},{24,8},{1,17},{9,25},{17,1},{25,9},{2,18},{10... | collective-permute-start | bytes 393224 | tf_op jit(solution)/shard_map/ppermute | solution.py:424
  12.0 1.7 %collective-permute-done.4.refs_0_ = bf16[512,128]{1,0:T(8,128)(2,1)S(1)} collective-permute-done((bf16[512,128]{1,0:T(8,128)(2,1)S(1)}, bf16[512,128]{1,0:T(8,128)(2,1)S(1)}, u32[]{:S(2)}, u32[]{:S(2)}) %collective-permute-start.4) | collective-permute-done | bytes 131104 | tf_op jit(solution)/shard_map/ppermute | solution.py:424
  13.6 4.6 %collective-permute-done.5.refs_1_ = bf16[512,128]{1,0:T(8,128)(2,1)S(1)} collective-permute-done((bf16[512,128]{1,0:T(8,128)(2,1)S(1)}, bf16[512,128]{1,0:T(8,128)(2,1)S(1)}, u32[]{:S(2)}, u32[]{:S(2)}) %collective-permute-start.5) | collective-permute-done | bytes 131104 | tf_op jit(solution)/shard_map/ppermute | solution.py:424
  18.3 1.5 %collective-permute-start.9 = (bf16[512,128]{1,0:T(8,128)(2,1)S(1)}, bf16[512,128]{1,0:T(8,128)(2,1)S(1)}, u32[]{:S(2)}, u32[]{:S(2)}) collective-permute-start(bf16[512,128]{1,0:T(8,128)(2,1)S(1)} %get-tuple-element.94.refs_2_.refs_8_), channel_id=1, source_target_pairs={{0,8},{8,0},{16,24},{24,16},{1,9},{9,1},{17,25},{25,17},{2,10},{10... | collective-permute-start | bytes 393224 | tf_op jit(solution)/shard_map/ppermute | solution.py:424
  25.2 1.9 %collective-permute-done.7.refs_2_.refs_10_ = bf16[512,128]{1,0:T(8,128)(2,1)S(1)} collective-permute-done((bf16[512,128]{1,0:T(8,128)(2,1)S(1)}, bf16[512,128]{1,0:T(8,128)(2,1)S(1)}, u32[]{:S(2)}, u32[]{:S(2)}) %collective-permute-start.7) | collective-permute-done | bytes 131104 | tf_op jit(solution)/shard_map/ppermute | solution.py:424
  28.5 3.6 %collective-permute-start.10 = (bf16[272,128]{1,0:T(8,128)(2,1)S(1)}, bf16[272,128]{1,0:T(8,128)(2,1)S(1)}, u32[]{:S(2)}, u32[]{:S(2)}) collective-permute-start(bf16[272,128]{1,0:T(8,128)(2,1)S(1)} %get-tuple-element.101), channel_id=1, source_target_pairs={{0,6},{1,7},{2,4},{3,5},{4,2},{5,3},{6,0},{7,1},{8,14},{9,15},{10,... | collective-permute-start | bytes 208904 | tf_op jit(solution)/shard_map/ppermute | solution.py:424
  32.9 2.2 %collective-permute-done.10.refs_0_ = bf16[272,128]{1,0:T(8,128)(2,1)S(1)} collective-permute-done((bf16[272,128]{1,0:T(8,128)(2,1)S(1)}, bf16[272,128]{1,0:T(8,128)(2,1)S(1)}, u32[]{:S(2)}, u32[]{:S(2)}) %collective-permute-start.10) | collective-permute-done | bytes 69664 | tf_op jit(solution)/shard_map/ppermute | solution.py:424
  37.4 1.7 %collective-permute-start.15 = (bf16[256,128]{1,0:T(8,128)(2,1)S(1)}, bf16[256,128]{1,0:T(8,128)(2,1)S(1)}, u32[]{:S(2)}, u32[]{:S(2)}) collective-permute-start(bf16[256,128]{1,0:T(8,128)(2,1)S(1)} %get-tuple-element.104.refs_2_.refs_20_), channel_id=1, source_target_pairs={{0,6},{1,7},{2,4},{3,5},{4,2},{5,3},{6,0},{7,1},{8,14},{9,15},{10,... | collective-permute-start | bytes 196616 | tf_op jit(solution)/shard_map/ppermute | solution.py:424
  39.6 2.3 %collective-permute-start.14 = (bf16[256,128]{1,0:T(8,128)(2,1)S(1)}, bf16[256,128]{1,0:T(8,128)(2,1)S(1)}, u32[]{:S(2)}, u32[]{:S(2)}) collective-permute-start(bf16[256,128]{1,0:T(8,128)(2,1)S(1)} %get-tuple-element.104.refs_2_.refs_20_), channel_id=1, source_target_pairs={{0,4},{1,5},{2,6},{3,7},{4,0},{5,1},{6,2},{7,3},{8,12},{9,13},{10,... | collective-permute-start | bytes 196616 | tf_op jit(solution)/shard_map/ppermute | solution.py:424
  49.7 1.5 %collective-permute-done.16.refs_0_ = bf16[528,128]{1,0:T(8,128)(2,1)S(1)} collective-permute-done((bf16[528,128]{1,0:T(8,128)(2,1)S(1)}, bf16[528,128]{1,0:T(8,128)(2,1)S(1)}, u32[]{:S(2)}, u32[]{:S(2)}) %collective-permute-start.16) | collective-permute-done | bytes 135200 | tf_op jit(solution)/shard_map/ppermute | solution.py:424
  52.5 3.0 %collective-permute-done.18.refs_2_ = bf16[528,128]{1,0:T(8,128)(2,1)S(1)} collective-permute-done((bf16[528,128]{1,0:T(8,128)(2,1)S(1)}, bf16[528,128]{1,0:T(8,128)(2,1)S(1)}, u32[]{:S(2)}, u32[]{:S(2)}) %collective-permute-start.18) | collective-permute-done | bytes 135200 | tf_op jit(solution)/shard_map/ppermute | solution.py:424
  57.2 1.8 %collective-permute-start.20 = (bf16[512,128]{1,0:T(8,128)(2,1)S(1)}, bf16[512,128]{1,0:T(8,128)(2,1)S(1)}, u32[]{:S(2)}, u32[]{:S(2)}) collective-permute-start(bf16[512,128]{1,0:T(8,128)(2,1)S(1)} %get-tuple-element.116.refs_2_.refs_12_), channel_id=1, source_target_pairs={{0,24},{8,16},{16,8},{24,0},{1,25},{9,17},{17,9},{25,1},{2,26},{10... | collective-permute-start | bytes 393224 | tf_op jit(solution)/shard_map/ppermute | solution.py:424
  61.6 1.5 %collective-permute-done.20.refs_3_.refs_15_ = bf16[512,128]{1,0:T(8,128)(2,1)S(1)} collective-permute-done((bf16[512,128]{1,0:T(8,128)(2,1)S(1)}, bf16[512,128]{1,0:T(8,128)(2,1)S(1)}, u32[]{:S(2)}, u32[]{:S(2)}) %collective-permute-start.20) | collective-permute-done | bytes 131104 | tf_op jit(solution)/shard_map/ppermute | solution.py:424
  64.6 4.2 %collective-permute-start.22 = (bf16[272,128]{1,0:T(8,128)(2,1)S(1)}, bf16[272,128]{1,0:T(8,128)(2,1)S(1)}, u32[]{:S(2)}, u32[]{:S(2)}) collective-permute-start(bf16[272,128]{1,0:T(8,128)(2,1)S(1)} %get-tuple-element.123), channel_id=1, source_target_pairs={{0,6},{1,7},{2,4},{3,5},{4,2},{5,3},{6,0},{7,1},{8,14},{9,15},{10,... | collective-permute-start | bytes 208904 | tf_op jit(solution)/shard_map/ppermute | solution.py:424
  69.4 2.4 %collective-permute-done.22.refs_0_ = bf16[272,128]{1,0:T(8,128)(2,1)S(1)} collective-permute-done((bf16[272,128]{1,0:T(8,128)(2,1)S(1)}, bf16[272,128]{1,0:T(8,128)(2,1)S(1)}, u32[]{:S(2)}, u32[]{:S(2)}) %collective-permute-start.22) | collective-permute-done | bytes 69664 | tf_op jit(solution)/shard_map/ppermute | solution.py:424
  71.8 1.5 %collective-permute-done.23.refs_1_ = bf16[272,128]{1,0:T(8,128)(2,1)S(1)} collective-permute-done((bf16[272,128]{1,0:T(8,128)(2,1)S(1)}, bf16[272,128]{1,0:T(8,128)(2,1)S(1)}, u32[]{:S(2)}, u32[]{:S(2)}) %collective-permute-start.23) | collective-permute-done | bytes 69664 | tf_op jit(solution)/shard_map/ppermute | solution.py:424
  74.3 1.8 %collective-permute-start.27 = (bf16[256,128]{1,0:T(8,128)(2,1)S(1)}, bf16[256,128]{1,0:T(8,128)(2,1)S(1)}, u32[]{:S(2)}, u32[]{:S(2)}) collective-permute-start(bf16[256,128]{1,0:T(8,128)(2,1)S(1)} %get-tuple-element.127.refs_2_.refs_24_), channel_id=1, source_target_pairs={{0,6},{1,7},{2,4},{3,5},{4,2},{5,3},{6,0},{7,1},{8,14},{9,15},{10,... | collective-permute-start | bytes 196616 | tf_op jit(solution)/shard_map/ppermute | solution.py:424
  76.5 2.3 %collective-permute-start.26 = (bf16[256,128]{1,0:T(8,128)(2,1)S(1)}, bf16[256,128]{1,0:T(8,128)(2,1)S(1)}, u32[]{:S(2)}, u32[]{:S(2)}) collective-permute-start(bf16[256,128]{1,0:T(8,128)(2,1)S(1)} %get-tuple-element.127.refs_2_.refs_24_), channel_id=1, source_target_pairs={{0,4},{1,5},{2,6},{3,7},{4,0},{5,1},{6,2},{7,3},{8,12},{9,13},{10,... | collective-permute-start | bytes 196616 | tf_op jit(solution)/shard_map/ppermute | solution.py:424
  86.7 2.4 %collective-permute-done.28.refs_0_ = bf16[528,128]{1,0:T(8,128)(2,1)S(1)} collective-permute-done((bf16[528,128]{1,0:T(8,128)(2,1)S(1)}, bf16[528,128]{1,0:T(8,128)(2,1)S(1)}, u32[]{:S(2)}, u32[]{:S(2)}) %collective-permute-start.28) | collective-permute-done | bytes 135200 | tf_op jit(solution)/shard_map/ppermute | solution.py:424
  89.1 2.3 %collective-permute-done.29.refs_1_ = bf16[528,128]{1,0:T(8,128)(2,1)S(1)} collective-permute-done((bf16[528,128]{1,0:T(8,128)(2,1)S(1)}, bf16[528,128]{1,0:T(8,128)(2,1)S(1)}, u32[]{:S(2)}, u32[]{:S(2)}) %collective-permute-start.29) | collective-permute-done | bytes 135200 | tf_op jit(solution)/shard_map/ppermute | solution.py:424
  97.7 1.7 %collective-permute-done.32.refs_3_.refs_19_ = bf16[512,128]{1,0:T(8,128)(2,1)S(1)} collective-permute-done((bf16[512,128]{1,0:T(8,128)(2,1)S(1)}, bf16[512,128]{1,0:T(8,128)(2,1)S(1)}, u32[]{:S(2)}, u32[]{:S(2)}) %collective-permute-start.32) | collective-permute-done | bytes 131104 | tf_op jit(solution)/shard_map/ppermute | solution.py:424
  99.5 1.5 %forward.17 = (f32[1152,128]{1,0:T(8,128)S(1)}, f32[256,128]{1,0:T(8,128)S(1)}, f32[8,128]{1,0:T(8,128)S(1)}, bf16[272,128]{1,0:T(8,128)(2,1)S(1)}, bf16[272,128...) custom-call(bf16[48,2,128,128]{3,2,1,0:T(8,128)(2,1)S(1)} %get-tuple-element.86.refs_0_, ...), custom_call_target="tpu_custom_call", output_to_operand_aliasing={{0}: (4, {})} | custom-call | tf_op jit(solution)/shard_map/forward/pallas_call | solution.py:52
  101.0 2.9 %collective-permute-start.34 = (bf16[272,128]{1,0:T(8,128)(2,1)S(1)}, bf16[272,128]{1,0:T(8,128)(2,1)S(1)}, u32[]{:S(2)}, u32[]{:S(2)}) collective-permute-start(bf16[272,128]{1,0:T(8,128)(2,1)S(1)} %get-tuple-element.146), channel_id=1, source_target_pairs={{0,6},{1,7},{2,4},{3,5},{4,2},{5,3},{6,0},{7,1},{8,14},{9,15},{10,... | collective-permute-start | bytes 208904 | tf_op jit(solution)/shard_map/ppermute | solution.py:424
  105.4 1.8 %collective-permute-done.34.refs_0_ = bf16[272,128]{1,0:T(8,128)(2,1)S(1)} collective-permute-done((bf16[272,128]{1,0:T(8,128)(2,1)S(1)}, bf16[272,128]{1,0:T(8,128)(2,1)S(1)}, u32[]{:S(2)}, u32[]{:S(2)}) %collective-permute-start.34) | collective-permute-done | bytes 69664 | tf_op jit(solution)/shard_map/ppermute | solution.py:424
  109.2 1.8 %collective-permute-start.37 = (bf16[256,128]{1,0:T(8,128)(2,1)S(1)}, bf16[256,128]{1,0:T(8,128)(2,1)S(1)}, u32[]{:S(2)}, u32[]{:S(2)}) collective-permute-start(bf16[256,128]{1,0:T(8,128)(2,1)S(1)} %get-tuple-element.151.refs_0_.refs_28_), channel_id=1, source_target_pairs={{0,6},{1,7},{2,4},{3,5},{4,2},{5,3},{6,0},{7,1},{8,14},{9,15},{10,... | collective-permute-start | bytes 196616 | tf_op jit(solution)/shard_map/ppermute | solution.py:424
  111.3 2.3 %collective-permute-start.39 = (bf16[256,128]{1,0:T(8,128)(2,1)S(1)}, bf16[256,128]{1,0:T(8,128)(2,1)S(1)}, u32[]{:S(2)}, u32[]{:S(2)}) collective-permute-start(bf16[256,128]{1,0:T(8,128)(2,1)S(1)} %get-tuple-element.151.refs_0_.refs_28_), channel_id=1, source_target_pairs={{0,4},{1,5},{2,6},{3,7},{4,0},{5,1},{6,2},{7,3},{8,12},{9,13},{10,... | collective-permute-start | bytes 196616 | tf_op jit(solution)/shard_map/ppermute | solution.py:424
  113.6 1.8 %collective-permute-done.37.refs_1_.refs_29_ = bf16[256,128]{1,0:T(8,128)(2,1)S(1)} collective-permute-done((bf16[256,128]{1,0:T(8,128)(2,1)S(1)}, bf16[256,128]{1,0:T(8,128)(2,1)S(1)}, u32[]{:S(2)}, u32[]{:S(2)}) %collective-permute-start.37) | collective-permute-done | bytes 65568 | tf_op jit(solution)/shard_map/ppermute | solution.py:424
  116.7 1.7 %collective-permute-start.40 = (f32[8,128]{1,0:T(8,128)S(1)}, f32[8,128]{1,0:T(8,128)S(1)}, u32[]{:S(2)}, u32[]{:S(2)}) collective-permute-start(f32[8,128]{1,0:T(8,128)S(1)} %norm.1.refs_0_), channel_id=1, source_target_pairs={{0,8},{8,0},{16,24},{24,16},{1,9},{9,1},{17,25},{25,17},{2,10},{10... | collective-permute-start | bytes 12296 | tf_op jit(solution)/shard_map/ppermute | solution.py:424
  120.3 1.7 %collective-permute-done.41.refs_2_ = f32[8,128]{1,0:T(8,128)S(1)} collective-permute-done((f32[8,128]{1,0:T(8,128)S(1)}, f32[8,128]{1,0:T(8,128)S(1)}, u32[]{:S(2)}, u32[]{:S(2)}) %collective-permute-start.41) | collective-permute-done | bytes 4128 | tf_op jit(solution)/shard_map/ppermute | solution.py:424
  126.0 1.5 %unpack.1 = (f32[2,1024,128]{2,1,0:T(8,128)}, f32[2,1024,128]{2,1,0:T(8,128)}) custom-call(f32[1024,128]{1,0:T(8,128)S(1)} %get-tuple-element.156.own_x, f32[1024,128]{1,0:T(8,128)S(1)} %get-tuple-element.157.own_r, bf16[1024,128]{1,0:T(8,128)(2,1)S(1)} %collective-permute-done.43.pair_x, bf16[1024,128]{1,0:T(8,128)(2,1)S(1)} %collective-permute-done.44.pair_r), custom_call_target="tpu_custom_call" | custom-call | tf_op jit(solution)/shard_map/unpack/pallas_call | solution.py:52
  (92 shorter events, 55.2 us)
Async XLA Ops:
  0.6 5.1 %collective-permute-start = (bf16[24,2,128,128]{3,2,1,0:T(8,128)(2,1)}, bf16[24,2,128,128]{3,2,1,0:T(8,128)(2,1)S(1)}, u32[]{:S(2)}, u32[]{:S(2)}) collective-permute-start(bf16[24,2,128,128]{3,2,1,0:T(8,128)(2,1)} %bitcast.11), channel_id=1, source_target_pairs={{0,1},{1,0},{2,3},{3,2},{4,5},{5,4},{6,7},{7,6},{8,9},{9,8},{10,11... | collective-permute-start | bytes 4718600 | tf_op jit(solution)/shard_map/ppermute | solution.py:424
  7.1 6.5 %collective-permute-start.4 = (bf16[512,128]{1,0:T(8,128)(2,1)S(1)}, bf16[512,128]{1,0:T(8,128)(2,1)S(1)}, u32[]{:S(2)}, u32[]{:S(2)}) collective-permute-start(bf16[512,128]{1,0:T(8,128)(2,1)S(1)} %get-tuple-element.91), channel_id=1, source_target_pairs={{0,8},{8,0},{16,24},{24,16},{1,9},{9,1},{17,25},{25,17},{2,10},{10... | collective-permute-start | bytes 393224 | tf_op jit(solution)/shard_map/ppermute | solution.py:424
  9.8 8.5 %collective-permute-start.5 = (bf16[512,128]{1,0:T(8,128)(2,1)S(1)}, bf16[512,128]{1,0:T(8,128)(2,1)S(1)}, u32[]{:S(2)}, u32[]{:S(2)}) collective-permute-start(bf16[512,128]{1,0:T(8,128)(2,1)S(1)} %get-tuple-element.92), channel_id=1, source_target_pairs={{0,16},{8,24},{16,0},{24,8},{1,17},{9,25},{17,1},{25,9},{2,18},{10... | collective-permute-start | bytes 393224 | tf_op jit(solution)/shard_map/ppermute | solution.py:424
  12.0 6.3 %collective-permute-start.6 = (bf16[512,128]{1,0:T(8,128)(2,1)S(1)}, bf16[512,128]{1,0:T(8,128)(2,1)S(1)}, u32[]{:S(2)}, u32[]{:S(2)}) collective-permute-start(bf16[512,128]{1,0:T(8,128)(2,1)S(1)} %get-tuple-element.93), channel_id=1, source_target_pairs={{0,24},{8,16},{16,8},{24,0},{1,25},{9,17},{17,9},{25,1},{2,26},{10... | collective-permute-start | bytes 393224 | tf_op jit(solution)/shard_map/ppermute | solution.py:424
  18.3 5.8 %collective-permute-start.9 = (bf16[512,128]{1,0:T(8,128)(2,1)S(1)}, bf16[512,128]{1,0:T(8,128)(2,1)S(1)}, u32[]{:S(2)}, u32[]{:S(2)}) collective-permute-start(bf16[512,128]{1,0:T(8,128)(2,1)S(1)} %get-tuple-element.94.refs_2_.refs_8_), channel_id=1, source_target_pairs={{0,8},{8,0},{16,24},{24,16},{1,9},{9,1},{17,25},{25,17},{2,10},{10... | collective-permute-start | bytes 393224 | tf_op jit(solution)/shard_map/ppermute | solution.py:424
  19.8 7.2 %collective-permute-start.7 = (bf16[512,128]{1,0:T(8,128)(2,1)S(1)}, bf16[512,128]{1,0:T(8,128)(2,1)S(1)}, u32[]{:S(2)}, u32[]{:S(2)}) collective-permute-start(bf16[512,128]{1,0:T(8,128)(2,1)S(1)} %get-tuple-element.94.refs_2_.refs_8_), channel_id=1, source_target_pairs={{0,16},{8,24},{16,0},{24,8},{1,17},{9,25},{17,1},{25,9},{2,18},{10... | collective-permute-start | bytes 393224 | tf_op jit(solution)/shard_map/ppermute | solution.py:424
  20.5 6.5 %collective-permute-start.8 = (bf16[512,128]{1,0:T(8,128)(2,1)S(1)}, bf16[512,128]{1,0:T(8,128)(2,1)S(1)}, u32[]{:S(2)}, u32[]{:S(2)}) collective-permute-start(bf16[512,128]{1,0:T(8,128)(2,1)S(1)} %get-tuple-element.94.refs_2_.refs_8_), channel_id=1, source_target_pairs={{0,24},{8,16},{16,8},{24,0},{1,25},{9,17},{17,9},{25,1},{2,26},{10... | collective-permute-start | bytes 393224 | tf_op jit(solution)/shard_map/ppermute | solution.py:424
  28.5 6.6 %collective-permute-start.10 = (bf16[272,128]{1,0:T(8,128)(2,1)S(1)}, bf16[272,128]{1,0:T(8,128)(2,1)S(1)}, u32[]{:S(2)}, u32[]{:S(2)}) collective-permute-start(bf16[272,128]{1,0:T(8,128)(2,1)S(1)} %get-tuple-element.101), channel_id=1, source_target_pairs={{0,6},{1,7},{2,4},{3,5},{4,2},{5,3},{6,0},{7,1},{8,14},{9,15},{10,... | collective-permute-start | bytes 208904 | tf_op jit(solution)/shard_map/ppermute | solution.py:424
  32.1 5.2 %collective-permute-start.12 = (bf16[272,128]{1,0:T(8,128)(2,1)S(1)}, bf16[272,128]{1,0:T(8,128)(2,1)S(1)}, u32[]{:S(2)}, u32[]{:S(2)}) collective-permute-start(bf16[272,128]{1,0:T(8,128)(2,1)S(1)} %get-tuple-element.103), channel_id=1, source_target_pairs={{0,4},{1,5},{2,6},{3,7},{4,0},{5,1},{6,2},{7,3},{8,12},{9,13},{10,... | collective-permute-start | bytes 208904 | tf_op jit(solution)/shard_map/ppermute | solution.py:424
  37.4 6.2 %collective-permute-start.15 = (bf16[256,128]{1,0:T(8,128)(2,1)S(1)}, bf16[256,128]{1,0:T(8,128)(2,1)S(1)}, u32[]{:S(2)}, u32[]{:S(2)}) collective-permute-start(bf16[256,128]{1,0:T(8,128)(2,1)S(1)} %get-tuple-element.104.refs_2_.refs_20_), channel_id=1, source_target_pairs={{0,6},{1,7},{2,4},{3,5},{4,2},{5,3},{6,0},{7,1},{8,14},{9,15},{10,... | collective-permute-start | bytes 196616 | tf_op jit(solution)/shard_map/ppermute | solution.py:424
  39.1 5.5 %collective-permute-start.13 = (bf16[256,128]{1,0:T(8,128)(2,1)S(1)}, bf16[256,128]{1,0:T(8,128)(2,1)S(1)}, u32[]{:S(2)}, u32[]{:S(2)}) collective-permute-start(bf16[256,128]{1,0:T(8,128)(2,1)S(1)} %get-tuple-element.104.refs_2_.refs_20_), channel_id=1, source_target_pairs={{0,2},{1,3},{2,0},{3,1},{4,6},{5,7},{6,4},{7,5},{8,10},{9,11},{10,... | collective-permute-start | bytes 196616 | tf_op jit(solution)/shard_map/ppermute | solution.py:424
  39.6 5.2 %collective-permute-start.14 = (bf16[256,128]{1,0:T(8,128)(2,1)S(1)}, bf16[256,128]{1,0:T(8,128)(2,1)S(1)}, u32[]{:S(2)}, u32[]{:S(2)}) collective-permute-start(bf16[256,128]{1,0:T(8,128)(2,1)S(1)} %get-tuple-element.104.refs_2_.refs_20_), channel_id=1, source_target_pairs={{0,4},{1,5},{2,6},{3,7},{4,0},{5,1},{6,2},{7,3},{8,12},{9,13},{10,... | collective-permute-start | bytes 196616 | tf_op jit(solution)/shard_map/ppermute | solution.py:424
  46.1 5.1 %collective-permute-start.16 = (bf16[528,128]{1,0:T(8,128)(2,1)S(1)}, bf16[528,128]{1,0:T(8,128)(2,1)S(1)}, u32[]{:S(2)}, u32[]{:S(2)}) collective-permute-start(bf16[528,128]{1,0:T(8,128)(2,1)S(1)} %get-tuple-element.111), channel_id=1, source_target_pairs={{0,8},{8,0},{16,24},{24,16},{1,9},{9,1},{17,25},{25,17},{2,10},{10... | collective-permute-start | bytes 405512 | tf_op jit(solution)/shard_map/ppermute | solution.py:424
  48.4 7.1 %collective-permute-start.18 = (bf16[528,128]{1,0:T(8,128)(2,1)S(1)}, bf16[528,128]{1,0:T(8,128)(2,1)S(1)}, u32[]{:S(2)}, u32[]{:S(2)}) collective-permute-start(bf16[528,128]{1,0:T(8,128)(2,1)S(1)} %get-tuple-element.113), channel_id=1, source_target_pairs={{0,24},{8,16},{16,8},{24,0},{1,25},{9,17},{17,9},{25,1},{2,26},{10... | collective-permute-start | bytes 405512 | tf_op jit(solution)/shard_map/ppermute | solution.py:424
  55.5 5.0 %collective-permute-start.21 = (bf16[512,128]{1,0:T(8,128)(2,1)S(1)}, bf16[512,128]{1,0:T(8,128)(2,1)S(1)}, u32[]{:S(2)}, u32[]{:S(2)}) collective-permute-start(bf16[512,128]{1,0:T(8,128)(2,1)S(1)} %get-tuple-element.116.refs_2_.refs_12_), channel_id=1, source_target_pairs={{0,8},{8,0},{16,24},{24,16},{1,9},{9,1},{17,25},{25,17},{2,10},{10... | collective-permute-start | bytes 393224 | tf_op jit(solution)/shard_map/ppermute | solution.py:424
  57.2 5.9 %collective-permute-start.20 = (bf16[512,128]{1,0:T(8,128)(2,1)S(1)}, bf16[512,128]{1,0:T(8,128)(2,1)S(1)}, u32[]{:S(2)}, u32[]{:S(2)}) collective-permute-start(bf16[512,128]{1,0:T(8,128)(2,1)S(1)} %get-tuple-element.116.refs_2_.refs_12_), channel_id=1, source_target_pairs={{0,24},{8,16},{16,8},{24,0},{1,25},{9,17},{17,9},{25,1},{2,26},{10... | collective-permute-start | bytes 393224 | tf_op jit(solution)/shard_map/ppermute | solution.py:424
  64.6 7.2 %collective-permute-start.22 = (bf16[272,128]{1,0:T(8,128)(2,1)S(1)}, bf16[272,128]{1,0:T(8,128)(2,1)S(1)}, u32[]{:S(2)}, u32[]{:S(2)}) collective-permute-start(bf16[272,128]{1,0:T(8,128)(2,1)S(1)} %get-tuple-element.123), channel_id=1, source_target_pairs={{0,6},{1,7},{2,4},{3,5},{4,2},{5,3},{6,0},{7,1},{8,14},{9,15},{10,... | collective-permute-start | bytes 208904 | tf_op jit(solution)/shard_map/ppermute | solution.py:424
  68.8 5.5 %collective-permute-start.24 = (bf16[272,128]{1,0:T(8,128)(2,1)S(1)}, bf16[272,128]{1,0:T(8,128)(2,1)S(1)}, u32[]{:S(2)}, u32[]{:S(2)}) collective-permute-start(bf16[272,128]{1,0:T(8,128)(2,1)S(1)} %get-tuple-element.125), channel_id=1, source_target_pairs={{0,4},{1,5},{2,6},{3,7},{4,0},{5,1},{6,2},{7,3},{8,12},{9,13},{10,... | collective-permute-start | bytes 208904 | tf_op jit(solution)/shard_map/ppermute | solution.py:424
  74.3 6.2 %collective-permute-start.27 = (bf16[256,128]{1,0:T(8,128)(2,1)S(1)}, bf16[256,128]{1,0:T(8,128)(2,1)S(1)}, u32[]{:S(2)}, u32[]{:S(2)}) collective-permute-start(bf16[256,128]{1,0:T(8,128)(2,1)S(1)} %get-tuple-element.127.refs_2_.refs_24_), channel_id=1, source_target_pairs={{0,6},{1,7},{2,4},{3,5},{4,2},{5,3},{6,0},{7,1},{8,14},{9,15},{10,... | collective-permute-start | bytes 196616 | tf_op jit(solution)/shard_map/ppermute | solution.py:424
  76.1 5.7 %collective-permute-start.25 = (bf16[256,128]{1,0:T(8,128)(2,1)S(1)}, bf16[256,128]{1,0:T(8,128)(2,1)S(1)}, u32[]{:S(2)}, u32[]{:S(2)}) collective-permute-start(bf16[256,128]{1,0:T(8,128)(2,1)S(1)} %get-tuple-element.127.refs_2_.refs_24_), channel_id=1, source_target_pairs={{0,2},{1,3},{2,0},{3,1},{4,6},{5,7},{6,4},{7,5},{8,10},{9,11},{10,... | collective-permute-start | bytes 196616 | tf_op jit(solution)/shard_map/ppermute | solution.py:424
  76.5 5.3 %collective-permute-start.26 = (bf16[256,128]{1,0:T(8,128)(2,1)S(1)}, bf16[256,128]{1,0:T(8,128)(2,1)S(1)}, u32[]{:S(2)}, u32[]{:S(2)}) collective-permute-start(bf16[256,128]{1,0:T(8,128)(2,1)S(1)} %get-tuple-element.127.refs_2_.refs_24_), channel_id=1, source_target_pairs={{0,4},{1,5},{2,6},{3,7},{4,0},{5,1},{6,2},{7,3},{8,12},{9,13},{10,... | collective-permute-start | bytes 196616 | tf_op jit(solution)/shard_map/ppermute | solution.py:424
  83.1 6.0 %collective-permute-start.28 = (bf16[528,128]{1,0:T(8,128)(2,1)S(1)}, bf16[528,128]{1,0:T(8,128)(2,1)S(1)}, u32[]{:S(2)}, u32[]{:S(2)}) collective-permute-start(bf16[528,128]{1,0:T(8,128)(2,1)S(1)} %get-tuple-element.134), channel_id=1, source_target_pairs={{0,8},{8,0},{16,24},{24,16},{1,9},{9,1},{17,25},{25,17},{2,10},{10... | collective-permute-start | bytes 405512 | tf_op jit(solution)/shard_map/ppermute | solution.py:424
  84.6 6.8 %collective-permute-start.29 = (bf16[528,128]{1,0:T(8,128)(2,1)S(1)}, bf16[528,128]{1,0:T(8,128)(2,1)S(1)}, u32[]{:S(2)}, u32[]{:S(2)}) collective-permute-start(bf16[528,128]{1,0:T(8,128)(2,1)S(1)} %get-tuple-element.135), channel_id=1, source_target_pairs={{0,16},{8,24},{16,0},{24,8},{1,17},{9,25},{17,1},{25,9},{2,18},{10... | collective-permute-start | bytes 405512 | tf_op jit(solution)/shard_map/ppermute | solution.py:424
  85.3 6.1 %collective-permute-start.30 = (bf16[528,128]{1,0:T(8,128)(2,1)S(1)}, bf16[528,128]{1,0:T(8,128)(2,1)S(1)}, u32[]{:S(2)}, u32[]{:S(2)}) collective-permute-start(bf16[528,128]{1,0:T(8,128)(2,1)S(1)} %get-tuple-element.136), channel_id=1, source_target_pairs={{0,24},{8,16},{16,8},{24,0},{1,25},{9,17},{17,9},{25,1},{2,26},{10... | collective-permute-start | bytes 405512 | tf_op jit(solution)/shard_map/ppermute | solution.py:424
  91.5 5.0 %collective-permute-start.33 = (bf16[512,128]{1,0:T(8,128)(2,1)S(1)}, bf16[512,128]{1,0:T(8,128)(2,1)S(1)}, u32[]{:S(2)}, u32[]{:S(2)}) collective-permute-start(bf16[512,128]{1,0:T(8,128)(2,1)S(1)} %get-tuple-element.139.refs_2_.refs_16_), channel_id=1, source_target_pairs={{0,8},{8,0},{16,24},{24,16},{1,9},{9,1},{17,25},{25,17},{2,10},{10... | collective-permute-start | bytes 393224 | tf_op jit(solution)/shard_map/ppermute | solution.py:424
  92.7 5.0 %collective-permute-start.31 = (bf16[512,128]{1,0:T(8,128)(2,1)S(1)}, bf16[512,128]{1,0:T(8,128)(2,1)S(1)}, u32[]{:S(2)}, u32[]{:S(2)}) collective-permute-start(bf16[512,128]{1,0:T(8,128)(2,1)S(1)} %get-tuple-element.139.refs_2_.refs_16_), channel_id=1, source_target_pairs={{0,16},{8,24},{16,0},{24,8},{1,17},{9,25},{17,1},{25,9},{2,18},{10... | collective-permute-start | bytes 393224 | tf_op jit(solution)/shard_map/ppermute | solution.py:424
  93.6 5.9 %collective-permute-start.32 = (bf16[512,128]{1,0:T(8,128)(2,1)S(1)}, bf16[512,128]{1,0:T(8,128)(2,1)S(1)}, u32[]{:S(2)}, u32[]{:S(2)}) collective-permute-start(bf16[512,128]{1,0:T(8,128)(2,1)S(1)} %get-tuple-element.139.refs_2_.refs_16_), channel_id=1, source_target_pairs={{0,24},{8,16},{16,8},{24,0},{1,25},{9,17},{17,9},{25,1},{2,26},{10... | collective-permute-start | bytes 393224 | tf_op jit(solution)/shard_map/ppermute | solution.py:424
  101.0 6.2 %collective-permute-start.34 = (bf16[272,128]{1,0:T(8,128)(2,1)S(1)}, bf16[272,128]{1,0:T(8,128)(2,1)S(1)}, u32[]{:S(2)}, u32[]{:S(2)}) collective-permute-start(bf16[272,128]{1,0:T(8,128)(2,1)S(1)} %get-tuple-element.146), channel_id=1, source_target_pairs={{0,6},{1,7},{2,4},{3,5},{4,2},{5,3},{6,0},{7,1},{8,14},{9,15},{10,... | collective-permute-start | bytes 208904 | tf_op jit(solution)/shard_map/ppermute | solution.py:424
  103.9 5.2 %collective-permute-start.36 = (bf16[272,128]{1,0:T(8,128)(2,1)S(1)}, bf16[272,128]{1,0:T(8,128)(2,1)S(1)}, u32[]{:S(2)}, u32[]{:S(2)}) collective-permute-start(bf16[272,128]{1,0:T(8,128)(2,1)S(1)} %get-tuple-element.148), channel_id=1, source_target_pairs={{0,4},{1,5},{2,6},{3,7},{4,0},{5,1},{6,2},{7,3},{8,12},{9,13},{10,... | collective-permute-start | bytes 208904 | tf_op jit(solution)/shard_map/ppermute | solution.py:424
  109.2 6.2 %collective-permute-start.37 = (bf16[256,128]{1,0:T(8,128)(2,1)S(1)}, bf16[256,128]{1,0:T(8,128)(2,1)S(1)}, u32[]{:S(2)}, u32[]{:S(2)}) collective-permute-start(bf16[256,128]{1,0:T(8,128)(2,1)S(1)} %get-tuple-element.151.refs_0_.refs_28_), channel_id=1, source_target_pairs={{0,6},{1,7},{2,4},{3,5},{4,2},{5,3},{6,0},{7,1},{8,14},{9,15},{10,... | collective-permute-start | bytes 196616 | tf_op jit(solution)/shard_map/ppermute | solution.py:424
  110.9 5.7 %collective-permute-start.38 = (bf16[256,128]{1,0:T(8,128)(2,1)S(1)}, bf16[256,128]{1,0:T(8,128)(2,1)S(1)}, u32[]{:S(2)}, u32[]{:S(2)}) collective-permute-start(bf16[256,128]{1,0:T(8,128)(2,1)S(1)} %get-tuple-element.151.refs_0_.refs_28_), channel_id=1, source_target_pairs={{0,2},{1,3},{2,0},{3,1},{4,6},{5,7},{6,4},{7,5},{8,10},{9,11},{10,... | collective-permute-start | bytes 196616 | tf_op jit(solution)/shard_map/ppermute | solution.py:424
  111.3 5.3 %collective-permute-start.39 = (bf16[256,128]{1,0:T(8,128)(2,1)S(1)}, bf16[256,128]{1,0:T(8,128)(2,1)S(1)}, u32[]{:S(2)}, u32[]{:S(2)}) collective-permute-start(bf16[256,128]{1,0:T(8,128)(2,1)S(1)} %get-tuple-element.151.refs_0_.refs_28_), channel_id=1, source_target_pairs={{0,4},{1,5},{2,6},{3,7},{4,0},{5,1},{6,2},{7,3},{8,12},{9,13},{10,... | collective-permute-start | bytes 196616 | tf_op jit(solution)/shard_map/ppermute | solution.py:424
  (16 other events, 105.7 us)

commit v14 on v10

--- a/solution.py
+++ b/solution.py
@@ -12,7 +12,7 @@
 ITERS = 3
 EPSILON = 1e-06
 GROUP = 8
-WIDTH = 8
+WIDTH = 12
 LAST_WIDTH = 12
 TAIL = 16
 VMEM_BYTES = 16 << 20

time: 128 us -> 129 us (level)
  waiting for transfers between devices: 45.8 us -> 47.2 us
    ppermute x45, waiting for transfers between devices: 45.8 us -> 47.2 us  [swap(): return lax.ppermute(value, axis, [(i, i ^ offset) for i in range(size)])]
  transfers between devices with their start and end apart: 45 -> 45, of which waited for: 35 -> 34; matrix products, arithmetic and copies ran while one was open for 0% -> 0% of each run, Pallas kernels for 11% -> 11%
where the time goes in v14:
time: 129 us
  starting transfers between devices  55.5 us (43%)
  waiting for transfers between devices  47.2 us (37%)
  Pallas kernels  24.1 us (19%)
  between operations  1.7 us (1%)
    ppermute x45, starting transfers between devices, swap(): return lax.ppermute(value, axis, [(i, i ^ offset) for i in range(size)])  55.5 us
    ppermute x45, waiting for transfers between devices, swap(): return lax.ppermute(value, axis, [(i, i ^ offset) for i in range(size)])  47.2 us
    pallas_call x27, Pallas kernels, call(): pl.pallas_call(kernel, name=name, out_shape=[jax.ShapeDtypeStruct(s, d) f...  24.1 us
  transfers between devices with their start and end apart: 45, of which 34 were waited for; matrix products, arithmetic and copies ran while one was open for 0% of the time, Pallas kernels for 11%

profile of v14, /device:TPU:0, one launch (start us, length us, event | category | flops | bytes accessed | tf_op | source)
XLA Modules:
  0.0 128.6 jit_solution(157286387100127195)
XLA Ops:
  2.5 3.2 %pack.1 = (bf16[48,2,128,128]{3,2,1,0:T(8,128)(2,1)S(1)}, bf16[48,128,256]{2,1,0:T(8,128)(2,1)S(1)}, f32[1152,128]{1,0:T(8,128)S(1)}, bf16[1024,128]{1,0:T(8,128)(2,1)S(1)}, bf16[1024,128]{1,0:T(8,128)(2,1)S(1)}) custom-call(f32[2,1024,128]{2,1,0:T(8,128)} %record_ref.1, bf16[24,2,128,128]{3,2,1,0:T(8,128)(2,1)} %bitcast.12, s32[1,24]{1,0:T(1,128)} %bitcast.6, ...), custom_call_target="tpu_custom_call" | custom-call | tf_op jit(solution)/shard_map/pack/pallas_call | solution.py:52
  6.8 3.0 %collective-permute-start.4 = (bf16[512,128]{1,0:T(8,128)(2,1)S(1)}, bf16[512,128]{1,0:T(8,128)(2,1)S(1)}, u32[]{:S(2)}, u32[]{:S(2)}) collective-permute-start(bf16[512,128]{1,0:T(8,128)(2,1)S(1)} %get-tuple-element.91), channel_id=1, source_target_pairs={{0,8},{8,0},{16,24},{24,16},{1,9},{9,1},{17,25},{25,17},{2,10},{10... | collective-permute-start | bytes 393224 | tf_op jit(solution)/shard_map/ppermute | solution.py:424
  9.8 1.5 %collective-permute-start.5 = (bf16[512,128]{1,0:T(8,128)(2,1)S(1)}, bf16[512,128]{1,0:T(8,128)(2,1)S(1)}, u32[]{:S(2)}, u32[]{:S(2)}) collective-permute-start(bf16[512,128]{1,0:T(8,128)(2,1)S(1)} %get-tuple-element.92), channel_id=1, source_target_pairs={{0,16},{8,24},{16,0},{24,8},{1,17},{9,25},{17,1},{25,9},{2,18},{10... | collective-permute-start | bytes 393224 | tf_op jit(solution)/shard_map/ppermute | solution.py:424
  11.9 1.7 %collective-permute-done.4.refs_0_ = bf16[512,128]{1,0:T(8,128)(2,1)S(1)} collective-permute-done((bf16[512,128]{1,0:T(8,128)(2,1)S(1)}, bf16[512,128]{1,0:T(8,128)(2,1)S(1)}, u32[]{:S(2)}, u32[]{:S(2)}) %collective-permute-start.4) | collective-permute-done | bytes 131104 | tf_op jit(solution)/shard_map/ppermute | solution.py:424
  13.7 3.1 %collective-permute-done.5.refs_1_ = bf16[512,128]{1,0:T(8,128)(2,1)S(1)} collective-permute-done((bf16[512,128]{1,0:T(8,128)(2,1)S(1)}, bf16[512,128]{1,0:T(8,128)(2,1)S(1)}, u32[]{:S(2)}, u32[]{:S(2)}) %collective-permute-start.5) | collective-permute-done | bytes 131104 | tf_op jit(solution)/shard_map/ppermute | solution.py:424
  27.8 4.1 %collective-permute-start.10 = (bf16[272,128]{1,0:T(8,128)(2,1)S(1)}, bf16[272,128]{1,0:T(8,128)(2,1)S(1)}, u32[]{:S(2)}, u32[]{:S(2)}) collective-permute-start(bf16[272,128]{1,0:T(8,128)(2,1)S(1)} %get-tuple-element.101), channel_id=1, source_target_pairs={{0,6},{1,7},{2,4},{3,5},{4,2},{5,3},{6,0},{7,1},{8,14},{9,15},{10,... | collective-permute-start | bytes 208904 | tf_op jit(solution)/shard_map/ppermute | solution.py:424
  32.5 2.0 %collective-permute-done.10.refs_0_ = bf16[272,128]{1,0:T(8,128)(2,1)S(1)} collective-permute-done((bf16[272,128]{1,0:T(8,128)(2,1)S(1)}, bf16[272,128]{1,0:T(8,128)(2,1)S(1)}, u32[]{:S(2)}, u32[]{:S(2)}) %collective-permute-start.10) | collective-permute-done | bytes 69664 | tf_op jit(solution)/shard_map/ppermute | solution.py:424
  34.6 1.7 %collective-permute-done.11.refs_1_ = bf16[272,128]{1,0:T(8,128)(2,1)S(1)} collective-permute-done((bf16[272,128]{1,0:T(8,128)(2,1)S(1)}, bf16[272,128]{1,0:T(8,128)(2,1)S(1)}, u32[]{:S(2)}, u32[]{:S(2)}) %collective-permute-start.11) | collective-permute-done | bytes 69664 | tf_op jit(solution)/shard_map/ppermute | solution.py:424
  37.2 1.7 %collective-permute-start.15 = (bf16[256,128]{1,0:T(8,128)(2,1)S(1)}, bf16[256,128]{1,0:T(8,128)(2,1)S(1)}, u32[]{:S(2)}, u32[]{:S(2)}) collective-permute-start(bf16[256,128]{1,0:T(8,128)(2,1)S(1)} %get-tuple-element.104.refs_2_.refs_20_), channel_id=1, source_target_pairs={{0,6},{1,7},{2,4},{3,5},{4,2},{5,3},{6,0},{7,1},{8,14},{9,15},{10,... | collective-permute-start | bytes 196616 | tf_op jit(solution)/shard_map/ppermute | solution.py:424
  39.4 2.2 %collective-permute-start.14 = (bf16[256,128]{1,0:T(8,128)(2,1)S(1)}, bf16[256,128]{1,0:T(8,128)(2,1)S(1)}, u32[]{:S(2)}, u32[]{:S(2)}) collective-permute-start(bf16[256,128]{1,0:T(8,128)(2,1)S(1)} %get-tuple-element.104.refs_2_.refs_20_), channel_id=1, source_target_pairs={{0,4},{1,5},{2,6},{3,7},{4,0},{5,1},{6,2},{7,3},{8,12},{9,13},{10,... | collective-permute-start | bytes 196616 | tf_op jit(solution)/shard_map/ppermute | solution.py:424
  49.3 1.5 %collective-permute-done.16.refs_0_ = bf16[528,128]{1,0:T(8,128)(2,1)S(1)} collective-permute-done((bf16[528,128]{1,0:T(8,128)(2,1)S(1)}, bf16[528,128]{1,0:T(8,128)(2,1)S(1)}, u32[]{:S(2)}, u32[]{:S(2)}) %collective-permute-start.16) | collective-permute-done | bytes 135200 | tf_op jit(solution)/shard_map/ppermute | solution.py:424
  52.2 3.0 %collective-permute-done.18.refs_2_ = bf16[528,128]{1,0:T(8,128)(2,1)S(1)} collective-permute-done((bf16[528,128]{1,0:T(8,128)(2,1)S(1)}, bf16[528,128]{1,0:T(8,128)(2,1)S(1)}, u32[]{:S(2)}, u32[]{:S(2)}) %collective-permute-start.18) | collective-permute-done | bytes 135200 | tf_op jit(solution)/shard_map/ppermute | solution.py:424
  56.6 2.1 %collective-permute-start.20 = (bf16[512,128]{1,0:T(8,128)(2,1)S(1)}, bf16[512,128]{1,0:T(8,128)(2,1)S(1)}, u32[]{:S(2)}, u32[]{:S(2)}) collective-permute-start(bf16[512,128]{1,0:T(8,128)(2,1)S(1)} %get-tuple-element.116.refs_2_.refs_12_), channel_id=1, source_target_pairs={{0,24},{8,16},{16,8},{24,0},{1,25},{9,17},{17,9},{25,1},{2,26},{10... | collective-permute-start | bytes 393224 | tf_op jit(solution)/shard_map/ppermute | solution.py:424
  64.0 3.8 %collective-permute-start.22 = (bf16[272,128]{1,0:T(8,128)(2,1)S(1)}, bf16[272,128]{1,0:T(8,128)(2,1)S(1)}, u32[]{:S(2)}, u32[]{:S(2)}) collective-permute-start(bf16[272,128]{1,0:T(8,128)(2,1)S(1)} %get-tuple-element.123), channel_id=1, source_target_pairs={{0,6},{1,7},{2,4},{3,5},{4,2},{5,3},{6,0},{7,1},{8,14},{9,15},{10,... | collective-permute-start | bytes 208904 | tf_op jit(solution)/shard_map/ppermute | solution.py:424
  68.5 1.9 %collective-permute-done.22.refs_0_ = bf16[272,128]{1,0:T(8,128)(2,1)S(1)} collective-permute-done((bf16[272,128]{1,0:T(8,128)(2,1)S(1)}, bf16[272,128]{1,0:T(8,128)(2,1)S(1)}, u32[]{:S(2)}, u32[]{:S(2)}) %collective-permute-start.22) | collective-permute-done | bytes 69664 | tf_op jit(solution)/shard_map/ppermute | solution.py:424
  70.4 3.6 %collective-permute-done.23.refs_1_ = bf16[272,128]{1,0:T(8,128)(2,1)S(1)} collective-permute-done((bf16[272,128]{1,0:T(8,128)(2,1)S(1)}, bf16[272,128]{1,0:T(8,128)(2,1)S(1)}, u32[]{:S(2)}, u32[]{:S(2)}) %collective-permute-start.23) | collective-permute-done | bytes 69664 | tf_op jit(solution)/shard_map/ppermute | solution.py:424
  74.6 2.6 %collective-permute-start.27 = (bf16[256,128]{1,0:T(8,128)(2,1)S(1)}, bf16[256,128]{1,0:T(8,128)(2,1)S(1)}, u32[]{:S(2)}, u32[]{:S(2)}) collective-permute-start(bf16[256,128]{1,0:T(8,128)(2,1)S(1)} %get-tuple-element.127.refs_2_.refs_24_), channel_id=1, source_target_pairs={{0,6},{1,7},{2,4},{3,5},{4,2},{5,3},{6,0},{7,1},{8,14},{9,15},{10,... | collective-permute-start | bytes 196616 | tf_op jit(solution)/shard_map/ppermute | solution.py:424
  77.2 1.9 %collective-permute-start.26 = (bf16[256,128]{1,0:T(8,128)(2,1)S(1)}, bf16[256,128]{1,0:T(8,128)(2,1)S(1)}, u32[]{:S(2)}, u32[]{:S(2)}) collective-permute-start(bf16[256,128]{1,0:T(8,128)(2,1)S(1)} %get-tuple-element.127.refs_2_.refs_24_), channel_id=1, source_target_pairs={{0,4},{1,5},{2,6},{3,7},{4,0},{5,1},{6,2},{7,3},{8,12},{9,13},{10,... | collective-permute-start | bytes 196616 | tf_op jit(solution)/shard_map/ppermute | solution.py:424
  87.1 2.6 %collective-permute-done.28.refs_0_ = bf16[528,128]{1,0:T(8,128)(2,1)S(1)} collective-permute-done((bf16[528,128]{1,0:T(8,128)(2,1)S(1)}, bf16[528,128]{1,0:T(8,128)(2,1)S(1)}, u32[]{:S(2)}, u32[]{:S(2)}) %collective-permute-start.28) | collective-permute-done | bytes 135200 | tf_op jit(solution)/shard_map/ppermute | solution.py:424
  89.7 2.7 %collective-permute-done.29.refs_1_ = bf16[528,128]{1,0:T(8,128)(2,1)S(1)} collective-permute-done((bf16[528,128]{1,0:T(8,128)(2,1)S(1)}, bf16[528,128]{1,0:T(8,128)(2,1)S(1)}, u32[]{:S(2)}, u32[]{:S(2)}) %collective-permute-start.29) | collective-permute-done | bytes 135200 | tf_op jit(solution)/shard_map/ppermute | solution.py:424
  94.6 1.6 %collective-permute-start.32 = (bf16[512,128]{1,0:T(8,128)(2,1)S(1)}, bf16[512,128]{1,0:T(8,128)(2,1)S(1)}, u32[]{:S(2)}, u32[]{:S(2)}) collective-permute-start(bf16[512,128]{1,0:T(8,128)(2,1)S(1)} %get-tuple-element.139.refs_2_.refs_16_), channel_id=1, source_target_pairs={{0,24},{8,16},{16,8},{24,0},{1,25},{9,17},{17,9},{25,1},{2,26},{10... | collective-permute-start | bytes 393224 | tf_op jit(solution)/shard_map/ppermute | solution.py:424
  98.7 1.7 %collective-permute-done.32.refs_3_.refs_19_ = bf16[512,128]{1,0:T(8,128)(2,1)S(1)} collective-permute-done((bf16[512,128]{1,0:T(8,128)(2,1)S(1)}, bf16[512,128]{1,0:T(8,128)(2,1)S(1)}, u32[]{:S(2)}, u32[]{:S(2)}) %collective-permute-start.32) | collective-permute-done | bytes 131104 | tf_op jit(solution)/shard_map/ppermute | solution.py:424
  101.8 2.4 %collective-permute-start.34 = (bf16[272,128]{1,0:T(8,128)(2,1)S(1)}, bf16[272,128]{1,0:T(8,128)(2,1)S(1)}, u32[]{:S(2)}, u32[]{:S(2)}) collective-permute-start(bf16[272,128]{1,0:T(8,128)(2,1)S(1)} %get-tuple-element.146), channel_id=1, source_target_pairs={{0,6},{1,7},{2,4},{3,5},{4,2},{5,3},{6,0},{7,1},{8,14},{9,15},{10,... | collective-permute-start | bytes 208904 | tf_op jit(solution)/shard_map/ppermute | solution.py:424
  104.3 2.0 %collective-permute-start.36 = (bf16[272,128]{1,0:T(8,128)(2,1)S(1)}, bf16[272,128]{1,0:T(8,128)(2,1)S(1)}, u32[]{:S(2)}, u32[]{:S(2)}) collective-permute-start(bf16[272,128]{1,0:T(8,128)(2,1)S(1)} %get-tuple-element.148), channel_id=1, source_target_pairs={{0,4},{1,5},{2,6},{3,7},{4,0},{5,1},{6,2},{7,3},{8,12},{9,13},{10,... | collective-permute-start | bytes 208904 | tf_op jit(solution)/shard_map/ppermute | solution.py:424
  106.3 1.7 %collective-permute-done.34.refs_0_ = bf16[272,128]{1,0:T(8,128)(2,1)S(1)} collective-permute-done((bf16[272,128]{1,0:T(8,128)(2,1)S(1)}, bf16[272,128]{1,0:T(8,128)(2,1)S(1)}, u32[]{:S(2)}, u32[]{:S(2)}) %collective-permute-start.34) | collective-permute-done | bytes 69664 | tf_op jit(solution)/shard_map/ppermute | solution.py:424
  109.5 2.1 %collective-permute-start.37 = (bf16[256,128]{1,0:T(8,128)(2,1)S(1)}, bf16[256,128]{1,0:T(8,128)(2,1)S(1)}, u32[]{:S(2)}, u32[]{:S(2)}) collective-permute-start(bf16[256,128]{1,0:T(8,128)(2,1)S(1)} %get-tuple-element.151.refs_0_.refs_28_), channel_id=1, source_target_pairs={{0,6},{1,7},{2,4},{3,5},{4,2},{5,3},{6,0},{7,1},{8,14},{9,15},{10,... | collective-permute-start | bytes 196616 | tf_op jit(solution)/shard_map/ppermute | solution.py:424
  112.2 1.8 %collective-permute-start.39 = (bf16[256,128]{1,0:T(8,128)(2,1)S(1)}, bf16[256,128]{1,0:T(8,128)(2,1)S(1)}, u32[]{:S(2)}, u32[]{:S(2)}) collective-permute-start(bf16[256,128]{1,0:T(8,128)(2,1)S(1)} %get-tuple-element.151.refs_0_.refs_28_), channel_id=1, source_target_pairs={{0,4},{1,5},{2,6},{3,7},{4,0},{5,1},{6,2},{7,3},{8,12},{9,13},{10,... | collective-permute-start | bytes 196616 | tf_op jit(solution)/shard_map/ppermute | solution.py:424
  114.0 1.8 %collective-permute-done.37.refs_1_.refs_29_ = bf16[256,128]{1,0:T(8,128)(2,1)S(1)} collective-permute-done((bf16[256,128]{1,0:T(8,128)(2,1)S(1)}, bf16[256,128]{1,0:T(8,128)(2,1)S(1)}, u32[]{:S(2)}, u32[]{:S(2)}) %collective-permute-start.37) | collective-permute-done | bytes 65568 | tf_op jit(solution)/shard_map/ppermute | solution.py:424
  117.5 2.4 %collective-permute-start.40 = (f32[8,128]{1,0:T(8,128)S(1)}, f32[8,128]{1,0:T(8,128)S(1)}, u32[]{:S(2)}, u32[]{:S(2)}) collective-permute-start(f32[8,128]{1,0:T(8,128)S(1)} %norm.1.refs_0_), channel_id=1, source_target_pairs={{0,8},{8,0},{16,24},{24,16},{1,9},{9,1},{17,25},{25,17},{2,10},{10... | collective-permute-start | bytes 12296 | tf_op jit(solution)/shard_map/ppermute | solution.py:424
  119.8 1.5 %collective-permute-start.42 = (f32[8,128]{1,0:T(8,128)S(1)}, f32[8,128]{1,0:T(8,128)S(1)}, u32[]{:S(2)}, u32[]{:S(2)}) collective-permute-start(f32[8,128]{1,0:T(8,128)S(1)} %norm.1.refs_0_), channel_id=1, source_target_pairs={{0,24},{8,16},{16,8},{24,0},{1,25},{9,17},{17,9},{25,1},{2,26},{10... | collective-permute-start | bytes 12296 | tf_op jit(solution)/shard_map/ppermute | solution.py:424
  121.4 2.0 %collective-permute-done.41.refs_2_ = f32[8,128]{1,0:T(8,128)S(1)} collective-permute-done((f32[8,128]{1,0:T(8,128)S(1)}, f32[8,128]{1,0:T(8,128)S(1)}, u32[]{:S(2)}, u32[]{:S(2)}) %collective-permute-start.41) | collective-permute-done | bytes 4128 | tf_op jit(solution)/shard_map/ppermute | solution.py:424
  126.9 1.5 %unpack.1 = (f32[2,1024,128]{2,1,0:T(8,128)}, f32[2,1024,128]{2,1,0:T(8,128)}) custom-call(f32[1024,128]{1,0:T(8,128)S(1)} %get-tuple-element.156.own_x, f32[1024,128]{1,0:T(8,128)S(1)} %get-tuple-element.157.own_r, bf16[1024,128]{1,0:T(8,128)(2,1)S(1)} %collective-permute-done.43.pair_x, bf16[1024,128]{1,0:T(8,128)(2,1)S(1)} %collective-permute-done.44.pair_r), custom_call_target="tpu_custom_call" | custom-call | tf_op jit(solution)/shard_map/unpack/pallas_call | solution.py:52
  (92 shorter events, 54.2 us)
Async XLA Ops:
  0.6 5.1 %collective-permute-start = (bf16[24,2,128,128]{3,2,1,0:T(8,128)(2,1)}, bf16[24,2,128,128]{3,2,1,0:T(8,128)(2,1)S(1)}, u32[]{:S(2)}, u32[]{:S(2)}) collective-permute-start(bf16[24,2,128,128]{3,2,1,0:T(8,128)(2,1)} %bitcast.11), channel_id=1, source_target_pairs={{0,1},{1,0},{2,3},{3,2},{4,5},{5,4},{6,7},{7,6},{8,9},{9,8},{10,11... | collective-permute-start | bytes 4718600 | tf_op jit(solution)/shard_map/ppermute | solution.py:424
  6.8 6.9 %collective-permute-start.4 = (bf16[512,128]{1,0:T(8,128)(2,1)S(1)}, bf16[512,128]{1,0:T(8,128)(2,1)S(1)}, u32[]{:S(2)}, u32[]{:S(2)}) collective-permute-start(bf16[512,128]{1,0:T(8,128)(2,1)S(1)} %get-tuple-element.91), channel_id=1, source_target_pairs={{0,8},{8,0},{16,24},{24,16},{1,9},{9,1},{17,25},{25,17},{2,10},{10... | collective-permute-start | bytes 393224 | tf_op jit(solution)/shard_map/ppermute | solution.py:424
  9.8 7.0 %collective-permute-start.5 = (bf16[512,128]{1,0:T(8,128)(2,1)S(1)}, bf16[512,128]{1,0:T(8,128)(2,1)S(1)}, u32[]{:S(2)}, u32[]{:S(2)}) collective-permute-start(bf16[512,128]{1,0:T(8,128)(2,1)S(1)} %get-tuple-element.92), channel_id=1, source_target_pairs={{0,16},{8,24},{16,0},{24,8},{1,17},{9,25},{17,1},{25,9},{2,18},{10... | collective-permute-start | bytes 393224 | tf_op jit(solution)/shard_map/ppermute | solution.py:424
  11.3 6.9 %collective-permute-start.6 = (bf16[512,128]{1,0:T(8,128)(2,1)S(1)}, bf16[512,128]{1,0:T(8,128)(2,1)S(1)}, u32[]{:S(2)}, u32[]{:S(2)}) collective-permute-start(bf16[512,128]{1,0:T(8,128)(2,1)S(1)} %get-tuple-element.93), channel_id=1, source_target_pairs={{0,24},{8,16},{16,8},{24,0},{1,25},{9,17},{17,9},{25,1},{2,26},{10... | collective-permute-start | bytes 393224 | tf_op jit(solution)/shard_map/ppermute | solution.py:424
  18.3 6.3 %collective-permute-start.9 = (bf16[512,128]{1,0:T(8,128)(2,1)S(1)}, bf16[512,128]{1,0:T(8,128)(2,1)S(1)}, u32[]{:S(2)}, u32[]{:S(2)}) collective-permute-start(bf16[512,128]{1,0:T(8,128)(2,1)S(1)} %get-tuple-element.94.refs_2_.refs_8_), channel_id=1, source_target_pairs={{0,8},{8,0},{16,24},{24,16},{1,9},{9,1},{17,25},{25,17},{2,10},{10... | collective-permute-start | bytes 393224 | tf_op jit(solution)/shard_map/ppermute | solution.py:424
  19.1 6.6 %collective-permute-start.7 = (bf16[512,128]{1,0:T(8,128)(2,1)S(1)}, bf16[512,128]{1,0:T(8,128)(2,1)S(1)}, u32[]{:S(2)}, u32[]{:S(2)}) collective-permute-start(bf16[512,128]{1,0:T(8,128)(2,1)S(1)} %get-tuple-element.94.refs_2_.refs_8_), channel_id=1, source_target_pairs={{0,16},{8,24},{16,0},{24,8},{1,17},{9,25},{17,1},{25,9},{2,18},{10... | collective-permute-start | bytes 393224 | tf_op jit(solution)/shard_map/ppermute | solution.py:424
  20.7 5.9 %collective-permute-start.8 = (bf16[512,128]{1,0:T(8,128)(2,1)S(1)}, bf16[512,128]{1,0:T(8,128)(2,1)S(1)}, u32[]{:S(2)}, u32[]{:S(2)}) collective-permute-start(bf16[512,128]{1,0:T(8,128)(2,1)S(1)} %get-tuple-element.94.refs_2_.refs_8_), channel_id=1, source_target_pairs={{0,24},{8,16},{16,8},{24,0},{1,25},{9,17},{17,9},{25,1},{2,26},{10... | collective-permute-start | bytes 393224 | tf_op jit(solution)/shard_map/ppermute | solution.py:424
  27.8 6.8 %collective-permute-start.10 = (bf16[272,128]{1,0:T(8,128)(2,1)S(1)}, bf16[272,128]{1,0:T(8,128)(2,1)S(1)}, u32[]{:S(2)}, u32[]{:S(2)}) collective-permute-start(bf16[272,128]{1,0:T(8,128)(2,1)S(1)} %get-tuple-element.101), channel_id=1, source_target_pairs={{0,6},{1,7},{2,4},{3,5},{4,2},{5,3},{6,0},{7,1},{8,14},{9,15},{10,... | collective-permute-start | bytes 208904 | tf_op jit(solution)/shard_map/ppermute | solution.py:424
  31.9 5.2 %collective-permute-start.12 = (bf16[272,128]{1,0:T(8,128)(2,1)S(1)}, bf16[272,128]{1,0:T(8,128)(2,1)S(1)}, u32[]{:S(2)}, u32[]{:S(2)}) collective-permute-start(bf16[272,128]{1,0:T(8,128)(2,1)S(1)} %get-tuple-element.103), channel_id=1, source_target_pairs={{0,4},{1,5},{2,6},{3,7},{4,0},{5,1},{6,2},{7,3},{8,12},{9,13},{10,... | collective-permute-start | bytes 208904 | tf_op jit(solution)/shard_map/ppermute | solution.py:424
  37.2 6.2 %collective-permute-start.15 = (bf16[256,128]{1,0:T(8,128)(2,1)S(1)}, bf16[256,128]{1,0:T(8,128)(2,1)S(1)}, u32[]{:S(2)}, u32[]{:S(2)}) collective-permute-start(bf16[256,128]{1,0:T(8,128)(2,1)S(1)} %get-tuple-element.104.refs_2_.refs_20_), channel_id=1, source_target_pairs={{0,6},{1,7},{2,4},{3,5},{4,2},{5,3},{6,0},{7,1},{8,14},{9,15},{10,... | collective-permute-start | bytes 196616 | tf_op jit(solution)/shard_map/ppermute | solution.py:424
  38.9 5.6 %collective-permute-start.13 = (bf16[256,128]{1,0:T(8,128)(2,1)S(1)}, bf16[256,128]{1,0:T(8,128)(2,1)S(1)}, u32[]{:S(2)}, u32[]{:S(2)}) collective-permute-start(bf16[256,128]{1,0:T(8,128)(2,1)S(1)} %get-tuple-element.104.refs_2_.refs_20_), channel_id=1, source_target_pairs={{0,2},{1,3},{2,0},{3,1},{4,6},{5,7},{6,4},{7,5},{8,10},{9,11},{10,... | collective-permute-start | bytes 196616 | tf_op jit(solution)/shard_map/ppermute | solution.py:424
  39.4 5.2 %collective-permute-start.14 = (bf16[256,128]{1,0:T(8,128)(2,1)S(1)}, bf16[256,128]{1,0:T(8,128)(2,1)S(1)}, u32[]{:S(2)}, u32[]{:S(2)}) collective-permute-start(bf16[256,128]{1,0:T(8,128)(2,1)S(1)} %get-tuple-element.104.refs_2_.refs_20_), channel_id=1, source_target_pairs={{0,4},{1,5},{2,6},{3,7},{4,0},{5,1},{6,2},{7,3},{8,12},{9,13},{10,... | collective-permute-start | bytes 196616 | tf_op jit(solution)/shard_map/ppermute | solution.py:424
  45.7 5.1 %collective-permute-start.16 = (bf16[528,128]{1,0:T(8,128)(2,1)S(1)}, bf16[528,128]{1,0:T(8,128)(2,1)S(1)}, u32[]{:S(2)}, u32[]{:S(2)}) collective-permute-start(bf16[528,128]{1,0:T(8,128)(2,1)S(1)} %get-tuple-element.111), channel_id=1, source_target_pairs={{0,8},{8,0},{16,24},{24,16},{1,9},{9,1},{17,25},{25,17},{2,10},{10... | collective-permute-start | bytes 405512 | tf_op jit(solution)/shard_map/ppermute | solution.py:424
  48.0 7.2 %collective-permute-start.18 = (bf16[528,128]{1,0:T(8,128)(2,1)S(1)}, bf16[528,128]{1,0:T(8,128)(2,1)S(1)}, u32[]{:S(2)}, u32[]{:S(2)}) collective-permute-start(bf16[528,128]{1,0:T(8,128)(2,1)S(1)} %get-tuple-element.113), channel_id=1, source_target_pairs={{0,24},{8,16},{16,8},{24,0},{1,25},{9,17},{17,9},{25,1},{2,26},{10... | collective-permute-start | bytes 405512 | tf_op jit(solution)/shard_map/ppermute | solution.py:424
  55.2 5.0 %collective-permute-start.21 = (bf16[512,128]{1,0:T(8,128)(2,1)S(1)}, bf16[512,128]{1,0:T(8,128)(2,1)S(1)}, u32[]{:S(2)}, u32[]{:S(2)}) collective-permute-start(bf16[512,128]{1,0:T(8,128)(2,1)S(1)} %get-tuple-element.116.refs_2_.refs_12_), channel_id=1, source_target_pairs={{0,8},{8,0},{16,24},{24,16},{1,9},{9,1},{17,25},{25,17},{2,10},{10... | collective-permute-start | bytes 393224 | tf_op jit(solution)/shard_map/ppermute | solution.py:424
  56.4 6.4 %collective-permute-start.19 = (bf16[512,128]{1,0:T(8,128)(2,1)S(1)}, bf16[512,128]{1,0:T(8,128)(2,1)S(1)}, u32[]{:S(2)}, u32[]{:S(2)}) collective-permute-start(bf16[512,128]{1,0:T(8,128)(2,1)S(1)} %get-tuple-element.116.refs_2_.refs_12_), channel_id=1, source_target_pairs={{0,16},{8,24},{16,0},{24,8},{1,17},{9,25},{17,1},{25,9},{2,18},{10... | collective-permute-start | bytes 393224 | tf_op jit(solution)/shard_map/ppermute | solution.py:424
  56.6 6.2 %collective-permute-start.20 = (bf16[512,128]{1,0:T(8,128)(2,1)S(1)}, bf16[512,128]{1,0:T(8,128)(2,1)S(1)}, u32[]{:S(2)}, u32[]{:S(2)}) collective-permute-start(bf16[512,128]{1,0:T(8,128)(2,1)S(1)} %get-tuple-element.116.refs_2_.refs_12_), channel_id=1, source_target_pairs={{0,24},{8,16},{16,8},{24,0},{1,25},{9,17},{17,9},{25,1},{2,26},{10... | collective-permute-start | bytes 393224 | tf_op jit(solution)/shard_map/ppermute | solution.py:424
  64.0 6.3 %collective-permute-start.22 = (bf16[272,128]{1,0:T(8,128)(2,1)S(1)}, bf16[272,128]{1,0:T(8,128)(2,1)S(1)}, u32[]{:S(2)}, u32[]{:S(2)}) collective-permute-start(bf16[272,128]{1,0:T(8,128)(2,1)S(1)} %get-tuple-element.123), channel_id=1, source_target_pairs={{0,6},{1,7},{2,4},{3,5},{4,2},{5,3},{6,0},{7,1},{8,14},{9,15},{10,... | collective-permute-start | bytes 208904 | tf_op jit(solution)/shard_map/ppermute | solution.py:424
  67.8 6.2 %collective-permute-start.23 = (bf16[272,128]{1,0:T(8,128)(2,1)S(1)}, bf16[272,128]{1,0:T(8,128)(2,1)S(1)}, u32[]{:S(2)}, u32[]{:S(2)}) collective-permute-start(bf16[272,128]{1,0:T(8,128)(2,1)S(1)} %get-tuple-element.124), channel_id=1, source_target_pairs={{0,2},{1,3},{2,0},{3,1},{4,6},{5,7},{6,4},{7,5},{8,10},{9,11},{10,... | collective-permute-start | bytes 208904 | tf_op jit(solution)/shard_map/ppermute | solution.py:424
  67.8 6.8 %collective-permute-start.24 = (bf16[272,128]{1,0:T(8,128)(2,1)S(1)}, bf16[272,128]{1,0:T(8,128)(2,1)S(1)}, u32[]{:S(2)}, u32[]{:S(2)}) collective-permute-start(bf16[272,128]{1,0:T(8,128)(2,1)S(1)} %get-tuple-element.125), channel_id=1, source_target_pairs={{0,4},{1,5},{2,6},{3,7},{4,0},{5,1},{6,2},{7,3},{8,12},{9,13},{10,... | collective-permute-start | bytes 208904 | tf_op jit(solution)/shard_map/ppermute | solution.py:424
  74.6 6.1 %collective-permute-start.27 = (bf16[256,128]{1,0:T(8,128)(2,1)S(1)}, bf16[256,128]{1,0:T(8,128)(2,1)S(1)}, u32[]{:S(2)}, u32[]{:S(2)}) collective-permute-start(bf16[256,128]{1,0:T(8,128)(2,1)S(1)} %get-tuple-element.127.refs_2_.refs_24_), channel_id=1, source_target_pairs={{0,6},{1,7},{2,4},{3,5},{4,2},{5,3},{6,0},{7,1},{8,14},{9,15},{10,... | collective-permute-start | bytes 196616 | tf_op jit(solution)/shard_map/ppermute | solution.py:424
  77.2 5.2 %collective-permute-start.26 = (bf16[256,128]{1,0:T(8,128)(2,1)S(1)}, bf16[256,128]{1,0:T(8,128)(2,1)S(1)}, u32[]{:S(2)}, u32[]{:S(2)}) collective-permute-start(bf16[256,128]{1,0:T(8,128)(2,1)S(1)} %get-tuple-element.127.refs_2_.refs_24_), channel_id=1, source_target_pairs={{0,4},{1,5},{2,6},{3,7},{4,0},{5,1},{6,2},{7,3},{8,12},{9,13},{10,... | collective-permute-start | bytes 196616 | tf_op jit(solution)/shard_map/ppermute | solution.py:424
  83.5 6.2 %collective-permute-start.28 = (bf16[528,128]{1,0:T(8,128)(2,1)S(1)}, bf16[528,128]{1,0:T(8,128)(2,1)S(1)}, u32[]{:S(2)}, u32[]{:S(2)}) collective-permute-start(bf16[528,128]{1,0:T(8,128)(2,1)S(1)} %get-tuple-element.134), channel_id=1, source_target_pairs={{0,8},{8,0},{16,24},{24,16},{1,9},{9,1},{17,25},{25,17},{2,10},{10... | collective-permute-start | bytes 405512 | tf_op jit(solution)/shard_map/ppermute | solution.py:424
  84.8 7.7 %collective-permute-start.29 = (bf16[528,128]{1,0:T(8,128)(2,1)S(1)}, bf16[528,128]{1,0:T(8,128)(2,1)S(1)}, u32[]{:S(2)}, u32[]{:S(2)}) collective-permute-start(bf16[528,128]{1,0:T(8,128)(2,1)S(1)} %get-tuple-element.135), channel_id=1, source_target_pairs={{0,16},{8,24},{16,0},{24,8},{1,17},{9,25},{17,1},{25,9},{2,18},{10... | collective-permute-start | bytes 405512 | tf_op jit(solution)/shard_map/ppermute | solution.py:424
  86.2 6.3 %collective-permute-start.30 = (bf16[528,128]{1,0:T(8,128)(2,1)S(1)}, bf16[528,128]{1,0:T(8,128)(2,1)S(1)}, u32[]{:S(2)}, u32[]{:S(2)}) collective-permute-start(bf16[528,128]{1,0:T(8,128)(2,1)S(1)} %get-tuple-element.136), channel_id=1, source_target_pairs={{0,24},{8,16},{16,8},{24,0},{1,25},{9,17},{17,9},{25,1},{2,26},{10... | collective-permute-start | bytes 405512 | tf_op jit(solution)/shard_map/ppermute | solution.py:424
  92.6 5.0 %collective-permute-start.33 = (bf16[512,128]{1,0:T(8,128)(2,1)S(1)}, bf16[512,128]{1,0:T(8,128)(2,1)S(1)}, u32[]{:S(2)}, u32[]{:S(2)}) collective-permute-start(bf16[512,128]{1,0:T(8,128)(2,1)S(1)} %get-tuple-element.139.refs_2_.refs_16_), channel_id=1, source_target_pairs={{0,8},{8,0},{16,24},{24,16},{1,9},{9,1},{17,25},{25,17},{2,10},{10... | collective-permute-start | bytes 393224 | tf_op jit(solution)/shard_map/ppermute | solution.py:424
  93.2 5.5 %collective-permute-start.31 = (bf16[512,128]{1,0:T(8,128)(2,1)S(1)}, bf16[512,128]{1,0:T(8,128)(2,1)S(1)}, u32[]{:S(2)}, u32[]{:S(2)}) collective-permute-start(bf16[512,128]{1,0:T(8,128)(2,1)S(1)} %get-tuple-element.139.refs_2_.refs_16_), channel_id=1, source_target_pairs={{0,16},{8,24},{16,0},{24,8},{1,17},{9,25},{17,1},{25,9},{2,18},{10... | collective-permute-start | bytes 393224 | tf_op jit(solution)/shard_map/ppermute | solution.py:424
  94.6 5.9 %collective-permute-start.32 = (bf16[512,128]{1,0:T(8,128)(2,1)S(1)}, bf16[512,128]{1,0:T(8,128)(2,1)S(1)}, u32[]{:S(2)}, u32[]{:S(2)}) collective-permute-start(bf16[512,128]{1,0:T(8,128)(2,1)S(1)} %get-tuple-element.139.refs_2_.refs_16_), channel_id=1, source_target_pairs={{0,24},{8,16},{16,8},{24,0},{1,25},{9,17},{17,9},{25,1},{2,26},{10... | collective-permute-start | bytes 393224 | tf_op jit(solution)/shard_map/ppermute | solution.py:424
  101.8 6.2 %collective-permute-start.34 = (bf16[272,128]{1,0:T(8,128)(2,1)S(1)}, bf16[272,128]{1,0:T(8,128)(2,1)S(1)}, u32[]{:S(2)}, u32[]{:S(2)}) collective-permute-start(bf16[272,128]{1,0:T(8,128)(2,1)S(1)} %get-tuple-element.146), channel_id=1, source_target_pairs={{0,6},{1,7},{2,4},{3,5},{4,2},{5,3},{6,0},{7,1},{8,14},{9,15},{10,... | collective-permute-start | bytes 208904 | tf_op jit(solution)/shard_map/ppermute | solution.py:424
  104.3 5.2 %collective-permute-start.36 = (bf16[272,128]{1,0:T(8,128)(2,1)S(1)}, bf16[272,128]{1,0:T(8,128)(2,1)S(1)}, u32[]{:S(2)}, u32[]{:S(2)}) collective-permute-start(bf16[272,128]{1,0:T(8,128)(2,1)S(1)} %get-tuple-element.148), channel_id=1, source_target_pairs={{0,4},{1,5},{2,6},{3,7},{4,0},{5,1},{6,2},{7,3},{8,12},{9,13},{10,... | collective-permute-start | bytes 208904 | tf_op jit(solution)/shard_map/ppermute | solution.py:424
  109.5 6.3 %collective-permute-start.37 = (bf16[256,128]{1,0:T(8,128)(2,1)S(1)}, bf16[256,128]{1,0:T(8,128)(2,1)S(1)}, u32[]{:S(2)}, u32[]{:S(2)}) collective-permute-start(bf16[256,128]{1,0:T(8,128)(2,1)S(1)} %get-tuple-element.151.refs_0_.refs_28_), channel_id=1, source_target_pairs={{0,6},{1,7},{2,4},{3,5},{4,2},{5,3},{6,0},{7,1},{8,14},{9,15},{10,... | collective-permute-start | bytes 196616 | tf_op jit(solution)/shard_map/ppermute | solution.py:424
  112.2 5.2 %collective-permute-start.39 = (bf16[256,128]{1,0:T(8,128)(2,1)S(1)}, bf16[256,128]{1,0:T(8,128)(2,1)S(1)}, u32[]{:S(2)}, u32[]{:S(2)}) collective-permute-start(bf16[256,128]{1,0:T(8,128)(2,1)S(1)} %get-tuple-element.151.refs_0_.refs_28_), channel_id=1, source_target_pairs={{0,4},{1,5},{2,6},{3,7},{4,0},{5,1},{6,2},{7,3},{8,12},{9,13},{10,... | collective-permute-start | bytes 196616 | tf_op jit(solution)/shard_map/ppermute | solution.py:424
  (16 other events, 105.9 us)
